TPU v7x, 32 devices: a whole 2x2x4 slice. The times are simulated.
32 devices in a mesh: groups: 2 (over x), dp: 16 (over z, y, core).
Axes of the slice: x: 2, y: 2, z: 4, core: 2. Of those that a mesh axis runs over, the one named last changes fastest.
Arguments:
- activations: bfloat16 [12288, 16384], P(('groups', 'dp')), parts along dimension 0, may hold values from -18 to 18
- labels: int32 [12288], P(('groups', 'dp')), parts along dimension 0, may hold values from 0 to 63, as said below
- counts: int32 [12288], P(('groups', 'dp')), parts along dimension 0, may hold values from 1 to 4
Outputs:
- solution: float32 [32768, 64], P(('groups', 'dp')), parts along dimension 0
- residual: float32 [32768, 64], P(('groups', 'dp')), parts along dimension 0
There are 2 independent parts, one for each index of `groups`. A program takes and returns all parts, laid end to end along the dimension named above; each array names one. Nothing has to cross between parts.
Inputs may be any that keep to these rules, and one draw needn't show every extreme that they name: `labels`: concept index of each row; every concept of 0 to 63 names at least one row. `counts`: integer sample weight of each row.
All inputs are finite; a program needn't handle non-finite values.
Results may differ from a plain program's by a relative error of at most 0.012.
The roundings to bfloat16 on the way count: a program that leaves them out, or rounds other values in their place, can miss the bound.
Values may be sent and summed in bfloat16 or wider, within the bound.
No kernel may reach another device: no remote copies, remote signals or barrier semaphores. Data moves between devices by JAX's collectives and lax.ppermute only.
A program may use at most 64 MiB of HBM per device.

v0:
```python
import jax
import jax.numpy as jnp
from jax import lax
from jax.sharding import PartitionSpec as P

K = 64
ITERS = 2


RIDGE = 0.1


def precise(left_side, right_side):
    return jnp.dot(
        left_side, right_side, precision=lax.Precision.HIGHEST, preferred_element_type=jnp.float32
    )


def symmetric(matrix):
    return 0.5 * (matrix + matrix.T)


def solve_positive(matrix, target):
    return jax.scipy.linalg.cho_solve((jnp.linalg.cholesky(matrix), True), target)


def contract_rows(left_side, right_side):
    return lax.dot_general(
        left_side, right_side, (((0,), (0,)), ((), ())), preferred_element_type=jnp.float32
    )


def per_device(activations, labels, counts):
    weights = counts.astype(jnp.float32)
    classes = jnp.arange(K, dtype=jnp.int32)
    member_full = jnp.where(labels[:, None] == classes[None, :], weights[:, None], jnp.float32(0.0))
    local_weight = jnp.sum(member_full, axis=0)
    member = member_full.astype(jnp.bfloat16)
    class_sums = lax.psum_scatter(
        contract_rows(activations, member), "dp", scatter_dimension=0, tiled=True
    )
    class_weight = lax.psum(local_weight, "dp")
    total_weight = jnp.sum(class_weight)
    class_means = class_sums / class_weight[None, :]
    mean_diff = class_means * jnp.sqrt(class_weight)[None, :]
    solution = jnp.zeros_like(mean_diff)
    residual = mean_diff
    direction = mean_diff
    current = symmetric(lax.psum(precise(residual.T, residual), "dp"))
    for iteration in range(ITERS):
        probed = jnp.dot(
            activations,
            lax.all_gather(direction.astype(jnp.bfloat16), "dp", axis=0, tiled=True),
            preferred_element_type=jnp.float32,
        )
        weighted = (weights[:, None] * probed).astype(jnp.bfloat16)
        panel = lax.psum_scatter(
            contract_rows(activations, weighted), "dp", scatter_dimension=0, tiled=True
        )
        cross, along_panel, along_along = lax.psum(
            (
                precise(class_means.T, direction),
                precise(direction.T, panel),
                precise(direction.T, direction),
            ),
            "dp",
        )
        scaled = class_weight[:, None] * cross
        curvature = symmetric(
            (along_panel - precise(cross.T, scaled)) / total_weight + RIDGE * along_along
        )
        step_alpha = solve_positive(curvature, current)
        image = (panel - precise(class_means, scaled)) / total_weight + RIDGE * direction
        solution = solution + precise(direction, step_alpha)
        residual = residual - precise(image, step_alpha)
        renewed = current
        if iteration + 1 < ITERS:
            renewed = symmetric(lax.psum(precise(residual.T, residual), "dp"))
        if iteration + 1 < ITERS:
            step_beta = solve_positive(current, renewed)
            direction = residual + precise(direction, step_beta)
            current = renewed
    return (solution, residual)


def solution(mesh):
    in_specs = (P(("groups", "dp"), None), P(("groups", "dp")), P(("groups", "dp")))
    out_specs = (P(("groups", "dp"), None), P(("groups", "dp"), None))
    return jax.shard_map(
        per_device, mesh=mesh, in_specs=in_specs, out_specs=out_specs, check_vma=False
    )
```

profile of v0, /device:TPU:0, one launch (start us, length us, event | category | flops | bytes accessed | tf_op | source)
XLA Modules:
  0.0 587.8 jit_solution(6999212861251710433)
XLA Ops:
  7.2 0.7 convert_element_type.20
  7.9 8.9 %convolution_bitcast_fusion.2 = f32[16384,64]{0,1:T(8,128)} fusion(bf16[384,16384]{1,0:T(8,128)(2,1)} %param.6, f32[384]{0:T(512)S(1)} %convert_element_type.20, s32[384]{0:T(512)} %param.7), kind=kOutput, calls=%fused_computation.2 | convolution fusion | flops 805355520 | bytes 16780288 | tf_op jit(solution)/shard_map/dot_general | solution.py:28
  17.0 35.0 %psum.59 = f32[64]{0:T(128)S(1)} all-reduce(f32[64]{0:T(128)S(1)} %select_reduce_fusion), channel_id=1, replica_groups=mesh['groups'=2,'dp'=16] {'dp'}, use_global_device_ids=true, to_apply=%region_2.3 | all-reduce | flops 64 | bytes 512 | tf_op jit(solution)/shard_map/psum | solution.py:42
  52.0 0.6 fusion.62
  52.6 39.5 %reduce-scatter.4.cloned.1.call-done = f32[1024,64]{0,1:T(8,128)} async-done(((f32[16384,64]{0,1:T(8,128)}), f32[1024,64]{0,1:T(8,128)}) %reduce-scatter.4.cloned.1.call-update) | async-done | bytes 262160 | tf_op jit(solution)/shard_map/reduce_scatter | solution.py:39
  92.1 1.7 multiply_convert_fusion
  93.9 41.7 %all-gather.3.cloned.1.call-done = bf16[16384,64]{0,1:T(8,128)(2,1)} async-done(((bf16[1024,64]{0,1:T(8,128)(2,1)}), bf16[16384,64]{0,1:T(8,128)(2,1)}) %all-gather.3.cloned.1.call-update) | async-done | bytes 2097168 | tf_op jit(solution)/shard_map/all_gather | solution.py:53
  135.5 18.5 %convolution_bitcast_fusion.1 = f32[16384,64]{0,1:T(8,128)} fusion(bf16[384,16384]{1,0:T(8,128)(2,1)} %param.6, bf16[16384,64]{0,1:T(8,128)(2,1)} %all-gather.3.cloned.1.call-done, f32[384]{0:T(512)S(1)} %convert_element_type.20), kind=kOutput, calls=%fused_computation.1 | convolution fusion | flops 1610661888 | bytes 18875904 | tf_op jit(solution)/shard_map/dot_general | solution.py:28
  154.1 0.5 fusion.13
  154.5 0.5 fusion.15
  155.0 70.3 %reduce-scatter.6.cloned.1.call-done = f32[1024,64]{0,1:T(8,128)} async-done(((f32[16384,64]{0,1:T(8,128)}), f32[1024,64]{0,1:T(8,128)}) %reduce-scatter.6.cloned.1.call-update) | async-done | bytes 262160 | tf_op jit(solution)/shard_map/reduce_scatter | solution.py:57
  225.3 1.4 fusion.17
  226.7 59.2 %all-reduce.1 = (f32[64,64]{1,0:T(8,128)S(1)}, f32[64,64]{1,0:T(8,128)S(1)}, f32[64,64]{1,0:T(8,128)S(1)}) all-reduce(f32[64,64]{1,0:T(8,128)S(1)} %fusion.13, f32[64,64]{1,0:T(8,128)S(1)} %fusion.17, f32[64,64]{1,0:T(8,128)S(1)} %fusion.15), channel_id=1, replica_groups=mesh['groups'=2,'dp'=16] {'dp'}, use_global_device_ids=true, to_apply=%region_7.8 | all-reduce | flops 12288 | bytes 98304 | tf_op jit(solution)/shard_map/psum | solution.py:60
  286.1 5.8 cholesky.70
  292.0 0.6 compare_reduce_fusion.1
  292.6 0.7 fusion.32
  293.3 4.9 custom-call.10
  298.2 0.9 fusion.9
  299.4 5.9 cholesky.59
  305.3 0.6 compare_reduce_fusion.2
  305.9 0.7 fusion.31
  306.6 4.9 custom-call.9
  311.5 0.2 fusion.48
  311.9 2.1 fusion.3
  314.0 0.4 convolution_subtract_fusion.2
  314.4 0.4 fusion.64
  314.8 57.6 %psum.63 = f32[64,64]{1,0:T(8,128)S(1)} all-reduce(f32[64,64]{1,0:T(8,128)S(1)} %fusion.64), channel_id=1, replica_groups=mesh['groups'=2,'dp'=16] {'dp'}, use_global_device_ids=true, to_apply=%region_10.13 | all-reduce | flops 4096 | bytes 32768 | tf_op jit(solution)/shard_map/psum | solution.py:78
  372.5 0.2 fusion.42
  372.8 0.2 fusion.40
  372.9 1.1 fusion.63
  374.1 0.3 reduce-scatter.8.cloned.1.call-start
  374.3 38.6 %all-gather.5.cloned.1.call-done = bf16[16384,64]{0,1:T(8,128)(2,1)} async-done(((bf16[1024,64]{0,1:T(8,128)(2,1)}), bf16[16384,64]{0,1:T(8,128)(2,1)}) %all-gather.5.cloned.1.call-update) | async-done | bytes 2097168 | tf_op jit(solution)/shard_map/all_gather | solution.py:53
  412.9 18.5 %convolution_bitcast_fusion = f32[16384,64]{0,1:T(8,128)} fusion(bf16[384,16384]{1,0:T(8,128)(2,1)} %param.6, bf16[16384,64]{0,1:T(8,128)(2,1)} %all-gather.5.cloned.1.call-done, f32[384]{0:T(512)S(1)} %convert_element_type.20), kind=kOutput, calls=%fused_computation | convolution fusion | flops 1610661888 | bytes 18875904 | tf_op jit(solution)/shard_map/dot_general | solution.py:28
  431.4 0.4 fusion.66
  431.7 0.4 fusion.61
  432.2 0.5 fusion.11
  432.6 70.1 %reduce-scatter.8.cloned.1.call-done = f32[1024,64]{0,1:T(8,128)} async-done(((f32[16384,64]{0,1:T(8,128)}), f32[1024,64]{0,1:T(8,128)}) %reduce-scatter.8.cloned.1.call-update) | async-done | bytes 262160 | tf_op jit(solution)/shard_map/reduce_scatter | solution.py:57
  502.8 1.3 fusion.65
  504.1 59.1 %all-reduce = (f32[64,64]{1,0:T(8,128)S(1)}, f32[64,64]{1,0:T(8,128)S(1)}, f32[64,64]{1,0:T(8,128)S(1)}) all-reduce(f32[64,64]{1,0:T(8,128)S(1)} %fusion.65, f32[64,64]{1,0:T(8,128)S(1)} %fusion.61, f32[64,64]{1,0:T(8,128)S(1)} %fusion.66), channel_id=1, replica_groups=mesh['groups'=2,'dp'=16] {'dp'}, use_global_device_ids=true, to_apply=%region_12.15 | all-reduce | flops 12288 | bytes 98304 | tf_op jit(solution)/shard_map/psum | solution.py:60
  563.2 0.9 fusion.7
  564.4 5.8 cholesky.81
  570.3 0.6 compare_reduce_fusion
  570.9 0.7 fusion.33
  571.6 4.9 custom-call.11
  576.5 0.2 fusion.36
  576.9 2.1 fusion.1
  579.0 1.1 convolution_subtract_fusion
  580.1 1.1 convolution_add_fusion
  (35 shorter events, 1.5 us)
Async XLA Ops:
  7.2 9.7 %copy-start.1 = (s32[384]{0:T(512)S(1)}, s32[384]{0:T(512)}, u32[]{:S(2)}) copy-start(s32[384]{0:T(512)} %param.7) | copy-start | bytes 4612
  7.2 84.9 %reduce-scatter.4.cloned.1.call-start = ((), (), s32[]{:S(2)}) async-start(), calls=%async_computation.3 | async-start | bytes 4456448 | tf_op jit(solution)/shard_map/reduce_scatter | solution.py:39
  16.8 118.7 %all-gather.3.cloned.1.call-start = ((), (), s32[]{:S(2)}) async-start(), calls=%async_computation.4 | async-start | bytes 2228224 | tf_op jit(solution)/shard_map/all_gather | solution.py:53
  93.8 60.3 %copy-start = (f32[1024,64]{0,1:T(8,128)S(1)}, f32[1024,64]{0,1:T(8,128)}, u32[]{:S(2)}) copy-start(f32[1024,64]{0,1:T(8,128)} %reduce-scatter.4.cloned.1.call-done) | copy-start | bytes 786436
  93.8 131.5 %reduce-scatter.6.cloned.1.call-start = ((), (), s32[]{:S(2)}) async-start(), calls=%async_computation.5 | async-start | bytes 4456448 | tf_op jit(solution)/shard_map/reduce_scatter | solution.py:57
  154.0 258.9 %all-gather.5.cloned.1.call-start = ((), (), s32[]{:S(2)}) async-start(), calls=%async_computation.6 | async-start | bytes 2228224 | tf_op jit(solution)/shard_map/all_gather | solution.py:53
  374.1 128.7 %reduce-scatter.8.cloned.1.call-start = ((), (), s32[]{:S(2)}) async-start(), calls=%async_computation.7 | async-start | bytes 4456448 | tf_op jit(solution)/shard_map/reduce_scatter | solution.py:57
Sparse Core Ops, SparseCore 0:
  16.9 75.1 reduce-scatter.3
  95.1 40.4 all-gather.2
  154.1 71.1 reduce-scatter.5
  374.2 38.6 all-gather.4
  431.5 71.2 reduce-scatter.7
where the time goes:
time: 588 us
  waiting for transfers between devices  260 us (44%)
  blocking collectives  211 us (36%)
  matrix products  62 us (11%)
  other arithmetic  39.4 us (7%)
  between operations  14.1 us (2%)
    reduce_scatter x2, waiting for transfers between devices, per_device(): lax.psum_scatter(contract_rows(activations, weighted), 'dp', scatter_dime...  140 us
    psum x2, blocking collectives, per_device(): lax.psum((precise(class_means.T, direction), precise(direction.T, panel),...  118 us
    all_gather x2, waiting for transfers between devices, per_device(): lax.all_gather(direction.astype(jnp.bfloat16), 'dp', axis=0, tiled=True)  80.2 us
    psum x1, blocking collectives, per_device(): renewed = symmetric(lax.psum(precise(residual.T, residual), 'dp'))  57.6 us
    dot_general x3, matrix products, contract_rows(): lax.dot_general(left_side, right_side, (((0,), (0,)), ((), ())), preferre...  45.8 us
    reduce_scatter x1, waiting for transfers between devices, per_device(): lax.psum_scatter(contract_rows(activations, member), 'dp', scatter_dimens...  39.5 us
    psum x1, blocking collectives, per_device(): class_weight = lax.psum(local_weight, 'dp')  35 us
    another operation x9, other arithmetic, solve_positive(): jnp.linalg.cholesky(matrix)  19.6 us
  transfers between devices with their start and end apart: 5, of which 5 were waited for; matrix products, arithmetic and copies ran while one was open for 0% of the time, Pallas kernels for 0%

commit v1 on v0

v1 whole, which is shorter than its diff:
```python
import functools

import jax
import jax.numpy as jnp
from jax import lax
from jax.experimental import pallas as pl
from jax.experimental.pallas import tpu as pltpu
from jax.sharding import PartitionSpec as P

K = 64
HALF = K // 2
RIDGE = 0.1
BOUND = 18.0
TOP = 60000.0
F32, BF16, F16 = jnp.float32, jnp.bfloat16, jnp.float16


def precise(left, right):
    return jnp.dot(left, right, precision=lax.Precision.HIGHEST, preferred_element_type=F32)


def outer(left, right):
    return lax.dot_general(
        left, right, (((1,), (1,)), ((), ())), precision=lax.Precision.HIGHEST, preferred_element_type=F32
    )


def symmetric(matrix):
    return 0.5 * (matrix + matrix.T)


def solve_positive(matrix, target):
    return jax.scipy.linalg.cho_solve((jnp.linalg.cholesky(matrix), True), target)


def swap(value, bit, n):
    return lax.ppermute(value, "dp", [(i, i ^ bit) for i in range(n)])


def total(value, n):
    bit = 1
    while bit < n:
        value = value + swap(value, bit, n)
        bit *= 2
    return value


def hop_bits(n):
    bits = [1 << i for i in range(1, n.bit_length() - 1)]
    return bits, bits[1:] + bits[:1]


def _rel(step, shifts):
    j = 0
    for place, shift in enumerate(shifts):
        j = j | (((step >> place) & 1) << shift)
    return j


def _pos(j, shifts):
    p = 0
    for place, shift in enumerate(shifts):
        p = p | (((j >> shift) & 1) << place)
    return p


def sums_kernel(me, labels, counts, acts, out, member):
    @pl.when(pl.program_id(0) == 0)
    def _():
        concept = lax.broadcasted_iota(jnp.int32, member.shape, 0)
        member[...] = jnp.where(labels[...] == concept, counts[...].astype(F32), 0.0).astype(BF16)

    out[0] = jnp.dot(member[...], acts[...], preferred_element_type=F32)


def class_sums(me, labels, counts, acts, n, half):
    rows, d = acts.shape
    f = d // n
    return pl.pallas_call(
        sums_kernel,
        out_shape=jax.ShapeDtypeStruct((n // 2, K, f), F32),
        grid_spec=pltpu.PrefetchScalarGridSpec(
            num_scalar_prefetch=1,
            grid=(n // 2,),
            in_specs=[
                pl.BlockSpec((1, rows), lambda i, me: (0, 0)),
                pl.BlockSpec((1, rows), lambda i, me: (0, 0)),
                pl.BlockSpec((rows, f), lambda i, me: (0, me[0] ^ (2 * i + half))),
            ],
            out_specs=pl.BlockSpec((1, K, f), lambda i, me: (i, 0, 0)),
            scratch_shapes=[pltpu.VMEM((K, rows), BF16)],
        ),
        compiler_params=pltpu.CompilerParams(vmem_limit_bytes=32 << 20),
        cost_estimate=pl.CostEstimate(flops=K * rows * d, bytes_accessed=rows * d + 2 * K * d, transcendentals=0),
        name="class_sums",
    )(me, labels, counts, acts)


def probe_kernel(me, v_a, v_b, acts, out):
    @pl.when(pl.program_id(0) == 0)
    def _():
        out[...] = jnp.zeros_like(out)

    v = jnp.concatenate([v_a[0], v_b[0]], axis=0)
    out[...] += lax.dot_general(v, acts[...], (((1,), (1,)), ((), ())), preferred_element_type=F32)


def probe(me, v_a, v_b, acts, n, shifts_a, shifts_b):
    rows, d = acts.shape
    f = d // n
    return pl.pallas_call(
        probe_kernel,
        out_shape=jax.ShapeDtypeStruct((K, rows), F32),
        grid_spec=pltpu.PrefetchScalarGridSpec(
            num_scalar_prefetch=1,
            grid=(n // 2,),
            in_specs=[
                pl.BlockSpec((1, HALF, f), lambda i, me: (_pos(_rel(i, shifts_a), shifts_a), 0, 0)),
                pl.BlockSpec((1, HALF, f), lambda i, me: (_pos(_rel(i, shifts_a), shifts_b), 0, 0)),
                pl.BlockSpec((rows, f), lambda i, me: (0, me[0] ^ _rel(i, shifts_a))),
            ],
            out_specs=pl.BlockSpec((K, rows), lambda i, me: (0, 0)),
        ),
        compiler_params=pltpu.CompilerParams(vmem_limit_bytes=32 << 20),
        cost_estimate=pl.CostEstimate(flops=K * rows * d, bytes_accessed=rows * d + K * d, transcendentals=0),
        name="probe",
    )(me, v_a, v_b, acts)


def send_kernel(steps, me, v_a, v_b, acts, start, counts, probed, gram, out, kept, weighted):
    step = pl.program_id(0)

    @pl.when(step == 0)
    def _():
        probed[...] = start[...]

    @pl.when(step < steps)
    def _():
        v = jnp.concatenate([v_a[0], v_b[0]], axis=0)
        kept[step] = acts[...]
        probed[...] += lax.dot_general(v, acts[...], (((1,), (1,)), ((), ())), preferred_element_type=F32)

    @pl.when(step == steps)
    def _():
        weighted[...] = (counts[...].astype(F32) * probed[...]).astype(BF16)
        gram[...] = outer(probed[...], weighted[...].astype(F32))

    @pl.when(step >= steps)
    def _():
        out[0] = jnp.dot(weighted[...], kept[step - steps], preferred_element_type=F32)


def probe_and_send(me, v_a, v_b, acts, start, counts, n, shifts_a, shifts_b):
    rows, d = acts.shape
    f = d // n
    s = n // 2

    def j_of(i):
        return _rel(jnp.minimum(i, s - 1), shifts_a)

    out_pos = [shift for shift in range(1, n.bit_length() - 1)]
    return pl.pallas_call(
        functools.partial(send_kernel, s),
        out_shape=(
            jax.ShapeDtypeStruct((K, rows), F32),
            jax.ShapeDtypeStruct((K, K), F32),
            jax.ShapeDtypeStruct((s, K, f), F32),
        ),
        grid_spec=pltpu.PrefetchScalarGridSpec(
            num_scalar_prefetch=1,
            grid=(2 * s,),
            in_specs=[
                pl.BlockSpec((1, HALF, f), lambda i, me: (_pos(j_of(i), shifts_a), 0, 0)),
                pl.BlockSpec((1, HALF, f), lambda i, me: (_pos(j_of(i), shifts_b), 0, 0)),
                pl.BlockSpec((rows, f), lambda i, me: (0, me[0] ^ 1 ^ j_of(i))),
                pl.BlockSpec((K, rows), lambda i, me: (0, 0)),
                pl.BlockSpec((1, rows), lambda i, me: (0, 0)),
            ],
            out_specs=(
                pl.BlockSpec((K, rows), lambda i, me: (0, 0)),
                pl.BlockSpec((K, K), lambda i, me: (0, 0)),
                pl.BlockSpec(
                    (1, K, f), lambda i, me: (_pos(_rel(jnp.maximum(i - s, 0), shifts_a), out_pos), 0, 0)
                ),
            ),
            scratch_shapes=[pltpu.VMEM((s, rows, f), BF16), pltpu.VMEM((K, rows), BF16)],
        ),
        compiler_params=pltpu.CompilerParams(vmem_limit_bytes=40 << 20),
        cost_estimate=pl.CostEstimate(flops=2 * K * rows * d, bytes_accessed=rows * d + 2 * K * d, transcendentals=0),
        name="probe_and_send",
    )(me, v_a, v_b, acts, start, counts)


def keep_kernel(me, probed, counts, acts, out, weighted):
    @pl.when(pl.program_id(0) == 0)
    def _():
        weighted[...] = (counts[...].astype(F32) * probed[...]).astype(BF16)

    out[0] = jnp.dot(weighted[...], acts[...], preferred_element_type=F32)


def panel_keep(me, probed, counts, acts, n):
    rows, d = acts.shape
    f = d // n
    return pl.pallas_call(
        keep_kernel,
        out_shape=jax.ShapeDtypeStruct((n // 2, K, f), F32),
        grid_spec=pltpu.PrefetchScalarGridSpec(
            num_scalar_prefetch=1,
            grid=(n // 2,),
            in_specs=[
                pl.BlockSpec((K, rows), lambda i, me: (0, 0)),
                pl.BlockSpec((1, rows), lambda i, me: (0, 0)),
                pl.BlockSpec((rows, f), lambda i, me: (0, me[0] ^ (2 * i))),
            ],
            out_specs=pl.BlockSpec((1, K, f), lambda i, me: (i, 0, 0)),
            scratch_shapes=[pltpu.VMEM((K, rows), BF16)],
        ),
        compiler_params=pltpu.CompilerParams(vmem_limit_bytes=32 << 20),
        cost_estimate=pl.CostEstimate(flops=K * rows * d, bytes_accessed=rows * d + 2 * K * d, transcendentals=0),
        name="panel_keep",
    )(me, probed, counts, acts)


def scatter_stream(blocks, order, n, inv, wire):
    bits = n.bit_length() - 2
    rows, f = blocks.shape[1:]
    value = blocks.reshape((2,) * bits + (rows, f))
    left = [1 << i for i in range(bits, 0, -1)]
    for bit in order:
        axis = left.index(bit)
        keep = lax.index_in_dim(value, 0, axis, keepdims=False)
        send = lax.index_in_dim(value, 1, axis, keepdims=False)
        left.remove(bit)
        if wire == F32:
            value = keep + swap(send, bit, n)
        else:
            value = keep + swap((send * inv).astype(wire), bit, n).astype(F32) / inv
    return value


def reduce_scatter(sent, make_keep, n, inv, wire):
    if wire == F32:
        got = swap(sent, 1, n)
    else:
        got = swap((sent * inv).astype(wire), 1, n).astype(F32) / inv
    blocks = make_keep() + got
    order_a, order_b = hop_bits(n)
    part = (lambda x, a, b: x) if wire == F32 else (lambda x, a, b: x[a:b])
    top = scatter_stream(blocks[:, :HALF], order_a, n, part(inv, 0, HALF), wire)
    low = scatter_stream(blocks[:, HALF:], order_b, n, part(inv, HALF, K), wire)
    return jnp.concatenate([top, low], axis=0)


def gather_stream(block, order, n):
    value = block[None]
    for bit in order:
        value = jnp.concatenate([value, swap(value, bit, n)], axis=0)
    return value


def per_device(n, activations, labels, counts):
    rows, d = activations.shape
    me = lax.axis_index("dp").astype(jnp.int32).reshape(1)
    labels = labels.reshape(1, rows)
    counts = counts.reshape(1, rows)
    order_a, order_b = hop_bits(n)
    order_a = order_a[::-1]
    shifts_a = [bit.bit_length() - 1 for bit in order_a]
    shifts_b = [bit.bit_length() - 1 for bit in order_b]

    concept = lax.broadcasted_iota(jnp.int32, (K, rows), 0)
    local_weight = jnp.sum(jnp.where(labels == concept, counts.astype(F32), 0.0), axis=1, keepdims=True)
    class_weight = total(local_weight, n)
    total_weight = jnp.sum(class_weight)

    sent = class_sums(me, labels, counts, activations, n, 1)
    sums = reduce_scatter(
        sent, lambda: class_sums(me, labels, counts, activations, n, 0), n, None, F32
    )
    base = (sums / class_weight) * jnp.sqrt(class_weight)

    def apply(panel, counts, combine, norms):
        v = panel.astype(BF16)
        v_a = gather_stream(v[:HALF], order_a, n)
        v_b = gather_stream(v[HALF:], order_b, n)
        far_a, far_b = swap(v_a, 1, n), swap(v_b, 1, n)
        start = combine(probe(me, v_a, v_b, activations, n, shifts_a, shifts_b))
        bound = (1.01 * BOUND * BOUND * d**0.5) * total_weight * norms
        inv = TOP / jnp.maximum(bound, 1e-30)
        probed, gram, sent = probe_and_send(
            me, far_a, far_b, activations, start, counts, n, shifts_a, shifts_b
        )
        gram = total(gram, n)
        own = reduce_scatter(
            sent, lambda: panel_keep(me, probed, counts, activations, n), n, inv, F16
        )
        return probed, gram, own

    current = symmetric(total(outer(base, base), n))
    norm_base = jnp.sqrt(jnp.diag(current))[:, None]
    probed, along_panel, panel = apply(base, counts, lambda x: x, norm_base)

    curvature = symmetric((along_panel - precise(current, current)) / total_weight + RIDGE * current)
    alpha = solve_positive(curvature, current).T
    from_base = base + precise(precise(alpha, current) / total_weight - RIDGE * alpha, base)
    residual = from_base - precise(alpha / total_weight, panel)

    grams = total(outer(jnp.concatenate([residual, base], axis=0), residual), n)
    renewed = symmetric(grams[:K])
    mixed = grams[K:]
    beta = solve_positive(current, renewed)
    beta_t = beta.T
    norm_next = jnp.sqrt(jnp.diag(renewed))[:, None] + precise(jnp.abs(beta_t), norm_base)
    first = probed
    _, along_panel, panel = apply(residual, counts, lambda x: x + precise(beta_t, first), norm_next)

    direction = residual + precise(beta_t, base)
    cross = mixed + precise(current, beta)
    along = renewed + precise(mixed.T, beta) + precise(beta_t, cross)
    curvature = symmetric((along_panel - precise(cross.T, cross)) / total_weight + RIDGE * along)
    step = solve_positive(curvature, renewed).T
    solution = precise(alpha, base) + precise(step, direction)
    rest = residual - precise(step, RIDGE * direction - precise(cross.T / total_weight, base))
    residual = rest - precise(step / total_weight, panel)
    return (solution.T, residual.T)


def solution(mesh):
    in_specs = (P(("groups", "dp"), None), P(("groups", "dp")), P(("groups", "dp")))
    out_specs = (P(("groups", "dp"), None), P(("groups", "dp"), None))
    return jax.shard_map(
        functools.partial(per_device, mesh.shape["dp"]),
        mesh=mesh,
        in_specs=in_specs,
        out_specs=out_specs,
        check_vma=False,
    )
```

time: 588 us -> 305 us (0.52)
  blocking collectives: 211 us -> 0 us
  waiting for transfers between devices: 260 us -> 121 us
  starting transfers between devices: 0.43 us -> 54 us
  matrix products: 62 us -> 13.2 us
  Pallas kernels: 0 us -> 37.3 us
  local copies, waits for them, and re-layouts: 0.68 us -> 28.4 us
  between operations: 14.1 us -> 2.33 us
  other arithmetic: 39.4 us -> 47.4 us
    psum x4 -> x0, blocking collectives: 211 us -> none  [the longest x2 118 us: per_device(): lax.psum((precise(class_means.T, direction), precise(direction.T, panel),...]
    reduce_scatter x3 -> x0, waiting for transfers between devices: 180 us -> none  [the longest x2 140 us: per_device(): lax.psum_scatter(contract_rows(activations, weighted), 'dp', scatter_dime...]
    ppermute x0 -> x57, waiting for transfers between devices: none -> 121 us  [swap(): return lax.ppermute(value, 'dp', [(i, i ^ bit) for i in range(n)])]
    all_gather x2 -> x0, waiting for transfers between devices: 80.2 us -> none  [per_device(): lax.all_gather(direction.astype(jnp.bfloat16), 'dp', axis=0, tiled=True)]
    ppermute x0 -> x57, starting transfers between devices: none -> 54 us  [swap(): return lax.ppermute(value, 'dp', [(i, i ^ bit) for i in range(n)])]
    dot_general x19 -> x18, matrix products: 60.7 us -> 11.9 us  [the longest x16 10.9 us: precise(): jnp.dot(left, right, precision=lax.Precision.HIGHEST, preferred_element_t...]
    pallas_call x0 -> x8, Pallas kernels: none -> 37.3 us  [the longest x2 19.2 us: probe_and_send(): pl.pallas_call(functools.partial(send_kernel, s), out_shape=(jax.ShapeDty...]
    unnamed x4 -> x25, local copies, waits for them, and re-layouts: 0.01 us -> 23.5 us
  transfers between devices with their start and end apart: 5 -> 57, of which waited for: 5 -> 37; matrix products, arithmetic and copies ran while one was open for 0% -> 18% of each run, Pallas kernels for 0% -> 5%
where the time goes in v1:
time: 305 us; the launch traced here: 304 us
  waiting for transfers between devices  121 us (40%)
  starting transfers between devices  54 us (18%)
  other arithmetic  47.4 us (16%)
  Pallas kernels  37.3 us (12%)
  local copies, waits for them, and re-layouts  28.4 us (9%)
  matrix products  13.2 us (4%)
    ppermute x57, waiting for transfers between devices, swap(): return lax.ppermute(value, 'dp', [(i, i ^ bit) for i in range(n)])  121 us
    ppermute x57, starting transfers between devices, swap(): return lax.ppermute(value, 'dp', [(i, i ^ bit) for i in range(n)])  54 us
    unnamed x25, local copies, waits for them, and re-layouts  23.5 us
    another operation x9, other arithmetic, solve_positive(): jnp.linalg.cholesky(matrix)  19.6 us
    pallas_call x2, Pallas kernels, probe_and_send(): pl.pallas_call(functools.partial(send_kernel, s), out_shape=(jax.ShapeDty...  19.2 us
    another operation x6, other arithmetic, solve_positive(): jax.scipy.linalg.cho_solve((jnp.linalg.cholesky(matrix), True), target)  16.6 us
    dot_general x16, matrix products, precise(): jnp.dot(left, right, precision=lax.Precision.HIGHEST, preferred_element_t...  10.9 us
    pallas_call x2, Pallas kernels, probe(): pl.pallas_call(probe_kernel, out_shape=jax.ShapeDtypeStruct((K, rows), F3...  7.12 us
  transfers between devices with their start and end apart: 57, of which 37 were waited for; matrix products, arithmetic and copies ran while one was open for 18% of the time, Pallas kernels for 5%

profile of v1, /device:TPU:0, one launch (start us, length us, event | category | flops | bytes accessed | tf_op | source)
XLA Modules:
  0.0 303.8 jit_solution(16255278550633700632)
XLA Ops:
  2.0 4.6 %copy-done = bf16[384,16384]{1,0:T(8,128)(2,1)S(1)} copy-done((bf16[384,16384]{1,0:T(8,128)(2,1)S(1)}, bf16[384,16384]{1,0:T(8,128)(2,1)}, u32[]{:S(2)}) %copy-start) | copy-done | bytes 12582936
  6.6 2.7 class_sums.3
  10.0 2.7 class_sums.2
  14.5 3.0 collective-permute-start.1
  17.6 12.2 %collective-permute-done.8 = f32[64,1]{0,1:T(1,128)S(1)} collective-permute-done((f32[64,1]{0,1:T(1,128)S(1)}, f32[64,1]{0,1:T(1,128)S(1)}, u32[]{:S(2)}, u32[]{:S(2)}) %collective-permute-start.8) | collective-permute-done | bytes 288 | tf_op jit(solution)/shard_map/ppermute | solution.py:37
  33.3 2.8 collective-permute-start.10
  40.5 13.0 %collective-permute-done.4 = f32[2,2,32,1024]{3,2,1,0:T(8,128)S(1)} collective-permute-done((f32[2,2,32,1024]{3,2,1,0:T(8,128)S(1)}, f32[2,2,32,1024]{3,2,1,0:T(8,128)S(1)}, u32[]{:S(2)}, u32[]{:S(2)}) %collective-permute-start.4) | collective-permute-done | bytes 524320 | tf_op jit(solution)/shard_map/ppermute | solution.py:37
  53.7 2.6 collective-permute-done.2
  57.0 9.1 %collective-permute-done.5 = f32[2,32,1024]{2,1,0:T(8,128)S(1)} collective-permute-done((f32[2,32,1024]{2,1,0:T(8,128)S(1)}, f32[2,32,1024]{2,1,0:T(8,128)S(1)}, u32[]{:S(2)}, u32[]{:S(2)}) %collective-permute-start.5) | collective-permute-done | bytes 262176 | tf_op jit(solution)/shard_map/ppermute | solution.py:37
  67.6 3.5 %collective-permute-done.6 = f32[32,1024]{1,0:T(8,128)S(1)} collective-permute-done((f32[32,1024]{1,0:T(8,128)S(1)}, f32[32,1024]{1,0:T(8,128)S(1)}, u32[]{:S(2)}, u32[]{:S(2)}) %collective-permute-start.6) | collective-permute-done | bytes 131104 | tf_op jit(solution)/shard_map/ppermute | solution.py:37
  75.0 2.5 collective-permute-done.24
  81.8 2.2 collective-permute-start.26
  87.8 3.8 %collective-permute-done.16 = bf16[2,32,1024]{2,1,0:T(8,128)(2,1)S(1)} collective-permute-done((bf16[2,32,1024]{2,1,0:T(8,128)(2,1)S(1)}, bf16[2,32,1024]{2,1,0:T(8,128)(2,1)S(1)}, u32[]{:S(2)}, u32[]{:S(2)}) %collective-permute-start.16) | collective-permute-done | bytes 131104 | tf_op jit(solution)/shard_map/ppermute | solution.py:37
  93.9 7.0 %collective-permute-done.17 = bf16[4,32,1024]{2,1,0:T(8,128)(2,1)S(1)} collective-permute-done((bf16[4,32,1024]{2,1,0:T(8,128)(2,1)S(1)}, bf16[4,32,1024]{2,1,0:T(8,128)(2,1)S(1)}, u32[]{:S(2)}, u32[]{:S(2)}) %collective-permute-start.17) | collective-permute-done | bytes 262176 | tf_op jit(solution)/shard_map/ppermute | solution.py:37
  101.0 3.2 %collective-permute-done.13 = bf16[4,32,1024]{2,1,0:T(8,128)(2,1)S(1)} collective-permute-done((bf16[4,32,1024]{2,1,0:T(8,128)(2,1)S(1)}, bf16[4,32,1024]{2,1,0:T(8,128)(2,1)S(1)}, u32[]{:S(2)}, u32[]{:S(2)}) %collective-permute-start.13) | collective-permute-done | bytes 262176 | tf_op jit(solution)/shard_map/ppermute | solution.py:37
  104.4 5.8 %cholesky.70 = f32[64,64]{1,0:T(8,128)S(1)} custom-call(f32[64,64]{1,0:T(8,128)S(1)} %fusion.76), custom_call_target="Cholesky" | custom-call | tf_op jit(solution)/shard_map/jit(cholesky)/cholesky | solution.py:33
  112.4 4.6 %copy-done.1 = bf16[384,16384]{1,0:T(8,128)(2,1)S(1)} copy-done((bf16[384,16384]{1,0:T(8,128)(2,1)S(1)}, bf16[384,16384]{1,0:T(8,128)(2,1)}, u32[]{:S(2)}) %copy-start.1) | copy-done | bytes 12582936
  117.0 3.6 %probe.2.start = f32[64,384]{1,0:T(8,128)S(1)} custom-call(s32[1]{0:T(128)} %bitcast.me, bf16[8,32,1024]{2,1,0:T(8,128)(2,1)S(1)} %pad_maximum_fusion.v_a, bf16[8,32,1024]{2,1,0:T(8,128)(2,1)S(1)} %pad_maximum_fusion.1.v_b, bf16[384,16384]{1,0:T(8,128)(2,1)S(1)} %copy-done.1), custom_call_target="tpu_custom_call" | custom-call | flops 402653184 | bytes 7340032 | tf_op jit(solution)/shard_map/probe/pallas_call | solution.py:111
  120.6 9.6 %probe_and_send.2 = (f32[64,384]{1,0:T(8,128)S(1)}, f32[64,64]{1,0:T(8,128)S(1)}, f32[8,64,1024]{2,1,0:T(8,128)S(1)}) custom-call(s32[1]{0:T(128)} %bitcast.me, bf16[8,32,1024]{2,1,0:T(8,128)(2,1)S(1)} %collective-permute-done.14.v_a, bf16[8,32,1024]{2,1,0:T(8,128)(2,1)S(1)} %collective-permute-done.18.v_b, bf16[384,16384]{1,0:T(8,128)(2,1)} %acts.15, ...), custom_call_target="tpu_custom_call" | custom-call | flops 805306368 | bytes 8388608 | tf_op jit(solution)/shard_map/probe_and_send/pallas_call | solution.py:162
  132.0 4.9 %custom-call.14 = f32[1,64,64]{1,2,0:T(8,128)S(1)} custom-call(f32[1,64,64]{2,1,0:T(8,128)S(1)} %fusion.62), custom_call_target="InvertDiagBlocksLowerTriangular" | custom-call | tf_op jit(solution)/shard_map/jit(_cho_solve)/triangular_solve | solution.py:33
  138.6 2.3 collective-permute-done.21
  140.9 2.6 collective-permute-start.22
  143.5 4.6 %copy-done.2 = bf16[384,16384]{1,0:T(8,128)(2,1)S(1)} copy-done((bf16[384,16384]{1,0:T(8,128)(2,1)S(1)}, bf16[384,16384]{1,0:T(8,128)(2,1)}, u32[]{:S(2)}) %copy-start.2) | copy-done | bytes 12582936
  148.1 2.8 panel_keep.2
  152.0 5.8 %cholesky.59 = f32[64,64]{1,0:T(8,128)S(1)} custom-call(f32[64,64]{1,0:T(8,128)S(1)} %fusion.81), custom_call_target="Cholesky" | custom-call | tf_op jit(solution)/shard_map/jit(cholesky)/cholesky | solution.py:33
  159.2 4.9 %custom-call.13 = f32[1,64,64]{1,2,0:T(8,128)S(1)} custom-call(f32[1,64,64]{2,1,0:T(8,128)S(1)} %fusion.61), custom_call_target="InvertDiagBlocksLowerTriangular" | custom-call | tf_op jit(solution)/shard_map/jit(_cho_solve)/triangular_solve | solution.py:33
  171.3 4.2 %collective-permute-done.28 = f16[2,2,32,1024]{3,2,0,1:T(8,128)(2,1)} collective-permute-done((f16[2,2,32,1024]{3,2,0,1:T(8,128)(2,1)}, f16[2,2,32,1024]{3,2,0,1:T(8,128)(2,1)}, u32[]{:S(2)}, u32[]{:S(2)}) %collective-permute-start.28) | collective-permute-done | bytes 262176 | tf_op jit(solution)/shard_map/ppermute | solution.py:37
  179.1 4.4 %collective-permute-done.29 = f16[2,32,1024]{2,1,0:T(8,128)(2,1)S(1)} collective-permute-done((f16[2,32,1024]{2,1,0:T(8,128)(2,1)S(1)}, f16[2,32,1024]{2,1,0:T(8,128)(2,1)S(1)}, u32[]{:S(2)}, u32[]{:S(2)}) %collective-permute-start.29) | collective-permute-done | bytes 131104 | tf_op jit(solution)/shard_map/ppermute | solution.py:37
  183.8 2.9 collective-permute-done.32
  196.1 2.1 collective-permute-done.35
  199.5 3.3 %collective-permute-done.36 = f32[128,64]{0,1:T(8,128)S(1)} collective-permute-done((f32[128,64]{0,1:T(8,128)S(1)}, f32[128,64]{0,1:T(8,128)S(1)}, u32[]{:S(2)}, u32[]{:S(2)}) %collective-permute-start.36) | collective-permute-done | bytes 32800 | tf_op jit(solution)/shard_map/ppermute | solution.py:37
  204.4 4.3 %collective-permute-done.37 = f32[128,64]{0,1:T(8,128)S(1)} collective-permute-done((f32[128,64]{0,1:T(8,128)S(1)}, f32[128,64]{0,1:T(8,128)S(1)}, u32[]{:S(2)}, u32[]{:S(2)}) %collective-permute-start.37) | collective-permute-done | bytes 32800 | tf_op jit(solution)/shard_map/ppermute | solution.py:37
  213.1 6.9 %collective-permute-done.44 = bf16[4,32,1024]{2,1,0:T(8,128)(2,1)S(1)} collective-permute-done((bf16[4,32,1024]{2,1,0:T(8,128)(2,1)S(1)}, bf16[4,32,1024]{2,1,0:T(8,128)(2,1)S(1)}, u32[]{:S(2)}, u32[]{:S(2)}) %collective-permute-start.44) | collective-permute-done | bytes 262176 | tf_op jit(solution)/shard_map/ppermute | solution.py:37
  220.2 3.7 %collective-permute-done.40 = bf16[4,32,1024]{2,1,0:T(8,128)(2,1)S(1)} collective-permute-done((bf16[4,32,1024]{2,1,0:T(8,128)(2,1)S(1)}, bf16[4,32,1024]{2,1,0:T(8,128)(2,1)S(1)}, u32[]{:S(2)}, u32[]{:S(2)}) %collective-permute-start.40) | collective-permute-done | bytes 262176 | tf_op jit(solution)/shard_map/ppermute | solution.py:37
  225.5 4.6 %copy-done.3 = bf16[384,16384]{1,0:T(8,128)(2,1)S(1)} copy-done((bf16[384,16384]{1,0:T(8,128)(2,1)S(1)}, bf16[384,16384]{1,0:T(8,128)(2,1)}, u32[]{:S(2)}) %copy-start.3) | copy-done | bytes 12582936
  230.1 3.6 %probe.3 = f32[64,384]{1,0:T(8,128)S(1)} custom-call(s32[1]{0:T(128)} %bitcast.me, bf16[8,32,1024]{2,1,0:T(8,128)(2,1)S(1)} %pad_maximum_fusion.2.v_a, bf16[8,32,1024]{2,1,0:T(8,128)(2,1)S(1)} %pad_maximum_fusion.3.v_b, bf16[384,16384]{1,0:T(8,128)(2,1)S(1)} %copy-done.3), custom_call_target="tpu_custom_call" | custom-call | flops 402653184 | bytes 7340032 | tf_op jit(solution)/shard_map/probe/pallas_call | solution.py:111
  233.7 9.6 %probe_and_send.3 = (f32[64,384]{1,0:T(8,128)S(1)}, f32[64,64]{1,0:T(8,128)S(1)}, f32[8,64,1024]{2,1,0:T(8,128)S(1)}) custom-call(s32[1]{0:T(128)} %bitcast.me, bf16[8,32,1024]{2,1,0:T(8,128)(2,1)S(1)} %collective-permute-done.41.v_a, bf16[8,32,1024]{2,1,0:T(8,128)(2,1)S(1)} %collective-permute-done.45.v_b, bf16[384,16384]{1,0:T(8,128)(2,1)} %acts.15, ...), custom_call_target="tpu_custom_call" | custom-call | flops 805306368 | bytes 8388608 | tf_op jit(solution)/shard_map/probe_and_send/pallas_call | solution.py:162
  246.6 2.1 collective-permute-done.47
  250.0 2.6 collective-permute-done.48
  252.6 4.6 %copy-done.4 = bf16[384,16384]{1,0:T(8,128)(2,1)S(1)} copy-done((bf16[384,16384]{1,0:T(8,128)(2,1)S(1)}, bf16[384,16384]{1,0:T(8,128)(2,1)}, u32[]{:S(2)}) %copy-start.4) | copy-done | bytes 12582936
  257.2 2.9 panel_keep.3
  261.2 5.8 %cholesky.81 = f32[64,64]{1,0:T(8,128)S(1)} custom-call(f32[64,64]{1,0:T(8,128)S(1)} %fusion.69), custom_call_target="Cholesky" | custom-call | tf_op jit(solution)/shard_map/jit(cholesky)/cholesky | solution.py:33
  268.4 4.9 %custom-call.15 = f32[1,64,64]{1,2,0:T(8,128)S(1)} custom-call(f32[1,64,64]{2,1,0:T(8,128)S(1)} %fusion.63), custom_call_target="InvertDiagBlocksLowerTriangular" | custom-call | tf_op jit(solution)/shard_map/jit(_cho_solve)/triangular_solve | solution.py:33
  281.4 3.4 %collective-permute-done.51 = f16[2,2,32,1024]{3,2,0,1:T(8,128)(2,1)S(1)} collective-permute-done((f16[2,2,32,1024]{3,2,0,1:T(8,128)(2,1)S(1)}, f16[2,2,32,1024]{3,2,0,1:T(8,128)(2,1)S(1)}, u32[]{:S(2)}, u32[]{:S(2)}) %collective-permute-start.51) | collective-permute-done | bytes 262176 | tf_op jit(solution)/shard_map/ppermute | solution.py:37
  287.8 3.3 %collective-permute-start.55 = (f16[2,32,1024]{2,1,0:T(8,128)(2,1)S(1)}, f16[2,32,1024]{2,1,0:T(8,128)(2,1)S(1)}, u32[]{:S(2)}, u32[]{:S(2)}) collective-permute-start(f16[2,32,1024]{2,1,0:T(8,128)(2,1)S(1)} %fusion.27), channel_id=1, source_target_pairs={{0,8},{1,9},{2,10},{3,11},{4,12},{5,13},{6,14},{7,15},{8,0},{9,1},... | collective-permute-start | bytes 393224 | tf_op jit(solution)/shard_map/ppermute | solution.py:37
  291.7 2.1 collective-permute-start.53
  293.8 3.6 %collective-permute-done.55 = f16[2,32,1024]{2,1,0:T(8,128)(2,1)S(1)} collective-permute-done((f16[2,32,1024]{2,1,0:T(8,128)(2,1)S(1)}, f16[2,32,1024]{2,1,0:T(8,128)(2,1)S(1)}, u32[]{:S(2)}, u32[]{:S(2)}) %collective-permute-start.55) | collective-permute-done | bytes 131104 | tf_op jit(solution)/shard_map/ppermute | solution.py:37
  298.2 3.7 %collective-permute-done.56 = f16[32,1024]{1,0:T(8,128)(2,1)S(1)} collective-permute-done((f16[32,1024]{1,0:T(8,128)(2,1)S(1)}, f16[32,1024]{1,0:T(8,128)(2,1)S(1)}, u32[]{:S(2)}, u32[]{:S(2)}) %collective-permute-start.56) | collective-permute-done | bytes 65568 | tf_op jit(solution)/shard_map/ppermute | solution.py:37
  (246 shorter events, 86.6 us)
Async XLA Ops:
  9.2 4.3 %collective-permute-start = (f32[8,64,1024]{2,1,0:T(8,128)S(1)}, f32[8,64,1024]{2,1,0:T(8,128)S(1)}, u32[]{:S(2)}, u32[]{:S(2)}) collective-permute-start(f32[8,64,1024]{2,1,0:T(8,128)S(1)} %class_sums.3), channel_id=1, source_target_pairs={{0,1},{1,0},{2,3},{3,2},{4,5},{5,4},{6,7},{7,6},{8,9},{9,8},{10,11... | collective-permute-start | bytes 6291464 | tf_op jit(solution)/shard_map/ppermute | solution.py:37
  9.9 7.6 %collective-permute-start.7 = (f32[64,1]{0,1:T(1,128)S(1)}, f32[64,1]{0,1:T(1,128)S(1)}, u32[]{:S(2)}, u32[]{:S(2)}) collective-permute-start(f32[64,1]{0,1:T(1,128)S(1)} %bitcast.304), channel_id=1, source_target_pairs={{0,1},{1,0},{2,3},{3,2},{4,5},{5,4},{6,7},{7,6},{8,9},{9,8},{10,11... | collective-permute-start | bytes 776 | tf_op jit(solution)/shard_map/ppermute | solution.py:37
  14.5 24.0 %collective-permute-start.1 = (f32[2,2,32,1024]{3,2,0,1:T(8,128)S(1)}, f32[2,2,32,1024]{3,2,0,1:T(8,128)S(1)}, u32[]{:S(2)}, u32[]{:S(2)}) collective-permute-start(f32[2,2,32,1024]{3,2,0,1:T(8,128)S(1)} %bitcast.303), channel_id=1, source_target_pairs={{0,2},{1,3},{2,0},{3,1},{4,6},{5,7},{6,4},{7,5},{8,10},{9,11},{10,... | collective-permute-start | bytes 1572872 | tf_op jit(solution)/shard_map/ppermute | solution.py:37
  17.5 12.3 %collective-permute-start.8 = (f32[64,1]{0,1:T(1,128)S(1)}, f32[64,1]{0,1:T(1,128)S(1)}, u32[]{:S(2)}, u32[]{:S(2)}) collective-permute-start(f32[64,1]{0,1:T(1,128)S(1)} %bitcast_add_fusion.7), channel_id=1, source_target_pairs={{0,2},{1,3},{2,0},{3,1},{4,6},{5,7},{6,4},{7,5},{8,10},{9,11},{10,... | collective-permute-start | bytes 776 | tf_op jit(solution)/shard_map/ppermute | solution.py:37
  33.3 4.5 %collective-permute-start.10 = (f32[64,1]{0,1:T(1,128)S(1)}, f32[64,1]{0,1:T(1,128)S(1)}, u32[]{:S(2)}, u32[]{:S(2)}) collective-permute-start(f32[64,1]{0,1:T(1,128)S(1)} %add.195), channel_id=1, source_target_pairs={{0,8},{1,9},{2,10},{3,11},{4,12},{5,13},{6,14},{7,15},{8,0},{9,1},... | collective-permute-start | bytes 776 | tf_op jit(solution)/shard_map/ppermute | solution.py:37
  36.2 17.3 %collective-permute-start.4 = (f32[2,2,32,1024]{3,2,1,0:T(8,128)S(1)}, f32[2,2,32,1024]{3,2,1,0:T(8,128)S(1)}, u32[]{:S(2)}, u32[]{:S(2)}) collective-permute-start(f32[2,2,32,1024]{3,2,1,0:T(8,128)S(1)} %slice_bitcast_fusion.4), channel_id=1, source_target_pairs={{0,4},{1,5},{2,6},{3,7},{4,0},{5,1},{6,2},{7,3},{8,12},{9,13},{10,... | collective-permute-start | bytes 1572872 | tf_op jit(solution)/shard_map/ppermute | solution.py:37
  38.6 17.7 %collective-permute-start.2 = (f32[2,32,1024]{2,1,0:T(8,128)S(1)}, f32[2,32,1024]{2,1,0:T(8,128)S(1)}, u32[]{:S(2)}, u32[]{:S(2)}) collective-permute-start(f32[2,32,1024]{2,1,0:T(8,128)S(1)} %slice_bitcast_fusion.16), channel_id=1, source_target_pairs={{0,4},{1,5},{2,6},{3,7},{4,0},{5,1},{6,2},{7,3},{8,12},{9,13},{10,... | collective-permute-start | bytes 786440 | tf_op jit(solution)/shard_map/ppermute | solution.py:37
  53.6 12.4 %collective-permute-start.5 = (f32[2,32,1024]{2,1,0:T(8,128)S(1)}, f32[2,32,1024]{2,1,0:T(8,128)S(1)}, u32[]{:S(2)}, u32[]{:S(2)}) collective-permute-start(f32[2,32,1024]{2,1,0:T(8,128)S(1)} %slice_bitcast_fusion.14), channel_id=1, source_target_pairs={{0,8},{1,9},{2,10},{3,11},{4,12},{5,13},{6,14},{7,15},{8,0},{9,1},... | collective-permute-start | bytes 786440 | tf_op jit(solution)/shard_map/ppermute | solution.py:37
  56.4 11.2 %collective-permute-start.3 = (f32[32,1024]{1,0:T(8,128)S(1)}, f32[32,1024]{1,0:T(8,128)S(1)}, u32[]{:S(2)}, u32[]{:S(2)}) collective-permute-start(f32[32,1024]{1,0:T(8,128)S(1)} %slice_bitcast_fusion.28), channel_id=1, source_target_pairs={{0,8},{1,9},{2,10},{3,11},{4,12},{5,13},{6,14},{7,15},{8,0},{9,1},... | collective-permute-start | bytes 393224 | tf_op jit(solution)/shard_map/ppermute | solution.py:37
  66.1 5.0 %collective-permute-start.6 = (f32[32,1024]{1,0:T(8,128)S(1)}, f32[32,1024]{1,0:T(8,128)S(1)}, u32[]{:S(2)}, u32[]{:S(2)}) collective-permute-start(f32[32,1024]{1,0:T(8,128)S(1)} %slice_bitcast_fusion.26), channel_id=1, source_target_pairs={{0,2},{1,3},{2,0},{3,1},{4,6},{5,7},{6,4},{7,5},{8,10},{9,11},{10,... | collective-permute-start | bytes 393224 | tf_op jit(solution)/shard_map/ppermute | solution.py:37
  71.3 12.7 %collective-permute-start.15 = (bf16[1,32,1024]{2,1,0:T(8,128)(2,1)S(1)}, bf16[1,32,1024]{2,1,0:T(8,128)(2,1)S(1)}, u32[]{:S(2)}, u32[]{:S(2)}) collective-permute-start(bf16[1,32,1024]{2,1,0:T(8,128)(2,1)S(1)} %get-tuple-element.32), channel_id=1, source_target_pairs={{0,4},{1,5},{2,6},{3,7},{4,0},{5,1},{6,2},{7,3},{8,12},{9,13},{10,... | collective-permute-start | bytes 196616 | tf_op jit(solution)/shard_map/ppermute | solution.py:37
  77.5 4.3 %collective-permute-start.25 = (f32[64,64]{1,0:T(8,128)S(1)}, f32[64,64]{1,0:T(8,128)S(1)}, u32[]{:S(2)}, u32[]{:S(2)}) collective-permute-start(f32[64,64]{1,0:T(8,128)S(1)} %add.202), channel_id=1, source_target_pairs={{0,4},{1,5},{2,6},{3,7},{4,0},{5,1},{6,2},{7,3},{8,12},{9,13},{10,... | collective-permute-start | bytes 49160 | tf_op jit(solution)/shard_map/ppermute | solution.py:37
  78.9 6.2 %collective-permute-start.11 = (bf16[1,32,1024]{2,1,0:T(8,128)(2,1)S(1)}, bf16[1,32,1024]{2,1,0:T(8,128)(2,1)S(1)}, u32[]{:S(2)}, u32[]{:S(2)}) collective-permute-start(bf16[1,32,1024]{2,1,0:T(8,128)(2,1)S(1)} %get-tuple-element.33), channel_id=1, source_target_pairs={{0,8},{1,9},{2,10},{3,11},{4,12},{5,13},{6,14},{7,15},{8,0},{9,1},... | collective-permute-start | bytes 196616 | tf_op jit(solution)/shard_map/ppermute | solution.py:37
  81.8 5.9 %collective-permute-start.26 = (f32[64,64]{1,0:T(8,128)S(1)}, f32[64,64]{1,0:T(8,128)S(1)}, u32[]{:S(2)}, u32[]{:S(2)}) collective-permute-start(f32[64,64]{1,0:T(8,128)S(1)} %add.203), channel_id=1, source_target_pairs={{0,8},{1,9},{2,10},{3,11},{4,12},{5,13},{6,14},{7,15},{8,0},{9,1},... | collective-permute-start | bytes 49160 | tf_op jit(solution)/shard_map/ppermute | solution.py:37
  84.0 7.6 %collective-permute-start.16 = (bf16[2,32,1024]{2,1,0:T(8,128)(2,1)S(1)}, bf16[2,32,1024]{2,1,0:T(8,128)(2,1)S(1)}, u32[]{:S(2)}, u32[]{:S(2)}) collective-permute-start(bf16[2,32,1024]{2,1,0:T(8,128)(2,1)S(1)} %pad_maximum_fusion.9), channel_id=1, source_target_pairs={{0,8},{1,9},{2,10},{3,11},{4,12},{5,13},{6,14},{7,15},{8,0},{9,1},... | collective-permute-start | bytes 393224 | tf_op jit(solution)/shard_map/ppermute | solution.py:37
  85.2 7.8 %collective-permute-start.12 = (bf16[2,32,1024]{2,1,0:T(8,128)(2,1)S(1)}, bf16[2,32,1024]{2,1,0:T(8,128)(2,1)S(1)}, u32[]{:S(2)}, u32[]{:S(2)}) collective-permute-start(bf16[2,32,1024]{2,1,0:T(8,128)(2,1)S(1)} %pad_maximum_fusion.8), channel_id=1, source_target_pairs={{0,4},{1,5},{2,6},{3,7},{4,0},{5,1},{6,2},{7,3},{8,12},{9,13},{10,... | collective-permute-start | bytes 393224 | tf_op jit(solution)/shard_map/ppermute | solution.py:37
  91.6 9.3 %collective-permute-start.17 = (bf16[4,32,1024]{2,1,0:T(8,128)(2,1)S(1)}, bf16[4,32,1024]{2,1,0:T(8,128)(2,1)S(1)}, u32[]{:S(2)}, u32[]{:S(2)}) collective-permute-start(bf16[4,32,1024]{2,1,0:T(8,128)(2,1)S(1)} %pad_maximum_fusion.5), channel_id=1, source_target_pairs={{0,2},{1,3},{2,0},{3,1},{4,6},{5,7},{6,4},{7,5},{8,10},{9,11},{10,... | collective-permute-start | bytes 786440 | tf_op jit(solution)/shard_map/ppermute | solution.py:37
  93.0 11.2 %collective-permute-start.13 = (bf16[4,32,1024]{2,1,0:T(8,128)(2,1)S(1)}, bf16[4,32,1024]{2,1,0:T(8,128)(2,1)S(1)}, u32[]{:S(2)}, u32[]{:S(2)}) collective-permute-start(bf16[4,32,1024]{2,1,0:T(8,128)(2,1)S(1)} %pad_maximum_fusion.4), channel_id=1, source_target_pairs={{0,2},{1,3},{2,0},{3,1},{4,6},{5,7},{6,4},{7,5},{8,10},{9,11},{10,... | collective-permute-start | bytes 786440 | tf_op jit(solution)/shard_map/ppermute | solution.py:37
  100.9 19.6 %collective-permute-start.18 = (bf16[8,32,1024]{2,1,0:T(8,128)(2,1)S(1)}, bf16[8,32,1024]{2,1,0:T(8,128)(2,1)S(1)}, u32[]{:S(2)}, u32[]{:S(2)}) collective-permute-start(bf16[8,32,1024]{2,1,0:T(8,128)(2,1)S(1)} %pad_maximum_fusion.1.v_b), channel_id=1, source_target_pairs={{0,1},{1,0},{2,3},{3,2},{4,5},{5,4},{6,7},{7,6},{8,9},{9,8},{10,11... | collective-permute-start | bytes 1572872 | tf_op jit(solution)/shard_map/ppermute | solution.py:37
  104.3 16.2 %collective-permute-start.14 = (bf16[8,32,1024]{2,1,0:T(8,128)(2,1)S(1)}, bf16[8,32,1024]{2,1,0:T(8,128)(2,1)S(1)}, u32[]{:S(2)}, u32[]{:S(2)}) collective-permute-start(bf16[8,32,1024]{2,1,0:T(8,128)(2,1)S(1)} %pad_maximum_fusion.v_a), channel_id=1, source_target_pairs={{0,1},{1,0},{2,3},{3,2},{4,5},{5,4},{6,7},{7,6},{8,9},{9,8},{10,11... | collective-permute-start | bytes 1572872 | tf_op jit(solution)/shard_map/ppermute | solution.py:37
  131.6 5.3 %collective-permute-start.20 = (f32[64,64]{0,1:T(8,128)S(1)}, f32[64,64]{0,1:T(8,128)S(1)}, u32[]{:S(2)}, u32[]{:S(2)}) collective-permute-start(f32[64,64]{0,1:T(8,128)S(1)} %add.197), channel_id=1, source_target_pairs={{0,2},{1,3},{2,0},{3,1},{4,6},{5,7},{6,4},{7,5},{8,10},{9,11},{10,... | collective-permute-start | bytes 49160 | tf_op jit(solution)/shard_map/ppermute | solution.py:37
  136.9 4.0 %collective-permute-start.21 = (f32[64,64]{0,1:T(8,128)S(1)}, f32[64,64]{0,1:T(8,128)S(1)}, u32[]{:S(2)}, u32[]{:S(2)}) collective-permute-start(f32[64,64]{0,1:T(8,128)S(1)} %add.198), channel_id=1, source_target_pairs={{0,4},{1,5},{2,6},{3,7},{4,0},{5,1},{6,2},{7,3},{8,12},{9,13},{10,... | collective-permute-start | bytes 49160 | tf_op jit(solution)/shard_map/ppermute | solution.py:37
  138.5 26.8 %collective-permute-start.27 = (f16[8,64,1024]{2,1,0:T(8,128)(2,1)S(1)}, f16[8,64,1024]{2,1,0:T(8,128)(2,1)}, u32[]{:S(2)}, u32[]{:S(2)}) collective-permute-start(f16[8,64,1024]{2,1,0:T(8,128)(2,1)S(1)} %multiply_convert_fusion.1), channel_id=1, source_target_pairs={{0,1},{1,0},{2,3},{3,2},{4,5},{5,4},{6,7},{7,6},{8,9},{9,8},{10,11... | collective-permute-start | bytes 3145736 | tf_op jit(solution)/shard_map/ppermute | solution.py:37
  140.9 10.0 %collective-permute-start.22 = (f32[64,64]{0,1:T(8,128)S(1)}, f32[64,64]{0,1:T(8,128)S(1)}, u32[]{:S(2)}, u32[]{:S(2)}) collective-permute-start(f32[64,64]{0,1:T(8,128)S(1)} %add.199), channel_id=1, source_target_pairs={{0,8},{1,9},{2,10},{3,11},{4,12},{5,13},{6,14},{7,15},{8,0},{9,1},... | collective-permute-start | bytes 49160 | tf_op jit(solution)/shard_map/ppermute | solution.py:37
  168.1 7.4 %collective-permute-start.28 = (f16[2,2,32,1024]{3,2,0,1:T(8,128)(2,1)}, f16[2,2,32,1024]{3,2,0,1:T(8,128)(2,1)}, u32[]{:S(2)}, u32[]{:S(2)}) collective-permute-start(f16[2,2,32,1024]{3,2,0,1:T(8,128)(2,1)} %fusion.23), channel_id=1, source_target_pairs={{0,2},{1,3},{2,0},{3,1},{4,6},{5,7},{6,4},{7,5},{8,10},{9,11},{10,... | collective-permute-start | bytes 786440 | tf_op jit(solution)/shard_map/ppermute | solution.py:37
  169.2 9.3 %collective-permute-start.31 = (f16[2,2,32,1024]{3,2,1,0:T(8,128)(2,1)S(1)}, f16[2,2,32,1024]{3,2,1,0:T(8,128)(2,1)S(1)}, u32[]{:S(2)}, u32[]{:S(2)}) collective-permute-start(f16[2,2,32,1024]{3,2,1,0:T(8,128)(2,1)S(1)} %fusion.12), channel_id=1, source_target_pairs={{0,4},{1,5},{2,6},{3,7},{4,0},{5,1},{6,2},{7,3},{8,12},{9,13},{10,... | collective-permute-start | bytes 786440 | tf_op jit(solution)/shard_map/ppermute | solution.py:37
  176.7 6.9 %collective-permute-start.29 = (f16[2,32,1024]{2,1,0:T(8,128)(2,1)S(1)}, f16[2,32,1024]{2,1,0:T(8,128)(2,1)S(1)}, u32[]{:S(2)}, u32[]{:S(2)}) collective-permute-start(f16[2,32,1024]{2,1,0:T(8,128)(2,1)S(1)} %fusion.36), channel_id=1, source_target_pairs={{0,4},{1,5},{2,6},{3,7},{4,0},{5,1},{6,2},{7,3},{8,12},{9,13},{10,... | collective-permute-start | bytes 393224 | tf_op jit(solution)/shard_map/ppermute | solution.py:37
  178.7 8.0 %collective-permute-start.32 = (f16[2,32,1024]{2,1,0:T(8,128)(2,1)S(1)}, f16[2,32,1024]{2,1,0:T(8,128)(2,1)S(1)}, u32[]{:S(2)}, u32[]{:S(2)}) collective-permute-start(f16[2,32,1024]{2,1,0:T(8,128)(2,1)S(1)} %fusion.33), channel_id=1, source_target_pairs={{0,8},{1,9},{2,10},{3,11},{4,12},{5,13},{6,14},{7,15},{8,0},{9,1},... | collective-permute-start | bytes 393224 | tf_op jit(solution)/shard_map/ppermute | solution.py:37
  183.7 5.7 %collective-permute-start.30 = (f16[32,1024]{1,0:T(8,128)(2,1)S(1)}, f16[32,1024]{1,0:T(8,128)(2,1)S(1)}, u32[]{:S(2)}, u32[]{:S(2)}) collective-permute-start(f16[32,1024]{1,0:T(8,128)(2,1)S(1)} %fusion.57), channel_id=1, source_target_pairs={{0,8},{1,9},{2,10},{3,11},{4,12},{5,13},{6,14},{7,15},{8,0},{9,1},... | collective-permute-start | bytes 196616 | tf_op jit(solution)/shard_map/ppermute | solution.py:37
  186.9 4.3 %collective-permute-start.33 = (f16[32,1024]{1,0:T(8,128)(2,1)S(1)}, f16[32,1024]{1,0:T(8,128)(2,1)S(1)}, u32[]{:S(2)}, u32[]{:S(2)}) collective-permute-start(f16[32,1024]{1,0:T(8,128)(2,1)S(1)} %fusion.54), channel_id=1, source_target_pairs={{0,2},{1,3},{2,0},{3,1},{4,6},{5,7},{6,4},{7,5},{8,10},{9,11},{10,... | collective-permute-start | bytes 196616 | tf_op jit(solution)/shard_map/ppermute | solution.py:37
  193.2 6.1 %collective-permute-start.42 = (bf16[1,32,1024]{2,1,0:T(8,128)(2,1)S(1)}, bf16[1,32,1024]{2,1,0:T(8,128)(2,1)S(1)}, u32[]{:S(2)}, u32[]{:S(2)}) collective-permute-start(bf16[1,32,1024]{2,1,0:T(8,128)(2,1)S(1)} %get-tuple-element.30), channel_id=1, source_target_pairs={{0,4},{1,5},{2,6},{3,7},{4,0},{5,1},{6,2},{7,3},{8,12},{9,13},{10,... | collective-permute-start | bytes 196616 | tf_op jit(solution)/shard_map/ppermute | solution.py:37
  195.4 7.4 %collective-permute-start.38 = (bf16[1,32,1024]{2,1,0:T(8,128)(2,1)S(1)}, bf16[1,32,1024]{2,1,0:T(8,128)(2,1)S(1)}, u32[]{:S(2)}, u32[]{:S(2)}) collective-permute-start(bf16[1,32,1024]{2,1,0:T(8,128)(2,1)S(1)} %get-tuple-element.31), channel_id=1, source_target_pairs={{0,8},{1,9},{2,10},{3,11},{4,12},{5,13},{6,14},{7,15},{8,0},{9,1},... | collective-permute-start | bytes 196616 | tf_op jit(solution)/shard_map/ppermute | solution.py:37
  198.3 4.5 %collective-permute-start.36 = (f32[128,64]{0,1:T(8,128)S(1)}, f32[128,64]{0,1:T(8,128)S(1)}, u32[]{:S(2)}, u32[]{:S(2)}) collective-permute-start(f32[128,64]{0,1:T(8,128)S(1)} %add.217), channel_id=1, source_target_pairs={{0,4},{1,5},{2,6},{3,7},{4,0},{5,1},{6,2},{7,3},{8,12},{9,13},{10,... | collective-permute-start | bytes 98312 | tf_op jit(solution)/shard_map/ppermute | solution.py:37
  199.3 11.5 %collective-permute-start.43 = (bf16[2,32,1024]{2,1,0:T(8,128)(2,1)S(1)}, bf16[2,32,1024]{2,1,0:T(8,128)(2,1)S(1)}, u32[]{:S(2)}, u32[]{:S(2)}) collective-permute-start(bf16[2,32,1024]{2,1,0:T(8,128)(2,1)S(1)} %pad_maximum_fusion.11), channel_id=1, source_target_pairs={{0,8},{1,9},{2,10},{3,11},{4,12},{5,13},{6,14},{7,15},{8,0},{9,1},... | collective-permute-start | bytes 393224 | tf_op jit(solution)/shard_map/ppermute | solution.py:37
  202.8 5.9 %collective-permute-start.37 = (f32[128,64]{0,1:T(8,128)S(1)}, f32[128,64]{0,1:T(8,128)S(1)}, u32[]{:S(2)}, u32[]{:S(2)}) collective-permute-start(f32[128,64]{0,1:T(8,128)S(1)} %add.218), channel_id=1, source_target_pairs={{0,8},{1,9},{2,10},{3,11},{4,12},{5,13},{6,14},{7,15},{8,0},{9,1},... | collective-permute-start | bytes 98312 | tf_op jit(solution)/shard_map/ppermute | solution.py:37
  202.8 9.4 %collective-permute-start.39 = (bf16[2,32,1024]{2,1,0:T(8,128)(2,1)S(1)}, bf16[2,32,1024]{2,1,0:T(8,128)(2,1)S(1)}, u32[]{:S(2)}, u32[]{:S(2)}) collective-permute-start(bf16[2,32,1024]{2,1,0:T(8,128)(2,1)S(1)} %pad_maximum_fusion.10), channel_id=1, source_target_pairs={{0,4},{1,5},{2,6},{3,7},{4,0},{5,1},{6,2},{7,3},{8,12},{9,13},{10,... | collective-permute-start | bytes 393224 | tf_op jit(solution)/shard_map/ppermute | solution.py:37
  210.8 9.3 %collective-permute-start.44 = (bf16[4,32,1024]{2,1,0:T(8,128)(2,1)S(1)}, bf16[4,32,1024]{2,1,0:T(8,128)(2,1)S(1)}, u32[]{:S(2)}, u32[]{:S(2)}) collective-permute-start(bf16[4,32,1024]{2,1,0:T(8,128)(2,1)S(1)} %pad_maximum_fusion.7), channel_id=1, source_target_pairs={{0,2},{1,3},{2,0},{3,1},{4,6},{5,7},{6,4},{7,5},{8,10},{9,11},{10,... | collective-permute-start | bytes 786440 | tf_op jit(solution)/shard_map/ppermute | solution.py:37
  212.2 11.7 %collective-permute-start.40 = (bf16[4,32,1024]{2,1,0:T(8,128)(2,1)S(1)}, bf16[4,32,1024]{2,1,0:T(8,128)(2,1)S(1)}, u32[]{:S(2)}, u32[]{:S(2)}) collective-permute-start(bf16[4,32,1024]{2,1,0:T(8,128)(2,1)S(1)} %pad_maximum_fusion.6), channel_id=1, source_target_pairs={{0,2},{1,3},{2,0},{3,1},{4,6},{5,7},{6,4},{7,5},{8,10},{9,11},{10,... | collective-permute-start | bytes 786440 | tf_op jit(solution)/shard_map/ppermute | solution.py:37
  220.1 13.6 %collective-permute-start.45 = (bf16[8,32,1024]{2,1,0:T(8,128)(2,1)S(1)}, bf16[8,32,1024]{2,1,0:T(8,128)(2,1)S(1)}, u32[]{:S(2)}, u32[]{:S(2)}) collective-permute-start(bf16[8,32,1024]{2,1,0:T(8,128)(2,1)S(1)} %pad_maximum_fusion.3.v_b), channel_id=1, source_target_pairs={{0,1},{1,0},{2,3},{3,2},{4,5},{5,4},{6,7},{7,6},{8,9},{9,8},{10,11... | collective-permute-start | bytes 1572872 | tf_op jit(solution)/shard_map/ppermute | solution.py:37
  224.0 9.7 %collective-permute-start.41 = (bf16[8,32,1024]{2,1,0:T(8,128)(2,1)S(1)}, bf16[8,32,1024]{2,1,0:T(8,128)(2,1)S(1)}, u32[]{:S(2)}, u32[]{:S(2)}) collective-permute-start(bf16[8,32,1024]{2,1,0:T(8,128)(2,1)S(1)} %pad_maximum_fusion.2.v_a), channel_id=1, source_target_pairs={{0,1},{1,0},{2,3},{3,2},{4,5},{5,4},{6,7},{7,6},{8,9},{9,8},{10,11... | collective-permute-start | bytes 1572872 | tf_op jit(solution)/shard_map/ppermute | solution.py:37
  250.0 24.8 %collective-permute-start.50 = (f16[8,64,1024]{2,1,0:T(8,128)(2,1)}, f16[8,64,1024]{2,1,0:T(8,128)(2,1)}, u32[]{:S(2)}, u32[]{:S(2)}) collective-permute-start(f16[8,64,1024]{2,1,0:T(8,128)(2,1)} %multiply_convert_fusion), channel_id=1, source_target_pairs={{0,1},{1,0},{2,3},{3,2},{4,5},{5,4},{6,7},{7,6},{8,9},{9,8},{10,11... | collective-permute-start | bytes 3145736 | tf_op jit(solution)/shard_map/ppermute | solution.py:37
  252.6 7.5 %collective-permute-start.49 = (f32[64,64]{0,1:T(8,128)S(1)}, f32[64,64]{0,1:T(8,128)S(1)}, u32[]{:S(2)}, u32[]{:S(2)}) collective-permute-start(f32[64,64]{0,1:T(8,128)S(1)} %add.225), channel_id=1, source_target_pairs={{0,8},{1,9},{2,10},{3,11},{4,12},{5,13},{6,14},{7,15},{8,0},{9,1},... | collective-permute-start | bytes 49160 | tf_op jit(solution)/shard_map/ppermute | solution.py:37
  276.9 7.9 %collective-permute-start.51 = (f16[2,2,32,1024]{3,2,0,1:T(8,128)(2,1)S(1)}, f16[2,2,32,1024]{3,2,0,1:T(8,128)(2,1)S(1)}, u32[]{:S(2)}, u32[]{:S(2)}) collective-permute-start(f16[2,2,32,1024]{3,2,0,1:T(8,128)(2,1)S(1)} %fusion.20), channel_id=1, source_target_pairs={{0,2},{1,3},{2,0},{3,1},{4,6},{5,7},{6,4},{7,5},{8,10},{9,11},{10,... | collective-permute-start | bytes 786440 | tf_op jit(solution)/shard_map/ppermute | solution.py:37
  280.0 7.5 %collective-permute-start.54 = (f16[2,2,32,1024]{3,2,1,0:T(8,128)(2,1)S(1)}, f16[2,2,32,1024]{3,2,1,0:T(8,128)(2,1)S(1)}, u32[]{:S(2)}, u32[]{:S(2)}) collective-permute-start(f16[2,2,32,1024]{3,2,1,0:T(8,128)(2,1)S(1)} %fusion.9), channel_id=1, source_target_pairs={{0,4},{1,5},{2,6},{3,7},{4,0},{5,1},{6,2},{7,3},{8,12},{9,13},{10,... | collective-permute-start | bytes 786440 | tf_op jit(solution)/shard_map/ppermute | solution.py:37
  285.1 6.4 %collective-permute-start.52 = (f16[2,32,1024]{2,1,0:T(8,128)(2,1)S(1)}, f16[2,32,1024]{2,1,0:T(8,128)(2,1)S(1)}, u32[]{:S(2)}, u32[]{:S(2)}) collective-permute-start(f16[2,32,1024]{2,1,0:T(8,128)(2,1)S(1)} %fusion.30), channel_id=1, source_target_pairs={{0,4},{1,5},{2,6},{3,7},{4,0},{5,1},{6,2},{7,3},{8,12},{9,13},{10,... | collective-permute-start | bytes 393224 | tf_op jit(solution)/shard_map/ppermute | solution.py:37
  287.8 9.6 %collective-permute-start.55 = (f16[2,32,1024]{2,1,0:T(8,128)(2,1)S(1)}, f16[2,32,1024]{2,1,0:T(8,128)(2,1)S(1)}, u32[]{:S(2)}, u32[]{:S(2)}) collective-permute-start(f16[2,32,1024]{2,1,0:T(8,128)(2,1)S(1)} %fusion.27), channel_id=1, source_target_pairs={{0,8},{1,9},{2,10},{3,11},{4,12},{5,13},{6,14},{7,15},{8,0},{9,1},... | collective-permute-start | bytes 393224 | tf_op jit(solution)/shard_map/ppermute | solution.py:37
  291.7 6.4 %collective-permute-start.53 = (f16[32,1024]{1,0:T(8,128)(2,1)S(1)}, f16[32,1024]{1,0:T(8,128)(2,1)S(1)}, u32[]{:S(2)}, u32[]{:S(2)}) collective-permute-start(f16[32,1024]{1,0:T(8,128)(2,1)S(1)} %fusion.51), channel_id=1, source_target_pairs={{0,8},{1,9},{2,10},{3,11},{4,12},{5,13},{6,14},{7,15},{8,0},{9,1},... | collective-permute-start | bytes 196616 | tf_op jit(solution)/shard_map/ppermute | solution.py:37
  297.6 4.3 %collective-permute-start.56 = (f16[32,1024]{1,0:T(8,128)(2,1)S(1)}, f16[32,1024]{1,0:T(8,128)(2,1)S(1)}, u32[]{:S(2)}, u32[]{:S(2)}) collective-permute-start(f16[32,1024]{1,0:T(8,128)(2,1)S(1)} %fusion.48), channel_id=1, source_target_pairs={{0,2},{1,3},{2,0},{3,1},{4,6},{5,7},{6,4},{7,5},{8,10},{9,11},{10,... | collective-permute-start | bytes 196616 | tf_op jit(solution)/shard_map/ppermute | solution.py:37
  (21 other events, 91.1 us)

commit v2 on v1

v2 whole, which is shorter than its diff:
```python
import functools

import jax
import jax.numpy as jnp
from jax import lax
from jax.experimental import pallas as pl
from jax.experimental.pallas import tpu as pltpu
from jax.sharding import PartitionSpec as P

K = 64
HALF = K // 2
RIDGE = 0.1
BOUND = 18.0
TOP = 60000.0
TINY = 1e-30
F32, BF16, F16 = jnp.float32, jnp.bfloat16, jnp.float16


def precise(left, right):
    return jnp.dot(left, right, precision=lax.Precision.HIGHEST, preferred_element_type=F32)


def outer(left, right):
    return lax.dot_general(
        left, right, (((1,), (1,)), ((), ())), precision=lax.Precision.HIGHEST, preferred_element_type=F32
    )


def symmetric(matrix):
    return 0.5 * (matrix + matrix.T)


def solve_positive(matrix, target):
    return jax.scipy.linalg.cho_solve((jnp.linalg.cholesky(matrix), True), target)


def swap(value, bit, n):
    return lax.ppermute(value, "dp", [(i, i ^ bit) for i in range(n)])


def total(value, n):
    bit = 1
    while bit < n:
        value = value + swap(value, bit, n)
        bit *= 2
    return value


def hop_bits(n):
    bits = [1 << i for i in range(1, n.bit_length() - 1)]
    return bits, bits[1:] + bits[:1]


def _rel(step, shifts):
    j = 0
    for place, shift in enumerate(shifts):
        j = j | (((step >> place) & 1) << shift)
    return j


def _pos(j, shifts):
    p = 0
    for place, shift in enumerate(shifts):
        p = p | (((j >> shift) & 1) << place)
    return p


def sums_kernel(me, labels, counts, acts, out, peak, weight, member):
    step = pl.program_id(0)

    @pl.when(step == 0)
    def _():
        concept = lax.broadcasted_iota(jnp.int32, member.shape, 0)
        full = jnp.where(labels[...] == concept, counts[...].astype(F32), 0.0)
        member[...] = full.astype(BF16)
        weight[...] = jnp.sum(full, axis=1, keepdims=True)
        peak[...] = jnp.zeros_like(peak)

    block = jnp.dot(member[...], acts[...], preferred_element_type=F32)
    out[0] = block
    peak[...] = jnp.maximum(peak[...], jnp.max(jnp.abs(block), axis=1, keepdims=True))


def class_sums(me, labels, counts, acts, n, half):
    rows, d = acts.shape
    f = d // n
    return pl.pallas_call(
        sums_kernel,
        out_shape=(
            jax.ShapeDtypeStruct((n // 2, K, f), F32),
            jax.ShapeDtypeStruct((K, 1), F32),
            jax.ShapeDtypeStruct((K, 1), F32),
        ),
        grid_spec=pltpu.PrefetchScalarGridSpec(
            num_scalar_prefetch=1,
            grid=(n // 2,),
            in_specs=[
                pl.BlockSpec((1, rows), lambda i, me: (0, 0)),
                pl.BlockSpec((1, rows), lambda i, me: (0, 0)),
                pl.BlockSpec((rows, f), lambda i, me: (0, me[0] ^ (2 * i + half))),
            ],
            out_specs=(
                pl.BlockSpec((1, K, f), lambda i, me: (i, 0, 0)),
                pl.BlockSpec((K, 1), lambda i, me: (0, 0)),
                pl.BlockSpec((K, 1), lambda i, me: (0, 0)),
            ),
            scratch_shapes=[pltpu.VMEM((K, rows), BF16)],
        ),
        compiler_params=pltpu.CompilerParams(vmem_limit_bytes=8 << 20),
        cost_estimate=pl.CostEstimate(flops=K * rows * d, bytes_accessed=rows * d + 2 * K * d, transcendentals=0),
        name="class_sums",
    )(me, labels, counts, acts)


def probe_kernel(me, v_a, v_b, acts, out):
    @pl.when(pl.program_id(0) == 0)
    def _():
        out[...] = jnp.zeros_like(out)

    v = jnp.concatenate([v_a[0], v_b[0]], axis=0)
    out[...] += lax.dot_general(v, acts[...], (((1,), (1,)), ((), ())), preferred_element_type=F32)


def probe(me, v_a, v_b, acts, n, shifts_a, shifts_b):
    rows, d = acts.shape
    f = d // n
    return pl.pallas_call(
        probe_kernel,
        out_shape=jax.ShapeDtypeStruct((K, rows), F32),
        grid_spec=pltpu.PrefetchScalarGridSpec(
            num_scalar_prefetch=1,
            grid=(n // 2,),
            in_specs=[
                pl.BlockSpec((1, HALF, f), lambda i, me: (_pos(_rel(i, shifts_a), shifts_a), 0, 0)),
                pl.BlockSpec((1, HALF, f), lambda i, me: (_pos(_rel(i, shifts_a), shifts_b), 0, 0)),
                pl.BlockSpec((rows, f), lambda i, me: (0, me[0] ^ _rel(i, shifts_a))),
            ],
            out_specs=pl.BlockSpec((K, rows), lambda i, me: (0, 0)),
        ),
        compiler_params=pltpu.CompilerParams(vmem_limit_bytes=8 << 20),
        cost_estimate=pl.CostEstimate(flops=K * rows * d, bytes_accessed=rows * d + K * d, transcendentals=0),
        name="probe",
    )(me, v_a, v_b, acts)


def send_kernel(steps, mixed, me, v_a, v_b, acts, start, counts, *refs):
    if mixed:
        offset, mix, probed, gram, out, weighted = refs
    else:
        probed, gram, out, weighted = refs
    step = pl.program_id(0)

    @pl.when(step == 0)
    def _():
        probed[...] = start[...]

    @pl.when(step < steps)
    def _():
        v = jnp.concatenate([v_a[0], v_b[0]], axis=0)
        probed[...] += lax.dot_general(v, acts[...], (((1,), (1,)), ((), ())), preferred_element_type=F32)

    @pl.when(step == steps)
    def _():
        if mixed:
            probed[...] = offset[...] - precise(mix[...], probed[...])
        weighted[...] = (counts[...].astype(F32) * probed[...]).astype(BF16)
        gram[...] = outer(probed[...], weighted[...].astype(F32))

    @pl.when(step >= steps)
    def _():
        out[0] = jnp.dot(weighted[...], acts[...], preferred_element_type=F32)


def probe_and_send(me, v_a, v_b, acts, start, counts, mixing, n, shifts_a, shifts_b):
    rows, d = acts.shape
    f = d // n
    s = n // 2

    def j_of(i):
        return _rel(jnp.minimum(i, s - 1), shifts_a)

    def out_of(i):
        return jnp.maximum(i - s, 0)

    return pl.pallas_call(
        functools.partial(send_kernel, s, bool(mixing)),
        out_shape=(
            jax.ShapeDtypeStruct((K, rows), F32),
            jax.ShapeDtypeStruct((K, K), F32),
            jax.ShapeDtypeStruct((s, K, f), F32),
        ),
        grid_spec=pltpu.PrefetchScalarGridSpec(
            num_scalar_prefetch=1,
            grid=(2 * s,),
            in_specs=[
                pl.BlockSpec((1, HALF, f), lambda i, me: (_pos(j_of(i), shifts_a), 0, 0)),
                pl.BlockSpec((1, HALF, f), lambda i, me: (_pos(j_of(i), shifts_b), 0, 0)),
                pl.BlockSpec(
                    (rows, f), lambda i, me: (0, me[0] ^ 1 ^ jnp.where(i < s, j_of(i), 2 * out_of(i)))
                ),
                pl.BlockSpec((K, rows), lambda i, me: (0, 0)),
                pl.BlockSpec((1, rows), lambda i, me: (0, 0)),
            ]
            + [pl.BlockSpec((K, x.shape[1]), lambda i, me: (0, 0)) for x in mixing],
            out_specs=(
                pl.BlockSpec((K, rows), lambda i, me: (0, 0)),
                pl.BlockSpec((K, K), lambda i, me: (0, 0)),
                pl.BlockSpec((1, K, f), lambda i, me: (out_of(i), 0, 0)),
            ),
            scratch_shapes=[pltpu.VMEM((K, rows), BF16)],
        ),
        compiler_params=pltpu.CompilerParams(vmem_limit_bytes=8 << 20),
        cost_estimate=pl.CostEstimate(flops=2 * K * rows * d, bytes_accessed=rows * d + 2 * K * d, transcendentals=0),
        name="probe_and_send",
    )(me, v_a, v_b, acts, start, counts, *mixing)


def keep_kernel(me, probed, counts, acts, out, weighted):
    @pl.when(pl.program_id(0) == 0)
    def _():
        weighted[...] = (counts[...].astype(F32) * probed[...]).astype(BF16)

    out[0] = jnp.dot(weighted[...], acts[...], preferred_element_type=F32)


def panel_keep(me, probed, counts, acts, n):
    rows, d = acts.shape
    f = d // n
    return pl.pallas_call(
        keep_kernel,
        out_shape=jax.ShapeDtypeStruct((n // 2, K, f), F32),
        grid_spec=pltpu.PrefetchScalarGridSpec(
            num_scalar_prefetch=1,
            grid=(n // 2,),
            in_specs=[
                pl.BlockSpec((K, rows), lambda i, me: (0, 0)),
                pl.BlockSpec((1, rows), lambda i, me: (0, 0)),
                pl.BlockSpec((rows, f), lambda i, me: (0, me[0] ^ (2 * i))),
            ],
            out_specs=pl.BlockSpec((1, K, f), lambda i, me: (i, 0, 0)),
            scratch_shapes=[pltpu.VMEM((K, rows), BF16)],
        ),
        compiler_params=pltpu.CompilerParams(vmem_limit_bytes=8 << 20),
        cost_estimate=pl.CostEstimate(flops=K * rows * d, bytes_accessed=rows * d + 2 * K * d, transcendentals=0),
        name="panel_keep",
    )(me, probed, counts, acts)


def shrink(value, bound):
    return (value * (TOP / jnp.maximum(bound, TINY))).astype(F16)


def grow(value, bound):
    return value.astype(F32) * (jnp.maximum(bound, TINY) * (1.0 / TOP))


def scatter_stream(blocks, order, n, bound, shared):
    bits = n.bit_length() - 2
    rows, f = blocks.shape[1:]
    value = blocks.reshape((2,) * bits + (rows, f))
    left = [1 << i for i in range(bits, 0, -1)]
    for bit in order:
        axis = left.index(bit)
        keep = lax.index_in_dim(value, 0, axis, keepdims=False)
        send = lax.index_in_dim(value, 1, axis, keepdims=False)
        left.remove(bit)
        got = swap(shrink(send, bound), bit, n)
        theirs = bound if shared else swap(bound, bit, n)
        value = keep + grow(got, theirs)
        if not shared:
            bound = 1.001 * (bound + theirs)
    return value


def gather_stream(block, order, n):
    value = block[None]
    for bit in order:
        value = jnp.concatenate([value, swap(value, bit, n)], axis=0)
    return value


def per_device(n, activations, labels, counts):
    rows, d = activations.shape
    activations = pltpu.with_memory_space_constraint(activations, pltpu.HBM)
    me = lax.axis_index("dp").astype(jnp.int32).reshape(1)
    labels = labels.reshape(1, rows)
    counts = counts.reshape(1, rows)
    order_y, order_z = hop_bits(n)
    order_a, order_b = order_y[::-1], order_z
    shifts_a = [bit.bit_length() - 1 for bit in order_a]
    shifts_b = [bit.bit_length() - 1 for bit in order_b]

    sent, peak_sent, weight = class_sums(me, labels, counts, activations, n, 1)
    peak_sent = jnp.max(peak_sent, keepdims=True)
    got = swap(shrink(sent, peak_sent), 1, n)
    peak_got = swap(peak_sent, 1, n)
    kept, peak, _ = class_sums(me, labels, counts, activations, n, 0)
    blocks = kept + grow(got, peak_got)
    bound = 1.001 * (jnp.max(peak, keepdims=True) + peak_got)
    class_weight = total(weight, n)
    total_weight = jnp.sum(class_weight)
    sums = jnp.concatenate(
        [
            scatter_stream(blocks[:, :HALF], order_y, n, bound, False),
            scatter_stream(blocks[:, HALF:], order_z, n, bound, False),
        ],
        axis=0,
    )
    base = (sums / class_weight) * jnp.sqrt(class_weight)

    def apply(panel, mixing, norms):
        v = panel.astype(BF16)
        v_a = gather_stream(v[:HALF], order_a, n)
        v_b = gather_stream(v[HALF:], order_b, n)
        far_a, far_b = swap(v_a, 1, n), swap(v_b, 1, n)
        start = probe(me, v_a, v_b, activations, n, shifts_a, shifts_b)
        mixing, norms = mixing(), norms()
        bound = (1.02 * BOUND * BOUND * d**0.5) * total_weight * norms
        probed, gram, sent = probe_and_send(
            me, far_a, far_b, activations, start, counts, mixing, n, shifts_a, shifts_b
        )
        got = swap(shrink(sent, bound), 1, n)
        blocks = panel_keep(me, probed, counts, activations, n) + grow(got, bound)
        gram = total(gram, n)
        own = jnp.concatenate(
            [
                scatter_stream(blocks[:, :HALF], order_y, n, bound[:HALF], True),
                scatter_stream(blocks[:, HALF:], order_z, n, bound[HALF:], True),
            ],
            axis=0,
        )
        return probed, gram, own

    current = symmetric(total(outer(base, base), n))
    norm_base = jnp.sqrt(jnp.diag(current))[:, None]
    first, along_panel, panel = apply(base, lambda: (), lambda: norm_base)

    image = panel / total_weight + (RIDGE * base - precise(current / total_weight, base))
    curvature = symmetric((along_panel - precise(current, current)) / total_weight + RIDGE * current)
    alpha = solve_positive(curvature, current)
    alpha_t = alpha.T
    grams = total(outer(jnp.concatenate([image, base], axis=0), image), n)
    image_image, base_image = symmetric(grams[:K]), grams[K:]
    moved = precise(base_image, alpha)
    renewed = symmetric(current - moved - moved.T + precise(alpha_t, precise(image_image, alpha)))
    mixed = current - moved
    beta = solve_positive(current, renewed)
    beta_t = beta.T

    def mixing():
        return first + precise(beta_t, first), alpha_t

    def norms():
        norm_image = jnp.sqrt(jnp.diag(image_image))[:, None]
        return norm_base + precise(jnp.abs(beta_t), norm_base) + precise(jnp.abs(alpha_t), norm_image)

    _, along_panel, panel = apply(image, mixing, norms)

    residual = base - precise(alpha_t, image)
    direction = residual + precise(beta_t, base)
    cross = mixed + precise(current, beta)
    along = renewed + precise(mixed.T, beta) + precise(beta_t, cross)
    curvature = symmetric((along_panel - precise(cross.T, cross)) / total_weight + RIDGE * along)
    step = solve_positive(curvature, renewed).T
    solution = precise(alpha_t, base) + precise(step, direction)
    rest = residual - precise(step, RIDGE * direction - precise(cross.T / total_weight, base))
    residual = rest - precise(step / total_weight, panel)
    return (solution.T, residual.T)


def solution(mesh):
    in_specs = (P(("groups", "dp"), None), P(("groups", "dp")), P(("groups", "dp")))
    out_specs = (P(("groups", "dp"), None), P(("groups", "dp"), None))
    return jax.shard_map(
        functools.partial(per_device, mesh.shape["dp"]),
        mesh=mesh,
        in_specs=in_specs,
        out_specs=out_specs,
        check_vma=False,
    )
```

time: 305 us -> 305 us (level)
  waiting for transfers between devices: 121 us -> 86.3 us
  Pallas kernels: 37.3 us -> 64.9 us
  local copies, waits for them, and re-layouts: 28.4 us -> 6.04 us
  starting transfers between devices: 54 us -> 70.9 us
  between operations: 2.33 us -> 11 us
  other arithmetic: 47.4 us -> 51 us
    ppermute x57 -> x64, waiting for transfers between devices: 121 us -> 86.3 us  [swap(): return lax.ppermute(value, 'dp', [(i, i ^ bit) for i in range(n)])]
    unnamed x25 -> x12, local copies, waits for them, and re-layouts: 23.5 us -> 1.14 us
    ppermute x57 -> x64, starting transfers between devices: 54 us -> 70.9 us  [swap(): return lax.ppermute(value, 'dp', [(i, i ^ bit) for i in range(n)])]
    pallas_call x4, Pallas kernels: 24.5 us -> 39 us  [the longest x2 25.5 us: probe_and_send(): pl.pallas_call(functools.partial(send_kernel, s, bool(mixing)), out_shape...]
    pallas_call x2, Pallas kernels: 5.71 us -> 12.6 us  [panel_keep(): pl.pallas_call(keep_kernel, out_shape=jax.ShapeDtypeStruct((n // 2, K, f)...]
    pallas_call x2, Pallas kernels: 7.12 us -> 13.3 us  [probe(): pl.pallas_call(probe_kernel, out_shape=jax.ShapeDtypeStruct((K, rows), F3...]
    add x22 -> x23, other arithmetic: 6.23 us -> 6.99 us  [the longest x2 3.33 us: apply(): blocks = panel_keep(me, probed, counts, activations, n) + grow(got, bound)]
    dot_general x16 -> x19, matrix products: 10.9 us -> 10.9 us  [precise(): jnp.dot(left, right, precision=lax.Precision.HIGHEST, preferred_element_t...]
  transfers between devices with their start and end apart: 57 -> 64, of which waited for: 37 -> 33; matrix products, arithmetic and copies ran while one was open for 18% -> 19% of each run, Pallas kernels for 5% -> 11%
where the time goes in v2:
time: 305 us; the launch traced here: 303 us
  waiting for transfers between devices  86.3 us (28%)
  starting transfers between devices  70.9 us (23%)
  Pallas kernels  64.9 us (21%)
  other arithmetic  51 us (17%)
  matrix products  13.1 us (4%)
  between operations  11 us (4%)
  local copies, waits for them, and re-layouts  6.04 us (2%)
    ppermute x64, waiting for transfers between devices, swap(): return lax.ppermute(value, 'dp', [(i, i ^ bit) for i in range(n)])  86.3 us
    ppermute x64, starting transfers between devices, swap(): return lax.ppermute(value, 'dp', [(i, i ^ bit) for i in range(n)])  70.9 us
    pallas_call x2, Pallas kernels, probe_and_send(): pl.pallas_call(functools.partial(send_kernel, s, bool(mixing)), out_shape...  25.5 us
    another operation x9, other arithmetic, solve_positive(): jnp.linalg.cholesky(matrix)  19.7 us
    another operation x6, other arithmetic, solve_positive(): jax.scipy.linalg.cho_solve((jnp.linalg.cholesky(matrix), True), target)  16.7 us
    pallas_call x2, Pallas kernels, class_sums(): pl.pallas_call(sums_kernel, out_shape=(jax.ShapeDtypeStruct((n // 2, K, f...  13.5 us
    pallas_call x2, Pallas kernels, probe(): pl.pallas_call(probe_kernel, out_shape=jax.ShapeDtypeStruct((K, rows), F3...  13.3 us
    pallas_call x2, Pallas kernels, panel_keep(): pl.pallas_call(keep_kernel, out_shape=jax.ShapeDtypeStruct((n // 2, K, f)...  12.6 us
  transfers between devices with their start and end apart: 64, of which 33 were waited for; matrix products, arithmetic and copies ran while one was open for 19% of the time, Pallas kernels for 11%

profile of v2, /device:TPU:0, one launch (start us, length us, event | category | flops | bytes accessed | tf_op | source)
XLA Modules:
  0.0 303.2 jit_solution(6074087826892004449)
XLA Ops:
  2.0 6.6 %class_sums.3 = (f32[8,64,1024]{2,1,0:T(8,128)S(1)}, f32[64,1]{1,0:T(8,128)S(1)}, f32[64,1]{1,0:T(8,128)S(1)}) custom-call(s32[1]{0:T(128)} %bitcast.me, s32[1,384]{1,0:T(1,128)S(1)} %reshape.159.labels, s32[1,384]{1,0:T(1,128)S(1)} %reshape.160.counts, bf16[384,16384]{1,0:T(8,128)(2,1)} %acts.15), custom_call_target="tpu_custom_call" | custom-call | flops 402653184 | bytes 8388608 | tf_op jit(solution)/shard_map/class_sums/pallas_call | solution.py:87
  11.2 6.9 %class_sums.2 = (f32[8,64,1024]{2,1,0:T(8,128)S(1)}, f32[64,1]{1,0:T(8,128)S(1)}, f32[64,1]{1,0:T(8,128)}) custom-call(s32[1]{0:T(128)} %bitcast.me, s32[1,384]{1,0:T(1,128)S(1)} %reshape.159.labels, s32[1,384]{1,0:T(1,128)S(1)} %reshape.160.counts, bf16[384,16384]{1,0:T(8,128)(2,1)} %acts.15), custom_call_target="tpu_custom_call" | custom-call | flops 402653184 | bytes 8388608 | tf_op jit(solution)/shard_map/class_sums/pallas_call | solution.py:87
  20.0 4.0 %collective-permute-start.9 = (f32[1,1]{1,0:T(1,128)}, f32[1,1]{1,0:T(1,128)}, u32[]{:S(2)}, u32[]{:S(2)}) collective-permute-start(f32[1,1]{1,0:T(1,128)} %mul.520), channel_id=1, source_target_pairs={{0,4},{1,5},{2,6},{3,7},{4,0},{5,1},{6,2},{7,3},{8,12},{9,13},{10,... | collective-permute-start | bytes 20 | tf_op jit(solution)/shard_map/ppermute | solution.py:38
  24.0 2.8 collective-permute-start.3
  28.1 4.0 %collective-permute-start.11 = (f32[1,1]{1,0:T(1,128)}, f32[1,1]{1,0:T(1,128)}, u32[]{:S(2)}, u32[]{:S(2)}) collective-permute-start(f32[1,1]{1,0:T(1,128)} %mul.550), channel_id=1, source_target_pairs={{0,8},{1,9},{2,10},{3,11},{4,12},{5,13},{6,14},{7,15},{8,0},{9,1},... | collective-permute-start | bytes 20 | tf_op jit(solution)/shard_map/ppermute | solution.py:38
  36.3 1.9 collective-permute-start.13
  46.2 2.6 collective-permute-start.17
  53.6 1.8 collective-permute-start.8
  57.2 4.4 %collective-permute-done.8 = f16[2,2,32,1024]{3,2,1,0:T(8,128)(2,1)S(1)} collective-permute-done((f16[2,2,32,1024]{3,2,1,0:T(8,128)(2,1)S(1)}, f16[2,2,32,1024]{3,2,1,0:T(8,128)(2,1)S(1)}, u32[]{:S(2)}, u32[]{:S(2)}) %collective-permute-start.8) | collective-permute-done | bytes 262176 | tf_op jit(solution)/shard_map/ppermute | solution.py:38
  63.3 2.4 collective-permute-start.4
  65.7 3.3 %collective-permute-done.10 = f16[2,32,1024]{2,1,0:T(8,128)(2,1)S(1)} collective-permute-done((f16[2,32,1024]{2,1,0:T(8,128)(2,1)S(1)}, f16[2,32,1024]{2,1,0:T(8,128)(2,1)S(1)}, u32[]{:S(2)}, u32[]{:S(2)}) %collective-permute-start.10) | collective-permute-done | bytes 131104 | tf_op jit(solution)/shard_map/ppermute | solution.py:38
  70.9 2.6 collective-permute-done.12
  73.5 2.6 collective-permute-done.6
  79.5 3.1 %collective-permute-done.31 = f32[64,64]{1,0:T(8,128)S(1)} collective-permute-done((f32[64,64]{1,0:T(8,128)S(1)}, f32[64,64]{1,0:T(8,128)S(1)}, u32[]{:S(2)}, u32[]{:S(2)}) %collective-permute-start.31) | collective-permute-done | bytes 16416 | tf_op jit(solution)/shard_map/ppermute | solution.py:38
  82.6 2.1 collective-permute-start.22
  88.0 2.0 collective-permute-start.18
  90.0 3.3 %collective-permute-done.33 = f32[64,64]{1,0:T(8,128)S(1)} collective-permute-done((f32[64,64]{1,0:T(8,128)S(1)}, f32[64,64]{1,0:T(8,128)S(1)}, u32[]{:S(2)}, u32[]{:S(2)}) %collective-permute-start.33) | collective-permute-done | bytes 16416 | tf_op jit(solution)/shard_map/ppermute | solution.py:38
  93.5 1.9 collective-permute-done.18
  95.9 3.7 %collective-permute-done.23 = bf16[2,32,1024]{2,1,0:T(8,128)(2,1)S(1)} collective-permute-done((bf16[2,32,1024]{2,1,0:T(8,128)(2,1)S(1)}, bf16[2,32,1024]{2,1,0:T(8,128)(2,1)S(1)}, u32[]{:S(2)}, u32[]{:S(2)}) %collective-permute-start.23) | collective-permute-done | bytes 131104 | tf_op jit(solution)/shard_map/ppermute | solution.py:38
  101.9 5.8 %cholesky.70 = f32[64,64]{1,0:T(8,128)S(1)} custom-call(f32[64,64]{1,0:T(8,128)S(1)} %fusion.88), custom_call_target="Cholesky" | custom-call | tf_op jit(solution)/shard_map/jit(cholesky)/cholesky | solution.py:34
  107.7 1.9 collective-permute-done.20
  112.6 6.6 %probe.2.start = f32[64,384]{1,0:T(8,128)S(1)} custom-call(s32[1]{0:T(128)} %bitcast.me, bf16[8,32,1024]{2,1,0:T(8,128)(2,1)S(1)} %pad_maximum_fusion.v_a, bf16[8,32,1024]{2,1,0:T(8,128)(2,1)S(1)} %pad_maximum_fusion.1.v_b, bf16[384,16384]{1,0:T(8,128)(2,1)} %acts.15), custom_call_target="tpu_custom_call" | custom-call | flops 402653184 | bytes 7340032 | tf_op jit(solution)/shard_map/probe/pallas_call | solution.py:127
  119.2 12.6 %probe_and_send.2 = (f32[64,384]{1,0:T(8,128)S(1)}, f32[64,64]{1,0:T(8,128)S(1)}, f32[8,64,1024]{2,1,0:T(8,128)S(1)}) custom-call(s32[1]{0:T(128)} %bitcast.me, bf16[8,32,1024]{2,1,0:T(8,128)(2,1)S(1)} %collective-permute-done.21.v_a, bf16[8,32,1024]{2,1,0:T(8,128)(2,1)S(1)} %collective-permute-done.25.v_b, bf16[384,16384]{1,0:T(8,128)(2,1)} %acts.15, ...), custom_call_target="tpu_custom_call" | custom-call | flops 805306368 | bytes 8388608 | tf_op jit(solution)/shard_map/probe_and_send/pallas_call | solution.py:185
  134.0 4.9 %custom-call.14 = f32[1,64,64]{1,2,0:T(8,128)S(1)} custom-call(f32[1,64,64]{2,1,0:T(8,128)S(1)} %fusion.70), custom_call_target="InvertDiagBlocksLowerTriangular" | custom-call | tf_op jit(solution)/shard_map/jit(_cho_solve)/triangular_solve | solution.py:34
  140.4 2.6 collective-permute-done.28
  143.3 6.3 %panel_keep.2 = f32[8,64,1024]{2,1,0:T(8,128)S(1)} custom-call(s32[1]{0:T(128)} %bitcast.me, f32[64,384]{1,0:T(8,128)S(1)} %get-tuple-element.21.probed, s32[1,384]{1,0:T(1,128)S(1)} %reshape.160.counts, bf16[384,16384]{1,0:T(8,128)(2,1)} %acts.15), custom_call_target="tpu_custom_call" | custom-call | flops 402653184 | bytes 8388608 | tf_op jit(solution)/shard_map/panel_keep/pallas_call | solution.py:229
  150.6 5.8 %cholesky.59 = f32[64,64]{1,0:T(8,128)S(1)} custom-call(f32[64,64]{1,0:T(8,128)S(1)} %fusion.93), custom_call_target="Cholesky" | custom-call | tf_op jit(solution)/shard_map/jit(cholesky)/cholesky | solution.py:34
  157.9 4.9 %custom-call.13 = f32[1,64,64]{1,2,0:T(8,128)S(1)} custom-call(f32[1,64,64]{2,1,0:T(8,128)S(1)} %fusion.69), custom_call_target="InvertDiagBlocksLowerTriangular" | custom-call | tf_op jit(solution)/shard_map/jit(_cho_solve)/triangular_solve | solution.py:34
  166.5 2.1 collective-permute-start.38
  169.9 4.6 %collective-permute-done.38 = f16[2,2,32,1024]{3,2,1,0:T(8,128)(2,1)S(1)} collective-permute-done((f16[2,2,32,1024]{3,2,1,0:T(8,128)(2,1)S(1)}, f16[2,2,32,1024]{3,2,1,0:T(8,128)(2,1)S(1)}, u32[]{:S(2)}, u32[]{:S(2)}) %collective-permute-start.38) | collective-permute-done | bytes 262176 | tf_op jit(solution)/shard_map/ppermute | solution.py:38
  177.6 4.6 %collective-permute-done.39 = f16[2,32,1024]{2,1,0:T(8,128)(2,1)S(1)} collective-permute-done((f16[2,32,1024]{2,1,0:T(8,128)(2,1)S(1)}, f16[2,32,1024]{2,1,0:T(8,128)(2,1)S(1)}, u32[]{:S(2)}, u32[]{:S(2)}) %collective-permute-start.39) | collective-permute-done | bytes 131104 | tf_op jit(solution)/shard_map/ppermute | solution.py:38
  184.2 2.6 collective-permute-done.40
  186.9 2.2 collective-permute-done.37
  199.0 2.4 collective-permute-done.43
  204.0 4.3 %collective-permute-done.44 = f32[128,64]{1,0:T(8,128)S(1)} collective-permute-done((f32[128,64]{1,0:T(8,128)S(1)}, f32[128,64]{1,0:T(8,128)S(1)}, u32[]{:S(2)}, u32[]{:S(2)}) %collective-permute-start.44) | collective-permute-done | bytes 32800 | tf_op jit(solution)/shard_map/ppermute | solution.py:38
  214.6 6.4 %collective-permute-done.47 = bf16[4,32,1024]{2,1,0:T(8,128)(2,1)S(1)} collective-permute-done((bf16[4,32,1024]{2,1,0:T(8,128)(2,1)S(1)}, bf16[4,32,1024]{2,1,0:T(8,128)(2,1)S(1)}, u32[]{:S(2)}, u32[]{:S(2)}) %collective-permute-start.47) | collective-permute-done | bytes 262176 | tf_op jit(solution)/shard_map/ppermute | solution.py:38
  221.1 2.8 collective-permute-done.51
  225.4 6.7 %probe.3.start = f32[64,384]{1,0:T(8,128)S(1)} custom-call(s32[1]{0:T(128)} %bitcast.me, bf16[8,32,1024]{2,1,0:T(8,128)(2,1)S(1)} %pad_maximum_fusion.2.v_a, bf16[8,32,1024]{2,1,0:T(8,128)(2,1)S(1)} %pad_maximum_fusion.3.v_b, bf16[384,16384]{1,0:T(8,128)(2,1)} %acts.15), custom_call_target="tpu_custom_call" | custom-call | flops 402653184 | bytes 7340032 | tf_op jit(solution)/shard_map/probe/pallas_call | solution.py:127
  232.1 12.9 %probe_and_send.3 = (f32[64,384]{1,0:T(8,128)S(1)}, f32[64,64]{1,0:T(8,128)S(1)}, f32[8,64,1024]{2,1,0:T(8,128)S(1)}) custom-call(s32[1]{0:T(128)} %bitcast.me, bf16[8,32,1024]{2,1,0:T(8,128)(2,1)S(1)} %collective-permute-done.48.v_a, bf16[8,32,1024]{2,1,0:T(8,128)(2,1)S(1)} %collective-permute-done.52.v_b, bf16[384,16384]{1,0:T(8,128)(2,1)} %acts.15, ...), custom_call_target="tpu_custom_call" | custom-call | flops 805306368 | bytes 8388608 | tf_op jit(solution)/shard_map/probe_and_send/pallas_call | solution.py:185
  251.6 2.6 collective-permute-done.55
  254.7 6.3 %panel_keep.3 = f32[8,64,1024]{2,1,0:T(8,128)S(1)} custom-call(s32[1]{0:T(128)} %bitcast.me, f32[64,384]{1,0:T(8,128)S(1)} %get-tuple-element.24.probed, s32[1,384]{1,0:T(1,128)S(1)} %reshape.160.counts, bf16[384,16384]{1,0:T(8,128)(2,1)} %acts.15), custom_call_target="tpu_custom_call" | custom-call | flops 402653184 | bytes 8388608 | tf_op jit(solution)/shard_map/panel_keep/pallas_call | solution.py:229
  261.8 5.8 %cholesky.81 = f32[64,64]{1,0:T(8,128)S(1)} custom-call(f32[64,64]{1,0:T(8,128)S(1)} %fusion.79), custom_call_target="Cholesky" | custom-call | tf_op jit(solution)/shard_map/jit(cholesky)/cholesky | solution.py:34
  269.0 4.9 %custom-call.15 = f32[1,64,64]{1,2,0:T(8,128)S(1)} custom-call(f32[1,64,64]{2,1,0:T(8,128)S(1)} %fusion.71), custom_call_target="InvertDiagBlocksLowerTriangular" | custom-call | tf_op jit(solution)/shard_map/jit(_cho_solve)/triangular_solve | solution.py:34
  278.5 2.1 collective-permute-start.61
  282.5 3.9 %collective-permute-done.61 = f16[2,2,32,1024]{3,2,1,0:T(8,128)(2,1)S(1)} collective-permute-done((f16[2,2,32,1024]{3,2,1,0:T(8,128)(2,1)S(1)}, f16[2,2,32,1024]{3,2,1,0:T(8,128)(2,1)S(1)}, u32[]{:S(2)}, u32[]{:S(2)}) %collective-permute-start.61) | collective-permute-done | bytes 262176 | tf_op jit(solution)/shard_map/ppermute | solution.py:38
  289.5 4.6 %collective-permute-done.62 = f16[2,32,1024]{2,1,0:T(8,128)(2,1)S(1)} collective-permute-done((f16[2,32,1024]{2,1,0:T(8,128)(2,1)S(1)}, f16[2,32,1024]{2,1,0:T(8,128)(2,1)S(1)}, u32[]{:S(2)}, u32[]{:S(2)}) %collective-permute-start.62) | collective-permute-done | bytes 131104 | tf_op jit(solution)/shard_map/ppermute | solution.py:38
  296.6 2.0 collective-permute-done.63
  298.7 2.8 collective-permute-done.60
  (257 shorter events, 92.3 us)
Async XLA Ops:
  10.1 41.6 %collective-permute-start = (f16[8,64,1024]{2,1,0:T(8,128)(2,1)S(1)}, f16[8,64,1024]{2,1,0:T(8,128)(2,1)}, u32[]{:S(2)}, u32[]{:S(2)}) collective-permute-start(f16[8,64,1024]{2,1,0:T(8,128)(2,1)S(1)} %multiply_convert_fusion.2), channel_id=1, source_target_pairs={{0,1},{1,0},{2,3},{3,2},{4,5},{5,4},{6,7},{7,6},{8,9},{9,8},{10,11... | collective-permute-start | bytes 3145736 | tf_op jit(solution)/shard_map/ppermute | solution.py:38
  10.7 8.0 %collective-permute-start.1 = (f32[1,1]{1,0:T(1,128)}, f32[1,1]{1,0:T(1,128)}, u32[]{:S(2)}, u32[]{:S(2)}) collective-permute-start(f32[1,1]{1,0:T(1,128)} %bitcast.1), channel_id=1, source_target_pairs={{0,1},{1,0},{2,3},{3,2},{4,5},{5,4},{6,7},{7,6},{8,9},{9,8},{10,11... | collective-permute-start | bytes 20 | tf_op jit(solution)/shard_map/ppermute | solution.py:38
  10.7 27.4 %collective-permute-start.14 = (f32[64,1]{1,0:T(8,128)S(1)}, f32[64,1]{1,0:T(8,128)S(1)}, u32[]{:S(2)}, u32[]{:S(2)}) collective-permute-start(f32[64,1]{1,0:T(8,128)S(1)} %get-tuple-element.19), channel_id=1, source_target_pairs={{0,1},{1,0},{2,3},{3,2},{4,5},{5,4},{6,7},{7,6},{8,9},{9,8},{10,11... | collective-permute-start | bytes 776 | tf_op jit(solution)/shard_map/ppermute | solution.py:38
  20.0 7.5 %collective-permute-start.9 = (f32[1,1]{1,0:T(1,128)}, f32[1,1]{1,0:T(1,128)}, u32[]{:S(2)}, u32[]{:S(2)}) collective-permute-start(f32[1,1]{1,0:T(1,128)} %mul.520), channel_id=1, source_target_pairs={{0,4},{1,5},{2,6},{3,7},{4,0},{5,1},{6,2},{7,3},{8,12},{9,13},{10,... | collective-permute-start | bytes 20 | tf_op jit(solution)/shard_map/ppermute | solution.py:38
  24.0 8.0 %collective-permute-start.3 = (f32[1,1]{1,0:T(1,128)}, f32[1,1]{1,0:T(1,128)}, u32[]{:S(2)}, u32[]{:S(2)}) collective-permute-start(f32[1,1]{1,0:T(1,128)} %mul.520), channel_id=1, source_target_pairs={{0,2},{1,3},{2,0},{3,1},{4,6},{5,7},{6,4},{7,5},{8,10},{9,11},{10,... | collective-permute-start | bytes 20 | tf_op jit(solution)/shard_map/ppermute | solution.py:38
  28.1 7.6 %collective-permute-start.11 = (f32[1,1]{1,0:T(1,128)}, f32[1,1]{1,0:T(1,128)}, u32[]{:S(2)}, u32[]{:S(2)}) collective-permute-start(f32[1,1]{1,0:T(1,128)} %mul.550), channel_id=1, source_target_pairs={{0,8},{1,9},{2,10},{3,11},{4,12},{5,13},{6,14},{7,15},{8,0},{9,1},... | collective-permute-start | bytes 20 | tf_op jit(solution)/shard_map/ppermute | solution.py:38
  32.6 7.1 %collective-permute-start.5 = (f32[1,1]{1,0:T(1,128)}, f32[1,1]{1,0:T(1,128)}, u32[]{:S(2)}, u32[]{:S(2)}) collective-permute-start(f32[1,1]{1,0:T(1,128)} %mul.528), channel_id=1, source_target_pairs={{0,4},{1,5},{2,6},{3,7},{4,0},{5,1},{6,2},{7,3},{8,12},{9,13},{10,... | collective-permute-start | bytes 20 | tf_op jit(solution)/shard_map/ppermute | solution.py:38
  36.3 12.4 %collective-permute-start.13 = (f32[1,1]{1,0:T(1,128)}, f32[1,1]{1,0:T(1,128)}, u32[]{:S(2)}, u32[]{:S(2)}) collective-permute-start(f32[1,1]{1,0:T(1,128)} %mul.558), channel_id=1, source_target_pairs={{0,2},{1,3},{2,0},{3,1},{4,6},{5,7},{6,4},{7,5},{8,10},{9,11},{10,... | collective-permute-start | bytes 20 | tf_op jit(solution)/shard_map/ppermute | solution.py:38
  40.4 9.0 %collective-permute-start.7 = (f32[1,1]{1,0:T(1,128)}, f32[1,1]{1,0:T(1,128)}, u32[]{:S(2)}, u32[]{:S(2)}) collective-permute-start(f32[1,1]{1,0:T(1,128)} %mul.536), channel_id=1, source_target_pairs={{0,8},{1,9},{2,10},{3,11},{4,12},{5,13},{6,14},{7,15},{8,0},{9,1},... | collective-permute-start | bytes 20 | tf_op jit(solution)/shard_map/ppermute | solution.py:38
  53.6 8.0 %collective-permute-start.8 = (f16[2,2,32,1024]{3,2,1,0:T(8,128)(2,1)S(1)}, f16[2,2,32,1024]{3,2,1,0:T(8,128)(2,1)S(1)}, u32[]{:S(2)}, u32[]{:S(2)}) collective-permute-start(f16[2,2,32,1024]{3,2,1,0:T(8,128)(2,1)S(1)} %fusion.27), channel_id=1, source_target_pairs={{0,4},{1,5},{2,6},{3,7},{4,0},{5,1},{6,2},{7,3},{8,12},{9,13},{10,... | collective-permute-start | bytes 786440 | tf_op jit(solution)/shard_map/ppermute | solution.py:38
  55.6 7.6 %collective-permute-start.2 = (f16[2,2,32,1024]{3,2,0,1:T(8,128)(2,1)S(1)}, f16[2,2,32,1024]{3,2,0,1:T(8,128)(2,1)S(1)}, u32[]{:S(2)}, u32[]{:S(2)}) collective-permute-start(f16[2,2,32,1024]{3,2,0,1:T(8,128)(2,1)S(1)} %fusion.26), channel_id=1, source_target_pairs={{0,2},{1,3},{2,0},{3,1},{4,6},{5,7},{6,4},{7,5},{8,10},{9,11},{10,... | collective-permute-start | bytes 786440 | tf_op jit(solution)/shard_map/ppermute | solution.py:38
  61.7 7.3 %collective-permute-start.10 = (f16[2,32,1024]{2,1,0:T(8,128)(2,1)S(1)}, f16[2,32,1024]{2,1,0:T(8,128)(2,1)S(1)}, u32[]{:S(2)}, u32[]{:S(2)}) collective-permute-start(f16[2,32,1024]{2,1,0:T(8,128)(2,1)S(1)} %fusion.50), channel_id=1, source_target_pairs={{0,8},{1,9},{2,10},{3,11},{4,12},{5,13},{6,14},{7,15},{8,0},{9,1},... | collective-permute-start | bytes 393224 | tf_op jit(solution)/shard_map/ppermute | solution.py:38
  63.3 7.0 %collective-permute-start.4 = (f16[2,32,1024]{2,1,0:T(8,128)(2,1)S(1)}, f16[2,32,1024]{2,1,0:T(8,128)(2,1)S(1)}, u32[]{:S(2)}, u32[]{:S(2)}) collective-permute-start(f16[2,32,1024]{2,1,0:T(8,128)(2,1)S(1)} %fusion.49), channel_id=1, source_target_pairs={{0,4},{1,5},{2,6},{3,7},{4,0},{5,1},{6,2},{7,3},{8,12},{9,13},{10,... | collective-permute-start | bytes 393224 | tf_op jit(solution)/shard_map/ppermute | solution.py:38
  70.4 5.7 %collective-permute-start.6 = (f16[32,1024]{1,0:T(8,128)(2,1)S(1)}, f16[32,1024]{1,0:T(8,128)(2,1)S(1)}, u32[]{:S(2)}, u32[]{:S(2)}) collective-permute-start(f16[32,1024]{1,0:T(8,128)(2,1)S(1)} %fusion.67), channel_id=1, source_target_pairs={{0,8},{1,9},{2,10},{3,11},{4,12},{5,13},{6,14},{7,15},{8,0},{9,1},... | collective-permute-start | bytes 196616 | tf_op jit(solution)/shard_map/ppermute | solution.py:38
  82.6 10.8 %collective-permute-start.22 = (bf16[1,32,1024]{2,1,0:T(8,128)(2,1)S(1)}, bf16[1,32,1024]{2,1,0:T(8,128)(2,1)S(1)}, u32[]{:S(2)}, u32[]{:S(2)}) collective-permute-start(bf16[1,32,1024]{2,1,0:T(8,128)(2,1)S(1)} %get-tuple-element.49), channel_id=1, source_target_pairs={{0,4},{1,5},{2,6},{3,7},{4,0},{5,1},{6,2},{7,3},{8,12},{9,13},{10,... | collective-permute-start | bytes 196616 | tf_op jit(solution)/shard_map/ppermute | solution.py:38
  86.5 6.9 %collective-permute-start.33 = (f32[64,64]{1,0:T(8,128)S(1)}, f32[64,64]{1,0:T(8,128)S(1)}, u32[]{:S(2)}, u32[]{:S(2)}) collective-permute-start(f32[64,64]{1,0:T(8,128)S(1)} %add.233), channel_id=1, source_target_pairs={{0,8},{1,9},{2,10},{3,11},{4,12},{5,13},{6,14},{7,15},{8,0},{9,1},... | collective-permute-start | bytes 49160 | tf_op jit(solution)/shard_map/ppermute | solution.py:38
  88.0 7.5 %collective-permute-start.18 = (bf16[1,32,1024]{2,1,0:T(8,128)(2,1)S(1)}, bf16[1,32,1024]{2,1,0:T(8,128)(2,1)S(1)}, u32[]{:S(2)}, u32[]{:S(2)}) collective-permute-start(bf16[1,32,1024]{2,1,0:T(8,128)(2,1)S(1)} %get-tuple-element.50), channel_id=1, source_target_pairs={{0,8},{1,9},{2,10},{3,11},{4,12},{5,13},{6,14},{7,15},{8,0},{9,1},... | collective-permute-start | bytes 196616 | tf_op jit(solution)/shard_map/ppermute | solution.py:38
  93.4 6.1 %collective-permute-start.23 = (bf16[2,32,1024]{2,1,0:T(8,128)(2,1)S(1)}, bf16[2,32,1024]{2,1,0:T(8,128)(2,1)S(1)}, u32[]{:S(2)}, u32[]{:S(2)}) collective-permute-start(bf16[2,32,1024]{2,1,0:T(8,128)(2,1)S(1)} %pad_maximum_fusion.9), channel_id=1, source_target_pairs={{0,8},{1,9},{2,10},{3,11},{4,12},{5,13},{6,14},{7,15},{8,0},{9,1},... | collective-permute-start | bytes 393224 | tf_op jit(solution)/shard_map/ppermute | solution.py:38
  95.4 5.5 %collective-permute-start.19 = (bf16[2,32,1024]{2,1,0:T(8,128)(2,1)S(1)}, bf16[2,32,1024]{2,1,0:T(8,128)(2,1)S(1)}, u32[]{:S(2)}, u32[]{:S(2)}) collective-permute-start(bf16[2,32,1024]{2,1,0:T(8,128)(2,1)S(1)} %pad_maximum_fusion.8), channel_id=1, source_target_pairs={{0,4},{1,5},{2,6},{3,7},{4,0},{5,1},{6,2},{7,3},{8,12},{9,13},{10,... | collective-permute-start | bytes 393224 | tf_op jit(solution)/shard_map/ppermute | solution.py:38
  99.6 10.2 %collective-permute-start.24 = (bf16[4,32,1024]{2,1,0:T(8,128)(2,1)S(1)}, bf16[4,32,1024]{2,1,0:T(8,128)(2,1)S(1)}, u32[]{:S(2)}, u32[]{:S(2)}) collective-permute-start(bf16[4,32,1024]{2,1,0:T(8,128)(2,1)S(1)} %pad_maximum_fusion.5), channel_id=1, source_target_pairs={{0,2},{1,3},{2,0},{3,1},{4,6},{5,7},{6,4},{7,5},{8,10},{9,11},{10,... | collective-permute-start | bytes 786440 | tf_op jit(solution)/shard_map/ppermute | solution.py:38
  101.0 8.7 %collective-permute-start.20 = (bf16[4,32,1024]{2,1,0:T(8,128)(2,1)S(1)}, bf16[4,32,1024]{2,1,0:T(8,128)(2,1)S(1)}, u32[]{:S(2)}, u32[]{:S(2)}) collective-permute-start(bf16[4,32,1024]{2,1,0:T(8,128)(2,1)S(1)} %pad_maximum_fusion.4), channel_id=1, source_target_pairs={{0,2},{1,3},{2,0},{3,1},{4,6},{5,7},{6,4},{7,5},{8,10},{9,11},{10,... | collective-permute-start | bytes 786440 | tf_op jit(solution)/shard_map/ppermute | solution.py:38
  109.7 9.5 %collective-permute-start.21 = (bf16[8,32,1024]{2,1,0:T(8,128)(2,1)S(1)}, bf16[8,32,1024]{2,1,0:T(8,128)(2,1)S(1)}, u32[]{:S(2)}, u32[]{:S(2)}) collective-permute-start(bf16[8,32,1024]{2,1,0:T(8,128)(2,1)S(1)} %pad_maximum_fusion.v_a), channel_id=1, source_target_pairs={{0,1},{1,0},{2,3},{3,2},{4,5},{5,4},{6,7},{7,6},{8,9},{9,8},{10,11... | collective-permute-start | bytes 1572872 | tf_op jit(solution)/shard_map/ppermute | solution.py:38
  109.9 9.4 %collective-permute-start.25 = (bf16[8,32,1024]{2,1,0:T(8,128)(2,1)S(1)}, bf16[8,32,1024]{2,1,0:T(8,128)(2,1)S(1)}, u32[]{:S(2)}, u32[]{:S(2)}) collective-permute-start(bf16[8,32,1024]{2,1,0:T(8,128)(2,1)S(1)} %pad_maximum_fusion.1.v_b), channel_id=1, source_target_pairs={{0,1},{1,0},{2,3},{3,2},{4,5},{5,4},{6,7},{7,6},{8,9},{9,8},{10,11... | collective-permute-start | bytes 1572872 | tf_op jit(solution)/shard_map/ppermute | solution.py:38
  133.2 5.8 %collective-permute-start.27 = (f32[64,64]{0,1:T(8,128)S(1)}, f32[64,64]{0,1:T(8,128)S(1)}, u32[]{:S(2)}, u32[]{:S(2)}) collective-permute-start(f32[64,64]{0,1:T(8,128)S(1)} %add.227), channel_id=1, source_target_pairs={{0,2},{1,3},{2,0},{3,1},{4,6},{5,7},{6,4},{7,5},{8,10},{9,11},{10,... | collective-permute-start | bytes 49160 | tf_op jit(solution)/shard_map/ppermute | solution.py:38
  140.4 24.0 %collective-permute-start.34 = (f16[8,64,1024]{2,1,0:T(8,128)(2,1)}, f16[8,64,1024]{2,1,0:T(8,128)(2,1)}, u32[]{:S(2)}, u32[]{:S(2)}) collective-permute-start(f16[8,64,1024]{2,1,0:T(8,128)(2,1)} %multiply_convert_fusion.1), channel_id=1, source_target_pairs={{0,1},{1,0},{2,3},{3,2},{4,5},{5,4},{6,7},{7,6},{8,9},{9,8},{10,11... | collective-permute-start | bytes 3145736 | tf_op jit(solution)/shard_map/ppermute | solution.py:38
  143.0 6.7 %collective-permute-start.29 = (f32[64,64]{0,1:T(8,128)S(1)}, f32[64,64]{0,1:T(8,128)S(1)}, u32[]{:S(2)}, u32[]{:S(2)}) collective-permute-start(f32[64,64]{0,1:T(8,128)S(1)} %add.229), channel_id=1, source_target_pairs={{0,8},{1,9},{2,10},{3,11},{4,12},{5,13},{6,14},{7,15},{8,0},{9,1},... | collective-permute-start | bytes 49160 | tf_op jit(solution)/shard_map/ppermute | solution.py:38
  166.5 8.0 %collective-permute-start.38 = (f16[2,2,32,1024]{3,2,1,0:T(8,128)(2,1)S(1)}, f16[2,2,32,1024]{3,2,1,0:T(8,128)(2,1)S(1)}, u32[]{:S(2)}, u32[]{:S(2)}) collective-permute-start(f16[2,2,32,1024]{3,2,1,0:T(8,128)(2,1)S(1)} %fusion.9), channel_id=1, source_target_pairs={{0,4},{1,5},{2,6},{3,7},{4,0},{5,1},{6,2},{7,3},{8,12},{9,13},{10,... | collective-permute-start | bytes 786440 | tf_op jit(solution)/shard_map/ppermute | solution.py:38
  168.7 7.3 %collective-permute-start.35 = (f16[2,2,32,1024]{3,2,0,1:T(8,128)(2,1)S(1)}, f16[2,2,32,1024]{3,2,0,1:T(8,128)(2,1)S(1)}, u32[]{:S(2)}, u32[]{:S(2)}) collective-permute-start(f16[2,2,32,1024]{3,2,0,1:T(8,128)(2,1)S(1)} %fusion.22), channel_id=1, source_target_pairs={{0,2},{1,3},{2,0},{3,1},{4,6},{5,7},{6,4},{7,5},{8,10},{9,11},{10,... | collective-permute-start | bytes 786440 | tf_op jit(solution)/shard_map/ppermute | solution.py:38
  174.7 7.6 %collective-permute-start.39 = (f16[2,32,1024]{2,1,0:T(8,128)(2,1)S(1)}, f16[2,32,1024]{2,1,0:T(8,128)(2,1)S(1)}, u32[]{:S(2)}, u32[]{:S(2)}) collective-permute-start(f16[2,32,1024]{2,1,0:T(8,128)(2,1)S(1)} %fusion.35), channel_id=1, source_target_pairs={{0,8},{1,9},{2,10},{3,11},{4,12},{5,13},{6,14},{7,15},{8,0},{9,1},... | collective-permute-start | bytes 393224 | tf_op jit(solution)/shard_map/ppermute | solution.py:38
  176.3 7.4 %collective-permute-start.36 = (f16[2,32,1024]{2,1,0:T(8,128)(2,1)S(1)}, f16[2,32,1024]{2,1,0:T(8,128)(2,1)S(1)}, u32[]{:S(2)}, u32[]{:S(2)}) collective-permute-start(f16[2,32,1024]{2,1,0:T(8,128)(2,1)S(1)} %fusion.38), channel_id=1, source_target_pairs={{0,4},{1,5},{2,6},{3,7},{4,0},{5,1},{6,2},{7,3},{8,12},{9,13},{10,... | collective-permute-start | bytes 393224 | tf_op jit(solution)/shard_map/ppermute | solution.py:38
  183.9 5.2 %collective-permute-start.37 = (f16[32,1024]{1,0:T(8,128)(2,1)S(1)}, f16[32,1024]{1,0:T(8,128)(2,1)S(1)}, u32[]{:S(2)}, u32[]{:S(2)}) collective-permute-start(f16[32,1024]{1,0:T(8,128)(2,1)S(1)} %fusion.61), channel_id=1, source_target_pairs={{0,8},{1,9},{2,10},{3,11},{4,12},{5,13},{6,14},{7,15},{8,0},{9,1},... | collective-permute-start | bytes 196616 | tf_op jit(solution)/shard_map/ppermute | solution.py:38
  190.9 6.5 %collective-permute-start.49 = (bf16[1,32,1024]{2,1,0:T(8,128)(2,1)S(1)}, bf16[1,32,1024]{2,1,0:T(8,128)(2,1)S(1)}, u32[]{:S(2)}, u32[]{:S(2)}) collective-permute-start(bf16[1,32,1024]{2,1,0:T(8,128)(2,1)S(1)} %get-tuple-element.47), channel_id=1, source_target_pairs={{0,4},{1,5},{2,6},{3,7},{4,0},{5,1},{6,2},{7,3},{8,12},{9,13},{10,... | collective-permute-start | bytes 196616 | tf_op jit(solution)/shard_map/ppermute | solution.py:38
  193.4 9.3 %collective-permute-start.45 = (bf16[1,32,1024]{2,1,0:T(8,128)(2,1)S(1)}, bf16[1,32,1024]{2,1,0:T(8,128)(2,1)S(1)}, u32[]{:S(2)}, u32[]{:S(2)}) collective-permute-start(bf16[1,32,1024]{2,1,0:T(8,128)(2,1)S(1)} %get-tuple-element.48), channel_id=1, source_target_pairs={{0,8},{1,9},{2,10},{3,11},{4,12},{5,13},{6,14},{7,15},{8,0},{9,1},... | collective-permute-start | bytes 196616 | tf_op jit(solution)/shard_map/ppermute | solution.py:38
  196.4 5.0 %collective-permute-start.43 = (f32[128,64]{1,0:T(8,128)S(1)}, f32[128,64]{1,0:T(8,128)S(1)}, u32[]{:S(2)}, u32[]{:S(2)}) collective-permute-start(f32[128,64]{1,0:T(8,128)S(1)} %add.247), channel_id=1, source_target_pairs={{0,4},{1,5},{2,6},{3,7},{4,0},{5,1},{6,2},{7,3},{8,12},{9,13},{10,... | collective-permute-start | bytes 98312 | tf_op jit(solution)/shard_map/ppermute | solution.py:38
  197.4 15.4 %collective-permute-start.50 = (bf16[2,32,1024]{2,1,0:T(8,128)(2,1)S(1)}, bf16[2,32,1024]{2,1,0:T(8,128)(2,1)S(1)}, u32[]{:S(2)}, u32[]{:S(2)}) collective-permute-start(bf16[2,32,1024]{2,1,0:T(8,128)(2,1)S(1)} %pad_maximum_fusion.11), channel_id=1, source_target_pairs={{0,8},{1,9},{2,10},{3,11},{4,12},{5,13},{6,14},{7,15},{8,0},{9,1},... | collective-permute-start | bytes 393224 | tf_op jit(solution)/shard_map/ppermute | solution.py:38
  201.4 6.8 %collective-permute-start.44 = (f32[128,64]{1,0:T(8,128)S(1)}, f32[128,64]{1,0:T(8,128)S(1)}, u32[]{:S(2)}, u32[]{:S(2)}) collective-permute-start(f32[128,64]{1,0:T(8,128)S(1)} %add.248), channel_id=1, source_target_pairs={{0,8},{1,9},{2,10},{3,11},{4,12},{5,13},{6,14},{7,15},{8,0},{9,1},... | collective-permute-start | bytes 98312 | tf_op jit(solution)/shard_map/ppermute | solution.py:38
  202.8 8.8 %collective-permute-start.46 = (bf16[2,32,1024]{2,1,0:T(8,128)(2,1)S(1)}, bf16[2,32,1024]{2,1,0:T(8,128)(2,1)S(1)}, u32[]{:S(2)}, u32[]{:S(2)}) collective-permute-start(bf16[2,32,1024]{2,1,0:T(8,128)(2,1)S(1)} %pad_maximum_fusion.10), channel_id=1, source_target_pairs={{0,4},{1,5},{2,6},{3,7},{4,0},{5,1},{6,2},{7,3},{8,12},{9,13},{10,... | collective-permute-start | bytes 393224 | tf_op jit(solution)/shard_map/ppermute | solution.py:38
  211.6 9.3 %collective-permute-start.47 = (bf16[4,32,1024]{2,1,0:T(8,128)(2,1)S(1)}, bf16[4,32,1024]{2,1,0:T(8,128)(2,1)S(1)}, u32[]{:S(2)}, u32[]{:S(2)}) collective-permute-start(bf16[4,32,1024]{2,1,0:T(8,128)(2,1)S(1)} %pad_maximum_fusion.6), channel_id=1, source_target_pairs={{0,2},{1,3},{2,0},{3,1},{4,6},{5,7},{6,4},{7,5},{8,10},{9,11},{10,... | collective-permute-start | bytes 786440 | tf_op jit(solution)/shard_map/ppermute | solution.py:38
  212.9 11.0 %collective-permute-start.51 = (bf16[4,32,1024]{2,1,0:T(8,128)(2,1)S(1)}, bf16[4,32,1024]{2,1,0:T(8,128)(2,1)S(1)}, u32[]{:S(2)}, u32[]{:S(2)}) collective-permute-start(bf16[4,32,1024]{2,1,0:T(8,128)(2,1)S(1)} %pad_maximum_fusion.7), channel_id=1, source_target_pairs={{0,2},{1,3},{2,0},{3,1},{4,6},{5,7},{6,4},{7,5},{8,10},{9,11},{10,... | collective-permute-start | bytes 786440 | tf_op jit(solution)/shard_map/ppermute | solution.py:38
  221.0 11.0 %collective-permute-start.48 = (bf16[8,32,1024]{2,1,0:T(8,128)(2,1)S(1)}, bf16[8,32,1024]{2,1,0:T(8,128)(2,1)S(1)}, u32[]{:S(2)}, u32[]{:S(2)}) collective-permute-start(bf16[8,32,1024]{2,1,0:T(8,128)(2,1)S(1)} %pad_maximum_fusion.2.v_a), channel_id=1, source_target_pairs={{0,1},{1,0},{2,3},{3,2},{4,5},{5,4},{6,7},{7,6},{8,9},{9,8},{10,11... | collective-permute-start | bytes 1572872 | tf_op jit(solution)/shard_map/ppermute | solution.py:38
  223.9 8.1 %collective-permute-start.52 = (bf16[8,32,1024]{2,1,0:T(8,128)(2,1)S(1)}, bf16[8,32,1024]{2,1,0:T(8,128)(2,1)S(1)}, u32[]{:S(2)}, u32[]{:S(2)}) collective-permute-start(bf16[8,32,1024]{2,1,0:T(8,128)(2,1)S(1)} %pad_maximum_fusion.3.v_b), channel_id=1, source_target_pairs={{0,1},{1,0},{2,3},{3,2},{4,5},{5,4},{6,7},{7,6},{8,9},{9,8},{10,11... | collective-permute-start | bytes 1572872 | tf_op jit(solution)/shard_map/ppermute | solution.py:38
  251.6 24.3 %collective-permute-start.57 = (f16[8,64,1024]{2,1,0:T(8,128)(2,1)}, f16[8,64,1024]{2,1,0:T(8,128)(2,1)}, u32[]{:S(2)}, u32[]{:S(2)}) collective-permute-start(f16[8,64,1024]{2,1,0:T(8,128)(2,1)} %multiply_convert_fusion), channel_id=1, source_target_pairs={{0,1},{1,0},{2,3},{3,2},{4,5},{5,4},{6,7},{7,6},{8,9},{9,8},{10,11... | collective-permute-start | bytes 3145736 | tf_op jit(solution)/shard_map/ppermute | solution.py:38
  254.2 6.8 %collective-permute-start.56 = (f32[64,64]{0,1:T(8,128)S(1)}, f32[64,64]{0,1:T(8,128)S(1)}, u32[]{:S(2)}, u32[]{:S(2)}) collective-permute-start(f32[64,64]{0,1:T(8,128)S(1)} %add.257), channel_id=1, source_target_pairs={{0,8},{1,9},{2,10},{3,11},{4,12},{5,13},{6,14},{7,15},{8,0},{9,1},... | collective-permute-start | bytes 49160 | tf_op jit(solution)/shard_map/ppermute | solution.py:38
  278.5 8.0 %collective-permute-start.61 = (f16[2,2,32,1024]{3,2,1,0:T(8,128)(2,1)S(1)}, f16[2,2,32,1024]{3,2,1,0:T(8,128)(2,1)S(1)}, u32[]{:S(2)}, u32[]{:S(2)}) collective-permute-start(f16[2,2,32,1024]{3,2,1,0:T(8,128)(2,1)S(1)} %fusion.6), channel_id=1, source_target_pairs={{0,4},{1,5},{2,6},{3,7},{4,0},{5,1},{6,2},{7,3},{8,12},{9,13},{10,... | collective-permute-start | bytes 786440 | tf_op jit(solution)/shard_map/ppermute | solution.py:38
  280.7 6.9 %collective-permute-start.58 = (f16[2,2,32,1024]{3,2,0,1:T(8,128)(2,1)S(1)}, f16[2,2,32,1024]{3,2,0,1:T(8,128)(2,1)S(1)}, u32[]{:S(2)}, u32[]{:S(2)}) collective-permute-start(f16[2,2,32,1024]{3,2,0,1:T(8,128)(2,1)S(1)} %fusion.19), channel_id=1, source_target_pairs={{0,2},{1,3},{2,0},{3,1},{4,6},{5,7},{6,4},{7,5},{8,10},{9,11},{10,... | collective-permute-start | bytes 786440 | tf_op jit(solution)/shard_map/ppermute | solution.py:38
  286.7 7.4 %collective-permute-start.62 = (f16[2,32,1024]{2,1,0:T(8,128)(2,1)S(1)}, f16[2,32,1024]{2,1,0:T(8,128)(2,1)S(1)}, u32[]{:S(2)}, u32[]{:S(2)}) collective-permute-start(f16[2,32,1024]{2,1,0:T(8,128)(2,1)S(1)} %fusion.29), channel_id=1, source_target_pairs={{0,8},{1,9},{2,10},{3,11},{4,12},{5,13},{6,14},{7,15},{8,0},{9,1},... | collective-permute-start | bytes 393224 | tf_op jit(solution)/shard_map/ppermute | solution.py:38
  287.9 8.2 %collective-permute-start.59 = (f16[2,32,1024]{2,1,0:T(8,128)(2,1)S(1)}, f16[2,32,1024]{2,1,0:T(8,128)(2,1)S(1)}, u32[]{:S(2)}, u32[]{:S(2)}) collective-permute-start(f16[2,32,1024]{2,1,0:T(8,128)(2,1)S(1)} %fusion.32), channel_id=1, source_target_pairs={{0,4},{1,5},{2,6},{3,7},{4,0},{5,1},{6,2},{7,3},{8,12},{9,13},{10,... | collective-permute-start | bytes 393224 | tf_op jit(solution)/shard_map/ppermute | solution.py:38
  296.3 5.2 %collective-permute-start.60 = (f16[32,1024]{1,0:T(8,128)(2,1)S(1)}, f16[32,1024]{1,0:T(8,128)(2,1)S(1)}, u32[]{:S(2)}, u32[]{:S(2)}) collective-permute-start(f16[32,1024]{1,0:T(8,128)(2,1)S(1)} %fusion.55), channel_id=1, source_target_pairs={{0,8},{1,9},{2,10},{3,11},{4,12},{5,13},{6,14},{7,15},{8,0},{9,1},... | collective-permute-start | bytes 196616 | tf_op jit(solution)/shard_map/ppermute | solution.py:38
  (22 other events, 125.0 us)

commit v3 on v0

v3 whole, which is shorter than its diff:
```python
import functools

import jax
import jax.numpy as jnp
from jax import lax
from jax.experimental import pallas as pl
from jax.experimental.pallas import tpu as pltpu
from jax.sharding import PartitionSpec as P

K = 64
HALF = K // 2
RIDGE = 0.1
BOUND = 18.0
TOP = 60000.0
TINY = 1e-30
F32, BF16, F16 = jnp.float32, jnp.bfloat16, jnp.float16


def precise(left, right):
    return jnp.dot(left, right, precision=lax.Precision.HIGHEST, preferred_element_type=F32)


def outer(left, right):
    return lax.dot_general(
        left, right, (((1,), (1,)), ((), ())), precision=lax.Precision.HIGHEST, preferred_element_type=F32
    )


def symmetric(matrix):
    return 0.5 * (matrix + matrix.T)


def solve_positive(matrix, target):
    work = jnp.concatenate([matrix, target], axis=1)
    index = lax.broadcasted_iota(jnp.int32, (K, 1), 0)
    for k in range(0, K, 2):
        a, b = work[k : k + 1], work[k + 1 : k + 2]
        col_a, col_b = work[:, k : k + 1], work[:, k + 1 : k + 2]
        p, q = work[k : k + 1, k : k + 1], work[k : k + 1, k + 1 : k + 2]
        t, r = work[k + 1 : k + 2, k : k + 1], work[k + 1 : k + 2, k + 1 : k + 2]
        inv = 1.0 / (p * r - q * t)
        new_a, new_b = (r * a - q * b) * inv, (p * b - t * a) * inv
        rest = work - (col_a * new_a + col_b * new_b)
        work = jnp.where(index == k, new_a, jnp.where(index == k + 1, new_b, rest))
    return work[:, K:]


def swap(value, bit, n):
    return lax.ppermute(value, "dp", [(i, i ^ bit) for i in range(n)])


def hop_bits(n):
    bits = [1 << i for i in range(1, n.bit_length() - 1)]
    return bits, bits[1:] + bits[:1]


def _pos(j, shifts):
    p = 0
    for place, shift in enumerate(shifts):
        p = p | (((j >> shift) & 1) << place)
    return p


def block_copy(acts, kept, sems, me, half, t):
    f = kept.shape[2]
    first = pl.multiple_of((me[0] ^ (2 * t + half)) * f, f)
    return pltpu.make_async_copy(acts.at[:, pl.ds(first, f)], kept.at[t], sems.at[t])


def start_copies(acts, kept, sems, me, half):
    def start(t, carry):
        block_copy(acts, kept, sems, me, half, t).start()
        return carry

    lax.fori_loop(0, kept.shape[0], start, 0)


def whole(*shape):
    return pl.BlockSpec(shape, lambda i, me: (0,) * len(shape))


HBM = pl.BlockSpec(memory_space=pltpu.HBM)


def call(kernel, name, n, grid, in_specs, out_shapes, out_specs, acts, scratch=()):
    rows, d = acts.shape
    return pl.pallas_call(
        kernel,
        out_shape=out_shapes,
        grid_spec=pltpu.PrefetchScalarGridSpec(
            num_scalar_prefetch=1,
            grid=(grid,),
            in_specs=in_specs,
            out_specs=out_specs,
            scratch_shapes=[
                pltpu.VMEM((n // 2, rows, d // n), BF16),
                pltpu.SemaphoreType.DMA((n // 2,)),
                *scratch,
            ],
        ),
        compiler_params=pltpu.CompilerParams(vmem_limit_bytes=16 << 20),
        cost_estimate=pl.CostEstimate(flops=K * rows * d, bytes_accessed=rows * d + 2 * K * d, transcendentals=0),
        name=name,
    )


def sums_kernel(half, me, labels, counts, acts, out, peak, weight, kept, sems, member):
    step = pl.program_id(0)

    @pl.when(step == 0)
    def _():
        start_copies(acts, kept, sems, me, half)
        concept = lax.broadcasted_iota(jnp.int32, member.shape, 0)
        full = jnp.where(labels[...] == concept, counts[...].astype(F32), 0.0)
        member[...] = full.astype(BF16)
        weight[...] = jnp.sum(full, axis=1, keepdims=True)
        peak[...] = jnp.zeros_like(peak)

    block_copy(acts, kept, sems, me, half, step).wait()
    block = jnp.dot(member[...], kept[step], preferred_element_type=F32)
    out[0] = block
    peak[...] = jnp.maximum(peak[...], jnp.max(jnp.max(jnp.abs(block), axis=1, keepdims=True), axis=0, keepdims=True))


def class_sums(me, labels, counts, acts, n, half):
    rows, d = acts.shape
    f = d // n
    return call(
        functools.partial(sums_kernel, half),
        "class_sums",
        n,
        n // 2,
        [whole(1, rows), whole(1, rows), HBM],
        (
            jax.ShapeDtypeStruct((n // 2, K, f), F32),
            jax.ShapeDtypeStruct((1, 1), F32),
            jax.ShapeDtypeStruct((K, 1), F32),
        ),
        (pl.BlockSpec((1, K, f), lambda i, me: (i, 0, 0)), whole(1, 1), whole(K, 1)),
        acts,
        [pltpu.VMEM((K, rows), BF16)],
    )(me, labels, counts, acts)


def inner(left, right):
    return lax.dot_general(left, right, (((1,), (1,)), ((), ())), preferred_element_type=F32)


def v_specs(n, f, shifts_a, shifts_b):
    s = n // 2
    return [
        pl.BlockSpec((1, HALF, f), lambda i, me: (_pos(2 * jnp.minimum(i, s - 1), shifts_a), 0, 0)),
        pl.BlockSpec((1, HALF, f), lambda i, me: (_pos(2 * jnp.minimum(i, s - 1), shifts_b), 0, 0)),
    ]


def add_block(panels, acts, probed, grams):
    both = [jnp.concatenate([panels[i][0], panels[i + 1][0]], axis=0) for i in range(0, len(panels), 2)]
    probed[...] += inner(both[0], acts)
    for gram, other in zip(grams, both):
        gram[...] += inner(other, both[0])


def probe_kernel(count, me, *refs):
    panels, (acts, probed, *grams) = refs[: 2 * count], refs[2 * count : -2]
    kept, sems = refs[-2:]
    step = pl.program_id(0)

    @pl.when(step == 0)
    def _():
        start_copies(acts, kept, sems, me, 0)
        for ref in (probed, *grams):
            ref[...] = jnp.zeros_like(ref)

    block_copy(acts, kept, sems, me, 0, step).wait()
    add_block(panels, kept[step], probed, grams)


def probe(me, panels, acts, n, shifts):
    rows, d = acts.shape
    count = len(panels) // 2
    return call(
        functools.partial(probe_kernel, count),
        "probe",
        n,
        n // 2,
        v_specs(n, d // n, *shifts) * count + [HBM],
        (jax.ShapeDtypeStruct((K, rows), F32),) + (jax.ShapeDtypeStruct((K, K), F32),) * count,
        (whole(K, rows),) + (whole(K, K),) * count,
        acts,
    )(me, *panels, acts)


def column(row_or_matrix):
    eye = lax.broadcasted_iota(jnp.int32, (K, K), 0) == lax.broadcasted_iota(jnp.int32, (K, K), 1)
    diagonal = jnp.where(eye, row_or_matrix, 0.0)
    return jnp.sum(diagonal, axis=1, keepdims=True), jnp.sum(diagonal, axis=0, keepdims=True)


def finish_first(gram, total_weight, bounded):
    current = symmetric(gram[...])
    gram[...] = current
    norms, _ = column(current)
    return bounded(jnp.sqrt(norms), total_weight[...])


def finish_second(probed, image_image, base_image, more, total_weight, bounded):
    first, current, alpha_t, inverse, renewed, mixed, beta_t = more
    moved = outer(base_image[...], alpha_t[...])
    twice = outer(precise(alpha_t[...], symmetric(image_image[...])), alpha_t[...])
    new = symmetric(current[...] - moved - moved.T + twice)
    beta = precise(new, inverse[...])
    renewed[...] = new
    mixed[...] = current[...] - moved
    beta_t[...] = beta
    probed[...] = first[...] + precise(beta, first[...]) - precise(alpha_t[...], probed[...])
    base_col, base_row = column(current[...])
    _, image_row = column(image_image[...])
    norms = jnp.sqrt(base_col)
    norms += jnp.sum(jnp.abs(beta) * jnp.sqrt(base_row), axis=1, keepdims=True)
    norms += jnp.sum(jnp.abs(alpha_t[...]) * jnp.sqrt(image_row), axis=1, keepdims=True)
    return bounded(norms, total_weight[...])


def send_kernel(steps, count, d, me, *refs):
    panels, refs = refs[: 2 * count], refs[2 * count :]
    acts, counts, total_weight, start, refs = refs[0], refs[1], refs[2], refs[3], refs[4:]
    starts, refs = refs[:count], refs[count:]
    second = count == 2
    given, refs = refs[: 4 * second], refs[4 * second :]
    probed, along, bound, out, *refs = refs
    grams, refs = refs[:count], refs[count:]
    made, (kept, sems, weighted) = refs[: 3 * second], refs[3 * second :]
    step = pl.program_id(0)

    @pl.when(step == 0)
    def _():
        start_copies(acts, kept, sems, me, 1)
        for ref, begin in zip((probed, *grams), (start, *starts)):
            ref[...] = begin[...]

    @pl.when(step < steps)
    def _():
        block_copy(acts, kept, sems, me, 1, step).wait()
        add_block(panels, kept[step], probed, grams)

    @pl.when(step == steps)
    def _():
        def bounded(norms, weight):
            return (1.02 * BOUND * BOUND * d**0.5) * weight * norms

        if second:
            bound[...] = finish_second(probed, *grams, (*given, *made), total_weight, bounded)
        else:
            bound[...] = finish_first(*grams, total_weight, bounded)
        weighted[...] = (counts[...].astype(F32) * probed[...]).astype(BF16)
        along[...] = outer(probed[...], weighted[...].astype(F32))

    @pl.when(step >= steps)
    def _():
        out[0] = jnp.dot(weighted[...], kept[step - steps], preferred_element_type=F32)


def probe_and_send(me, panels, acts, counts, total_weight, starts, given, n, shifts):
    rows, d = acts.shape
    f = d // n
    s = n // 2
    count = len(panels) // 2
    square = jax.ShapeDtypeStruct((K, K), F32)
    made = 3 if given else 0
    return call(
        functools.partial(send_kernel, s, count, d),
        "probe_and_send",
        n,
        2 * s,
        v_specs(n, f, *shifts) * count
        + [HBM, whole(1, rows), whole(1, 1)]
        + [whole(*x.shape) for x in (*starts, *given)],
        (
            jax.ShapeDtypeStruct((K, rows), F32),
            square,
            jax.ShapeDtypeStruct((K, 1), F32),
            jax.ShapeDtypeStruct((s, K, f), F32),
        )
        + (square,) * (count + made),
        (
            whole(K, rows),
            whole(K, K),
            whole(K, 1),
            pl.BlockSpec((1, K, f), lambda i, me: (jnp.maximum(i - s, 0), 0, 0)),
        )
        + (whole(K, K),) * (count + made),
        acts,
        [pltpu.VMEM((K, rows), BF16)],
    )(me, *panels, acts, counts, total_weight, *starts, *given)


def keep_kernel(me, probed, counts, acts, out, kept, sems, weighted):
    step = pl.program_id(0)

    @pl.when(step == 0)
    def _():
        start_copies(acts, kept, sems, me, 0)
        weighted[...] = (counts[...].astype(F32) * probed[...]).astype(BF16)

    block_copy(acts, kept, sems, me, 0, step).wait()
    out[0] = jnp.dot(weighted[...], kept[step], preferred_element_type=F32)


def panel_keep(me, probed, counts, acts, n):
    rows, d = acts.shape
    f = d // n
    return call(
        keep_kernel,
        "panel_keep",
        n,
        n // 2,
        [whole(K, rows), whole(1, rows), HBM],
        jax.ShapeDtypeStruct((n // 2, K, f), F32),
        pl.BlockSpec((1, K, f), lambda i, me: (i, 0, 0)),
        acts,
        [pltpu.VMEM((K, rows), BF16)],
    )(me, probed, counts, acts)


def alpha_kernel(along, current, total_weight, alpha_t, inverse):
    now = current[...]
    curvature = (along[...] - precise(now, now)) / total_weight[...] + RIDGE * now
    eye = lax.broadcasted_iota(jnp.int32, (K, K), 0) == lax.broadcasted_iota(jnp.int32, (K, K), 1)
    alpha_t[...] = solve_positive(symmetric(curvature), now).T
    inverse[...] = symmetric(solve_positive(now, jnp.where(eye, 1.0, 0.0)))


def last_kernel(along, current, renewed, mixed, beta_t, alpha_t, total_weight, on_base, on_image, on_panel, out_base, out_image):
    now, beta, alpha, weight = current[...], beta_t[...], alpha_t[...], total_weight[...]
    cross = mixed[...] + outer(now, beta)
    half = outer(mixed[...].T, beta)
    length = renewed[...] + half + precise(beta, cross)
    cross_t = cross.T
    curvature = (along[...] - outer(cross_t, cross_t)) / weight + RIDGE * length
    step = solve_positive(symmetric(curvature), renewed[...]).T
    eye = lax.broadcasted_iota(jnp.int32, (K, K), 0) == lax.broadcasted_iota(jnp.int32, (K, K), 1)
    identity = jnp.where(eye, 1.0, 0.0)
    direction_base = precise(step, identity + beta)
    direction_image = precise(step, alpha)
    out_base[...] = alpha + direction_base
    out_image[...] = -direction_image
    on_base[...] = identity - RIDGE * direction_base + precise(step, cross_t) / weight
    on_image[...] = RIDGE * direction_image - alpha
    on_panel[...] = step / weight


def small(kernel, name, outs, *args):
    return pl.pallas_call(
        kernel, out_shape=(jax.ShapeDtypeStruct((K, K), F32),) * outs, name=name,
        cost_estimate=pl.CostEstimate(flops=1 << 26, bytes_accessed=1 << 20, transcendentals=0),
    )(*args)


def shrink(value, bound):
    return (value * (TOP / jnp.maximum(bound, TINY))).astype(F16)


def grow(value, bound):
    return value.astype(F32) * (jnp.maximum(bound, TINY) * (1.0 / TOP))


def split_blocks(value, left, bit):
    axis = left.index(bit)
    keep = lax.index_in_dim(value, 0, axis, keepdims=False)
    send = lax.index_in_dim(value, 1, axis, keepdims=False)
    return keep, send, [other for other in left if other != bit]


def reduce_scatter(blocks, n, swap_a, swap_b, along=None):
    bits = n.bit_length() - 2
    shape = (2,) * bits + (HALF, blocks.shape[2])
    a, b = blocks[:, :HALF].reshape(shape), blocks[:, HALF:].reshape(shape)
    left_a = left_b = [1 << i for i in range(bits, 0, -1)]
    for bit_a, bit_b in zip(*hop_bits(n)):
        keep_a, send_a, left_a = split_blocks(a, left_a, bit_a)
        keep_b, send_b, left_b = split_blocks(b, left_b, bit_b)
        a, b = keep_a + swap_a(send_a, bit_a), keep_b + swap_b(send_b, bit_b)
        if along is not None:
            along = along + swap(along, bit_a, n)
    return jnp.concatenate([a, b], axis=0), along


class Packed:
    def __init__(self, n, bound, weight):
        self.n, self.bound, self.weight = n, bound, weight

    def __call__(self, send, bit):
        f = send.shape[-1]
        power = jnp.ceil(jnp.log2(jnp.maximum(self.bound, TINY)))
        value = (send * jnp.exp2(15.0 - power)).astype(F16).reshape(-1, f)
        row = lax.broadcasted_iota(jnp.int32, (16, f), 0)
        tail = jnp.where(row == 0, power, 0.0)
        if self.weight is not None:
            high = jnp.floor(self.weight * (1.0 / 1024.0))
            low = self.weight - 1024.0 * high
            tail = jnp.where(row == 1, _widen(high, f), jnp.where(row == 2, _widen(low, f), tail))
        got = swap(jnp.concatenate([value, tail.astype(F16)], axis=0), bit, self.n)
        count = value.shape[0]
        theirs = got[count : count + 1, :1].astype(F32)
        if self.weight is not None:
            other = got[count + 1 : count + 3, :K].astype(F32)
            self.weight = self.weight + (1024.0 * other[:1] + other[1:])
        self.bound = 1.001 * (self.bound + jnp.exp2(theirs))
        return got[:count].reshape(send.shape).astype(F32) * jnp.exp2(theirs - 15.0)


def _widen(row, f):
    return row if f == K else jnp.pad(row, ((0, 0), (0, f - K)))


def gather_stream(block, order, n):
    value = block[None]
    for bit in order:
        value = jnp.concatenate([value, swap(value, bit, n)], axis=0)
    return value


def per_device(n, activations, labels, counts):
    rows, d = activations.shape
    activations = pltpu.with_memory_space_constraint(activations, pltpu.HBM)
    me = lax.axis_index("dp").astype(jnp.int32).reshape(1)
    labels = labels.reshape(1, rows)
    counts = counts.reshape(1, rows)
    order_y, order_z = hop_bits(n)
    order_a, order_b = order_y[::-1], order_z
    shifts = [[bit.bit_length() - 1 for bit in order] for order in (order_a, order_b)]

    sent, peak_sent, weight = class_sums(me, labels, counts, activations, n, 1)
    core = Packed(n, peak_sent, weight.T)
    got = core(sent, 1)
    kept, peak, _ = class_sums(me, labels, counts, activations, n, 0)
    bound = 1.001 * (peak + core.bound)
    stream = Packed(n, bound, core.weight)
    sums, _ = reduce_scatter(kept + got, n, stream, Packed(n, bound, None))
    class_weight = stream.weight.T
    total_weight = jnp.sum(class_weight, keepdims=True)
    base = (sums / class_weight) * jnp.sqrt(class_weight)

    def gather(panel):
        v = panel.astype(BF16)
        near = gather_stream(v[:HALF], order_a, n), gather_stream(v[HALF:], order_b, n)
        return near, tuple(swap(x, 1, n) for x in near)

    def scatter(probed, along, bound, sent):
        got = grow(swap(shrink(sent, bound), 1, n), bound)
        along = along + swap(along, 1, n)
        blocks = panel_keep(me, probed, counts, activations, n) + got
        top, low = bound[:HALF], bound[HALF:]
        return reduce_scatter(
            blocks,
            n,
            lambda x, bit: grow(swap(shrink(x, top), bit, n), top),
            lambda x, bit: grow(swap(shrink(x, low), bit, n), low),
            along,
        )

    base_near, base_far = gather(base)
    starts = probe(me, base_near, activations, n, shifts)
    first, along, bound, sent, current = probe_and_send(
        me, base_far, activations, counts, total_weight, starts, (), n, shifts
    )
    panel, along = scatter(first, along, bound, sent)
    image = panel / total_weight + (RIDGE * base - precise(current / total_weight, base))
    alpha_t, inverse = small(alpha_kernel, "alpha", 2, along, current, total_weight)

    near, far = gather(image)
    starts = probe(me, near + base_near, activations, n, shifts)
    probed, along, bound, sent, _, _, renewed, mixed, beta_t = probe_and_send(
        me, far + base_far, activations, counts, total_weight, starts, (first, current, alpha_t, inverse), n, shifts
    )
    panel, along = scatter(probed, along, bound, sent)
    on_base, on_image, on_panel, out_base, out_image = small(
        last_kernel, "last", 5, along, current, renewed, mixed, beta_t, alpha_t, total_weight
    )
    solution = precise(out_base, base) + precise(out_image, image)
    residual = (precise(on_base, base) + precise(on_image, image)) - precise(on_panel, panel)
    return (solution.T, residual.T)


def solution(mesh):
    in_specs = (P(("groups", "dp"), None), P(("groups", "dp")), P(("groups", "dp")))
    out_specs = (P(("groups", "dp"), None), P(("groups", "dp"), None))
    return jax.shard_map(
        functools.partial(per_device, mesh.shape["dp"]),
        mesh=mesh,
        in_specs=in_specs,
        out_specs=out_specs,
        check_vma=False,
    )
```

time: 588 us -> 246 us (0.42)
  blocking collectives: 211 us -> 0 us
  waiting for transfers between devices: 260 us -> 83.8 us
  Pallas kernels: 0 us -> 67.2 us
  starting transfers between devices: 0.43 us -> 59.6 us
  matrix products: 62 us -> 7.75 us
  other arithmetic: 39.4 us -> 11.1 us
  local copies, waits for them, and re-layouts: 0.68 us -> 6.59 us
    psum x4 -> x0, blocking collectives: 211 us -> none  [the longest x2 118 us: per_device(): lax.psum((precise(class_means.T, direction), precise(direction.T, panel),...]
    reduce_scatter x3 -> x0, waiting for transfers between devices: 180 us -> none  [the longest x2 140 us: per_device(): lax.psum_scatter(contract_rows(activations, weighted), 'dp', scatter_dime...]
    ppermute x0 -> x45, waiting for transfers between devices: none -> 83.8 us  [swap(): return lax.ppermute(value, 'dp', [(i, i ^ bit) for i in range(n)])]
    all_gather x2 -> x0, waiting for transfers between devices: 80.2 us -> none  [per_device(): lax.all_gather(direction.astype(jnp.bfloat16), 'dp', axis=0, tiled=True)]
    pallas_call x0 -> x10, Pallas kernels: none -> 67.2 us  [the longest x2 20.7 us: probe_and_send(): call(functools.partial(send_kernel, s, count, d), 'probe_and_send', n, 2...]
    ppermute x0 -> x45, starting transfers between devices: none -> 59.6 us  [swap(): return lax.ppermute(value, 'dp', [(i, i ^ bit) for i in range(n)])]
    dot_general x19 -> x6, matrix products: 60.7 us -> 7.75 us  [precise(): jnp.dot(left, right, precision=lax.Precision.HIGHEST, preferred_element_t...]
    another operation x15 -> x0, other arithmetic: 36.2 us -> none  [the longest x9 19.6 us: solve_positive(): jnp.linalg.cholesky(matrix)]
  transfers between devices with their start and end apart: 5 -> 45, of which waited for: 5 -> 32; matrix products, arithmetic and copies ran while one was open for 0% -> 4% of each run, Pallas kernels for 0% -> 17%
where the time goes in v3:
time: 246 us; the launch traced here: 245 us
  waiting for transfers between devices  83.8 us (34%)
  Pallas kernels  67.2 us (27%)
  starting transfers between devices  59.6 us (24%)
  other arithmetic  11.1 us (5%)
  between operations  9.24 us (4%)
  matrix products  7.75 us (3%)
  local copies, waits for them, and re-layouts  6.59 us (3%)
    ppermute x45, waiting for transfers between devices, swap(): return lax.ppermute(value, 'dp', [(i, i ^ bit) for i in range(n)])  83.8 us
    ppermute x45, starting transfers between devices, swap(): return lax.ppermute(value, 'dp', [(i, i ^ bit) for i in range(n)])  59.6 us
    pallas_call x2, Pallas kernels, probe_and_send(): call(functools.partial(send_kernel, s, count, d), 'probe_and_send', n, 2...  20.7 us
    pallas_call x2, Pallas kernels, small(): pl.pallas_call(kernel, out_shape=(jax.ShapeDtypeStruct((K, K), F32),) * o...  20.6 us
    pallas_call x2, Pallas kernels, probe(): call(functools.partial(probe_kernel, count), 'probe', n, n // 2, v_specs(...  9.63 us
    pallas_call x2, Pallas kernels, class_sums(): call(functools.partial(sums_kernel, half), 'class_sums', n, n // 2, [whol...  9.13 us
    dot_general x6, matrix products, precise(): jnp.dot(left, right, precision=lax.Precision.HIGHEST, preferred_element_t...  7.75 us
    pallas_call x2, Pallas kernels, panel_keep(): call(keep_kernel, 'panel_keep', n, n // 2, [whole(K, rows), whole(1, rows...  7.13 us
  transfers between devices with their start and end apart: 45, of which 32 were waited for; matrix products, arithmetic and copies ran while one was open for 4% of the time, Pallas kernels for 17%

profile of v3, /device:TPU:0, one launch (start us, length us, event | category | flops | bytes accessed | tf_op | source)
XLA Modules:
  0.0 245.3 jit_solution(8296275056360885632)
XLA Ops:
  2.0 4.6 %class_sums.3 = (f32[8,64,1024]{2,1,0:T(8,128)S(1)}, f32[1,1]{1,0:T(1,128)}, f32[64,1]{1,0:T(8,128)S(1)}) custom-call(s32[1]{0:T(128)} %bitcast.me, s32[1,384]{1,0:T(1,128)S(1)} %reshape.155.labels, s32[1,384]{1,0:T(1,128)S(1)} %reshape.156.counts.refs_3_.refs_5_, bf16[384,16384]{1,0:T(8,128)(2,1)} %acts.7), custom_call_target="tpu_custom_call" | custom-call | flops 402653184 | bytes 8388608 | tf_op jit(solution)/shard_map/class_sums/pallas_call | solution.py:128
  8.6 4.6 %class_sums.2 = (f32[8,64,1024]{2,1,0:T(8,128)S(1)}, f32[1,1]{1,0:T(1,128)}, f32[64,1]{1,0:T(8,128)}) custom-call(s32[1]{0:T(128)} %bitcast.me, s32[1,384]{1,0:T(1,128)S(1)} %reshape.155.labels, s32[1,384]{1,0:T(1,128)S(1)} %reshape.156.counts.refs_3_.refs_5_, bf16[384,16384]{1,0:T(8,128)(2,1)} %acts.7), custom_call_target="tpu_custom_call" | custom-call | flops 402653184 | bytes 8388608 | tf_op jit(solution)/shard_map/class_sums/pallas_call | solution.py:128
  17.2 2.7 %collective-permute-start.4 = (f16[144,1024]{1,0:T(8,128)(2,1)S(1)}, f16[144,1024]{1,0:T(8,128)(2,1)S(1)}, u32[]{:S(2)}, u32[]{:S(2)}) collective-permute-start(f16[144,1024]{1,0:T(8,128)(2,1)S(1)} %pad_maximum_fusion.6), channel_id=1, source_target_pairs={{0,4},{1,5},{2,6},{3,7},{4,0},{5,1},{6,2},{7,3},{8,12},{9,13},{10,... | collective-permute-start | bytes 884744 | tf_op jit(solution)/shard_map/ppermute | solution.py:49
  21.7 5.9 %collective-permute-done.4 = f16[144,1024]{1,0:T(8,128)(2,1)S(1)} collective-permute-done((f16[144,1024]{1,0:T(8,128)(2,1)S(1)}, f16[144,1024]{1,0:T(8,128)(2,1)S(1)}, u32[]{:S(2)}, u32[]{:S(2)}) %collective-permute-start.4) | collective-permute-done | bytes 294944 | tf_op jit(solution)/shard_map/ppermute | solution.py:49
  31.0 2.7 %collective-permute-start.5 = (f16[80,1024]{1,0:T(8,128)(2,1)S(1)}, f16[80,1024]{1,0:T(8,128)(2,1)S(1)}, u32[]{:S(2)}, u32[]{:S(2)}) collective-permute-start(f16[80,1024]{1,0:T(8,128)(2,1)S(1)} %pad_maximum_fusion.12), channel_id=1, source_target_pairs={{0,8},{1,9},{2,10},{3,11},{4,12},{5,13},{6,14},{7,15},{8,0},{9,1},... | collective-permute-start | bytes 491528 | tf_op jit(solution)/shard_map/ppermute | solution.py:49
  35.5 5.6 %collective-permute-done.5 = f16[80,1024]{1,0:T(8,128)(2,1)S(1)} collective-permute-done((f16[80,1024]{1,0:T(8,128)(2,1)S(1)}, f16[80,1024]{1,0:T(8,128)(2,1)S(1)}, u32[]{:S(2)}, u32[]{:S(2)}) %collective-permute-start.5) | collective-permute-done | bytes 163872 | tf_op jit(solution)/shard_map/ppermute | solution.py:49
  46.6 1.9 collective-permute-done.6
  49.7 3.3 %collective-permute-done.3 = f16[48,1024]{1,0:T(8,128)(2,1)S(1)} collective-permute-done((f16[48,1024]{1,0:T(8,128)(2,1)S(1)}, f16[48,1024]{1,0:T(8,128)(2,1)S(1)}, u32[]{:S(2)}, u32[]{:S(2)}) %collective-permute-start.3) | collective-permute-done | bytes 98336 | tf_op jit(solution)/shard_map/ppermute | solution.py:49
  55.2 2.6 %collective-permute-start.11 = (bf16[1,32,1024]{2,1,0:T(8,128)(2,1)S(1)}, bf16[1,32,1024]{2,1,0:T(8,128)(2,1)S(1)}, u32[]{:S(2)}, u32[]{:S(2)}) collective-permute-start(bf16[1,32,1024]{2,1,0:T(8,128)(2,1)S(1)} %get-tuple-element.94), channel_id=1, source_target_pairs={{0,4},{1,5},{2,6},{3,7},{4,0},{5,1},{6,2},{7,3},{8,12},{9,13},{10,... | collective-permute-start | bytes 196616 | tf_op jit(solution)/shard_map/ppermute | solution.py:49
  57.8 2.7 %collective-permute-done.7 = bf16[1,32,1024]{2,1,0:T(8,128)(2,1)S(1)} collective-permute-done((bf16[1,32,1024]{2,1,0:T(8,128)(2,1)S(1)}, bf16[1,32,1024]{2,1,0:T(8,128)(2,1)S(1)}, u32[]{:S(2)}, u32[]{:S(2)}) %collective-permute-start.7) | collective-permute-done | bytes 65568 | tf_op jit(solution)/shard_map/ppermute | solution.py:49
  63.2 2.6 %collective-permute-done.8 = bf16[2,32,1024]{2,1,0:T(8,128)(2,1)S(1)} collective-permute-done((bf16[2,32,1024]{2,1,0:T(8,128)(2,1)S(1)}, bf16[2,32,1024]{2,1,0:T(8,128)(2,1)S(1)}, u32[]{:S(2)}, u32[]{:S(2)}) %collective-permute-start.8) | collective-permute-done | bytes 131104 | tf_op jit(solution)/shard_map/ppermute | solution.py:49
  66.4 2.4 collective-permute-done.12
  69.4 3.7 %collective-permute-done.9 = bf16[4,32,1024]{2,1,0:T(8,128)(2,1)S(1)} collective-permute-done((bf16[4,32,1024]{2,1,0:T(8,128)(2,1)S(1)}, bf16[4,32,1024]{2,1,0:T(8,128)(2,1)S(1)}, u32[]{:S(2)}, u32[]{:S(2)}) %collective-permute-start.9) | collective-permute-done | bytes 262176 | tf_op jit(solution)/shard_map/ppermute | solution.py:49
  73.2 2.7 %collective-permute-done.13 = bf16[4,32,1024]{2,1,0:T(8,128)(2,1)S(1)} collective-permute-done((bf16[4,32,1024]{2,1,0:T(8,128)(2,1)S(1)}, bf16[4,32,1024]{2,1,0:T(8,128)(2,1)S(1)}, u32[]{:S(2)}, u32[]{:S(2)}) %collective-permute-start.13) | collective-permute-done | bytes 262176 | tf_op jit(solution)/shard_map/ppermute | solution.py:49
  76.0 4.8 %probe.2 = (f32[64,384]{1,0:T(8,128)S(1)}, f32[64,64]{1,0:T(8,128)S(1)}) custom-call(s32[1]{0:T(128)} %bitcast.me, bf16[8,32,1024]{2,1,0:T(8,128)(2,1)S(1)} %pad_maximum_fusion.1.refs_0_.refs_2_, bf16[8,32,1024]{2,1,0:T(8,128)(2,1)S(1)} %pad_maximum_fusion.2.refs_1_.refs_3_, bf16[384,16384]{1,0:T(8,128)(2,1)} %acts.7), custom_call_target="tpu_custom_call" | custom-call | flops 402653184 | bytes 8388608 | tf_op jit(solution)/shard_map/probe/pallas_call | solution.py:182
  80.8 8.1 %probe_and_send.2 = (f32[64,384]{1,0:T(8,128)S(1)}, f32[64,64]{1,0:T(8,128)S(1)}, f32[64,1]{1,0:T(8,128)S(1)}, f32[8,64,1024]{2,1,0:T(8,128)S(1)}, f32[64,64]{1,0:T(8,128)S(1)}) custom-call(s32[1]{0:T(128)} %bitcast.me, bf16[8,32,1024]{2,1,0:T(8,128)(2,1)S(1)} %collective-permute-done.10.refs_0_.refs_2_, ...), custom_call_target="tpu_custom_call" | custom-call | flops 402653184 | bytes 8388608 | tf_op jit(solution)/shard_map/probe_and_send/pallas_call | solution.py:271
  89.9 3.5 %panel_keep.2 = f32[8,64,1024]{2,1,0:T(8,128)S(1)} custom-call(s32[1]{0:T(128)} %bitcast.me, f32[64,384]{1,0:T(8,128)S(1)} %get-tuple-element.38.probed.refs_10_, s32[1,384]{1,0:T(1,128)S(1)} %reshape.156.counts.refs_3_.refs_5_, bf16[384,16384]{1,0:T(8,128)(2,1)} %acts.7), custom_call_target="tpu_custom_call" | custom-call | flops 402653184 | bytes 8388608 | tf_op jit(solution)/shard_map/panel_keep/pallas_call | solution.py:313
  97.0 5.8 %collective-permute-done.19 = f16[2,2,32,1024]{3,2,1,0:T(8,128)(2,1)S(1)} collective-permute-done((f16[2,2,32,1024]{3,2,1,0:T(8,128)(2,1)S(1)}, f16[2,2,32,1024]{3,2,1,0:T(8,128)(2,1)S(1)}, u32[]{:S(2)}, u32[]{:S(2)}) %collective-permute-start.19) | collective-permute-done | bytes 262176 | tf_op jit(solution)/shard_map/ppermute | solution.py:49
  103.0 4.1 %collective-permute-start.20 = (f16[2,32,1024]{2,1,0:T(8,128)(2,1)S(1)}, f16[2,32,1024]{2,1,0:T(8,128)(2,1)S(1)}, u32[]{:S(2)}, u32[]{:S(2)}) collective-permute-start(f16[2,32,1024]{2,1,0:T(8,128)(2,1)S(1)} %fusion.25), channel_id=1, source_target_pairs={{0,8},{1,9},{2,10},{3,11},{4,12},{5,13},{6,14},{7,15},{8,0},{9,1},... | collective-permute-start | bytes 393224 | tf_op jit(solution)/shard_map/ppermute | solution.py:49
  107.4 1.8 collective-permute-start.17
  109.2 4.0 %collective-permute-done.20 = f16[2,32,1024]{2,1,0:T(8,128)(2,1)S(1)} collective-permute-done((f16[2,32,1024]{2,1,0:T(8,128)(2,1)S(1)}, f16[2,32,1024]{2,1,0:T(8,128)(2,1)S(1)}, u32[]{:S(2)}, u32[]{:S(2)}) %collective-permute-start.20) | collective-permute-done | bytes 131104 | tf_op jit(solution)/shard_map/ppermute | solution.py:49
  115.4 2.3 collective-permute-done.21
  117.8 2.4 collective-permute-done.18
  122.6 2.7 %collective-permute-start.26 = (bf16[1,32,1024]{2,1,0:T(8,128)(2,1)S(1)}, bf16[1,32,1024]{2,1,0:T(8,128)(2,1)S(1)}, u32[]{:S(2)}, u32[]{:S(2)}) collective-permute-start(bf16[1,32,1024]{2,1,0:T(8,128)(2,1)S(1)} %get-tuple-element.92), channel_id=1, source_target_pairs={{0,4},{1,5},{2,6},{3,7},{4,0},{5,1},{6,2},{7,3},{8,12},{9,13},{10,... | collective-permute-start | bytes 196616 | tf_op jit(solution)/shard_map/ppermute | solution.py:49
  125.4 2.5 %collective-permute-done.22 = bf16[1,32,1024]{2,1,0:T(8,128)(2,1)S(1)} collective-permute-done((bf16[1,32,1024]{2,1,0:T(8,128)(2,1)S(1)}, bf16[1,32,1024]{2,1,0:T(8,128)(2,1)S(1)}, u32[]{:S(2)}, u32[]{:S(2)}) %collective-permute-start.22) | collective-permute-done | bytes 65568 | tf_op jit(solution)/shard_map/ppermute | solution.py:49
  130.7 2.5 %collective-permute-done.23 = bf16[2,32,1024]{2,1,0:T(8,128)(2,1)S(1)} collective-permute-done((bf16[2,32,1024]{2,1,0:T(8,128)(2,1)S(1)}, bf16[2,32,1024]{2,1,0:T(8,128)(2,1)S(1)}, u32[]{:S(2)}, u32[]{:S(2)}) %collective-permute-start.23) | collective-permute-done | bytes 131104 | tf_op jit(solution)/shard_map/ppermute | solution.py:49
  137.9 2.6 %collective-permute-done.24 = bf16[4,32,1024]{2,1,0:T(8,128)(2,1)S(1)} collective-permute-done((bf16[4,32,1024]{2,1,0:T(8,128)(2,1)S(1)}, bf16[4,32,1024]{2,1,0:T(8,128)(2,1)S(1)}, u32[]{:S(2)}, u32[]{:S(2)}) %collective-permute-start.24) | collective-permute-done | bytes 262176 | tf_op jit(solution)/shard_map/ppermute | solution.py:49
  140.6 2.7 %collective-permute-done.28 = bf16[4,32,1024]{2,1,0:T(8,128)(2,1)S(1)} collective-permute-done((bf16[4,32,1024]{2,1,0:T(8,128)(2,1)S(1)}, bf16[4,32,1024]{2,1,0:T(8,128)(2,1)S(1)}, u32[]{:S(2)}, u32[]{:S(2)}) %collective-permute-start.28) | collective-permute-done | bytes 262176 | tf_op jit(solution)/shard_map/ppermute | solution.py:49
  146.9 2.4 collective-permute-done.31
  150.5 2.8 %collective-permute-done.32 = f32[64,64]{1,0:T(8,128)S(1)} collective-permute-done((f32[64,64]{1,0:T(8,128)S(1)}, f32[64,64]{1,0:T(8,128)S(1)}, u32[]{:S(2)}, u32[]{:S(2)}) %collective-permute-start.32) | collective-permute-done | bytes 16416 | tf_op jit(solution)/shard_map/ppermute | solution.py:49
  153.2 3.5 %collective-permute-start.33 = (f32[64,64]{1,0:T(8,128)S(1)}, f32[64,64]{1,0:T(8,128)S(1)}, u32[]{:S(2)}, u32[]{:S(2)}) collective-permute-start(f32[64,64]{1,0:T(8,128)S(1)} %add.194), channel_id=1, source_target_pairs={{0,8},{1,9},{2,10},{3,11},{4,12},{5,13},{6,14},{7,15},{8,0},{9,1},... | collective-permute-start | bytes 49160 | tf_op jit(solution)/shard_map/ppermute | solution.py:49
  156.8 1.9 collective-permute-done.33
  159.3 10.4 %alpha.1 = (f32[64,64]{1,0:T(8,128)}, f32[64,64]{1,0:T(8,128)}) custom-call(f32[64,64]{1,0:T(8,128)} %add.195.along, f32[64,64]{1,0:T(8,128)} %copy-done, f32[1,1]{1,0:T(1,128)} %bitcast.51.refs_4_.total_weight.refs_6_), custom_call_target="tpu_custom_call" | custom-call | flops 67108864 | bytes 1048576 | tf_op jit(solution)/shard_map/alpha/pallas_call | solution.py:354
  169.6 4.8 %probe.3 = (f32[64,384]{1,0:T(8,128)S(1)}, f32[64,64]{1,0:T(8,128)S(1)}, f32[64,64]{1,0:T(8,128)S(1)}) custom-call(s32[1]{0:T(128)} %bitcast.me, bf16[8,32,1024]{2,1,0:T(8,128)(2,1)S(1)} %pad_maximum_fusion.3.refs_0_, bf16[8,32,1024]{2,1,0:T(8,128)(2,1)S(1)} %pad_maximum_fusion.4.refs_1_, bf16[8,32,1024]{2,1,0:T(8,128)(2,1)S(1)} %pad_maximum_fusion.1.refs_0_.refs_2_, ...), custom_call_target="tpu_custom_call" | custom-call | flops 402653184 | bytes 8388608 | tf_op jit(solution)/shard_map/probe/pallas_call | solution.py:182
  174.5 12.6 %probe_and_send.3 = (f32[64,384]{1,0:T(8,128)S(1)}, f32[64,64]{1,0:T(8,128)S(1)}, f32[64,1]{1,0:T(8,128)S(1)}, f32[8,64,1024]{2,1,0:T(8,128)S(1)}, f32[64,64]{1,...) custom-call(s32[1]{0:T(128)} %bitcast.me, ...), custom_call_target="tpu_custom_call" | custom-call | flops 402653184 | bytes 8388608 | tf_op jit(solution)/shard_map/probe_and_send/pallas_call | solution.py:271
  188.8 1.8 collective-permute-done.34
  192.2 2.4 collective-permute-done.35
  194.6 2.0 collective-permute-start.36
  198.5 2.9 %collective-permute-start.37 = (f32[64,64]{1,0:T(8,128)S(1)}, f32[64,64]{1,0:T(8,128)S(1)}, u32[]{:S(2)}, u32[]{:S(2)}) collective-permute-start(f32[64,64]{1,0:T(8,128)S(1)} %add.198), channel_id=1, source_target_pairs={{0,8},{1,9},{2,10},{3,11},{4,12},{5,13},{6,14},{7,15},{8,0},{9,1},... | collective-permute-start | bytes 49160 | tf_op jit(solution)/shard_map/ppermute | solution.py:49
  201.4 3.6 %panel_keep.3 = f32[8,64,1024]{2,1,0:T(8,128)S(1)} custom-call(s32[1]{0:T(128)} %bitcast.me, f32[64,384]{1,0:T(8,128)S(1)} %get-tuple-element.56.probed, s32[1,384]{1,0:T(1,128)S(1)} %reshape.156.counts.refs_3_.refs_5_, bf16[384,16384]{1,0:T(8,128)(2,1)} %acts.7), custom_call_target="tpu_custom_call" | custom-call | flops 402653184 | bytes 8388608 | tf_op jit(solution)/shard_map/panel_keep/pallas_call | solution.py:313
  205.7 10.2 %last.1 = (f32[64,64]{1,0:T(8,128)}, f32[64,64]{1,0:T(8,128)}, f32[64,64]{1,0:T(8,128)}, f32[64,64]{1,0:T(8,128)}, f32[64,64]{1,0:T(8,128)}) custom-call(f32[64,64]{1,0:T(8,128)} %add.199.along, f32[64,64]{1,0:T(8,128)} %copy-done, f32[64,64]{1,0:T(8,128)} %copy-done.4, f32[64,64]{1,0:T(8,128)} %copy-done.5, f32[64,64]{1,0:T(8,128)} %copy-done.6, ...), custom_call_target="tpu_custom_call" | custom-call | flops 67108864 | bytes 1048576 | tf_op jit(solution)/shard_map/last/pallas_call | solution.py:354
  218.2 2.2 convolution_add_fusion.1
  222.3 2.1 collective-permute-start.42
  226.2 3.9 %collective-permute-done.42 = f16[2,2,32,1024]{3,2,1,0:T(8,128)(2,1)S(1)} collective-permute-done((f16[2,2,32,1024]{3,2,1,0:T(8,128)(2,1)S(1)}, f16[2,2,32,1024]{3,2,1,0:T(8,128)(2,1)S(1)}, u32[]{:S(2)}, u32[]{:S(2)}) %collective-permute-start.42) | collective-permute-done | bytes 262176 | tf_op jit(solution)/shard_map/ppermute | solution.py:49
  231.3 2.0 collective-permute-start.40
  233.3 3.1 %collective-permute-done.43 = f16[2,32,1024]{2,1,0:T(8,128)(2,1)S(1)} collective-permute-done((f16[2,32,1024]{2,1,0:T(8,128)(2,1)S(1)}, f16[2,32,1024]{2,1,0:T(8,128)(2,1)S(1)}, u32[]{:S(2)}, u32[]{:S(2)}) %collective-permute-start.43) | collective-permute-done | bytes 131104 | tf_op jit(solution)/shard_map/ppermute | solution.py:49
  238.4 2.8 %collective-permute-start.41 = (f16[32,1024]{1,0:T(8,128)(2,1)S(1)}, f16[32,1024]{1,0:T(8,128)(2,1)S(1)}, u32[]{:S(2)}, u32[]{:S(2)}) collective-permute-start(f16[32,1024]{1,0:T(8,128)(2,1)S(1)} %fusion.43), channel_id=1, source_target_pairs={{0,8},{1,9},{2,10},{3,11},{4,12},{5,13},{6,14},{7,15},{8,0},{9,1},... | collective-permute-start | bytes 196616 | tf_op jit(solution)/shard_map/ppermute | solution.py:49
  241.3 2.3 collective-permute-done.41
  (218 shorter events, 58.7 us)
Async XLA Ops:
  8.1 5.1 %collective-permute-start = (f16[528,1024]{1,0:T(8,128)(2,1)S(1)}, f16[528,1024]{1,0:T(8,128)(2,1)S(1)}, u32[]{:S(2)}, u32[]{:S(2)}) collective-permute-start(f16[528,1024]{1,0:T(8,128)(2,1)S(1)} %pad_maximum_fusion), channel_id=1, source_target_pairs={{0,1},{1,0},{2,3},{3,2},{4,5},{5,4},{6,7},{7,6},{8,9},{9,8},{10,11... | collective-permute-start | bytes 3244040 | tf_op jit(solution)/shard_map/ppermute | solution.py:49
  17.2 10.3 %collective-permute-start.4 = (f16[144,1024]{1,0:T(8,128)(2,1)S(1)}, f16[144,1024]{1,0:T(8,128)(2,1)S(1)}, u32[]{:S(2)}, u32[]{:S(2)}) collective-permute-start(f16[144,1024]{1,0:T(8,128)(2,1)S(1)} %pad_maximum_fusion.6), channel_id=1, source_target_pairs={{0,4},{1,5},{2,6},{3,7},{4,0},{5,1},{6,2},{7,3},{8,12},{9,13},{10,... | collective-permute-start | bytes 884744 | tf_op jit(solution)/shard_map/ppermute | solution.py:49
  20.1 9.2 %collective-permute-start.1 = (f16[144,1024]{1,0:T(8,128)(2,1)S(1)}, f16[144,1024]{1,0:T(8,128)(2,1)S(1)}, u32[]{:S(2)}, u32[]{:S(2)}) collective-permute-start(f16[144,1024]{1,0:T(8,128)(2,1)S(1)} %pad_maximum_fusion.5), channel_id=1, source_target_pairs={{0,2},{1,3},{2,0},{3,1},{4,6},{5,7},{6,4},{7,5},{8,10},{9,11},{10,... | collective-permute-start | bytes 884744 | tf_op jit(solution)/shard_map/ppermute | solution.py:49
  31.0 10.1 %collective-permute-start.5 = (f16[80,1024]{1,0:T(8,128)(2,1)S(1)}, f16[80,1024]{1,0:T(8,128)(2,1)S(1)}, u32[]{:S(2)}, u32[]{:S(2)}) collective-permute-start(f16[80,1024]{1,0:T(8,128)(2,1)S(1)} %pad_maximum_fusion.12), channel_id=1, source_target_pairs={{0,8},{1,9},{2,10},{3,11},{4,12},{5,13},{6,14},{7,15},{8,0},{9,1},... | collective-permute-start | bytes 491528 | tf_op jit(solution)/shard_map/ppermute | solution.py:49
  34.2 8.0 %collective-permute-start.2 = (f16[80,1024]{1,0:T(8,128)(2,1)S(1)}, f16[80,1024]{1,0:T(8,128)(2,1)S(1)}, u32[]{:S(2)}, u32[]{:S(2)}) collective-permute-start(f16[80,1024]{1,0:T(8,128)(2,1)S(1)} %pad_maximum_fusion.11), channel_id=1, source_target_pairs={{0,4},{1,5},{2,6},{3,7},{4,0},{5,1},{6,2},{7,3},{8,12},{9,13},{10,... | collective-permute-start | bytes 491528 | tf_op jit(solution)/shard_map/ppermute | solution.py:49
  43.8 4.7 %collective-permute-start.6 = (f16[48,1024]{1,0:T(8,128)(2,1)S(1)}, f16[48,1024]{1,0:T(8,128)(2,1)S(1)}, u32[]{:S(2)}, u32[]{:S(2)}) collective-permute-start(f16[48,1024]{1,0:T(8,128)(2,1)S(1)} %pad_maximum_fusion.18), channel_id=1, source_target_pairs={{0,2},{1,3},{2,0},{3,1},{4,6},{5,7},{6,4},{7,5},{8,10},{9,11},{10,... | collective-permute-start | bytes 294920 | tf_op jit(solution)/shard_map/ppermute | solution.py:49
  45.9 7.2 %collective-permute-start.3 = (f16[48,1024]{1,0:T(8,128)(2,1)S(1)}, f16[48,1024]{1,0:T(8,128)(2,1)S(1)}, u32[]{:S(2)}, u32[]{:S(2)}) collective-permute-start(f16[48,1024]{1,0:T(8,128)(2,1)S(1)} %pad_maximum_fusion.17), channel_id=1, source_target_pairs={{0,8},{1,9},{2,10},{3,11},{4,12},{5,13},{6,14},{7,15},{8,0},{9,1},... | collective-permute-start | bytes 294920 | tf_op jit(solution)/shard_map/ppermute | solution.py:49
  54.9 65.3 %copy-start.8 = (f32[32,1024]{1,0:T(8,128)}, f32[32,1024]{1,0:T(8,128)S(1)}, u32[]{:S(2)}) copy-start(f32[32,1024]{1,0:T(8,128)S(1)} %fusion.52) | copy-start | bytes 393220
  55.0 65.3 %copy-start.10 = (f32[32,1024]{1,0:T(8,128)}, f32[32,1024]{1,0:T(8,128)S(1)}, u32[]{:S(2)}) copy-start(f32[32,1024]{1,0:T(8,128)S(1)} %fusion.54) | copy-start | bytes 393220
  55.1 5.3 %collective-permute-start.7 = (bf16[1,32,1024]{2,1,0:T(8,128)(2,1)S(1)}, bf16[1,32,1024]{2,1,0:T(8,128)(2,1)S(1)}, u32[]{:S(2)}, u32[]{:S(2)}) collective-permute-start(bf16[1,32,1024]{2,1,0:T(8,128)(2,1)S(1)} %get-tuple-element.95), channel_id=1, source_target_pairs={{0,8},{1,9},{2,10},{3,11},{4,12},{5,13},{6,14},{7,15},{8,0},{9,1},... | collective-permute-start | bytes 196616 | tf_op jit(solution)/shard_map/ppermute | solution.py:49
  55.2 6.2 %collective-permute-start.11 = (bf16[1,32,1024]{2,1,0:T(8,128)(2,1)S(1)}, bf16[1,32,1024]{2,1,0:T(8,128)(2,1)S(1)}, u32[]{:S(2)}, u32[]{:S(2)}) collective-permute-start(bf16[1,32,1024]{2,1,0:T(8,128)(2,1)S(1)} %get-tuple-element.94), channel_id=1, source_target_pairs={{0,4},{1,5},{2,6},{3,7},{4,0},{5,1},{6,2},{7,3},{8,12},{9,13},{10,... | collective-permute-start | bytes 196616 | tf_op jit(solution)/shard_map/ppermute | solution.py:49
  60.4 5.3 %collective-permute-start.8 = (bf16[2,32,1024]{2,1,0:T(8,128)(2,1)S(1)}, bf16[2,32,1024]{2,1,0:T(8,128)(2,1)S(1)}, u32[]{:S(2)}, u32[]{:S(2)}) collective-permute-start(bf16[2,32,1024]{2,1,0:T(8,128)(2,1)S(1)} %pad_maximum_fusion.13), channel_id=1, source_target_pairs={{0,4},{1,5},{2,6},{3,7},{4,0},{5,1},{6,2},{7,3},{8,12},{9,13},{10,... | collective-permute-start | bytes 393224 | tf_op jit(solution)/shard_map/ppermute | solution.py:49
  61.4 7.4 %collective-permute-start.12 = (bf16[2,32,1024]{2,1,0:T(8,128)(2,1)S(1)}, bf16[2,32,1024]{2,1,0:T(8,128)(2,1)S(1)}, u32[]{:S(2)}, u32[]{:S(2)}) collective-permute-start(bf16[2,32,1024]{2,1,0:T(8,128)(2,1)S(1)} %pad_maximum_fusion.14), channel_id=1, source_target_pairs={{0,8},{1,9},{2,10},{3,11},{4,12},{5,13},{6,14},{7,15},{8,0},{9,1},... | collective-permute-start | bytes 393224 | tf_op jit(solution)/shard_map/ppermute | solution.py:49
  65.8 7.3 %collective-permute-start.9 = (bf16[4,32,1024]{2,1,0:T(8,128)(2,1)S(1)}, bf16[4,32,1024]{2,1,0:T(8,128)(2,1)S(1)}, u32[]{:S(2)}, u32[]{:S(2)}) collective-permute-start(bf16[4,32,1024]{2,1,0:T(8,128)(2,1)S(1)} %pad_maximum_fusion.7), channel_id=1, source_target_pairs={{0,2},{1,3},{2,0},{3,1},{4,6},{5,7},{6,4},{7,5},{8,10},{9,11},{10,... | collective-permute-start | bytes 786440 | tf_op jit(solution)/shard_map/ppermute | solution.py:49
  68.8 7.1 %collective-permute-start.13 = (bf16[4,32,1024]{2,1,0:T(8,128)(2,1)S(1)}, bf16[4,32,1024]{2,1,0:T(8,128)(2,1)S(1)}, u32[]{:S(2)}, u32[]{:S(2)}) collective-permute-start(bf16[4,32,1024]{2,1,0:T(8,128)(2,1)S(1)} %pad_maximum_fusion.8), channel_id=1, source_target_pairs={{0,2},{1,3},{2,0},{3,1},{4,6},{5,7},{6,4},{7,5},{8,10},{9,11},{10,... | collective-permute-start | bytes 786440 | tf_op jit(solution)/shard_map/ppermute | solution.py:49
  73.1 7.7 %collective-permute-start.10 = (bf16[8,32,1024]{2,1,0:T(8,128)(2,1)S(1)}, bf16[8,32,1024]{2,1,0:T(8,128)(2,1)S(1)}, u32[]{:S(2)}, u32[]{:S(2)}) collective-permute-start(bf16[8,32,1024]{2,1,0:T(8,128)(2,1)S(1)} %pad_maximum_fusion.1.refs_0_.refs_2_), channel_id=1, source_target_pairs={{0,1},{1,0},{2,3},{3,2},{4,5},{5,4},{6,7},{7,6},{8,9},{9,8},{10,11... | collective-permute-start | bytes 1572872 | tf_op jit(solution)/shard_map/ppermute | solution.py:49
  75.9 4.9 %collective-permute-start.14 = (bf16[8,32,1024]{2,1,0:T(8,128)(2,1)S(1)}, bf16[8,32,1024]{2,1,0:T(8,128)(2,1)S(1)}, u32[]{:S(2)}, u32[]{:S(2)}) collective-permute-start(bf16[8,32,1024]{2,1,0:T(8,128)(2,1)S(1)} %pad_maximum_fusion.2.refs_1_.refs_3_), channel_id=1, source_target_pairs={{0,1},{1,0},{2,3},{3,2},{4,5},{5,4},{6,7},{7,6},{8,9},{9,8},{10,11... | collective-permute-start | bytes 1572872 | tf_op jit(solution)/shard_map/ppermute | solution.py:49
  88.9 31.4 %copy-start = (f32[64,64]{1,0:T(8,128)}, f32[64,64]{1,0:T(8,128)S(1)}, u32[]{:S(2)}) copy-start(f32[64,64]{1,0:T(8,128)S(1)} %get-tuple-element.41.current.refs_11_) | copy-start | bytes 49156
  89.4 4.2 %collective-permute-start.15 = (f16[8,64,1024]{2,1,0:T(8,128)(2,1)S(1)}, f16[8,64,1024]{2,1,0:T(8,128)(2,1)S(1)}, u32[]{:S(2)}, u32[]{:S(2)}) collective-permute-start(f16[8,64,1024]{2,1,0:T(8,128)(2,1)S(1)} %multiply_convert_fusion.1), channel_id=1, source_target_pairs={{0,1},{1,0},{2,3},{3,2},{4,5},{5,4},{6,7},{7,6},{8,9},{9,8},{10,11... | collective-permute-start | bytes 3145736 | tf_op jit(solution)/shard_map/ppermute | solution.py:49
  94.4 8.3 %collective-permute-start.19 = (f16[2,2,32,1024]{3,2,1,0:T(8,128)(2,1)S(1)}, f16[2,2,32,1024]{3,2,1,0:T(8,128)(2,1)S(1)}, u32[]{:S(2)}, u32[]{:S(2)}) collective-permute-start(f16[2,2,32,1024]{3,2,1,0:T(8,128)(2,1)S(1)} %fusion.6), channel_id=1, source_target_pairs={{0,4},{1,5},{2,6},{3,7},{4,0},{5,1},{6,2},{7,3},{8,12},{9,13},{10,... | collective-permute-start | bytes 786440 | tf_op jit(solution)/shard_map/ppermute | solution.py:49
  96.4 10.7 %collective-permute-start.16 = (f16[2,2,32,1024]{3,2,0,1:T(8,128)(2,1)S(1)}, f16[2,2,32,1024]{3,2,0,1:T(8,128)(2,1)S(1)}, u32[]{:S(2)}, u32[]{:S(2)}) collective-permute-start(f16[2,2,32,1024]{3,2,0,1:T(8,128)(2,1)S(1)} %fusion.15), channel_id=1, source_target_pairs={{0,2},{1,3},{2,0},{3,1},{4,6},{5,7},{6,4},{7,5},{8,10},{9,11},{10,... | collective-permute-start | bytes 786440 | tf_op jit(solution)/shard_map/ppermute | solution.py:49
  103.0 10.1 %collective-permute-start.20 = (f16[2,32,1024]{2,1,0:T(8,128)(2,1)S(1)}, f16[2,32,1024]{2,1,0:T(8,128)(2,1)S(1)}, u32[]{:S(2)}, u32[]{:S(2)}) collective-permute-start(f16[2,32,1024]{2,1,0:T(8,128)(2,1)S(1)} %fusion.25), channel_id=1, source_target_pairs={{0,8},{1,9},{2,10},{3,11},{4,12},{5,13},{6,14},{7,15},{8,0},{9,1},... | collective-permute-start | bytes 393224 | tf_op jit(solution)/shard_map/ppermute | solution.py:49
  107.4 6.6 %collective-permute-start.17 = (f16[2,32,1024]{2,1,0:T(8,128)(2,1)S(1)}, f16[2,32,1024]{2,1,0:T(8,128)(2,1)S(1)}, u32[]{:S(2)}, u32[]{:S(2)}) collective-permute-start(f16[2,32,1024]{2,1,0:T(8,128)(2,1)S(1)} %fusion.28), channel_id=1, source_target_pairs={{0,4},{1,5},{2,6},{3,7},{4,0},{5,1},{6,2},{7,3},{8,12},{9,13},{10,... | collective-permute-start | bytes 393224 | tf_op jit(solution)/shard_map/ppermute | solution.py:49
  113.3 4.3 %collective-permute-start.21 = (f16[32,1024]{1,0:T(8,128)(2,1)S(1)}, f16[32,1024]{1,0:T(8,128)(2,1)S(1)}, u32[]{:S(2)}, u32[]{:S(2)}) collective-permute-start(f16[32,1024]{1,0:T(8,128)(2,1)S(1)} %fusion.46), channel_id=1, source_target_pairs={{0,2},{1,3},{2,0},{3,1},{4,6},{5,7},{6,4},{7,5},{8,10},{9,11},{10,... | collective-permute-start | bytes 196616 | tf_op jit(solution)/shard_map/ppermute | solution.py:49
  114.1 6.1 %collective-permute-start.18 = (f16[32,1024]{1,0:T(8,128)(2,1)S(1)}, f16[32,1024]{1,0:T(8,128)(2,1)S(1)}, u32[]{:S(2)}, u32[]{:S(2)}) collective-permute-start(f16[32,1024]{1,0:T(8,128)(2,1)S(1)} %fusion.49), channel_id=1, source_target_pairs={{0,8},{1,9},{2,10},{3,11},{4,12},{5,13},{6,14},{7,15},{8,0},{9,1},... | collective-permute-start | bytes 196616 | tf_op jit(solution)/shard_map/ppermute | solution.py:49
  122.1 5.8 %collective-permute-start.22 = (bf16[1,32,1024]{2,1,0:T(8,128)(2,1)S(1)}, bf16[1,32,1024]{2,1,0:T(8,128)(2,1)S(1)}, u32[]{:S(2)}, u32[]{:S(2)}) collective-permute-start(bf16[1,32,1024]{2,1,0:T(8,128)(2,1)S(1)} %get-tuple-element.93), channel_id=1, source_target_pairs={{0,8},{1,9},{2,10},{3,11},{4,12},{5,13},{6,14},{7,15},{8,0},{9,1},... | collective-permute-start | bytes 196616 | tf_op jit(solution)/shard_map/ppermute | solution.py:49
  122.6 6.3 %collective-permute-start.26 = (bf16[1,32,1024]{2,1,0:T(8,128)(2,1)S(1)}, bf16[1,32,1024]{2,1,0:T(8,128)(2,1)S(1)}, u32[]{:S(2)}, u32[]{:S(2)}) collective-permute-start(bf16[1,32,1024]{2,1,0:T(8,128)(2,1)S(1)} %get-tuple-element.92), channel_id=1, source_target_pairs={{0,4},{1,5},{2,6},{3,7},{4,0},{5,1},{6,2},{7,3},{8,12},{9,13},{10,... | collective-permute-start | bytes 196616 | tf_op jit(solution)/shard_map/ppermute | solution.py:49
  127.9 5.3 %collective-permute-start.23 = (bf16[2,32,1024]{2,1,0:T(8,128)(2,1)S(1)}, bf16[2,32,1024]{2,1,0:T(8,128)(2,1)S(1)}, u32[]{:S(2)}, u32[]{:S(2)}) collective-permute-start(bf16[2,32,1024]{2,1,0:T(8,128)(2,1)S(1)} %pad_maximum_fusion.15), channel_id=1, source_target_pairs={{0,4},{1,5},{2,6},{3,7},{4,0},{5,1},{6,2},{7,3},{8,12},{9,13},{10,... | collective-permute-start | bytes 393224 | tf_op jit(solution)/shard_map/ppermute | solution.py:49
  129.0 7.3 %collective-permute-start.27 = (bf16[2,32,1024]{2,1,0:T(8,128)(2,1)S(1)}, bf16[2,32,1024]{2,1,0:T(8,128)(2,1)S(1)}, u32[]{:S(2)}, u32[]{:S(2)}) collective-permute-start(bf16[2,32,1024]{2,1,0:T(8,128)(2,1)S(1)} %pad_maximum_fusion.16), channel_id=1, source_target_pairs={{0,8},{1,9},{2,10},{3,11},{4,12},{5,13},{6,14},{7,15},{8,0},{9,1},... | collective-permute-start | bytes 393224 | tf_op jit(solution)/shard_map/ppermute | solution.py:49
  133.2 7.3 %collective-permute-start.24 = (bf16[4,32,1024]{2,1,0:T(8,128)(2,1)S(1)}, bf16[4,32,1024]{2,1,0:T(8,128)(2,1)S(1)}, u32[]{:S(2)}, u32[]{:S(2)}) collective-permute-start(bf16[4,32,1024]{2,1,0:T(8,128)(2,1)S(1)} %pad_maximum_fusion.9), channel_id=1, source_target_pairs={{0,2},{1,3},{2,0},{3,1},{4,6},{5,7},{6,4},{7,5},{8,10},{9,11},{10,... | collective-permute-start | bytes 786440 | tf_op jit(solution)/shard_map/ppermute | solution.py:49
  136.4 7.0 %collective-permute-start.28 = (bf16[4,32,1024]{2,1,0:T(8,128)(2,1)S(1)}, bf16[4,32,1024]{2,1,0:T(8,128)(2,1)S(1)}, u32[]{:S(2)}, u32[]{:S(2)}) collective-permute-start(bf16[4,32,1024]{2,1,0:T(8,128)(2,1)S(1)} %pad_maximum_fusion.10), channel_id=1, source_target_pairs={{0,2},{1,3},{2,0},{3,1},{4,6},{5,7},{6,4},{7,5},{8,10},{9,11},{10,... | collective-permute-start | bytes 786440 | tf_op jit(solution)/shard_map/ppermute | solution.py:49
  140.6 33.9 %collective-permute-start.25 = (bf16[8,32,1024]{2,1,0:T(8,128)(2,1)S(1)}, bf16[8,32,1024]{2,1,0:T(8,128)(2,1)}, u32[]{:S(2)}, u32[]{:S(2)}) collective-permute-start(bf16[8,32,1024]{2,1,0:T(8,128)(2,1)S(1)} %pad_maximum_fusion.3.refs_0_), channel_id=1, source_target_pairs={{0,1},{1,0},{2,3},{3,2},{4,5},{5,4},{6,7},{7,6},{8,9},{9,8},{10,11... | collective-permute-start | bytes 1572872 | tf_op jit(solution)/shard_map/ppermute | solution.py:49
  143.4 31.1 %collective-permute-start.29 = (bf16[8,32,1024]{2,1,0:T(8,128)(2,1)S(1)}, bf16[8,32,1024]{2,1,0:T(8,128)(2,1)}, u32[]{:S(2)}, u32[]{:S(2)}) collective-permute-start(bf16[8,32,1024]{2,1,0:T(8,128)(2,1)S(1)} %pad_maximum_fusion.4.refs_1_), channel_id=1, source_target_pairs={{0,1},{1,0},{2,3},{3,2},{4,5},{5,4},{6,7},{7,6},{8,9},{9,8},{10,11... | collective-permute-start | bytes 1572872 | tf_op jit(solution)/shard_map/ppermute | solution.py:49
  143.5 1.9 collective-permute-start.30
  145.4 3.9 %collective-permute-start.31 = (f32[64,64]{1,0:T(8,128)S(1)}, f32[64,64]{1,0:T(8,128)S(1)}, u32[]{:S(2)}, u32[]{:S(2)}) collective-permute-start(f32[64,64]{1,0:T(8,128)S(1)} %add.192), channel_id=1, source_target_pairs={{0,2},{1,3},{2,0},{3,1},{4,6},{5,7},{6,4},{7,5},{8,10},{9,11},{10,... | collective-permute-start | bytes 49160 | tf_op jit(solution)/shard_map/ppermute | solution.py:49
  149.3 3.9 %collective-permute-start.32 = (f32[64,64]{1,0:T(8,128)S(1)}, f32[64,64]{1,0:T(8,128)S(1)}, u32[]{:S(2)}, u32[]{:S(2)}) collective-permute-start(f32[64,64]{1,0:T(8,128)S(1)} %add.193), channel_id=1, source_target_pairs={{0,4},{1,5},{2,6},{3,7},{4,0},{5,1},{6,2},{7,3},{8,12},{9,13},{10,... | collective-permute-start | bytes 49160 | tf_op jit(solution)/shard_map/ppermute | solution.py:49
  153.2 5.4 %collective-permute-start.33 = (f32[64,64]{1,0:T(8,128)S(1)}, f32[64,64]{1,0:T(8,128)S(1)}, u32[]{:S(2)}, u32[]{:S(2)}) collective-permute-start(f32[64,64]{1,0:T(8,128)S(1)} %add.194), channel_id=1, source_target_pairs={{0,8},{1,9},{2,10},{3,11},{4,12},{5,13},{6,14},{7,15},{8,0},{9,1},... | collective-permute-start | bytes 49160 | tf_op jit(solution)/shard_map/ppermute | solution.py:49
  188.3 32.1 %collective-permute-start.38 = (f16[8,64,1024]{2,1,0:T(8,128)(2,1)S(1)}, f16[8,64,1024]{2,1,0:T(8,128)(2,1)}, u32[]{:S(2)}, u32[]{:S(2)}) collective-permute-start(f16[8,64,1024]{2,1,0:T(8,128)(2,1)S(1)} %multiply_convert_fusion), channel_id=1, source_target_pairs={{0,1},{1,0},{2,3},{3,2},{4,5},{5,4},{6,7},{7,6},{8,9},{9,8},{10,11... | collective-permute-start | bytes 3145736 | tf_op jit(solution)/shard_map/ppermute | solution.py:49
  188.3 2.3 collective-permute-start.34
  190.7 3.9 %collective-permute-start.35 = (f32[64,64]{1,0:T(8,128)S(1)}, f32[64,64]{1,0:T(8,128)S(1)}, u32[]{:S(2)}, u32[]{:S(2)}) collective-permute-start(f32[64,64]{1,0:T(8,128)S(1)} %add.196), channel_id=1, source_target_pairs={{0,2},{1,3},{2,0},{3,1},{4,6},{5,7},{6,4},{7,5},{8,10},{9,11},{10,... | collective-permute-start | bytes 49160 | tf_op jit(solution)/shard_map/ppermute | solution.py:49
  194.6 3.9 %collective-permute-start.36 = (f32[64,64]{1,0:T(8,128)S(1)}, f32[64,64]{1,0:T(8,128)S(1)}, u32[]{:S(2)}, u32[]{:S(2)}) collective-permute-start(f32[64,64]{1,0:T(8,128)S(1)} %add.197), channel_id=1, source_target_pairs={{0,4},{1,5},{2,6},{3,7},{4,0},{5,1},{6,2},{7,3},{8,12},{9,13},{10,... | collective-permute-start | bytes 49160 | tf_op jit(solution)/shard_map/ppermute | solution.py:49
  198.5 6.6 %collective-permute-start.37 = (f32[64,64]{1,0:T(8,128)S(1)}, f32[64,64]{1,0:T(8,128)S(1)}, u32[]{:S(2)}, u32[]{:S(2)}) collective-permute-start(f32[64,64]{1,0:T(8,128)S(1)} %add.198), channel_id=1, source_target_pairs={{0,8},{1,9},{2,10},{3,11},{4,12},{5,13},{6,14},{7,15},{8,0},{9,1},... | collective-permute-start | bytes 49160 | tf_op jit(solution)/shard_map/ppermute | solution.py:49
  222.3 7.8 %collective-permute-start.42 = (f16[2,2,32,1024]{3,2,1,0:T(8,128)(2,1)S(1)}, f16[2,2,32,1024]{3,2,1,0:T(8,128)(2,1)S(1)}, u32[]{:S(2)}, u32[]{:S(2)}) collective-permute-start(f16[2,2,32,1024]{3,2,1,0:T(8,128)(2,1)S(1)} %fusion.3), channel_id=1, source_target_pairs={{0,4},{1,5},{2,6},{3,7},{4,0},{5,1},{6,2},{7,3},{8,12},{9,13},{10,... | collective-permute-start | bytes 786440 | tf_op jit(solution)/shard_map/ppermute | solution.py:49
  224.6 6.4 %collective-permute-start.39 = (f16[2,2,32,1024]{3,2,0,1:T(8,128)(2,1)S(1)}, f16[2,2,32,1024]{3,2,0,1:T(8,128)(2,1)S(1)}, u32[]{:S(2)}, u32[]{:S(2)}) collective-permute-start(f16[2,2,32,1024]{3,2,0,1:T(8,128)(2,1)S(1)} %fusion.12), channel_id=1, source_target_pairs={{0,2},{1,3},{2,0},{3,1},{4,6},{5,7},{6,4},{7,5},{8,10},{9,11},{10,... | collective-permute-start | bytes 786440 | tf_op jit(solution)/shard_map/ppermute | solution.py:49
  230.4 6.0 %collective-permute-start.43 = (f16[2,32,1024]{2,1,0:T(8,128)(2,1)S(1)}, f16[2,32,1024]{2,1,0:T(8,128)(2,1)S(1)}, u32[]{:S(2)}, u32[]{:S(2)}) collective-permute-start(f16[2,32,1024]{2,1,0:T(8,128)(2,1)S(1)} %fusion.19), channel_id=1, source_target_pairs={{0,8},{1,9},{2,10},{3,11},{4,12},{5,13},{6,14},{7,15},{8,0},{9,1},... | collective-permute-start | bytes 393224 | tf_op jit(solution)/shard_map/ppermute | solution.py:49
  231.3 6.9 %collective-permute-start.40 = (f16[2,32,1024]{2,1,0:T(8,128)(2,1)S(1)}, f16[2,32,1024]{2,1,0:T(8,128)(2,1)S(1)}, u32[]{:S(2)}, u32[]{:S(2)}) collective-permute-start(f16[2,32,1024]{2,1,0:T(8,128)(2,1)S(1)} %fusion.22), channel_id=1, source_target_pairs={{0,4},{1,5},{2,6},{3,7},{4,0},{5,1},{6,2},{7,3},{8,12},{9,13},{10,... | collective-permute-start | bytes 393224 | tf_op jit(solution)/shard_map/ppermute | solution.py:49
  236.6 4.6 %collective-permute-start.44 = (f16[32,1024]{1,0:T(8,128)(2,1)S(1)}, f16[32,1024]{1,0:T(8,128)(2,1)S(1)}, u32[]{:S(2)}, u32[]{:S(2)}) collective-permute-start(f16[32,1024]{1,0:T(8,128)(2,1)S(1)} %fusion.40), channel_id=1, source_target_pairs={{0,2},{1,3},{2,0},{3,1},{4,6},{5,7},{6,4},{7,5},{8,10},{9,11},{10,... | collective-permute-start | bytes 196616 | tf_op jit(solution)/shard_map/ppermute | solution.py:49
  238.4 5.2 %collective-permute-start.41 = (f16[32,1024]{1,0:T(8,128)(2,1)S(1)}, f16[32,1024]{1,0:T(8,128)(2,1)S(1)}, u32[]{:S(2)}, u32[]{:S(2)}) collective-permute-start(f16[32,1024]{1,0:T(8,128)(2,1)S(1)} %fusion.43), channel_id=1, source_target_pairs={{0,8},{1,9},{2,10},{3,11},{4,12},{5,13},{6,14},{7,15},{8,0},{9,1},... | collective-permute-start | bytes 196616 | tf_op jit(solution)/shard_map/ppermute | solution.py:49
  (11 other events, 116.7 us)

commit v4 on v3

--- a/solution.py
+++ b/solution.py
@@ -30,19 +30,29 @@
     return 0.5 * (matrix + matrix.T)
 
 
-def solve_positive(matrix, target):
-    work = jnp.concatenate([matrix, target], axis=1)
+def solve_positive(*works):
     index = lax.broadcasted_iota(jnp.int32, (K, 1), 0)
+    works = list(works)
     for k in range(0, K, 2):
-        a, b = work[k : k + 1], work[k + 1 : k + 2]
-        col_a, col_b = work[:, k : k + 1], work[:, k + 1 : k + 2]
-        p, q = work[k : k + 1, k : k + 1], work[k : k + 1, k + 1 : k + 2]
-        t, r = work[k + 1 : k + 2, k : k + 1], work[k + 1 : k + 2, k + 1 : k + 2]
-        inv = 1.0 / (p * r - q * t)
-        new_a, new_b = (r * a - q * b) * inv, (p * b - t * a) * inv
-        rest = work - (col_a * new_a + col_b * new_b)
-        work = jnp.where(index == k, new_a, jnp.where(index == k + 1, new_b, rest))
-    return work[:, K:]
+        for i, work in enumerate(works):
+            a, b = work[k : k + 1], work[k + 1 : k + 2]
+            col_a, col_b = work[:, k : k + 1], work[:, k + 1 : k + 2]
+            p, q = work[k : k + 1, k : k + 1], work[k : k + 1, k + 1 : k + 2]
+            t, r = work[k + 1 : k + 2, k : k + 1], work[k + 1 : k + 2, k + 1 : k + 2]
+            inv = 1.0 / (p * r - q * t)
+            new_a, new_b = (r * a - q * b) * inv, (p * b - t * a) * inv
+            rest = work - (col_a * new_a + col_b * new_b)
+            works[i] = jnp.where(index == k, new_a, jnp.where(index == k + 1, new_b, rest))
+    return [work[:, K:] for work in works]
+
+
+def beside(matrix, target):
+    return jnp.concatenate([matrix, target], axis=1)
+
+
+def identity():
+    eye = lax.broadcasted_iota(jnp.int32, (K, K), 0) == lax.broadcasted_iota(jnp.int32, (K, K), 1)
+    return jnp.where(eye, 1.0, 0.0)
 
 
 def swap(value, bit, n):
@@ -104,7 +114,7 @@
     )
 
 
-def sums_kernel(half, me, labels, counts, acts, out, peak, weight, kept, sems, member):
+def sums_kernel(half, me, labels, counts, acts, out, weight, kept, sems, member):
     step = pl.program_id(0)
 
     @pl.when(step == 0)
@@ -114,12 +124,9 @@
         full = jnp.where(labels[...] == concept, counts[...].astype(F32), 0.0)
         member[...] = full.astype(BF16)
         weight[...] = jnp.sum(full, axis=1, keepdims=True)
-        peak[...] = jnp.zeros_like(peak)
 
     block_copy(acts, kept, sems, me, half, step).wait()
-    block = jnp.dot(member[...], kept[step], preferred_element_type=F32)
-    out[0] = block
-    peak[...] = jnp.maximum(peak[...], jnp.max(jnp.max(jnp.abs(block), axis=1, keepdims=True), axis=0, keepdims=True))
+    out[0] = jnp.dot(member[...], kept[step], preferred_element_type=F32)
 
 
 def class_sums(me, labels, counts, acts, n, half):
@@ -133,10 +140,9 @@
         [whole(1, rows), whole(1, rows), HBM],
         (
             jax.ShapeDtypeStruct((n // 2, K, f), F32),
-            jax.ShapeDtypeStruct((1, 1), F32),
             jax.ShapeDtypeStruct((K, 1), F32),
         ),
-        (pl.BlockSpec((1, K, f), lambda i, me: (i, 0, 0)), whole(1, 1), whole(K, 1)),
+        (pl.BlockSpec((1, K, f), lambda i, me: (i, 0, 0)), whole(K, 1)),
         acts,
         [pltpu.VMEM((K, rows), BF16)],
     )(me, labels, counts, acts)
@@ -156,7 +162,7 @@
 
 def add_block(panels, acts, probed, grams):
     both = [jnp.concatenate([panels[i][0], panels[i + 1][0]], axis=0) for i in range(0, len(panels), 2)]
-    probed[...] += inner(both[0], acts)
+    probed[...] += inner(acts, both[0])
     for gram, other in zip(grams, both):
         gram[...] += inner(other, both[0])
 
@@ -185,8 +191,8 @@
         n,
         n // 2,
         v_specs(n, d // n, *shifts) * count + [HBM],
-        (jax.ShapeDtypeStruct((K, rows), F32),) + (jax.ShapeDtypeStruct((K, K), F32),) * count,
-        (whole(K, rows),) + (whole(K, K),) * count,
+        (jax.ShapeDtypeStruct((rows, K), F32),) + (jax.ShapeDtypeStruct((K, K), F32),) * count,
+        (whole(rows, K),) + (whole(K, K),) * count,
         acts,
     )(me, *panels, acts)
 
@@ -230,22 +236,24 @@
     given, refs = refs[: 4 * second], refs[4 * second :]
     probed, along, bound, out, *refs = refs
     grams, refs = refs[:count], refs[count:]
-    made, (kept, sems, weighted) = refs[: 3 * second], refs[3 * second :]
+    made, (kept, sems, weighted, sum_of) = refs[: 3 * second], refs[3 * second :]
     step = pl.program_id(0)
 
     @pl.when(step == 0)
     def _():
         start_copies(acts, kept, sems, me, 1)
-        for ref, begin in zip((probed, *grams), (start, *starts)):
+        for ref, begin in zip((sum_of, *grams), (start, *starts)):
             ref[...] = begin[...]
 
     @pl.when(step < steps)
     def _():
         block_copy(acts, kept, sems, me, 1, step).wait()
-        add_block(panels, kept[step], probed, grams)
+        add_block(panels, kept[step], sum_of, grams)
 
     @pl.when(step == steps)
     def _():
+        probed[...] = sum_of[...].T
+
         def bounded(norms, weight):
             return (1.02 * BOUND * BOUND * d**0.5) * weight * norms
 
@@ -291,7 +299,7 @@
         )
         + (whole(K, K),) * (count + made),
         acts,
-        [pltpu.VMEM((K, rows), BF16)],
+        [pltpu.VMEM((K, rows), BF16), pltpu.VMEM((rows, K), F32)],
     )(me, *panels, acts, counts, total_weight, *starts, *given)
 
 
@@ -326,33 +334,39 @@
 def alpha_kernel(along, current, total_weight, alpha_t, inverse):
     now = current[...]
     curvature = (along[...] - precise(now, now)) / total_weight[...] + RIDGE * now
-    eye = lax.broadcasted_iota(jnp.int32, (K, K), 0) == lax.broadcasted_iota(jnp.int32, (K, K), 1)
-    alpha_t[...] = solve_positive(symmetric(curvature), now).T
-    inverse[...] = symmetric(solve_positive(now, jnp.where(eye, 1.0, 0.0)))
-
-
-def last_kernel(along, current, renewed, mixed, beta_t, alpha_t, total_weight, on_base, on_image, on_panel, out_base, out_image):
-    now, beta, alpha, weight = current[...], beta_t[...], alpha_t[...], total_weight[...]
+    alpha, inv = solve_positive(beside(symmetric(curvature), now), beside(now, identity()))
+    alpha_t[...] = alpha.T
+    inverse[...] = symmetric(inv)
+
+
+def before_kernel(current, renewed, mixed, beta_t, total_weight, fixed, cross_t):
+    now, beta, weight = current[...], beta_t[...], total_weight[...]
     cross = mixed[...] + outer(now, beta)
-    half = outer(mixed[...].T, beta)
-    length = renewed[...] + half + precise(beta, cross)
-    cross_t = cross.T
-    curvature = (along[...] - outer(cross_t, cross_t)) / weight + RIDGE * length
-    step = solve_positive(symmetric(curvature), renewed[...]).T
-    eye = lax.broadcasted_iota(jnp.int32, (K, K), 0) == lax.broadcasted_iota(jnp.int32, (K, K), 1)
-    identity = jnp.where(eye, 1.0, 0.0)
-    direction_base = precise(step, identity + beta)
-    direction_image = precise(step, alpha)
-    out_base[...] = alpha + direction_base
-    out_image[...] = -direction_image
-    on_base[...] = identity - RIDGE * direction_base + precise(step, cross_t) / weight
-    on_image[...] = RIDGE * direction_image - alpha
+    length = renewed[...] + outer(mixed[...].T, beta) + precise(beta, cross)
+    turned = cross.T
+    cross_t[...] = turned
+    fixed[...] = RIDGE * length - outer(turned, turned) / weight
+
+
+def last_kernel(along, fixed, cross_t, renewed, beta_t, alpha_t, total_weight, base, image, solved, rest, on_panel):
+    weight = total_weight[...]
+    curvature = symmetric(along[...] / weight + fixed[...])
+    step = solve_positive(beside(curvature, renewed[...]))[0].T
     on_panel[...] = step / weight
+    alpha = alpha_t[...]
+    all_three = precise(step, jnp.concatenate([identity() + beta_t[...], alpha, cross_t[...]], axis=1))
+    direction_base, direction_image = all_three[:, :K], all_three[:, K : 2 * K]
+    crossed = all_three[:, 2 * K :] / weight
+    both = jnp.concatenate([base[...], image[...]], axis=0)
+    solved[...] = precise(beside(alpha + direction_base, -direction_image), both)
+    rest[...] = precise(
+        beside(identity() - RIDGE * direction_base + crossed, RIDGE * direction_image - alpha), both
+    )
 
 
 def small(kernel, name, outs, *args):
     return pl.pallas_call(
-        kernel, out_shape=(jax.ShapeDtypeStruct((K, K), F32),) * outs, name=name,
+        kernel, out_shape=tuple(jax.ShapeDtypeStruct(shape, F32) for shape in outs), name=name,
         cost_estimate=pl.CostEstimate(flops=1 << 26, bytes_accessed=1 << 20, transcendentals=0),
     )(*args)
 
@@ -372,46 +386,32 @@
     return keep, send, [other for other in left if other != bit]
 
 
-def reduce_scatter(blocks, n, swap_a, swap_b, along=None):
+def reduce_scatter(blocks, n, swap_a, swap_b, along):
     bits = n.bit_length() - 2
     shape = (2,) * bits + (HALF, blocks.shape[2])
     a, b = blocks[:, :HALF].reshape(shape), blocks[:, HALF:].reshape(shape)
     left_a = left_b = [1 << i for i in range(bits, 0, -1)]
-    for bit_a, bit_b in zip(*hop_bits(n)):
+    order_a, order_b = hop_bits(n)
+    waiting = list(order_a)
+    for bit_a, bit_b in zip(order_a, order_b):
         keep_a, send_a, left_a = split_blocks(a, left_a, bit_a)
         keep_b, send_b, left_b = split_blocks(b, left_b, bit_b)
+        send_a, send_b, along = lax.optimization_barrier((send_a, send_b, along))
         a, b = keep_a + swap_a(send_a, bit_a), keep_b + swap_b(send_b, bit_b)
-        if along is not None:
-            along = along + swap(along, bit_a, n)
-    return jnp.concatenate([a, b], axis=0), along
-
-
-class Packed:
-    def __init__(self, n, bound, weight):
-        self.n, self.bound, self.weight = n, bound, weight
+        for bit in waiting[:2]:
+            along = along + swap(along, bit, n)
+        waiting = waiting[2:]
+    return a, b, along
+
+
+class Root:
+    def __init__(self, n, bound):
+        self.n, self.scale = n, TOP / bound**0.5
 
     def __call__(self, send, bit):
-        f = send.shape[-1]
-        power = jnp.ceil(jnp.log2(jnp.maximum(self.bound, TINY)))
-        value = (send * jnp.exp2(15.0 - power)).astype(F16).reshape(-1, f)
-        row = lax.broadcasted_iota(jnp.int32, (16, f), 0)
-        tail = jnp.where(row == 0, power, 0.0)
-        if self.weight is not None:
-            high = jnp.floor(self.weight * (1.0 / 1024.0))
-            low = self.weight - 1024.0 * high
-            tail = jnp.where(row == 1, _widen(high, f), jnp.where(row == 2, _widen(low, f), tail))
-        got = swap(jnp.concatenate([value, tail.astype(F16)], axis=0), bit, self.n)
-        count = value.shape[0]
-        theirs = got[count : count + 1, :1].astype(F32)
-        if self.weight is not None:
-            other = got[count + 1 : count + 3, :K].astype(F32)
-            self.weight = self.weight + (1024.0 * other[:1] + other[1:])
-        self.bound = 1.001 * (self.bound + jnp.exp2(theirs))
-        return got[:count].reshape(send.shape).astype(F32) * jnp.exp2(theirs - 15.0)
-
-
-def _widen(row, f):
-    return row if f == K else jnp.pad(row, ((0, 0), (0, f - K)))
+        root = jnp.sqrt(jnp.abs(send)) * self.scale
+        got = swap(jnp.where(send < 0, -root, root).astype(F16), bit, self.n).astype(F32)
+        return got * jnp.abs(got) * (1.0 / self.scale**2)
 
 
 def gather_stream(block, order, n):
@@ -431,16 +431,16 @@
     order_a, order_b = order_y[::-1], order_z
     shifts = [[bit.bit_length() - 1 for bit in order] for order in (order_a, order_b)]
 
-    sent, peak_sent, weight = class_sums(me, labels, counts, activations, n, 1)
-    core = Packed(n, peak_sent, weight.T)
-    got = core(sent, 1)
-    kept, peak, _ = class_sums(me, labels, counts, activations, n, 0)
-    bound = 1.001 * (peak + core.bound)
-    stream = Packed(n, bound, core.weight)
-    sums, _ = reduce_scatter(kept + got, n, stream, Packed(n, bound, None))
-    class_weight = stream.weight.T
+    root = Root(n, BOUND * 4 * rows * n)
+    sent, weight = class_sums(me, labels, counts, activations, n, 1)
+    weight = weight.T
+    got = root(sent, 1)
+    weight = weight + swap(weight, 1, n)
+    kept, _ = class_sums(me, labels, counts, activations, n, 0)
+    top, low, weight = reduce_scatter(kept + got, n, root, root, weight)
+    class_weight = weight.T
     total_weight = jnp.sum(class_weight, keepdims=True)
-    base = (sums / class_weight) * jnp.sqrt(class_weight)
+    base = (jnp.concatenate([top, low], axis=0) / class_weight) * jnp.sqrt(class_weight)
 
     def gather(panel):
         v = panel.astype(BF16)
@@ -452,14 +452,16 @@
         along = along + swap(along, 1, n)
         blocks = panel_keep(me, probed, counts, activations, n) + got
         top, low = bound[:HALF], bound[HALF:]
-        return reduce_scatter(
+        a, b, along = reduce_scatter(
             blocks,
             n,
             lambda x, bit: grow(swap(shrink(x, top), bit, n), top),
             lambda x, bit: grow(swap(shrink(x, low), bit, n), low),
             along,
         )
-
+        return jnp.concatenate([a, b], axis=0), along
+
+    square, strip = (K, K), (K, d // n)
     base_near, base_far = gather(base)
     starts = probe(me, base_near, activations, n, shifts)
     first, along, bound, sent, current = probe_and_send(
@@ -467,20 +469,21 @@
     )
     panel, along = scatter(first, along, bound, sent)
     image = panel / total_weight + (RIDGE * base - precise(current / total_weight, base))
-    alpha_t, inverse = small(alpha_kernel, "alpha", 2, along, current, total_weight)
+    alpha_t, inverse = small(alpha_kernel, "alpha", (square,) * 2, along, current, total_weight)
 
     near, far = gather(image)
     starts = probe(me, near + base_near, activations, n, shifts)
     probed, along, bound, sent, _, _, renewed, mixed, beta_t = probe_and_send(
         me, far + base_far, activations, counts, total_weight, starts, (first, current, alpha_t, inverse), n, shifts
     )
+    fixed, cross_t = small(before_kernel, "before", (square,) * 2, current, renewed, mixed, beta_t, total_weight)
     panel, along = scatter(probed, along, bound, sent)
-    on_base, on_image, on_panel, out_base, out_image = small(
-        last_kernel, "last", 5, along, current, renewed, mixed, beta_t, alpha_t, total_weight
-    )
-    solution = precise(out_base, base) + precise(out_image, image)
-    residual = (precise(on_base, base) + precise(on_image, image)) - precise(on_panel, panel)
-    return (solution.T, residual.T)
+    solved, rest, on_panel = small(
+        last_kernel, "last", (strip, strip, square),
+        along, fixed, cross_t, renewed, beta_t, alpha_t, total_weight, base, image,
+    )
+    residual = rest - precise(on_panel, panel)
+    return (solved.T, residual.T)
 
 
 def solution(mesh):

time: 246 us -> 218 us (0.89)
  starting transfers between devices: 59.6 us -> 51 us
  between operations: 9.24 us -> 1.54 us
  waiting for transfers between devices: 83.8 us -> 78.7 us
  matrix products: 7.75 us -> 2.85 us
  local copies, waits for them, and re-layouts: 6.59 us -> 3.73 us
    ppermute x45 -> x49, starting transfers between devices: 59.6 us -> 51 us  [swap(): return lax.ppermute(value, 'dp', [(i, i ^ bit) for i in range(n)])]
    ppermute x45 -> x49, waiting for transfers between devices: 83.8 us -> 78.7 us  [swap(): return lax.ppermute(value, 'dp', [(i, i ^ bit) for i in range(n)])]
    dot_general x6 -> x2, matrix products: 7.75 us -> 2.85 us  [precise(): jnp.dot(left, right, precision=lax.Precision.HIGHEST, preferred_element_t...]
    slice x7 -> x2, local copies, waits for them, and re-layouts: 3.6 us -> 0.14 us  [split_blocks(): keep = lax.index_in_dim(value, 0, axis, keepdims=False)]
    pallas_call x2 -> x3, Pallas kernels: 20.6 us -> 23.5 us  [small(): pl.pallas_call(kernel, out_shape=tuple((jax.ShapeDtypeStruct(shape, F32)...]
  transfers between devices with their start and end apart: 45 -> 49, of which waited for: 32 -> 25; matrix products, arithmetic and copies ran while one was open for 4% -> 2% of each run, Pallas kernels for 17% -> 20%
where the time goes in v4:
time: 218 us
  waiting for transfers between devices  78.7 us (36%)
  Pallas kernels  67.3 us (31%)
  starting transfers between devices  51 us (23%)
  other arithmetic  12.3 us (6%)
  local copies, waits for them, and re-layouts  3.73 us (2%)
  matrix products  2.85 us (1%)
    ppermute x49, waiting for transfers between devices, swap(): return lax.ppermute(value, 'dp', [(i, i ^ bit) for i in range(n)])  78.7 us
    ppermute x49, starting transfers between devices, swap(): return lax.ppermute(value, 'dp', [(i, i ^ bit) for i in range(n)])  51 us
    pallas_call x3, Pallas kernels, small(): pl.pallas_call(kernel, out_shape=tuple((jax.ShapeDtypeStruct(shape, F32)...  23.5 us
    pallas_call x2, Pallas kernels, probe_and_send(): call(functools.partial(send_kernel, s, count, d), 'probe_and_send', n, 2...  20.5 us
    pallas_call x2, Pallas kernels, probe(): call(functools.partial(probe_kernel, count), 'probe', n, n // 2, v_specs(...  9.13 us
    pallas_call x2, Pallas kernels, panel_keep(): call(keep_kernel, 'panel_keep', n, n // 2, [whole(K, rows), whole(1, rows...  7.15 us
    pallas_call x2, Pallas kernels, class_sums(): call(functools.partial(sums_kernel, half), 'class_sums', n, n // 2, [whol...  7.06 us
  transfers between devices with their start and end apart: 49, of which 25 were waited for; matrix products, arithmetic and copies ran while one was open for 2% of the time, Pallas kernels for 20%

profile of v4, /device:TPU:0, one launch (start us, length us, event | category | flops | bytes accessed | tf_op | source)
XLA Modules:
  0.0 217.5 jit_solution(10930492288644451862)
XLA Ops:
  2.0 3.3 %class_sums.3 = (f32[8,64,1024]{2,1,0:T(8,128)S(1)}, f32[64,1]{1,0:T(8,128)S(1)}) custom-call(s32[1]{0:T(128)} %bitcast.me, s32[1,384]{1,0:T(1,128)S(1)} %reshape.61.labels, s32[1,384]{1,0:T(1,128)S(1)} %reshape.62.counts.refs_3_.refs_5_, bf16[384,16384]{1,0:T(8,128)(2,1)} %acts.7), custom_call_target="tpu_custom_call" | custom-call | flops 402653184 | bytes 8388608 | tf_op jit(solution)/shard_map/class_sums/pallas_call | solution.py:135
  7.0 3.7 %class_sums.2 = (f32[8,64,1024]{2,1,0:T(8,128)S(1)}, f32[64,1]{1,0:T(8,128)}) custom-call(s32[1]{0:T(128)} %bitcast.me, s32[1,384]{1,0:T(1,128)S(1)} %reshape.61.labels, s32[1,384]{1,0:T(1,128)S(1)} %reshape.62.counts.refs_3_.refs_5_, bf16[384,16384]{1,0:T(8,128)(2,1)} %acts.7), custom_call_target="tpu_custom_call" | custom-call | flops 402653184 | bytes 8388608 | tf_op jit(solution)/shard_map/class_sums/pallas_call | solution.py:135
  12.0 3.1 %collective-permute-start.3 = (f16[2,2,32,1024]{3,2,0,1:T(8,128)(2,1)S(1)}, f16[2,2,32,1024]{3,2,0,1:T(8,128)(2,1)S(1)}, u32[]{:S(2)}, u32[]{:S(2)}) collective-permute-start(f16[2,2,32,1024]{3,2,0,1:T(8,128)(2,1)S(1)} %fusion.7), channel_id=1, source_target_pairs={{0,4},{1,5},{2,6},{3,7},{4,0},{5,1},{6,2},{7,3},{8,12},{9,13},{10,... | collective-permute-start | bytes 786440 | tf_op jit(solution)/shard_map/ppermute | solution.py:59
  16.6 2.0 collective-permute-done.4
  18.9 2.0 collective-permute-start.2
  22.3 3.7 %collective-permute-done.2 = f16[2,2,32,1024]{3,2,0,1:T(8,128)(2,1)S(1)} collective-permute-done((f16[2,2,32,1024]{3,2,0,1:T(8,128)(2,1)S(1)}, f16[2,2,32,1024]{3,2,0,1:T(8,128)(2,1)S(1)}, u32[]{:S(2)}, u32[]{:S(2)}) %collective-permute-start.2) | collective-permute-done | bytes 262176 | tf_op jit(solution)/shard_map/ppermute | solution.py:59
  26.2 2.7 %collective-permute-start.8 = (f32[1,64]{1,0:T(1,128)S(1)}, f32[1,64]{1,0:T(1,128)S(1)}, u32[]{:S(2)}, u32[]{:S(2)}) collective-permute-start(f32[1,64]{1,0:T(1,128)S(1)} %add.107), channel_id=1, source_target_pairs={{0,8},{1,9},{2,10},{3,11},{4,12},{5,13},{6,14},{7,15},{8,0},{9,1},... | collective-permute-start | bytes 776 | tf_op jit(solution)/shard_map/ppermute | solution.py:59
  29.5 1.8 collective-permute-start.6
  31.3 5.0 %collective-permute-done.7 = f16[2,32,1024]{2,1,0:T(8,128)(2,1)S(1)} collective-permute-done((f16[2,32,1024]{2,1,0:T(8,128)(2,1)S(1)}, f16[2,32,1024]{2,1,0:T(8,128)(2,1)S(1)}, u32[]{:S(2)}, u32[]{:S(2)}) %collective-permute-start.7) | collective-permute-done | bytes 131104 | tf_op jit(solution)/shard_map/ppermute | solution.py:59
  38.2 2.0 collective-permute-start.9
  41.0 4.4 %collective-permute-done.9 = f16[32,1024]{1,0:T(8,128)(2,1)S(1)} collective-permute-done((f16[32,1024]{1,0:T(8,128)(2,1)S(1)}, f16[32,1024]{1,0:T(8,128)(2,1)S(1)}, u32[]{:S(2)}, u32[]{:S(2)}) %collective-permute-start.9) | collective-permute-done | bytes 65568 | tf_op jit(solution)/shard_map/ppermute | solution.py:59
  47.0 2.0 collective-permute-start.15
  49.1 4.3 %collective-permute-done.11 = bf16[1,32,1024]{2,1,0:T(8,128)(2,1)S(1)} collective-permute-done((bf16[1,32,1024]{2,1,0:T(8,128)(2,1)S(1)}, bf16[1,32,1024]{2,1,0:T(8,128)(2,1)S(1)}, u32[]{:S(2)}, u32[]{:S(2)}) %collective-permute-start.11) | collective-permute-done | bytes 65568 | tf_op jit(solution)/shard_map/ppermute | solution.py:59
  53.5 3.0 %collective-permute-start.16 = (bf16[2,32,1024]{2,1,0:T(8,128)(2,1)S(1)}, bf16[2,32,1024]{2,1,0:T(8,128)(2,1)S(1)}, u32[]{:S(2)}, u32[]{:S(2)}) collective-permute-start(bf16[2,32,1024]{2,1,0:T(8,128)(2,1)S(1)} %pad_maximum_fusion.9), channel_id=1, source_target_pairs={{0,8},{1,9},{2,10},{3,11},{4,12},{5,13},{6,14},{7,15},{8,0},{9,1},... | collective-permute-start | bytes 393224 | tf_op jit(solution)/shard_map/ppermute | solution.py:59
  56.5 3.4 %collective-permute-done.12 = bf16[2,32,1024]{2,1,0:T(8,128)(2,1)S(1)} collective-permute-done((bf16[2,32,1024]{2,1,0:T(8,128)(2,1)S(1)}, bf16[2,32,1024]{2,1,0:T(8,128)(2,1)S(1)}, u32[]{:S(2)}, u32[]{:S(2)}) %collective-permute-start.12) | collective-permute-done | bytes 131104 | tf_op jit(solution)/shard_map/ppermute | solution.py:59
  62.0 4.2 %collective-permute-done.13 = bf16[4,32,1024]{2,1,0:T(8,128)(2,1)S(1)} collective-permute-done((bf16[4,32,1024]{2,1,0:T(8,128)(2,1)S(1)}, bf16[4,32,1024]{2,1,0:T(8,128)(2,1)S(1)}, u32[]{:S(2)}, u32[]{:S(2)}) %collective-permute-start.13) | collective-permute-done | bytes 262176 | tf_op jit(solution)/shard_map/ppermute | solution.py:59
  66.4 2.7 %collective-permute-done.17 = bf16[4,32,1024]{2,1,0:T(8,128)(2,1)S(1)} collective-permute-done((bf16[4,32,1024]{2,1,0:T(8,128)(2,1)S(1)}, bf16[4,32,1024]{2,1,0:T(8,128)(2,1)S(1)}, u32[]{:S(2)}, u32[]{:S(2)}) %collective-permute-start.17) | collective-permute-done | bytes 262176 | tf_op jit(solution)/shard_map/ppermute | solution.py:59
  69.9 4.4 %probe.2 = (f32[384,64]{1,0:T(8,128)S(1)}, f32[64,64]{1,0:T(8,128)S(1)}) custom-call(s32[1]{0:T(128)} %bitcast.me, bf16[8,32,1024]{2,1,0:T(8,128)(2,1)S(1)} %pad_maximum_fusion.refs_0_.refs_2_, bf16[8,32,1024]{2,1,0:T(8,128)(2,1)S(1)} %pad_maximum_fusion.1.refs_1_.refs_3_, bf16[384,16384]{1,0:T(8,128)(2,1)} %acts.7), custom_call_target="tpu_custom_call" | custom-call | flops 402653184 | bytes 8388608 | tf_op jit(solution)/shard_map/probe/pallas_call | solution.py:188
  74.3 7.9 %probe_and_send.2 = (f32[64,384]{1,0:T(8,128)S(1)}, f32[64,64]{1,0:T(8,128)S(1)}, f32[64,1]{1,0:T(8,128)S(1)}, f32[8,64,1024]{2,1,0:T(8,128)S(1)}, f32[64,64]{1,0:T(8,128)S(1)}) custom-call(s32[1]{0:T(128)} %bitcast.me, bf16[8,32,1024]{2,1,0:T(8,128)(2,1)S(1)} %collective-permute-done.14.refs_0_.refs_2_, ...), custom_call_target="tpu_custom_call" | custom-call | flops 402653184 | bytes 8388608 | tf_op jit(solution)/shard_map/probe_and_send/pallas_call | solution.py:279
  83.5 3.6 %panel_keep.2 = f32[8,64,1024]{2,1,0:T(8,128)S(1)} custom-call(s32[1]{0:T(128)} %bitcast.me, f32[64,384]{1,0:T(8,128)S(1)} %get-tuple-element.70.probed.refs_10_, s32[1,384]{1,0:T(1,128)S(1)} %reshape.62.counts.refs_3_.refs_5_, bf16[384,16384]{1,0:T(8,128)(2,1)} %acts.7), custom_call_target="tpu_custom_call" | custom-call | flops 402653184 | bytes 8388608 | tf_op jit(solution)/shard_map/panel_keep/pallas_call | solution.py:321
  88.9 3.2 %collective-permute-done.23 = f32[64,64]{1,0:T(8,128)S(1)} collective-permute-done((f32[64,64]{1,0:T(8,128)S(1)}, f32[64,64]{1,0:T(8,128)S(1)}, u32[]{:S(2)}, u32[]{:S(2)}) %collective-permute-start.23) | collective-permute-done | bytes 16416 | tf_op jit(solution)/shard_map/ppermute | solution.py:59
  92.1 1.9 collective-permute-start.24
  95.0 2.5 %collective-permute-done.24 = f32[64,64]{1,0:T(8,128)S(1)} collective-permute-done((f32[64,64]{1,0:T(8,128)S(1)}, f32[64,64]{1,0:T(8,128)S(1)}, u32[]{:S(2)}, u32[]{:S(2)}) %collective-permute-start.24) | collective-permute-done | bytes 16416 | tf_op jit(solution)/shard_map/ppermute | solution.py:59
  97.7 3.8 %collective-permute-done.21 = f16[2,2,32,1024]{3,2,0,1:T(8,128)(2,1)S(1)} collective-permute-done((f16[2,2,32,1024]{3,2,0,1:T(8,128)(2,1)S(1)}, f16[2,2,32,1024]{3,2,0,1:T(8,128)(2,1)S(1)}, u32[]{:S(2)}, u32[]{:S(2)}) %collective-permute-start.21) | collective-permute-done | bytes 262176 | tf_op jit(solution)/shard_map/ppermute | solution.py:59
  103.1 1.8 collective-permute-start.26
  105.3 2.9 %collective-permute-done.27 = f32[64,64]{1,0:T(8,128)S(1)} collective-permute-done((f32[64,64]{1,0:T(8,128)S(1)}, f32[64,64]{1,0:T(8,128)S(1)}, u32[]{:S(2)}, u32[]{:S(2)}) %collective-permute-start.27) | collective-permute-done | bytes 16416 | tf_op jit(solution)/shard_map/ppermute | solution.py:59
  108.8 2.2 %collective-permute-done.26 = f16[2,32,1024]{2,1,0:T(8,128)(2,1)S(1)} collective-permute-done((f16[2,32,1024]{2,1,0:T(8,128)(2,1)S(1)}, f16[2,32,1024]{2,1,0:T(8,128)(2,1)S(1)}, u32[]{:S(2)}, u32[]{:S(2)}) %collective-permute-start.26) | collective-permute-done | bytes 131104 | tf_op jit(solution)/shard_map/ppermute | solution.py:59
  113.1 2.5 %collective-permute-done.29 = f16[32,1024]{1,0:T(8,128)(2,1)S(1)} collective-permute-done((f16[32,1024]{1,0:T(8,128)(2,1)S(1)}, f16[32,1024]{1,0:T(8,128)(2,1)S(1)}, u32[]{:S(2)}, u32[]{:S(2)}) %collective-permute-start.29) | collective-permute-done | bytes 65568 | tf_op jit(solution)/shard_map/ppermute | solution.py:59
  115.7 2.0 collective-permute-done.28
  117.8 1.7 fusion.51
  120.3 2.0 collective-permute-start.34
  122.3 5.0 %collective-permute-done.30 = bf16[1,32,1024]{2,1,0:T(8,128)(2,1)S(1)} collective-permute-done((bf16[1,32,1024]{2,1,0:T(8,128)(2,1)S(1)}, bf16[1,32,1024]{2,1,0:T(8,128)(2,1)S(1)}, u32[]{:S(2)}, u32[]{:S(2)}) %collective-permute-start.30) | collective-permute-done | bytes 65568 | tf_op jit(solution)/shard_map/ppermute | solution.py:59
  127.4 2.7 %collective-permute-start.35 = (bf16[2,32,1024]{2,1,0:T(8,128)(2,1)S(1)}, bf16[2,32,1024]{2,1,0:T(8,128)(2,1)S(1)}, u32[]{:S(2)}, u32[]{:S(2)}) collective-permute-start(bf16[2,32,1024]{2,1,0:T(8,128)(2,1)S(1)} %pad_maximum_fusion.11), channel_id=1, source_target_pairs={{0,8},{1,9},{2,10},{3,11},{4,12},{5,13},{6,14},{7,15},{8,0},{9,1},... | collective-permute-start | bytes 393224 | tf_op jit(solution)/shard_map/ppermute | solution.py:59
  130.1 3.7 %collective-permute-done.31 = bf16[2,32,1024]{2,1,0:T(8,128)(2,1)S(1)} collective-permute-done((bf16[2,32,1024]{2,1,0:T(8,128)(2,1)S(1)}, bf16[2,32,1024]{2,1,0:T(8,128)(2,1)S(1)}, u32[]{:S(2)}, u32[]{:S(2)}) %collective-permute-start.31) | collective-permute-done | bytes 131104 | tf_op jit(solution)/shard_map/ppermute | solution.py:59
  136.0 4.2 %collective-permute-done.32 = bf16[4,32,1024]{2,1,0:T(8,128)(2,1)S(1)} collective-permute-done((bf16[4,32,1024]{2,1,0:T(8,128)(2,1)S(1)}, bf16[4,32,1024]{2,1,0:T(8,128)(2,1)S(1)}, u32[]{:S(2)}, u32[]{:S(2)}) %collective-permute-start.32) | collective-permute-done | bytes 262176 | tf_op jit(solution)/shard_map/ppermute | solution.py:59
  140.3 2.7 %collective-permute-done.36 = bf16[4,32,1024]{2,1,0:T(8,128)(2,1)S(1)} collective-permute-done((bf16[4,32,1024]{2,1,0:T(8,128)(2,1)S(1)}, bf16[4,32,1024]{2,1,0:T(8,128)(2,1)S(1)}, u32[]{:S(2)}, u32[]{:S(2)}) %collective-permute-start.36) | collective-permute-done | bytes 262176 | tf_op jit(solution)/shard_map/ppermute | solution.py:59
  143.2 10.1 %alpha.1 = (f32[64,64]{1,0:T(8,128)}, f32[64,64]{1,0:T(8,128)}) custom-call(f32[64,64]{1,0:T(8,128)} %add.121.along, f32[64,64]{1,0:T(8,128)} %copy-done.1, f32[1,1]{1,0:T(1,128)} %bitcast.18.refs_4_.total_weight.refs_6_), custom_call_target="tpu_custom_call" | custom-call | flops 67108864 | bytes 1048576 | tf_op jit(solution)/shard_map/alpha/pallas_call | solution.py:368
  153.3 4.7 %probe.3 = (f32[384,64]{1,0:T(8,128)S(1)}, f32[64,64]{1,0:T(8,128)S(1)}, f32[64,64]{1,0:T(8,128)S(1)}) custom-call(s32[1]{0:T(128)} %bitcast.me, bf16[8,32,1024]{2,1,0:T(8,128)(2,1)S(1)} %pad_maximum_fusion.2.refs_0_, bf16[8,32,1024]{2,1,0:T(8,128)(2,1)S(1)} %pad_maximum_fusion.3.refs_1_, bf16[8,32,1024]{2,1,0:T(8,128)(2,1)S(1)} %pad_maximum_fusion.refs_0_.refs_2_, ...), custom_call_target="tpu_custom_call" | custom-call | flops 402653184 | bytes 8388608 | tf_op jit(solution)/shard_map/probe/pallas_call | solution.py:188
  158.1 12.6 %probe_and_send.3 = (f32[64,384]{1,0:T(8,128)S(1)}, f32[64,64]{1,0:T(8,128)S(1)}, f32[64,1]{1,0:T(8,128)S(1)}, f32[8,64,1024]{2,1,0:T(8,128)S(1)}, f32[64,64]{1,...) custom-call(s32[1]{0:T(128)} %bitcast.me, ...), custom_call_target="tpu_custom_call" | custom-call | flops 402653184 | bytes 8388608 | tf_op jit(solution)/shard_map/probe_and_send/pallas_call | solution.py:279
  173.2 3.6 %panel_keep.3 = f32[8,64,1024]{2,1,0:T(8,128)S(1)} custom-call(s32[1]{0:T(128)} %bitcast.me, f32[64,384]{1,0:T(8,128)S(1)} %get-tuple-element.89.probed, s32[1,384]{1,0:T(1,128)S(1)} %reshape.62.counts.refs_3_.refs_5_, bf16[384,16384]{1,0:T(8,128)(2,1)} %acts.7), custom_call_target="tpu_custom_call" | custom-call | flops 402653184 | bytes 8388608 | tf_op jit(solution)/shard_map/panel_keep/pallas_call | solution.py:321
  179.3 2.6 %before.1 = (f32[64,64]{1,0:T(8,128)}, f32[64,64]{1,0:T(8,128)}) custom-call(f32[64,64]{1,0:T(8,128)} %copy-done.1, f32[64,64]{1,0:T(8,128)} %copy-done.4, f32[64,64]{1,0:T(8,128)} %copy-done.6, f32[64,64]{1,0:T(8,128)} %copy-done.5, f32[1,1]{1,0:T(1,128)} %bitcast.18.refs_4_.total_weight.refs_6_), custom_call_target="tpu_custom_call" | custom-call | flops 67108864 | bytes 1048576 | tf_op jit(solution)/shard_map/before/pallas_call | solution.py:368
  182.0 2.0 collective-permute-start.43
  185.4 1.8 collective-permute-done.43
  187.4 4.5 %collective-permute-done.40 = f16[2,2,32,1024]{3,2,0,1:T(8,128)(2,1)S(1)} collective-permute-done((f16[2,2,32,1024]{3,2,0,1:T(8,128)(2,1)S(1)}, f16[2,2,32,1024]{3,2,0,1:T(8,128)(2,1)S(1)}, u32[]{:S(2)}, u32[]{:S(2)}) %collective-permute-start.40) | collective-permute-done | bytes 262176 | tf_op jit(solution)/shard_map/ppermute | solution.py:59
  193.6 1.7 collective-permute-start.45
  195.8 3.2 %collective-permute-done.46 = f32[64,64]{1,0:T(8,128)S(1)} collective-permute-done((f32[64,64]{1,0:T(8,128)S(1)}, f32[64,64]{1,0:T(8,128)S(1)}, u32[]{:S(2)}, u32[]{:S(2)}) %collective-permute-start.46) | collective-permute-done | bytes 16416 | tf_op jit(solution)/shard_map/ppermute | solution.py:59
  199.6 2.6 %collective-permute-done.45 = f16[2,32,1024]{2,1,0:T(8,128)(2,1)S(1)} collective-permute-done((f16[2,32,1024]{2,1,0:T(8,128)(2,1)S(1)}, f16[2,32,1024]{2,1,0:T(8,128)(2,1)S(1)}, u32[]{:S(2)}, u32[]{:S(2)}) %collective-permute-start.45) | collective-permute-done | bytes 131104 | tf_op jit(solution)/shard_map/ppermute | solution.py:59
  203.8 10.7 %last.1 = (f32[64,1024]{1,0:T(8,128)}, f32[64,1024]{1,0:T(8,128)}, f32[64,64]{1,0:T(8,128)}) custom-call(f32[64,64]{1,0:T(8,128)} %add.133.along, f32[64,64]{1,0:T(8,128)} %get-tuple-element.103.fixed, f32[64,64]{1,0:T(8,128)} %get-tuple-element.104.cross_t, f32[64,64]{1,0:T(8,128)} %copy-done.4, f32[64,64]{1,0:T(8,128)} %copy-done.5, ...), custom_call_target="tpu_custom_call" | custom-call | flops 67108864 | bytes 1048576 | tf_op jit(solution)/shard_map/last/pallas_call | solution.py:368
  (183 shorter events, 41.7 us)
Async XLA Ops:
  6.3 4.5 %collective-permute-start = (f16[8,64,1024]{2,1,0:T(8,128)(2,1)S(1)}, f16[8,64,1024]{2,1,0:T(8,128)(2,1)S(1)}, u32[]{:S(2)}, u32[]{:S(2)}) collective-permute-start(f16[8,64,1024]{2,1,0:T(8,128)(2,1)S(1)} %fusion), channel_id=1, source_target_pairs={{0,1},{1,0},{2,3},{3,2},{4,5},{5,4},{6,7},{7,6},{8,9},{9,8},{10,11... | collective-permute-start | bytes 3145736 | tf_op jit(solution)/shard_map/ppermute | solution.py:59
  6.9 3.9 %collective-permute-start.1 = (f32[1,64]{1,0:T(1,128)S(1)}, f32[1,64]{1,0:T(1,128)S(1)}, u32[]{:S(2)}, u32[]{:S(2)}) collective-permute-start(f32[1,64]{1,0:T(1,128)S(1)} %bitcast.156), channel_id=1, source_target_pairs={{0,1},{1,0},{2,3},{3,2},{4,5},{5,4},{6,7},{7,6},{8,9},{9,8},{10,11... | collective-permute-start | bytes 776 | tf_op jit(solution)/shard_map/ppermute | solution.py:59
  12.0 10.2 %collective-permute-start.3 = (f16[2,2,32,1024]{3,2,0,1:T(8,128)(2,1)S(1)}, f16[2,2,32,1024]{3,2,0,1:T(8,128)(2,1)S(1)}, u32[]{:S(2)}, u32[]{:S(2)}) collective-permute-start(f16[2,2,32,1024]{3,2,0,1:T(8,128)(2,1)S(1)} %fusion.7), channel_id=1, source_target_pairs={{0,4},{1,5},{2,6},{3,7},{4,0},{5,1},{6,2},{7,3},{8,12},{9,13},{10,... | collective-permute-start | bytes 786440 | tf_op jit(solution)/shard_map/ppermute | solution.py:59
  15.1 3.5 %collective-permute-start.4 = (f32[1,64]{1,0:T(1,128)S(1)}, f32[1,64]{1,0:T(1,128)S(1)}, u32[]{:S(2)}, u32[]{:S(2)}) collective-permute-start(f32[1,64]{1,0:T(1,128)S(1)} %bitcast_add_fusion), channel_id=1, source_target_pairs={{0,2},{1,3},{2,0},{3,1},{4,6},{5,7},{6,4},{7,5},{8,10},{9,11},{10,... | collective-permute-start | bytes 776 | tf_op jit(solution)/shard_map/ppermute | solution.py:59
  18.9 7.1 %collective-permute-start.2 = (f16[2,2,32,1024]{3,2,0,1:T(8,128)(2,1)S(1)}, f16[2,2,32,1024]{3,2,0,1:T(8,128)(2,1)S(1)}, u32[]{:S(2)}, u32[]{:S(2)}) collective-permute-start(f16[2,2,32,1024]{3,2,0,1:T(8,128)(2,1)S(1)} %fusion.4), channel_id=1, source_target_pairs={{0,2},{1,3},{2,0},{3,1},{4,6},{5,7},{6,4},{7,5},{8,10},{9,11},{10,... | collective-permute-start | bytes 786440 | tf_op jit(solution)/shard_map/ppermute | solution.py:59
  26.2 5.1 %collective-permute-start.8 = (f32[1,64]{1,0:T(1,128)S(1)}, f32[1,64]{1,0:T(1,128)S(1)}, u32[]{:S(2)}, u32[]{:S(2)}) collective-permute-start(f32[1,64]{1,0:T(1,128)S(1)} %add.107), channel_id=1, source_target_pairs={{0,8},{1,9},{2,10},{3,11},{4,12},{5,13},{6,14},{7,15},{8,0},{9,1},... | collective-permute-start | bytes 776 | tf_op jit(solution)/shard_map/ppermute | solution.py:59
  28.9 7.4 %collective-permute-start.7 = (f16[2,32,1024]{2,1,0:T(8,128)(2,1)S(1)}, f16[2,32,1024]{2,1,0:T(8,128)(2,1)S(1)}, u32[]{:S(2)}, u32[]{:S(2)}) collective-permute-start(f16[2,32,1024]{2,1,0:T(8,128)(2,1)S(1)} %fusion.17), channel_id=1, source_target_pairs={{0,8},{1,9},{2,10},{3,11},{4,12},{5,13},{6,14},{7,15},{8,0},{9,1},... | collective-permute-start | bytes 393224 | tf_op jit(solution)/shard_map/ppermute | solution.py:59
  29.5 6.9 %collective-permute-start.6 = (f16[2,32,1024]{2,1,0:T(8,128)(2,1)S(1)}, f16[2,32,1024]{2,1,0:T(8,128)(2,1)S(1)}, u32[]{:S(2)}, u32[]{:S(2)}) collective-permute-start(f16[2,32,1024]{2,1,0:T(8,128)(2,1)S(1)} %fusion.14), channel_id=1, source_target_pairs={{0,4},{1,5},{2,6},{3,7},{4,0},{5,1},{6,2},{7,3},{8,12},{9,13},{10,... | collective-permute-start | bytes 393224 | tf_op jit(solution)/shard_map/ppermute | solution.py:59
  36.6 4.3 %collective-permute-start.10 = (f16[32,1024]{1,0:T(8,128)(2,1)S(1)}, f16[32,1024]{1,0:T(8,128)(2,1)S(1)}, u32[]{:S(2)}, u32[]{:S(2)}) collective-permute-start(f16[32,1024]{1,0:T(8,128)(2,1)S(1)} %fusion.32), channel_id=1, source_target_pairs={{0,2},{1,3},{2,0},{3,1},{4,6},{5,7},{6,4},{7,5},{8,10},{9,11},{10,... | collective-permute-start | bytes 196616 | tf_op jit(solution)/shard_map/ppermute | solution.py:59
  38.2 7.2 %collective-permute-start.9 = (f16[32,1024]{1,0:T(8,128)(2,1)S(1)}, f16[32,1024]{1,0:T(8,128)(2,1)S(1)}, u32[]{:S(2)}, u32[]{:S(2)}) collective-permute-start(f16[32,1024]{1,0:T(8,128)(2,1)S(1)} %fusion.29), channel_id=1, source_target_pairs={{0,8},{1,9},{2,10},{3,11},{4,12},{5,13},{6,14},{7,15},{8,0},{9,1},... | collective-permute-start | bytes 196616 | tf_op jit(solution)/shard_map/ppermute | solution.py:59
  46.2 7.1 %collective-permute-start.11 = (bf16[1,32,1024]{2,1,0:T(8,128)(2,1)S(1)}, bf16[1,32,1024]{2,1,0:T(8,128)(2,1)S(1)}, u32[]{:S(2)}, u32[]{:S(2)}) collective-permute-start(bf16[1,32,1024]{2,1,0:T(8,128)(2,1)S(1)} %get-tuple-element.141), channel_id=1, source_target_pairs={{0,8},{1,9},{2,10},{3,11},{4,12},{5,13},{6,14},{7,15},{8,0},{9,1},... | collective-permute-start | bytes 196616 | tf_op jit(solution)/shard_map/ppermute | solution.py:59
  47.0 6.4 %collective-permute-start.15 = (bf16[1,32,1024]{2,1,0:T(8,128)(2,1)S(1)}, bf16[1,32,1024]{2,1,0:T(8,128)(2,1)S(1)}, u32[]{:S(2)}, u32[]{:S(2)}) collective-permute-start(bf16[1,32,1024]{2,1,0:T(8,128)(2,1)S(1)} %get-tuple-element.140), channel_id=1, source_target_pairs={{0,4},{1,5},{2,6},{3,7},{4,0},{5,1},{6,2},{7,3},{8,12},{9,13},{10,... | collective-permute-start | bytes 196616 | tf_op jit(solution)/shard_map/ppermute | solution.py:59
  53.4 6.4 %collective-permute-start.12 = (bf16[2,32,1024]{2,1,0:T(8,128)(2,1)S(1)}, bf16[2,32,1024]{2,1,0:T(8,128)(2,1)S(1)}, u32[]{:S(2)}, u32[]{:S(2)}) collective-permute-start(bf16[2,32,1024]{2,1,0:T(8,128)(2,1)S(1)} %pad_maximum_fusion.8), channel_id=1, source_target_pairs={{0,4},{1,5},{2,6},{3,7},{4,0},{5,1},{6,2},{7,3},{8,12},{9,13},{10,... | collective-permute-start | bytes 393224 | tf_op jit(solution)/shard_map/ppermute | solution.py:59
  53.5 7.1 %collective-permute-start.16 = (bf16[2,32,1024]{2,1,0:T(8,128)(2,1)S(1)}, bf16[2,32,1024]{2,1,0:T(8,128)(2,1)S(1)}, u32[]{:S(2)}, u32[]{:S(2)}) collective-permute-start(bf16[2,32,1024]{2,1,0:T(8,128)(2,1)S(1)} %pad_maximum_fusion.9), channel_id=1, source_target_pairs={{0,8},{1,9},{2,10},{3,11},{4,12},{5,13},{6,14},{7,15},{8,0},{9,1},... | collective-permute-start | bytes 393224 | tf_op jit(solution)/shard_map/ppermute | solution.py:59
  59.8 6.4 %collective-permute-start.13 = (bf16[4,32,1024]{2,1,0:T(8,128)(2,1)S(1)}, bf16[4,32,1024]{2,1,0:T(8,128)(2,1)S(1)}, u32[]{:S(2)}, u32[]{:S(2)}) collective-permute-start(bf16[4,32,1024]{2,1,0:T(8,128)(2,1)S(1)} %pad_maximum_fusion.4), channel_id=1, source_target_pairs={{0,2},{1,3},{2,0},{3,1},{4,6},{5,7},{6,4},{7,5},{8,10},{9,11},{10,... | collective-permute-start | bytes 786440 | tf_op jit(solution)/shard_map/ppermute | solution.py:59
  60.6 8.5 %collective-permute-start.17 = (bf16[4,32,1024]{2,1,0:T(8,128)(2,1)S(1)}, bf16[4,32,1024]{2,1,0:T(8,128)(2,1)S(1)}, u32[]{:S(2)}, u32[]{:S(2)}) collective-permute-start(bf16[4,32,1024]{2,1,0:T(8,128)(2,1)S(1)} %pad_maximum_fusion.5), channel_id=1, source_target_pairs={{0,2},{1,3},{2,0},{3,1},{4,6},{5,7},{6,4},{7,5},{8,10},{9,11},{10,... | collective-permute-start | bytes 786440 | tf_op jit(solution)/shard_map/ppermute | solution.py:59
  66.3 8.0 %collective-permute-start.14 = (bf16[8,32,1024]{2,1,0:T(8,128)(2,1)S(1)}, bf16[8,32,1024]{2,1,0:T(8,128)(2,1)S(1)}, u32[]{:S(2)}, u32[]{:S(2)}) collective-permute-start(bf16[8,32,1024]{2,1,0:T(8,128)(2,1)S(1)} %pad_maximum_fusion.refs_0_.refs_2_), channel_id=1, source_target_pairs={{0,1},{1,0},{2,3},{3,2},{4,5},{5,4},{6,7},{7,6},{8,9},{9,8},{10,11... | collective-permute-start | bytes 1572872 | tf_op jit(solution)/shard_map/ppermute | solution.py:59
  69.2 5.2 %collective-permute-start.18 = (bf16[8,32,1024]{2,1,0:T(8,128)(2,1)S(1)}, bf16[8,32,1024]{2,1,0:T(8,128)(2,1)S(1)}, u32[]{:S(2)}, u32[]{:S(2)}) collective-permute-start(bf16[8,32,1024]{2,1,0:T(8,128)(2,1)S(1)} %pad_maximum_fusion.1.refs_1_.refs_3_), channel_id=1, source_target_pairs={{0,1},{1,0},{2,3},{3,2},{4,5},{5,4},{6,7},{7,6},{8,9},{9,8},{10,11... | collective-permute-start | bytes 1572872 | tf_op jit(solution)/shard_map/ppermute | solution.py:59
  82.7 4.4 %collective-permute-start.19 = (f16[8,64,1024]{2,1,0:T(8,128)(2,1)S(1)}, f16[8,64,1024]{2,1,0:T(8,128)(2,1)S(1)}, u32[]{:S(2)}, u32[]{:S(2)}) collective-permute-start(f16[8,64,1024]{2,1,0:T(8,128)(2,1)S(1)} %multiply_convert_fusion.1), channel_id=1, source_target_pairs={{0,1},{1,0},{2,3},{3,2},{4,5},{5,4},{6,7},{7,6},{8,9},{9,8},{10,11... | collective-permute-start | bytes 3145736 | tf_op jit(solution)/shard_map/ppermute | solution.py:59
  83.2 3.8 %collective-permute-start.20 = (f32[64,64]{1,0:T(8,128)S(1)}, f32[64,64]{1,0:T(8,128)S(1)}, u32[]{:S(2)}, u32[]{:S(2)}) collective-permute-start(f32[64,64]{1,0:T(8,128)S(1)} %get-tuple-element.73), channel_id=1, source_target_pairs={{0,1},{1,0},{2,3},{3,2},{4,5},{5,4},{6,7},{7,6},{8,9},{9,8},{10,11... | collective-permute-start | bytes 49160 | tf_op jit(solution)/shard_map/ppermute | solution.py:59
  88.1 9.4 %collective-permute-start.22 = (f16[2,2,32,1024]{3,2,1,0:T(8,128)(2,1)S(1)}, f16[2,2,32,1024]{3,2,1,0:T(8,128)(2,1)S(1)}, u32[]{:S(2)}, u32[]{:S(2)}) collective-permute-start(f16[2,2,32,1024]{3,2,1,0:T(8,128)(2,1)S(1)} %multiply_convert_fusion.4), channel_id=1, source_target_pairs={{0,4},{1,5},{2,6},{3,7},{4,0},{5,1},{6,2},{7,3},{8,12},{9,13},{10,... | collective-permute-start | bytes 786440 | tf_op jit(solution)/shard_map/ppermute | solution.py:59
  88.2 4.0 %collective-permute-start.23 = (f32[64,64]{1,0:T(8,128)S(1)}, f32[64,64]{1,0:T(8,128)S(1)}, u32[]{:S(2)}, u32[]{:S(2)}) collective-permute-start(f32[64,64]{1,0:T(8,128)S(1)} %add.114), channel_id=1, source_target_pairs={{0,2},{1,3},{2,0},{3,1},{4,6},{5,7},{6,4},{7,5},{8,10},{9,11},{10,... | collective-permute-start | bytes 49160 | tf_op jit(solution)/shard_map/ppermute | solution.py:59
  92.1 5.4 %collective-permute-start.24 = (f32[64,64]{1,0:T(8,128)S(1)}, f32[64,64]{1,0:T(8,128)S(1)}, u32[]{:S(2)}, u32[]{:S(2)}) collective-permute-start(f32[64,64]{1,0:T(8,128)S(1)} %add.117), channel_id=1, source_target_pairs={{0,4},{1,5},{2,6},{3,7},{4,0},{5,1},{6,2},{7,3},{8,12},{9,13},{10,... | collective-permute-start | bytes 49160 | tf_op jit(solution)/shard_map/ppermute | solution.py:59
  94.2 7.3 %collective-permute-start.21 = (f16[2,2,32,1024]{3,2,0,1:T(8,128)(2,1)S(1)}, f16[2,2,32,1024]{3,2,0,1:T(8,128)(2,1)S(1)}, u32[]{:S(2)}, u32[]{:S(2)}) collective-permute-start(f16[2,2,32,1024]{3,2,0,1:T(8,128)(2,1)S(1)} %multiply_convert_fusion.5), channel_id=1, source_target_pairs={{0,2},{1,3},{2,0},{3,1},{4,6},{5,7},{6,4},{7,5},{8,10},{9,11},{10,... | collective-permute-start | bytes 786440 | tf_op jit(solution)/shard_map/ppermute | solution.py:59
  101.7 6.5 %collective-permute-start.27 = (f32[64,64]{1,0:T(8,128)S(1)}, f32[64,64]{1,0:T(8,128)S(1)}, u32[]{:S(2)}, u32[]{:S(2)}) collective-permute-start(f32[64,64]{1,0:T(8,128)S(1)} %add.118), channel_id=1, source_target_pairs={{0,8},{1,9},{2,10},{3,11},{4,12},{5,13},{6,14},{7,15},{8,0},{9,1},... | collective-permute-start | bytes 49160 | tf_op jit(solution)/shard_map/ppermute | solution.py:59
  103.1 7.9 %collective-permute-start.26 = (f16[2,32,1024]{2,1,0:T(8,128)(2,1)S(1)}, f16[2,32,1024]{2,1,0:T(8,128)(2,1)S(1)}, u32[]{:S(2)}, u32[]{:S(2)}) collective-permute-start(f16[2,32,1024]{2,1,0:T(8,128)(2,1)S(1)} %multiply_convert_fusion.8), channel_id=1, source_target_pairs={{0,8},{1,9},{2,10},{3,11},{4,12},{5,13},{6,14},{7,15},{8,0},{9,1},... | collective-permute-start | bytes 393224 | tf_op jit(solution)/shard_map/ppermute | solution.py:59
  104.9 6.2 %collective-permute-start.25 = (f16[2,32,1024]{2,1,0:T(8,128)(2,1)S(1)}, f16[2,32,1024]{2,1,0:T(8,128)(2,1)S(1)}, u32[]{:S(2)}, u32[]{:S(2)}) collective-permute-start(f16[2,32,1024]{2,1,0:T(8,128)(2,1)S(1)} %multiply_convert_fusion.9), channel_id=1, source_target_pairs={{0,4},{1,5},{2,6},{3,7},{4,0},{5,1},{6,2},{7,3},{8,12},{9,13},{10,... | collective-permute-start | bytes 393224 | tf_op jit(solution)/shard_map/ppermute | solution.py:59
  111.3 4.3 %collective-permute-start.29 = (f16[32,1024]{1,0:T(8,128)(2,1)S(1)}, f16[32,1024]{1,0:T(8,128)(2,1)S(1)}, u32[]{:S(2)}, u32[]{:S(2)}) collective-permute-start(f16[32,1024]{1,0:T(8,128)(2,1)S(1)} %multiply_convert_fusion.12), channel_id=1, source_target_pairs={{0,2},{1,3},{2,0},{3,1},{4,6},{5,7},{6,4},{7,5},{8,10},{9,11},{10,... | collective-permute-start | bytes 196616 | tf_op jit(solution)/shard_map/ppermute | solution.py:59
  111.9 5.8 %collective-permute-start.28 = (f16[32,1024]{1,0:T(8,128)(2,1)S(1)}, f16[32,1024]{1,0:T(8,128)(2,1)S(1)}, u32[]{:S(2)}, u32[]{:S(2)}) collective-permute-start(f16[32,1024]{1,0:T(8,128)(2,1)S(1)} %multiply_convert_fusion.13), channel_id=1, source_target_pairs={{0,8},{1,9},{2,10},{3,11},{4,12},{5,13},{6,14},{7,15},{8,0},{9,1},... | collective-permute-start | bytes 196616 | tf_op jit(solution)/shard_map/ppermute | solution.py:59
  119.6 7.7 %collective-permute-start.30 = (bf16[1,32,1024]{2,1,0:T(8,128)(2,1)S(1)}, bf16[1,32,1024]{2,1,0:T(8,128)(2,1)S(1)}, u32[]{:S(2)}, u32[]{:S(2)}) collective-permute-start(bf16[1,32,1024]{2,1,0:T(8,128)(2,1)S(1)} %get-tuple-element.139), channel_id=1, source_target_pairs={{0,8},{1,9},{2,10},{3,11},{4,12},{5,13},{6,14},{7,15},{8,0},{9,1},... | collective-permute-start | bytes 196616 | tf_op jit(solution)/shard_map/ppermute | solution.py:59
  120.3 7.0 %collective-permute-start.34 = (bf16[1,32,1024]{2,1,0:T(8,128)(2,1)S(1)}, bf16[1,32,1024]{2,1,0:T(8,128)(2,1)S(1)}, u32[]{:S(2)}, u32[]{:S(2)}) collective-permute-start(bf16[1,32,1024]{2,1,0:T(8,128)(2,1)S(1)} %get-tuple-element.138), channel_id=1, source_target_pairs={{0,4},{1,5},{2,6},{3,7},{4,0},{5,1},{6,2},{7,3},{8,12},{9,13},{10,... | collective-permute-start | bytes 196616 | tf_op jit(solution)/shard_map/ppermute | solution.py:59
  127.3 6.4 %collective-permute-start.31 = (bf16[2,32,1024]{2,1,0:T(8,128)(2,1)S(1)}, bf16[2,32,1024]{2,1,0:T(8,128)(2,1)S(1)}, u32[]{:S(2)}, u32[]{:S(2)}) collective-permute-start(bf16[2,32,1024]{2,1,0:T(8,128)(2,1)S(1)} %pad_maximum_fusion.10), channel_id=1, source_target_pairs={{0,4},{1,5},{2,6},{3,7},{4,0},{5,1},{6,2},{7,3},{8,12},{9,13},{10,... | collective-permute-start | bytes 393224 | tf_op jit(solution)/shard_map/ppermute | solution.py:59
  127.4 7.8 %collective-permute-start.35 = (bf16[2,32,1024]{2,1,0:T(8,128)(2,1)S(1)}, bf16[2,32,1024]{2,1,0:T(8,128)(2,1)S(1)}, u32[]{:S(2)}, u32[]{:S(2)}) collective-permute-start(bf16[2,32,1024]{2,1,0:T(8,128)(2,1)S(1)} %pad_maximum_fusion.11), channel_id=1, source_target_pairs={{0,8},{1,9},{2,10},{3,11},{4,12},{5,13},{6,14},{7,15},{8,0},{9,1},... | collective-permute-start | bytes 393224 | tf_op jit(solution)/shard_map/ppermute | solution.py:59
  133.8 6.4 %collective-permute-start.32 = (bf16[4,32,1024]{2,1,0:T(8,128)(2,1)S(1)}, bf16[4,32,1024]{2,1,0:T(8,128)(2,1)S(1)}, u32[]{:S(2)}, u32[]{:S(2)}) collective-permute-start(bf16[4,32,1024]{2,1,0:T(8,128)(2,1)S(1)} %pad_maximum_fusion.6), channel_id=1, source_target_pairs={{0,2},{1,3},{2,0},{3,1},{4,6},{5,7},{6,4},{7,5},{8,10},{9,11},{10,... | collective-permute-start | bytes 786440 | tf_op jit(solution)/shard_map/ppermute | solution.py:59
  135.3 7.8 %collective-permute-start.36 = (bf16[4,32,1024]{2,1,0:T(8,128)(2,1)S(1)}, bf16[4,32,1024]{2,1,0:T(8,128)(2,1)S(1)}, u32[]{:S(2)}, u32[]{:S(2)}) collective-permute-start(bf16[4,32,1024]{2,1,0:T(8,128)(2,1)S(1)} %pad_maximum_fusion.7), channel_id=1, source_target_pairs={{0,2},{1,3},{2,0},{3,1},{4,6},{5,7},{6,4},{7,5},{8,10},{9,11},{10,... | collective-permute-start | bytes 786440 | tf_op jit(solution)/shard_map/ppermute | solution.py:59
  140.3 17.7 %collective-permute-start.33 = (bf16[8,32,1024]{2,1,0:T(8,128)(2,1)S(1)}, bf16[8,32,1024]{2,1,0:T(8,128)(2,1)}, u32[]{:S(2)}, u32[]{:S(2)}) collective-permute-start(bf16[8,32,1024]{2,1,0:T(8,128)(2,1)S(1)} %pad_maximum_fusion.2.refs_0_), channel_id=1, source_target_pairs={{0,1},{1,0},{2,3},{3,2},{4,5},{5,4},{6,7},{7,6},{8,9},{9,8},{10,11... | collective-permute-start | bytes 1572872 | tf_op jit(solution)/shard_map/ppermute | solution.py:59
  143.1 14.9 %collective-permute-start.37 = (bf16[8,32,1024]{2,1,0:T(8,128)(2,1)S(1)}, bf16[8,32,1024]{2,1,0:T(8,128)(2,1)}, u32[]{:S(2)}, u32[]{:S(2)}) collective-permute-start(bf16[8,32,1024]{2,1,0:T(8,128)(2,1)S(1)} %pad_maximum_fusion.3.refs_1_), channel_id=1, source_target_pairs={{0,1},{1,0},{2,3},{3,2},{4,5},{5,4},{6,7},{7,6},{8,9},{9,8},{10,11... | collective-permute-start | bytes 1572872 | tf_op jit(solution)/shard_map/ppermute | solution.py:59
  172.4 4.4 %collective-permute-start.38 = (f16[8,64,1024]{2,1,0:T(8,128)(2,1)S(1)}, f16[8,64,1024]{2,1,0:T(8,128)(2,1)S(1)}, u32[]{:S(2)}, u32[]{:S(2)}) collective-permute-start(f16[8,64,1024]{2,1,0:T(8,128)(2,1)S(1)} %multiply_convert_fusion), channel_id=1, source_target_pairs={{0,1},{1,0},{2,3},{3,2},{4,5},{5,4},{6,7},{7,6},{8,9},{9,8},{10,11... | collective-permute-start | bytes 3145736 | tf_op jit(solution)/shard_map/ppermute | solution.py:59
  172.9 3.8 %collective-permute-start.39 = (f32[64,64]{1,0:T(8,128)S(1)}, f32[64,64]{1,0:T(8,128)S(1)}, u32[]{:S(2)}, u32[]{:S(2)}) collective-permute-start(f32[64,64]{1,0:T(8,128)S(1)} %get-tuple-element.92), channel_id=1, source_target_pairs={{0,1},{1,0},{2,3},{3,2},{4,5},{5,4},{6,7},{7,6},{8,9},{9,8},{10,11... | collective-permute-start | bytes 49160 | tf_op jit(solution)/shard_map/ppermute | solution.py:59
  177.8 9.4 %collective-permute-start.41 = (f16[2,2,32,1024]{3,2,1,0:T(8,128)(2,1)S(1)}, f16[2,2,32,1024]{3,2,1,0:T(8,128)(2,1)S(1)}, u32[]{:S(2)}, u32[]{:S(2)}) collective-permute-start(f16[2,2,32,1024]{3,2,1,0:T(8,128)(2,1)S(1)} %multiply_convert_fusion.2), channel_id=1, source_target_pairs={{0,4},{1,5},{2,6},{3,7},{4,0},{5,1},{6,2},{7,3},{8,12},{9,13},{10,... | collective-permute-start | bytes 786440 | tf_op jit(solution)/shard_map/ppermute | solution.py:59
  177.9 4.1 %collective-permute-start.42 = (f32[64,64]{1,0:T(8,128)S(1)}, f32[64,64]{1,0:T(8,128)S(1)}, u32[]{:S(2)}, u32[]{:S(2)}) collective-permute-start(f32[64,64]{1,0:T(8,128)S(1)} %add.126), channel_id=1, source_target_pairs={{0,2},{1,3},{2,0},{3,1},{4,6},{5,7},{6,4},{7,5},{8,10},{9,11},{10,... | collective-permute-start | bytes 49160 | tf_op jit(solution)/shard_map/ppermute | solution.py:59
  182.0 5.3 %collective-permute-start.43 = (f32[64,64]{1,0:T(8,128)S(1)}, f32[64,64]{1,0:T(8,128)S(1)}, u32[]{:S(2)}, u32[]{:S(2)}) collective-permute-start(f32[64,64]{1,0:T(8,128)S(1)} %add.129), channel_id=1, source_target_pairs={{0,4},{1,5},{2,6},{3,7},{4,0},{5,1},{6,2},{7,3},{8,12},{9,13},{10,... | collective-permute-start | bytes 49160 | tf_op jit(solution)/shard_map/ppermute | solution.py:59
  184.1 7.9 %collective-permute-start.40 = (f16[2,2,32,1024]{3,2,0,1:T(8,128)(2,1)S(1)}, f16[2,2,32,1024]{3,2,0,1:T(8,128)(2,1)S(1)}, u32[]{:S(2)}, u32[]{:S(2)}) collective-permute-start(f16[2,2,32,1024]{3,2,0,1:T(8,128)(2,1)S(1)} %multiply_convert_fusion.3), channel_id=1, source_target_pairs={{0,2},{1,3},{2,0},{3,1},{4,6},{5,7},{6,4},{7,5},{8,10},{9,11},{10,... | collective-permute-start | bytes 786440 | tf_op jit(solution)/shard_map/ppermute | solution.py:59
  192.1 6.8 %collective-permute-start.46 = (f32[64,64]{1,0:T(8,128)S(1)}, f32[64,64]{1,0:T(8,128)S(1)}, u32[]{:S(2)}, u32[]{:S(2)}) collective-permute-start(f32[64,64]{1,0:T(8,128)S(1)} %add.130), channel_id=1, source_target_pairs={{0,8},{1,9},{2,10},{3,11},{4,12},{5,13},{6,14},{7,15},{8,0},{9,1},... | collective-permute-start | bytes 49160 | tf_op jit(solution)/shard_map/ppermute | solution.py:59
  193.6 8.6 %collective-permute-start.45 = (f16[2,32,1024]{2,1,0:T(8,128)(2,1)S(1)}, f16[2,32,1024]{2,1,0:T(8,128)(2,1)S(1)}, u32[]{:S(2)}, u32[]{:S(2)}) collective-permute-start(f16[2,32,1024]{2,1,0:T(8,128)(2,1)S(1)} %multiply_convert_fusion.6), channel_id=1, source_target_pairs={{0,8},{1,9},{2,10},{3,11},{4,12},{5,13},{6,14},{7,15},{8,0},{9,1},... | collective-permute-start | bytes 393224 | tf_op jit(solution)/shard_map/ppermute | solution.py:59
  195.4 6.9 %collective-permute-start.44 = (f16[2,32,1024]{2,1,0:T(8,128)(2,1)S(1)}, f16[2,32,1024]{2,1,0:T(8,128)(2,1)S(1)}, u32[]{:S(2)}, u32[]{:S(2)}) collective-permute-start(f16[2,32,1024]{2,1,0:T(8,128)(2,1)S(1)} %multiply_convert_fusion.7), channel_id=1, source_target_pairs={{0,4},{1,5},{2,6},{3,7},{4,0},{5,1},{6,2},{7,3},{8,12},{9,13},{10,... | collective-permute-start | bytes 393224 | tf_op jit(solution)/shard_map/ppermute | solution.py:59
  202.5 12.0 %collective-permute-start.48 = (f16[32,1024]{1,0:T(8,128)(2,1)S(1)}, f16[32,1024]{1,0:T(8,128)(2,1)S(1)}, u32[]{:S(2)}, u32[]{:S(2)}) collective-permute-start(f16[32,1024]{1,0:T(8,128)(2,1)S(1)} %multiply_convert_fusion.10), channel_id=1, source_target_pairs={{0,2},{1,3},{2,0},{3,1},{4,6},{5,7},{6,4},{7,5},{8,10},{9,11},{10,... | collective-permute-start | bytes 196616 | tf_op jit(solution)/shard_map/ppermute | solution.py:59
  202.7 11.9 %collective-permute-start.47 = (f16[32,1024]{1,0:T(8,128)(2,1)S(1)}, f16[32,1024]{1,0:T(8,128)(2,1)S(1)}, u32[]{:S(2)}, u32[]{:S(2)}) collective-permute-start(f16[32,1024]{1,0:T(8,128)(2,1)S(1)} %multiply_convert_fusion.11), channel_id=1, source_target_pairs={{0,8},{1,9},{2,10},{3,11},{4,12},{5,13},{6,14},{7,15},{8,0},{9,1},... | collective-permute-start | bytes 196616 | tf_op jit(solution)/shard_map/ppermute | solution.py:59
  (9 other events, 72.2 us)

commit v5 on v4

v5 whole, which is shorter than its diff:
```python
import functools

import jax
import jax.numpy as jnp
from jax import lax
from jax.experimental import pallas as pl
from jax.experimental.pallas import tpu as pltpu
from jax.sharding import PartitionSpec as P

K = 64
HALF = K // 2
RIDGE = 0.1
BOUND = 18.0
TOP = 60000.0
TINY = 1e-30
UNROLL = 4
F32, BF16, F16 = jnp.float32, jnp.bfloat16, jnp.float16


def precise(left, right):
    return jnp.dot(left, right, precision=lax.Precision.HIGHEST, preferred_element_type=F32)


def outer(left, right):
    return lax.dot_general(
        left, right, (((1,), (1,)), ((), ())), precision=lax.Precision.HIGHEST, preferred_element_type=F32
    )


def symmetric(matrix):
    return 0.5 * (matrix + matrix.T)


def solve_positive(*works):
    index = lax.broadcasted_iota(jnp.int32, (K, 1), 0)
    works = list(works)
    for first in range(0, K, 8):
        spread = [[jnp.broadcast_to(w[:, first + j : first + j + 1], w.shape) for j in range(8)] for w in works]
        for k in range(8):
            at = slice(first + k, first + k + 1)
            row = index == first + k
            for i, columns in enumerate(spread):
                column, inv = columns[k], 1.0 / columns[k][at]
                scaled = works[i][at] * inv
                works[i] = jnp.where(row, scaled, works[i] - column * scaled)
                for j in range(k + 1, 8):
                    scaled = columns[j][at] * inv
                    columns[j] = jnp.where(row, scaled, columns[j] - column * scaled)
    return [work[:, K:] for work in works]


def beside(matrix, target):
    return jnp.concatenate([matrix, target], axis=1)


def identity():
    eye = lax.broadcasted_iota(jnp.int32, (K, K), 0) == lax.broadcasted_iota(jnp.int32, (K, K), 1)
    return jnp.where(eye, 1.0, 0.0)


def swap(value, bit, n):
    return lax.ppermute(value, "dp", [(i, i ^ bit) for i in range(n)])


def hop_bits(n):
    bits = [1 << i for i in range(1, n.bit_length() - 1)]
    return bits, bits[1:] + bits[:1]


def _pos(j, shifts):
    p = 0
    for place, shift in enumerate(shifts):
        p = p | (((j >> shift) & 1) << place)
    return p


def block_copy(acts, kept, sems, me, half, t):
    f = kept.shape[2]
    first = pl.multiple_of((me[0] ^ (2 * t + half)) * f, f)
    return pltpu.make_async_copy(acts.at[:, pl.ds(first, f)], kept.at[t], sems.at[t])


def start_copies(acts, kept, sems, me, half):
    def start(t, carry):
        block_copy(acts, kept, sems, me, half, t).start()
        return carry

    lax.fori_loop(0, kept.shape[0], start, 0)


def whole(*shape):
    return pl.BlockSpec(shape, lambda i, me: (0,) * len(shape))


HBM = pl.BlockSpec(memory_space=pltpu.HBM)


def call(kernel, name, n, grid, in_specs, out_shapes, out_specs, acts, scratch=()):
    rows, d = acts.shape
    return pl.pallas_call(
        kernel,
        out_shape=out_shapes,
        grid_spec=pltpu.PrefetchScalarGridSpec(
            num_scalar_prefetch=1,
            grid=(grid,),
            in_specs=in_specs,
            out_specs=out_specs,
            scratch_shapes=[
                pltpu.VMEM((n // 2, rows, d // n), BF16),
                pltpu.SemaphoreType.DMA((n // 2,)),
                *scratch,
            ],
        ),
        compiler_params=pltpu.CompilerParams(vmem_limit_bytes=20 << 20),
        cost_estimate=pl.CostEstimate(flops=K * rows * d, bytes_accessed=rows * d + 2 * K * d, transcendentals=0),
        name=name,
    )


def sums_kernel(half, me, labels, counts, acts, out, weight, kept, sems, member):
    step = pl.program_id(0)

    @pl.when(step == 0)
    def _():
        start_copies(acts, kept, sems, me, half)
        concept = lax.broadcasted_iota(jnp.int32, member.shape, 0)
        full = jnp.where(labels[...] == concept, counts[...].astype(F32), 0.0)
        member[...] = full.astype(BF16)
        weight[...] = jnp.sum(full, axis=1, keepdims=True)

    for u in range(UNROLL):
        t = step * UNROLL + u
        block_copy(acts, kept, sems, me, half, t).wait()
        out[u] = jnp.dot(member[...], kept[t], preferred_element_type=F32)


def class_sums(me, labels, counts, acts, n, half):
    rows, d = acts.shape
    f = d // n
    return call(
        functools.partial(sums_kernel, half),
        "class_sums",
        n,
        n // 2 // UNROLL,
        [whole(1, rows), whole(1, rows), HBM],
        (
            jax.ShapeDtypeStruct((n // 2, K, f), F32),
            jax.ShapeDtypeStruct((K, 1), F32),
        ),
        (pl.BlockSpec((UNROLL, K, f), lambda i, me: (i, 0, 0)), whole(K, 1)),
        acts,
        [pltpu.VMEM((K, rows), BF16)],
    )(me, labels, counts, acts)


def inner(left, right):
    return lax.dot_general(left, right, (((1,), (1,)), ((), ())), preferred_element_type=F32)


def panel_operands(panels, n, f, shifts):
    last = n // 2 // UNROLL - 1
    specs, operands = [], []
    for panel in panels:
        for u in range(UNROLL):
            for stream, order in zip(panel, shifts):
                pick = lambda i, me, u=u, order=order: (_pos(2 * (jnp.minimum(i, last) * UNROLL + u), order), 0, 0)
                specs.append(pl.BlockSpec((1, HALF, f), pick))
                operands.append(stream)
    return specs, operands


def add_blocks(refs, count, block, probed, grams):
    total = probed[...]
    sums = [gram[...] for gram in grams]
    for u in range(UNROLL):
        at = [2 * (panel * UNROLL + u) for panel in range(count)]
        both = [jnp.concatenate([refs[i][0], refs[i + 1][0]], axis=0) for i in at]
        total = total + inner(block(u), both[0])
        sums = [x + inner(other, both[0]) for x, other in zip(sums, both)]
    probed[...] = total
    for gram, x in zip(grams, sums):
        gram[...] = x


def probe_kernel(count, me, *refs):
    panels, refs = refs[: 2 * UNROLL * count], refs[2 * UNROLL * count :]
    acts, probed, *grams, kept, sems = refs
    step = pl.program_id(0)

    @pl.when(step == 0)
    def _():
        start_copies(acts, kept, sems, me, 0)
        for ref in (probed, *grams):
            ref[...] = jnp.zeros_like(ref)

    def block(u):
        block_copy(acts, kept, sems, me, 0, step * UNROLL + u).wait()
        return kept[step * UNROLL + u]

    add_blocks(panels, count, block, probed, grams)


def probe(me, panels, acts, n, shifts):
    rows, d = acts.shape
    count = len(panels)
    specs, operands = panel_operands(panels, n, d // n, shifts)
    return call(
        functools.partial(probe_kernel, count),
        "probe",
        n,
        n // 2 // UNROLL,
        specs + [HBM],
        (jax.ShapeDtypeStruct((rows, K), F32),) + (jax.ShapeDtypeStruct((K, K), F32),) * count,
        (whole(rows, K),) + (whole(K, K),) * count,
        acts,
    )(me, *operands, acts)


def diagonal(matrix):
    kept = matrix * identity()
    return jnp.sum(kept, axis=1, keepdims=True), jnp.sum(kept, axis=0, keepdims=True)


def finish_first(gram):
    current = symmetric(gram[...])
    gram[...] = current
    return jnp.sqrt(diagonal(current)[0])


def finish_second(probed, image_image, base_image, more):
    first, current, alpha_t, inverse, renewed, mixed, beta_t = more
    both = jnp.concatenate([base_image[...], symmetric(image_image[...])], axis=0)
    moved = outer(both, alpha_t[...])
    moved, twice = moved[:K], precise(alpha_t[...], moved[K:])
    new = symmetric(current[...] - moved - moved.T + twice)
    beta = precise(new, inverse[...])
    renewed[...] = new
    mixed[...] = current[...] - moved
    beta_t[...] = beta
    mix = jnp.concatenate([beta, -alpha_t[...]], axis=1)
    probed[...] = first[...] + precise(mix, jnp.concatenate([first[...], probed[...]], axis=0))
    base_col, base_row = diagonal(current[...])
    _, image_row = diagonal(image_image[...])
    norms = jnp.sqrt(base_col)
    norms += jnp.sum(jnp.abs(beta) * jnp.sqrt(base_row), axis=1, keepdims=True)
    return norms + jnp.sum(jnp.abs(alpha_t[...]) * jnp.sqrt(image_row), axis=1, keepdims=True)


def send_kernel(steps, count, d, me, *refs):
    second = count == 2
    parts = [2 * UNROLL * count, 4, count, 4 * second, 4, count, 3 * second, 4]
    refs = list(refs)
    panels, ins, starts, given, outs, grams, made, scratch = (
        [refs.pop(0) for _ in range(size)] for size in parts
    )
    acts, counts, total_weight, start = ins
    probed, along, bound, out = outs
    kept, sems, weighted, sum_of = scratch
    step = pl.program_id(0)

    @pl.when(step == 0)
    def _():
        start_copies(acts, kept, sems, me, 1)
        for ref, begin in zip((sum_of, *grams), (start, *starts)):
            ref[...] = begin[...]

    @pl.when(step < steps)
    def _():
        def block(u):
            block_copy(acts, kept, sems, me, 1, step * UNROLL + u).wait()
            return kept[step * UNROLL + u]

        add_blocks(panels, count, block, sum_of, grams)

    @pl.when(step == steps)
    def _():
        probed[...] = sum_of[...].T
        norms = finish_second(probed, *grams, (*given, *made)) if second else finish_first(*grams)
        bound[...] = (1.02 * BOUND * BOUND * d**0.5) * total_weight[...] * norms
        weighted[...] = (counts[...].astype(F32) * probed[...]).astype(BF16)
        along[...] = outer(probed[...], weighted[...].astype(F32))

    @pl.when(step >= steps)
    def _():
        for u in range(UNROLL):
            out[u] = jnp.dot(weighted[...], kept[(step - steps) * UNROLL + u], preferred_element_type=F32)


def probe_and_send(me, panels, acts, counts, total_weight, starts, given, n, shifts):
    rows, d = acts.shape
    f = d // n
    s = n // 2 // UNROLL
    count = len(panels)
    square = jax.ShapeDtypeStruct((K, K), F32)
    made = 3 if given else 0
    specs, operands = panel_operands(panels, n, f, shifts)
    return call(
        functools.partial(send_kernel, s, count, d),
        "probe_and_send",
        n,
        2 * s,
        specs + [HBM, whole(1, rows), whole(1, 1)] + [whole(*x.shape) for x in (*starts, *given)],
        (
            jax.ShapeDtypeStruct((K, rows), F32),
            square,
            jax.ShapeDtypeStruct((K, 1), F32),
            jax.ShapeDtypeStruct((n // 2, K, f), F32),
        )
        + (square,) * (count + made),
        (
            whole(K, rows),
            whole(K, K),
            whole(K, 1),
            pl.BlockSpec((UNROLL, K, f), lambda i, me: (jnp.maximum(i - s, 0), 0, 0)),
        )
        + (whole(K, K),) * (count + made),
        acts,
        [pltpu.VMEM((K, rows), BF16), pltpu.VMEM((rows, K), F32)],
    )(me, *operands, acts, counts, total_weight, *starts, *given)


def keep_kernel(me, probed, counts, acts, out, kept, sems, weighted):
    step = pl.program_id(0)

    @pl.when(step == 0)
    def _():
        start_copies(acts, kept, sems, me, 0)
        weighted[...] = (counts[...].astype(F32) * probed[...]).astype(BF16)

    for u in range(UNROLL):
        t = step * UNROLL + u
        block_copy(acts, kept, sems, me, 0, t).wait()
        out[u] = jnp.dot(weighted[...], kept[t], preferred_element_type=F32)


def panel_keep(me, probed, counts, acts, n):
    rows, d = acts.shape
    f = d // n
    return call(
        keep_kernel,
        "panel_keep",
        n,
        n // 2 // UNROLL,
        [whole(K, rows), whole(1, rows), HBM],
        jax.ShapeDtypeStruct((n // 2, K, f), F32),
        pl.BlockSpec((UNROLL, K, f), lambda i, me: (i, 0, 0)),
        acts,
        [pltpu.VMEM((K, rows), BF16)],
    )(me, probed, counts, acts)


def alpha_kernel(along, current, total_weight, alpha_t, inverse):
    now = current[...]
    curvature = (along[...] - precise(now, now)) / total_weight[...] + RIDGE * now
    alpha, inv = solve_positive(beside(symmetric(curvature), now), beside(now, identity()))
    alpha_t[...] = alpha.T
    inverse[...] = symmetric(inv)


def offset_kernel(base_a, base_b, current, total_weight, offset):
    base = jnp.concatenate([base_a[...], base_b[...]], axis=0)
    offset[...] = RIDGE * base - precise(current[...] / total_weight[...], base)


def before_kernel(current, renewed, mixed, beta_t, total_weight, fixed, cross_t):
    now, beta, weight = current[...], beta_t[...], total_weight[...]
    cross = mixed[...] + outer(now, beta)
    length = renewed[...] + outer(mixed[...].T, beta) + precise(beta, cross)
    turned = cross.T
    cross_t[...] = turned
    fixed[...] = RIDGE * length - outer(turned, turned) / weight


def last_kernel(
    along, fixed, cross_t, renewed, beta_t, alpha_t, total_weight, base_a, base_b, image_a, image_b,
    solved, rest, on_panel,
):
    weight = total_weight[...]
    curvature = symmetric(along[...] / weight + fixed[...])
    step = solve_positive(beside(curvature, renewed[...]))[0].T
    on_panel[...] = step / weight
    alpha = alpha_t[...]
    all_three = precise(step, jnp.concatenate([identity() + beta_t[...], alpha, cross_t[...]], axis=1))
    direction_base, direction_image = all_three[:, :K], all_three[:, K : 2 * K]
    crossed = all_three[:, 2 * K :] / weight
    both = jnp.concatenate([base_a[...], base_b[...], image_a[...], image_b[...]], axis=0)
    solved[...] = precise(beside(alpha + direction_base, -direction_image), both)
    rest[...] = precise(
        beside(identity() - RIDGE * direction_base + crossed, RIDGE * direction_image - alpha), both
    )


def end_kernel(rest, on_panel, panel_a, panel_b, residual):
    panel = jnp.concatenate([panel_a[...], panel_b[...]], axis=0)
    residual[...] = rest[...] - precise(on_panel[...], panel)


def small(kernel, name, outs, *args):
    return pl.pallas_call(
        kernel, out_shape=tuple(jax.ShapeDtypeStruct(shape, F32) for shape in outs), name=name,
        cost_estimate=pl.CostEstimate(flops=1 << 26, bytes_accessed=1 << 20, transcendentals=0),
    )(*args)


def shrink(value, bound):
    return (value * (TOP / jnp.maximum(bound, TINY))).astype(F16)


def grow(value, bound):
    return value.astype(F32) * (jnp.maximum(bound, TINY) * (1.0 / TOP))


def split_blocks(value, left, bit):
    axis = left.index(bit)
    keep = lax.index_in_dim(value, 0, axis, keepdims=False)
    send = lax.index_in_dim(value, 1, axis, keepdims=False)
    return keep, send, [other for other in left if other != bit]


def reduce_scatter(blocks, n, swap_a, swap_b, along, work=None, args=()):
    bits = n.bit_length() - 2
    shape = (2,) * bits + (HALF, blocks.shape[2])
    a, b = blocks[:, :HALF].reshape(shape), blocks[:, HALF:].reshape(shape)
    left_a = left_b = [1 << i for i in range(bits, 0, -1)]
    order_a, order_b = hop_bits(n)
    waiting, done = list(order_a), ()
    for phase, (bit_a, bit_b) in enumerate(zip(order_a, order_b)):
        keep_a, send_a, left_a = split_blocks(a, left_a, bit_a)
        keep_b, send_b, left_b = split_blocks(b, left_b, bit_b)
        tied = args if phase == 1 else done
        send_a, send_b, along, tied = lax.optimization_barrier((send_a, send_b, along, tied))
        a, b = keep_a + swap_a(send_a, bit_a), keep_b + swap_b(send_b, bit_b)
        for bit in waiting[:2]:
            along = along + swap(along, bit, n)
        waiting = waiting[2:]
        if work is not None and phase >= 1:
            done = work(*tied) if phase == 1 else tied
    return a, b, along, done


class Root:
    def __init__(self, n, bound):
        self.n, self.scale = n, TOP / bound**0.5

    def __call__(self, send, bit):
        root = jnp.sqrt(jnp.abs(send)) * self.scale
        got = swap(jnp.where(send < 0, -root, root).astype(F16), bit, self.n).astype(F32)
        return got * jnp.abs(got) * (1.0 / self.scale**2)


def gather(top, low, n, orders, work=None, args=()):
    a, b = top.astype(BF16)[None], low.astype(BF16)[None]
    done = ()
    for phase, (bit_a, bit_b) in enumerate(zip(*orders)):
        if work is not None and phase >= 1:
            tied = args if phase == 1 else done
            a, b, tied = lax.optimization_barrier((a, b, tied))
            done = work(*tied) if phase == 1 else tied
        a = jnp.concatenate([a, swap(a, bit_a, n)], axis=0)
        b = jnp.concatenate([b, swap(b, bit_b, n)], axis=0)
    return (a, b), (swap(a, 1, n), swap(b, 1, n)), done


def per_device(n, activations, labels, counts):
    rows, d = activations.shape
    activations = pltpu.with_memory_space_constraint(activations, pltpu.HBM)
    me = lax.axis_index("dp").astype(jnp.int32).reshape(1)
    labels = labels.reshape(1, rows)
    counts = counts.reshape(1, rows)
    order_y, order_z = hop_bits(n)
    order_a, order_b = order_y[::-1], order_z
    shifts = [[bit.bit_length() - 1 for bit in order] for order in (order_a, order_b)]

    root = Root(n, BOUND * 4 * rows * n)
    sent, weight = class_sums(me, labels, counts, activations, n, 1)
    weight = weight.T
    got = root(sent, 1)
    weight = weight + swap(weight, 1, n)
    kept, _ = class_sums(me, labels, counts, activations, n, 0)
    top, low, weight, _ = reduce_scatter(kept + got, n, root, root, weight)
    class_weight = weight.T
    total_weight = jnp.sum(class_weight, keepdims=True)
    over, back = class_weight, jnp.sqrt(class_weight)
    base = (top / over[:HALF]) * back[:HALF], (low / over[HALF:]) * back[HALF:]

    def scatter(probed, along, bound, sent, work, args):
        got = grow(swap(shrink(sent, bound), 1, n), bound)
        along = along + swap(along, 1, n)
        blocks = panel_keep(me, probed, counts, activations, n) + got
        top, low = bound[:HALF], bound[HALF:]
        return reduce_scatter(
            blocks,
            n,
            lambda x, bit: grow(swap(shrink(x, top), bit, n), top),
            lambda x, bit: grow(swap(shrink(x, low), bit, n), low),
            along,
            work,
            args,
        )

    square, strip = (K, K), (K, d // n)
    orders = order_a, order_b
    base_near, base_far, _ = gather(*base, n, orders)
    starts = probe(me, (base_near,), activations, n, shifts)
    first, along, bound, sent, current = probe_and_send(
        me, (base_far,), activations, counts, total_weight, starts, (), n, shifts
    )
    panel_a, panel_b, along, (offset,) = scatter(
        first, along, bound, sent,
        lambda *args: small(offset_kernel, "offset", (strip,), *args), (*base, current, total_weight),
    )
    image = panel_a / total_weight + offset[:HALF], panel_b / total_weight + offset[HALF:]

    near, far, (alpha_t, inverse) = gather(
        *image, n, orders,
        lambda *args: small(alpha_kernel, "alpha", (square,) * 2, *args), (along, current, total_weight),
    )
    starts = probe(me, (near, base_near), activations, n, shifts)
    probed, along, bound, sent, _, _, renewed, mixed, beta_t = probe_and_send(
        me, (far, base_far), activations, counts, total_weight, starts, (first, current, alpha_t, inverse), n, shifts
    )
    panel_a, panel_b, along, (fixed, cross_t) = scatter(
        probed, along, bound, sent,
        lambda *args: small(before_kernel, "before", (square,) * 2, *args),
        (current, renewed, mixed, beta_t, total_weight),
    )
    solved, rest, on_panel = small(
        last_kernel, "last", (strip, strip, square),
        along, fixed, cross_t, renewed, beta_t, alpha_t, total_weight, *base, *image,
    )
    (residual,) = small(end_kernel, "end", (strip,), rest, on_panel, panel_a, panel_b)
    return (solved.T, residual.T)


def solution(mesh):
    in_specs = (P(("groups", "dp"), None), P(("groups", "dp")), P(("groups", "dp")))
    out_specs = (P(("groups", "dp"), None), P(("groups", "dp"), None))
    return jax.shard_map(
        functools.partial(per_device, mesh.shape["dp"]),
        mesh=mesh,
        in_specs=in_specs,
        out_specs=out_specs,
        check_vma=False,
    )
```

time: 218 us -> 200 us (0.917)
  Pallas kernels: 67.3 us -> 57.6 us
  waiting for transfers between devices: 78.7 us -> 70.1 us
  other arithmetic: 12.3 us -> 16 us
  matrix products: 2.85 us -> 0 us
    ppermute x49, waiting for transfers between devices: 78.7 us -> 70.1 us  [swap(): return lax.ppermute(value, 'dp', [(i, i ^ bit) for i in range(n)])]
    pallas_call x3 -> x5, Pallas kernels: 23.5 us -> 17 us  [small(): pl.pallas_call(kernel, out_shape=tuple((jax.ShapeDtypeStruct(shape, F32)...]
    pallas_call x2, Pallas kernels: 20.5 us -> 16.5 us  [probe_and_send(): call(functools.partial(send_kernel, s, count, d), 'probe_and_send', n, 2...]
    add x18 -> x14, other arithmetic: 1.64 us -> 4.52 us  [reduce_scatter(): a, b = (keep_a + swap_a(send_a, bit_a), keep_b + swap_b(send_b, bit_b))]
    dot_general x2 -> x0, matrix products: 2.85 us -> none  [precise(): jnp.dot(left, right, precision=lax.Precision.HIGHEST, preferred_element_t...]
    broadcast_in_dim x0 -> x3, other arithmetic: none -> 2.85 us  [gather(): a, b = (top.astype(BF16)[None], low.astype(BF16)[None])]
  transfers between devices with their start and end apart: 49 -> 49, of which waited for: 25 -> 23; matrix products, arithmetic and copies ran while one was open for 2% -> 4% of each run, Pallas kernels for 20% -> 18%
where the time goes in v5:
time: 200 us; the launch traced here: 199 us
  waiting for transfers between devices  70.1 us (35%)
  Pallas kernels  57.6 us (29%)
  starting transfers between devices  51.2 us (26%)
  other arithmetic  16 us (8%)
  local copies, waits for them, and re-layouts  2.95 us (1%)
    ppermute x49, waiting for transfers between devices, swap(): return lax.ppermute(value, 'dp', [(i, i ^ bit) for i in range(n)])  70.1 us
    ppermute x49, starting transfers between devices, swap(): return lax.ppermute(value, 'dp', [(i, i ^ bit) for i in range(n)])  51.2 us
    pallas_call x5, Pallas kernels, small(): pl.pallas_call(kernel, out_shape=tuple((jax.ShapeDtypeStruct(shape, F32)...  17 us
    pallas_call x2, Pallas kernels, probe_and_send(): call(functools.partial(send_kernel, s, count, d), 'probe_and_send', n, 2...  16.5 us
    pallas_call x2, Pallas kernels, probe(): call(functools.partial(probe_kernel, count), 'probe', n, n // 2 // UNROLL...  10.1 us
    pallas_call x2, Pallas kernels, panel_keep(): call(keep_kernel, 'panel_keep', n, n // 2 // UNROLL, [whole(K, rows), who...  7.09 us
    pallas_call x2, Pallas kernels, class_sums(): call(functools.partial(sums_kernel, half), 'class_sums', n, n // 2 // UNR...  7 us
    add x14, other arithmetic, reduce_scatter(): a, b = (keep_a + swap_a(send_a, bit_a), keep_b + swap_b(send_b, bit_b))  4.52 us
  transfers between devices with their start and end apart: 49, of which 23 were waited for; matrix products, arithmetic and copies ran while one was open for 4% of the time, Pallas kernels for 18%

profile of v5, /device:TPU:0, one launch (start us, length us, event | category | flops | bytes accessed | tf_op | source)
XLA Modules:
  0.0 199.3 jit_solution(16254937022117355432)
XLA Ops:
  2.0 3.3 %class_sums.3 = (f32[8,64,1024]{2,1,0:T(8,128)S(1)}, f32[64,1]{1,0:T(8,128)S(1)}) custom-call(s32[1]{0:T(128)} %bitcast.me, s32[1,384]{1,0:T(1,128)S(1)} %reshape.75.labels, s32[1,384]{1,0:T(1,128)S(1)} %reshape.76.counts.refs_9_.refs_17_, bf16[384,16384]{1,0:T(8,128)(2,1)} %acts.7), custom_call_target="tpu_custom_call" | custom-call | flops 402653184 | bytes 8388608 | tf_op jit(solution)/shard_map/class_sums/pallas_call | solution.py:140
  7.0 3.7 %class_sums.2 = (f32[8,64,1024]{2,1,0:T(8,128)S(1)}, f32[64,1]{1,0:T(8,128)}) custom-call(s32[1]{0:T(128)} %bitcast.me, s32[1,384]{1,0:T(1,128)S(1)} %reshape.75.labels, s32[1,384]{1,0:T(1,128)S(1)} %reshape.76.counts.refs_9_.refs_17_, bf16[384,16384]{1,0:T(8,128)(2,1)} %acts.7), custom_call_target="tpu_custom_call" | custom-call | flops 402653184 | bytes 8388608 | tf_op jit(solution)/shard_map/class_sums/pallas_call | solution.py:140
  12.0 3.1 %collective-permute-start.3 = (f16[2,2,32,1024]{3,2,0,1:T(8,128)(2,1)S(1)}, f16[2,2,32,1024]{3,2,0,1:T(8,128)(2,1)S(1)}, u32[]{:S(2)}, u32[]{:S(2)}) collective-permute-start(f16[2,2,32,1024]{3,2,0,1:T(8,128)(2,1)S(1)} %fusion.6), channel_id=1, source_target_pairs={{0,4},{1,5},{2,6},{3,7},{4,0},{5,1},{6,2},{7,3},{8,12},{9,13},{10,... | collective-permute-start | bytes 786440 | tf_op jit(solution)/shard_map/ppermute | solution.py:62
  16.6 2.0 %collective-permute-done.4 = f32[1,64]{1,0:T(1,128)S(1)} collective-permute-done((f32[1,64]{1,0:T(1,128)S(1)}, f32[1,64]{1,0:T(1,128)S(1)}, u32[]{:S(2)}, u32[]{:S(2)}) %collective-permute-start.4) | collective-permute-done | bytes 288 | tf_op jit(solution)/shard_map/ppermute | solution.py:62
  19.0 2.0 collective-permute-start.2
  22.3 3.7 %collective-permute-done.2 = f16[2,2,32,1024]{3,2,0,1:T(8,128)(2,1)S(1)} collective-permute-done((f16[2,2,32,1024]{3,2,0,1:T(8,128)(2,1)S(1)}, f16[2,2,32,1024]{3,2,0,1:T(8,128)(2,1)S(1)}, u32[]{:S(2)}, u32[]{:S(2)}) %collective-permute-start.2) | collective-permute-done | bytes 262176 | tf_op jit(solution)/shard_map/ppermute | solution.py:62
  26.2 2.7 %collective-permute-start.8 = (f32[1,64]{1,0:T(1,128)S(1)}, f32[1,64]{1,0:T(1,128)S(1)}, u32[]{:S(2)}, u32[]{:S(2)}) collective-permute-start(f32[1,64]{1,0:T(1,128)S(1)} %add.110), channel_id=1, source_target_pairs={{0,8},{1,9},{2,10},{3,11},{4,12},{5,13},{6,14},{7,15},{8,0},{9,1},... | collective-permute-start | bytes 776 | tf_op jit(solution)/shard_map/ppermute | solution.py:62
  29.5 1.8 collective-permute-start.6
  31.3 5.0 %collective-permute-done.7 = f16[2,32,1024]{2,1,0:T(8,128)(2,1)S(1)} collective-permute-done((f16[2,32,1024]{2,1,0:T(8,128)(2,1)S(1)}, f16[2,32,1024]{2,1,0:T(8,128)(2,1)S(1)}, u32[]{:S(2)}, u32[]{:S(2)}) %collective-permute-start.7) | collective-permute-done | bytes 131104 | tf_op jit(solution)/shard_map/ppermute | solution.py:62
  37.3 1.7 collective-permute-start.9
  39.1 1.9 collective-permute-start.14
  40.9 3.6 %collective-permute-done.9 = f16[32,1024]{1,0:T(8,128)(2,1)S(1)} collective-permute-done((f16[32,1024]{1,0:T(8,128)(2,1)S(1)}, f16[32,1024]{1,0:T(8,128)(2,1)S(1)}, u32[]{:S(2)}, u32[]{:S(2)}) %collective-permute-start.9) | collective-permute-done | bytes 65568 | tf_op jit(solution)/shard_map/ppermute | solution.py:62
  46.1 3.0 %collective-permute-start.15 = (bf16[1,32,1024]{2,1,0:T(8,128)(2,1)S(1)}, bf16[1,32,1024]{2,1,0:T(8,128)(2,1)S(1)}, u32[]{:S(2)}, u32[]{:S(2)}) collective-permute-start(bf16[1,32,1024]{2,1,0:T(8,128)(2,1)S(1)} %get-tuple-element.168), channel_id=1, source_target_pairs={{0,4},{1,5},{2,6},{3,7},{4,0},{5,1},{6,2},{7,3},{8,12},{9,13},{10,... | collective-permute-start | bytes 196616 | tf_op jit(solution)/shard_map/ppermute | solution.py:62
  49.1 3.6 %collective-permute-done.10 = bf16[1,32,1024]{2,1,0:T(8,128)(2,1)S(1)} collective-permute-done((bf16[1,32,1024]{2,1,0:T(8,128)(2,1)S(1)}, bf16[1,32,1024]{2,1,0:T(8,128)(2,1)S(1)}, u32[]{:S(2)}, u32[]{:S(2)}) %collective-permute-start.10) | collective-permute-done | bytes 65568 | tf_op jit(solution)/shard_map/ppermute | solution.py:62
  52.9 2.8 %collective-permute-start.16 = (bf16[2,32,1024]{2,1,0:T(8,128)(2,1)S(1)}, bf16[2,32,1024]{2,1,0:T(8,128)(2,1)S(1)}, u32[]{:S(2)}, u32[]{:S(2)}) collective-permute-start(bf16[2,32,1024]{2,1,0:T(8,128)(2,1)S(1)} %pad_maximum_fusion.7), channel_id=1, source_target_pairs={{0,8},{1,9},{2,10},{3,11},{4,12},{5,13},{6,14},{7,15},{8,0},{9,1},... | collective-permute-start | bytes 393224 | tf_op jit(solution)/shard_map/ppermute | solution.py:62
  55.7 3.5 %collective-permute-done.11 = bf16[2,32,1024]{2,1,0:T(8,128)(2,1)S(1)} collective-permute-done((bf16[2,32,1024]{2,1,0:T(8,128)(2,1)S(1)}, bf16[2,32,1024]{2,1,0:T(8,128)(2,1)S(1)}, u32[]{:S(2)}, u32[]{:S(2)}) %collective-permute-start.11) | collective-permute-done | bytes 131104 | tf_op jit(solution)/shard_map/ppermute | solution.py:62
  61.4 4.2 %collective-permute-done.12 = bf16[4,32,1024]{2,1,0:T(8,128)(2,1)S(1)} collective-permute-done((bf16[4,32,1024]{2,1,0:T(8,128)(2,1)S(1)}, bf16[4,32,1024]{2,1,0:T(8,128)(2,1)S(1)}, u32[]{:S(2)}, u32[]{:S(2)}) %collective-permute-start.12) | collective-permute-done | bytes 262176 | tf_op jit(solution)/shard_map/ppermute | solution.py:62
  65.8 2.7 %collective-permute-done.17 = bf16[4,32,1024]{2,1,0:T(8,128)(2,1)S(1)} collective-permute-done((bf16[4,32,1024]{2,1,0:T(8,128)(2,1)S(1)}, bf16[4,32,1024]{2,1,0:T(8,128)(2,1)S(1)}, u32[]{:S(2)}, u32[]{:S(2)}) %collective-permute-start.17) | collective-permute-done | bytes 262176 | tf_op jit(solution)/shard_map/ppermute | solution.py:62
  68.6 5.1 %probe.2 = (f32[384,64]{1,0:T(8,128)S(1)}, f32[64,64]{1,0:T(8,128)S(1)}) custom-call(s32[1]{0:T(128)} %bitcast.me, bf16[8,32,1024]{2,1,0:T(8,128)(2,1)S(1)} %pad_maximum_fusion.refs_0_.refs_2_.refs_4_.refs_6_.refs_8_.refs_10_.refs_12_.refs_14_, bf16[8,32,1024]{2,1,0:T(8,128)(2,1)S(1)} %pad_maximum_fusion.1.refs_1_.refs_3_.refs_5_.refs_7_.refs_9_.refs_11_.refs_13_.refs_15_, ...), custom_call_target="tpu_custom_call" | custom-call | flops 402653184 | bytes 8388608 | tf_op jit(solution)/shard_map/probe/pallas_call | solution.py:207
  73.7 7.5 %probe_and_send.2 = (f32[64,384]{1,0:T(8,128)S(1)}, f32[64,64]{1,0:T(8,128)S(1)}, f32[64,1]{1,0:T(8,128)S(1)}, f32[8,64,1024]{2,1,0:T(8,128)S(1)}, f32[64,64]{1,0:T(8,128)S(1)}) custom-call(s32[1]{0:T(128)} %bitcast.me, bf16[8,32,1024]{2,1,0:T(8,128)(2,1)S(1)} %collective-permute-done.13.refs_0_.refs_2_.refs_4_.refs_6_.refs_8_.refs_10_.refs_12_.refs_14_, ...), custom_call_target="tpu_custom_call" | custom-call | flops 402653184 | bytes 8388608 | tf_op jit(solution)/shard_map/probe_and_send/pallas_call | solution.py:297
  82.4 3.5 %panel_keep.2 = f32[8,64,1024]{2,1,0:T(8,128)S(1)} custom-call(s32[1]{0:T(128)} %bitcast.me, f32[64,384]{1,0:T(8,128)S(1)} %get-tuple-element.91.probed.refs_22_, s32[1,384]{1,0:T(1,128)S(1)} %reshape.76.counts.refs_9_.refs_17_, bf16[384,16384]{1,0:T(8,128)(2,1)} %acts.7), custom_call_target="tpu_custom_call" | custom-call | flops 402653184 | bytes 8388608 | tf_op jit(solution)/shard_map/panel_keep/pallas_call | solution.py:339
  88.7 2.4 %collective-permute-done.23 = f32[64,64]{1,0:T(8,128)S(1)} collective-permute-done((f32[64,64]{1,0:T(8,128)S(1)}, f32[64,64]{1,0:T(8,128)S(1)}, u32[]{:S(2)}, u32[]{:S(2)}) %collective-permute-start.23) | collective-permute-done | bytes 16416 | tf_op jit(solution)/shard_map/ppermute | solution.py:62
  91.1 1.9 collective-permute-start.24
  96.7 3.8 %collective-permute-done.21 = f16[2,2,32,1024]{3,2,0,1:T(8,128)(2,1)S(1)} collective-permute-done((f16[2,2,32,1024]{3,2,0,1:T(8,128)(2,1)S(1)}, f16[2,2,32,1024]{3,2,0,1:T(8,128)(2,1)S(1)}, u32[]{:S(2)}, u32[]{:S(2)}) %collective-permute-start.21) | collective-permute-done | bytes 262176 | tf_op jit(solution)/shard_map/ppermute | solution.py:62
  102.5 1.9 collective-permute-start.26
  104.9 2.6 %offset.1 = f32[64,1024]{1,0:T(8,128)} custom-call(f32[32,1024]{1,0:T(8,128)} %get-tuple-element.102.base_a, f32[32,1024]{1,0:T(8,128)} %get-tuple-element.103.base_b, f32[64,64]{1,0:T(8,128)} %copy-done, f32[1,1]{1,0:T(1,128)} %bitcast.21.refs_10_.total_weight.refs_18_), custom_call_target="tpu_custom_call" | custom-call | flops 67108864 | bytes 1048576 | tf_op jit(solution)/shard_map/offset/pallas_call | solution.py:399
  108.1 2.5 %collective-permute-done.26 = f16[2,32,1024]{2,1,0:T(8,128)(2,1)} collective-permute-done((f16[2,32,1024]{2,1,0:T(8,128)(2,1)}, f16[2,32,1024]{2,1,0:T(8,128)(2,1)}, u32[]{:S(2)}, u32[]{:S(2)}) %collective-permute-start.26) | collective-permute-done | bytes 131104 | tf_op jit(solution)/shard_map/ppermute | solution.py:62
  114.6 2.7 %collective-permute-done.30 = f16[32,1024]{1,0:T(8,128)(2,1)S(1)} collective-permute-done((f16[32,1024]{1,0:T(8,128)(2,1)S(1)}, f16[32,1024]{1,0:T(8,128)(2,1)S(1)}, u32[]{:S(2)}, u32[]{:S(2)}) %collective-permute-start.30) | collective-permute-done | bytes 65568 | tf_op jit(solution)/shard_map/ppermute | solution.py:62
  117.2 2.3 %collective-permute-done.28 = f16[32,1024]{1,0:T(8,128)(2,1)S(1)} collective-permute-done((f16[32,1024]{1,0:T(8,128)(2,1)S(1)}, f16[32,1024]{1,0:T(8,128)(2,1)S(1)}, u32[]{:S(2)}, u32[]{:S(2)}) %collective-permute-start.28) | collective-permute-done | bytes 65568 | tf_op jit(solution)/shard_map/ppermute | solution.py:62
  120.9 2.4 %collective-permute-start.29 = (bf16[1,32,1024]{2,1,0:T(8,128)(2,1)S(1)}, bf16[1,32,1024]{2,1,0:T(8,128)(2,1)S(1)}, u32[]{:S(2)}, u32[]{:S(2)}) collective-permute-start(bf16[1,32,1024]{2,1,0:T(8,128)(2,1)S(1)} %get-tuple-element.186), channel_id=1, source_target_pairs={{0,8},{1,9},{2,10},{3,11},{4,12},{5,13},{6,14},{7,15},{8,0},{9,1},... | collective-permute-start | bytes 196616 | tf_op jit(solution)/shard_map/ppermute | solution.py:62
  123.3 3.8 %collective-permute-done.31 = bf16[1,32,1024]{2,1,0:T(8,128)(2,1)S(1)} collective-permute-done((bf16[1,32,1024]{2,1,0:T(8,128)(2,1)S(1)}, bf16[1,32,1024]{2,1,0:T(8,128)(2,1)S(1)}, u32[]{:S(2)}, u32[]{:S(2)}) %collective-permute-start.31) | collective-permute-done | bytes 65568 | tf_op jit(solution)/shard_map/ppermute | solution.py:62
  127.1 1.9 collective-permute-start.32
  129.8 4.3 %alpha.1 = (f32[64,64]{1,0:T(8,128)}, f32[64,64]{1,0:T(8,128)}) custom-call(f32[64,64]{1,0:T(8,128)} %add.124.along, f32[64,64]{1,0:T(8,128)} %copy-done, f32[1,1]{1,0:T(1,128)} %bitcast.21.refs_10_.total_weight.refs_18_), custom_call_target="tpu_custom_call" | custom-call | flops 67108864 | bytes 1048576 | tf_op jit(solution)/shard_map/alpha/pallas_call | solution.py:399
  134.1 2.2 %collective-permute-done.33 = bf16[2,32,1024]{2,1,0:T(8,128)(2,1)S(1)} collective-permute-done((bf16[2,32,1024]{2,1,0:T(8,128)(2,1)S(1)}, bf16[2,32,1024]{2,1,0:T(8,128)(2,1)S(1)}, u32[]{:S(2)}, u32[]{:S(2)}) %collective-permute-start.33) | collective-permute-done | bytes 131104 | tf_op jit(solution)/shard_map/ppermute | solution.py:62
  138.5 4.3 %collective-permute-done.36 = bf16[4,32,1024]{2,1,0:T(8,128)(2,1)S(1)} collective-permute-done((bf16[4,32,1024]{2,1,0:T(8,128)(2,1)S(1)}, bf16[4,32,1024]{2,1,0:T(8,128)(2,1)S(1)}, u32[]{:S(2)}, u32[]{:S(2)}) %collective-permute-start.36) | collective-permute-done | bytes 262176 | tf_op jit(solution)/shard_map/ppermute | solution.py:62
  142.9 2.7 %collective-permute-done.34 = bf16[4,32,1024]{2,1,0:T(8,128)(2,1)S(1)} collective-permute-done((bf16[4,32,1024]{2,1,0:T(8,128)(2,1)S(1)}, bf16[4,32,1024]{2,1,0:T(8,128)(2,1)S(1)}, u32[]{:S(2)}, u32[]{:S(2)}) %collective-permute-start.34) | collective-permute-done | bytes 262176 | tf_op jit(solution)/shard_map/ppermute | solution.py:62
  145.7 5.1 %probe.3 = (f32[384,64]{1,0:T(8,128)S(1)}, f32[64,64]{1,0:T(8,128)S(1)}, f32[64,64]{1,0:T(8,128)S(1)}) custom-call(s32[1]{0:T(128)} %bitcast.me, bf16[8,32,1024]{2,1,0:T(8,128)(2,1)S(1)} %constant_dynamic-update-slice_fusion.refs_0_.refs_2_.refs_4_.refs_6_, bf16[8,32,1024]{2,1,0:T(8,128)(2,1)S(1)} %constant_dynamic-update-slice_fusion.2.refs_1_.refs_3_.refs_5_.refs_7_, ...), custom_call_target="tpu_custom_call" | custom-call | flops 402653184 | bytes 8388608 | tf_op jit(solution)/shard_map/probe/pallas_call | solution.py:207
  150.8 9.0 %probe_and_send.3 = (f32[64,384]{1,0:T(8,128)S(1)}, f32[64,64]{1,0:T(8,128)S(1)}, f32[64,1]{1,0:T(8,128)S(1)}, f32[8,64,1024]{2,1,0:T(8,128)S(1)}, f32[64,64]{1,...) custom-call(s32[1]{0:T(128)} %bitcast.me, ...), custom_call_target="tpu_custom_call" | custom-call | flops 402653184 | bytes 8388608 | tf_op jit(solution)/shard_map/probe_and_send/pallas_call | solution.py:297
  161.0 3.6 %panel_keep.3 = f32[8,64,1024]{2,1,0:T(8,128)S(1)} custom-call(s32[1]{0:T(128)} %bitcast.me, f32[64,384]{1,0:T(8,128)S(1)} %get-tuple-element.124.probed, s32[1,384]{1,0:T(1,128)S(1)} %reshape.76.counts.refs_9_.refs_17_, bf16[384,16384]{1,0:T(8,128)(2,1)} %acts.7), custom_call_target="tpu_custom_call" | custom-call | flops 402653184 | bytes 8388608 | tf_op jit(solution)/shard_map/panel_keep/pallas_call | solution.py:339
  166.5 3.3 %collective-permute-done.42 = f32[64,64]{1,0:T(8,128)S(1)} collective-permute-done((f32[64,64]{1,0:T(8,128)S(1)}, f32[64,64]{1,0:T(8,128)S(1)}, u32[]{:S(2)}, u32[]{:S(2)}) %collective-permute-start.42) | collective-permute-done | bytes 16416 | tf_op jit(solution)/shard_map/ppermute | solution.py:62
  169.8 1.9 collective-permute-start.43
  172.6 2.6 %collective-permute-done.43 = f32[64,64]{1,0:T(8,128)S(1)} collective-permute-done((f32[64,64]{1,0:T(8,128)S(1)}, f32[64,64]{1,0:T(8,128)S(1)}, u32[]{:S(2)}, u32[]{:S(2)}) %collective-permute-start.43) | collective-permute-done | bytes 16416 | tf_op jit(solution)/shard_map/ppermute | solution.py:62
  175.4 3.8 %collective-permute-done.40 = f16[2,2,32,1024]{3,2,0,1:T(8,128)(2,1)S(1)} collective-permute-done((f16[2,2,32,1024]{3,2,0,1:T(8,128)(2,1)S(1)}, f16[2,2,32,1024]{3,2,0,1:T(8,128)(2,1)S(1)}, u32[]{:S(2)}, u32[]{:S(2)}) %collective-permute-start.40) | collective-permute-done | bytes 262176 | tf_op jit(solution)/shard_map/ppermute | solution.py:62
  180.2 2.4 %collective-permute-start.45 = (f16[2,32,1024]{2,1,0:T(8,128)(2,1)S(1)}, f16[2,32,1024]{2,1,0:T(8,128)(2,1)S(1)}, u32[]{:S(2)}, u32[]{:S(2)}) collective-permute-start(f16[2,32,1024]{2,1,0:T(8,128)(2,1)S(1)} %multiply_convert_fusion.6), channel_id=1, source_target_pairs={{0,8},{1,9},{2,10},{3,11},{4,12},{5,13},{6,14},{7,15},{8,0},{9,1},... | collective-permute-start | bytes 393224 | tf_op jit(solution)/shard_map/ppermute | solution.py:62
  183.0 2.5 %before.1 = (f32[64,64]{1,0:T(8,128)}, f32[64,64]{1,0:T(8,128)}) custom-call(f32[64,64]{1,0:T(8,128)} %copy-done, f32[64,64]{1,0:T(8,128)} %copy-done.4, f32[64,64]{1,0:T(8,128)} %copy-done.6, f32[64,64]{1,0:T(8,128)} %copy-done.5, f32[1,1]{1,0:T(1,128)} %bitcast.21.refs_10_.total_weight.refs_18_), custom_call_target="tpu_custom_call" | custom-call | flops 67108864 | bytes 1048576 | tf_op jit(solution)/shard_map/before/pallas_call | solution.py:399
  186.1 2.1 %collective-permute-done.45 = f16[2,32,1024]{2,1,0:T(8,128)(2,1)S(1)} collective-permute-done((f16[2,32,1024]{2,1,0:T(8,128)(2,1)S(1)}, f16[2,32,1024]{2,1,0:T(8,128)(2,1)S(1)}, u32[]{:S(2)}, u32[]{:S(2)}) %collective-permute-start.45) | collective-permute-done | bytes 131104 | tf_op jit(solution)/shard_map/ppermute | solution.py:62
  190.3 5.4 %last.1 = (f32[64,1024]{1,0:T(8,128)}, f32[64,1024]{1,0:T(8,128)}, f32[64,64]{1,0:T(8,128)}) custom-call(f32[64,64]{1,0:T(8,128)} %add.137.along, f32[64,64]{1,0:T(8,128)} %get-tuple-element.145.fixed, f32[64,64]{1,0:T(8,128)} %get-tuple-element.146.cross_t, f32[64,64]{1,0:T(8,128)} %copy-done.4, f32[64,64]{1,0:T(8,128)} %copy-done.5, ...), custom_call_target="tpu_custom_call" | custom-call | flops 67108864 | bytes 1048576 | tf_op jit(solution)/shard_map/last/pallas_call | solution.py:399
  197.2 2.1 %end.1 = f32[64,1024]{1,0:T(8,128)} custom-call(f32[64,1024]{1,0:T(8,128)} %get-tuple-element.148.rest, f32[64,64]{1,0:T(8,128)} %get-tuple-element.149.on_panel, f32[32,1024]{1,0:T(8,128)} %fusion.34.panel_a, f32[32,1024]{1,0:T(8,128)} %fusion.33.panel_b), custom_call_target="tpu_custom_call" | custom-call | flops 67108864 | bytes 1048576 | tf_op jit(solution)/shard_map/end/pallas_call | solution.py:399
  (180 shorter events, 41.8 us)
Async XLA Ops:
  6.2 4.5 %collective-permute-start = (f16[8,64,1024]{2,1,0:T(8,128)(2,1)S(1)}, f16[8,64,1024]{2,1,0:T(8,128)(2,1)S(1)}, u32[]{:S(2)}, u32[]{:S(2)}) collective-permute-start(f16[8,64,1024]{2,1,0:T(8,128)(2,1)S(1)} %fusion), channel_id=1, source_target_pairs={{0,1},{1,0},{2,3},{3,2},{4,5},{5,4},{6,7},{7,6},{8,9},{9,8},{10,11... | collective-permute-start | bytes 3145736 | tf_op jit(solution)/shard_map/ppermute | solution.py:62
  6.9 3.8 %collective-permute-start.1 = (f32[1,64]{1,0:T(1,128)S(1)}, f32[1,64]{1,0:T(1,128)S(1)}, u32[]{:S(2)}, u32[]{:S(2)}) collective-permute-start(f32[1,64]{1,0:T(1,128)S(1)} %bitcast.173), channel_id=1, source_target_pairs={{0,1},{1,0},{2,3},{3,2},{4,5},{5,4},{6,7},{7,6},{8,9},{9,8},{10,11... | collective-permute-start | bytes 776 | tf_op jit(solution)/shard_map/ppermute | solution.py:62
  12.0 10.2 %collective-permute-start.3 = (f16[2,2,32,1024]{3,2,0,1:T(8,128)(2,1)S(1)}, f16[2,2,32,1024]{3,2,0,1:T(8,128)(2,1)S(1)}, u32[]{:S(2)}, u32[]{:S(2)}) collective-permute-start(f16[2,2,32,1024]{3,2,0,1:T(8,128)(2,1)S(1)} %fusion.6), channel_id=1, source_target_pairs={{0,4},{1,5},{2,6},{3,7},{4,0},{5,1},{6,2},{7,3},{8,12},{9,13},{10,... | collective-permute-start | bytes 786440 | tf_op jit(solution)/shard_map/ppermute | solution.py:62
  15.1 3.5 %collective-permute-start.4 = (f32[1,64]{1,0:T(1,128)S(1)}, f32[1,64]{1,0:T(1,128)S(1)}, u32[]{:S(2)}, u32[]{:S(2)}) collective-permute-start(f32[1,64]{1,0:T(1,128)S(1)} %bitcast_add_fusion), channel_id=1, source_target_pairs={{0,2},{1,3},{2,0},{3,1},{4,6},{5,7},{6,4},{7,5},{8,10},{9,11},{10,... | collective-permute-start | bytes 776 | tf_op jit(solution)/shard_map/ppermute | solution.py:62
  19.0 7.1 %collective-permute-start.2 = (f16[2,2,32,1024]{3,2,0,1:T(8,128)(2,1)S(1)}, f16[2,2,32,1024]{3,2,0,1:T(8,128)(2,1)S(1)}, u32[]{:S(2)}, u32[]{:S(2)}) collective-permute-start(f16[2,2,32,1024]{3,2,0,1:T(8,128)(2,1)S(1)} %fusion.3), channel_id=1, source_target_pairs={{0,2},{1,3},{2,0},{3,1},{4,6},{5,7},{6,4},{7,5},{8,10},{9,11},{10,... | collective-permute-start | bytes 786440 | tf_op jit(solution)/shard_map/ppermute | solution.py:62
  26.2 5.1 %collective-permute-start.8 = (f32[1,64]{1,0:T(1,128)S(1)}, f32[1,64]{1,0:T(1,128)S(1)}, u32[]{:S(2)}, u32[]{:S(2)}) collective-permute-start(f32[1,64]{1,0:T(1,128)S(1)} %add.110), channel_id=1, source_target_pairs={{0,8},{1,9},{2,10},{3,11},{4,12},{5,13},{6,14},{7,15},{8,0},{9,1},... | collective-permute-start | bytes 776 | tf_op jit(solution)/shard_map/ppermute | solution.py:62
  29.0 7.4 %collective-permute-start.7 = (f16[2,32,1024]{2,1,0:T(8,128)(2,1)S(1)}, f16[2,32,1024]{2,1,0:T(8,128)(2,1)S(1)}, u32[]{:S(2)}, u32[]{:S(2)}) collective-permute-start(f16[2,32,1024]{2,1,0:T(8,128)(2,1)S(1)} %fusion.16), channel_id=1, source_target_pairs={{0,8},{1,9},{2,10},{3,11},{4,12},{5,13},{6,14},{7,15},{8,0},{9,1},... | collective-permute-start | bytes 393224 | tf_op jit(solution)/shard_map/ppermute | solution.py:62
  29.5 6.9 %collective-permute-start.6 = (f16[2,32,1024]{2,1,0:T(8,128)(2,1)S(1)}, f16[2,32,1024]{2,1,0:T(8,128)(2,1)S(1)}, u32[]{:S(2)}, u32[]{:S(2)}) collective-permute-start(f16[2,32,1024]{2,1,0:T(8,128)(2,1)S(1)} %fusion.13), channel_id=1, source_target_pairs={{0,4},{1,5},{2,6},{3,7},{4,0},{5,1},{6,2},{7,3},{8,12},{9,13},{10,... | collective-permute-start | bytes 393224 | tf_op jit(solution)/shard_map/ppermute | solution.py:62
  37.3 7.2 %collective-permute-start.9 = (f16[32,1024]{1,0:T(8,128)(2,1)S(1)}, f16[32,1024]{1,0:T(8,128)(2,1)S(1)}, u32[]{:S(2)}, u32[]{:S(2)}) collective-permute-start(f16[32,1024]{1,0:T(8,128)(2,1)S(1)} %fusion.23), channel_id=1, source_target_pairs={{0,8},{1,9},{2,10},{3,11},{4,12},{5,13},{6,14},{7,15},{8,0},{9,1},... | collective-permute-start | bytes 196616 | tf_op jit(solution)/shard_map/ppermute | solution.py:62
  39.1 6.3 %collective-permute-start.14 = (f16[32,1024]{1,0:T(8,128)(2,1)S(1)}, f16[32,1024]{1,0:T(8,128)(2,1)S(1)}, u32[]{:S(2)}, u32[]{:S(2)}) collective-permute-start(f16[32,1024]{1,0:T(8,128)(2,1)S(1)} %fusion.28), channel_id=1, source_target_pairs={{0,2},{1,3},{2,0},{3,1},{4,6},{5,7},{6,4},{7,5},{8,10},{9,11},{10,... | collective-permute-start | bytes 196616 | tf_op jit(solution)/shard_map/ppermute | solution.py:62
  45.2 7.5 %collective-permute-start.10 = (bf16[1,32,1024]{2,1,0:T(8,128)(2,1)S(1)}, bf16[1,32,1024]{2,1,0:T(8,128)(2,1)S(1)}, u32[]{:S(2)}, u32[]{:S(2)}) collective-permute-start(bf16[1,32,1024]{2,1,0:T(8,128)(2,1)S(1)} %get-tuple-element.170), channel_id=1, source_target_pairs={{0,8},{1,9},{2,10},{3,11},{4,12},{5,13},{6,14},{7,15},{8,0},{9,1},... | collective-permute-start | bytes 196616 | tf_op jit(solution)/shard_map/ppermute | solution.py:62
  46.1 6.7 %collective-permute-start.15 = (bf16[1,32,1024]{2,1,0:T(8,128)(2,1)S(1)}, bf16[1,32,1024]{2,1,0:T(8,128)(2,1)S(1)}, u32[]{:S(2)}, u32[]{:S(2)}) collective-permute-start(bf16[1,32,1024]{2,1,0:T(8,128)(2,1)S(1)} %get-tuple-element.168), channel_id=1, source_target_pairs={{0,4},{1,5},{2,6},{3,7},{4,0},{5,1},{6,2},{7,3},{8,12},{9,13},{10,... | collective-permute-start | bytes 196616 | tf_op jit(solution)/shard_map/ppermute | solution.py:62
  52.8 6.4 %collective-permute-start.11 = (bf16[2,32,1024]{2,1,0:T(8,128)(2,1)S(1)}, bf16[2,32,1024]{2,1,0:T(8,128)(2,1)S(1)}, u32[]{:S(2)}, u32[]{:S(2)}) collective-permute-start(bf16[2,32,1024]{2,1,0:T(8,128)(2,1)S(1)} %pad_maximum_fusion.6), channel_id=1, source_target_pairs={{0,4},{1,5},{2,6},{3,7},{4,0},{5,1},{6,2},{7,3},{8,12},{9,13},{10,... | collective-permute-start | bytes 393224 | tf_op jit(solution)/shard_map/ppermute | solution.py:62
  52.9 7.9 %collective-permute-start.16 = (bf16[2,32,1024]{2,1,0:T(8,128)(2,1)S(1)}, bf16[2,32,1024]{2,1,0:T(8,128)(2,1)S(1)}, u32[]{:S(2)}, u32[]{:S(2)}) collective-permute-start(bf16[2,32,1024]{2,1,0:T(8,128)(2,1)S(1)} %pad_maximum_fusion.7), channel_id=1, source_target_pairs={{0,8},{1,9},{2,10},{3,11},{4,12},{5,13},{6,14},{7,15},{8,0},{9,1},... | collective-permute-start | bytes 393224 | tf_op jit(solution)/shard_map/ppermute | solution.py:62
  59.2 6.4 %collective-permute-start.12 = (bf16[4,32,1024]{2,1,0:T(8,128)(2,1)S(1)}, bf16[4,32,1024]{2,1,0:T(8,128)(2,1)S(1)}, u32[]{:S(2)}, u32[]{:S(2)}) collective-permute-start(bf16[4,32,1024]{2,1,0:T(8,128)(2,1)S(1)} %pad_maximum_fusion.2), channel_id=1, source_target_pairs={{0,2},{1,3},{2,0},{3,1},{4,6},{5,7},{6,4},{7,5},{8,10},{9,11},{10,... | collective-permute-start | bytes 786440 | tf_op jit(solution)/shard_map/ppermute | solution.py:62
  60.9 7.6 %collective-permute-start.17 = (bf16[4,32,1024]{2,1,0:T(8,128)(2,1)S(1)}, bf16[4,32,1024]{2,1,0:T(8,128)(2,1)S(1)}, u32[]{:S(2)}, u32[]{:S(2)}) collective-permute-start(bf16[4,32,1024]{2,1,0:T(8,128)(2,1)S(1)} %pad_maximum_fusion.3), channel_id=1, source_target_pairs={{0,2},{1,3},{2,0},{3,1},{4,6},{5,7},{6,4},{7,5},{8,10},{9,11},{10,... | collective-permute-start | bytes 786440 | tf_op jit(solution)/shard_map/ppermute | solution.py:62
  65.7 8.0 %collective-permute-start.13 = (bf16[8,32,1024]{2,1,0:T(8,128)(2,1)S(1)}, bf16[8,32,1024]{2,1,0:T(8,128)(2,1)S(1)}, u32[]{:S(2)}, u32[]{:S(2)}) collective-permute-start(bf16[8,32,1024]{2,1,0:T(8,128)(2,1)S(1)} %pad_maximum_fusion.refs_0_.refs_2_.refs_4_.refs_6_.refs_8_.refs_10_.refs_12_.refs_14_), channel_id=1, source_target_pairs={{0,1},{1,0},{2,3},{3,2},{4,5},{5,4},{6,7},{7,6},{8,9},{9,8},{10,11... | collective-permute-start | bytes 1572872 | tf_op jit(solution)/shard_map/ppermute | solution.py:62
  68.5 5.2 %collective-permute-start.18 = (bf16[8,32,1024]{2,1,0:T(8,128)(2,1)S(1)}, bf16[8,32,1024]{2,1,0:T(8,128)(2,1)S(1)}, u32[]{:S(2)}, u32[]{:S(2)}) collective-permute-start(bf16[8,32,1024]{2,1,0:T(8,128)(2,1)S(1)} %pad_maximum_fusion.1.refs_1_.refs_3_.refs_5_.refs_7_.refs_9_.refs_11_.refs_13_.refs_15_), channel_id=1, source_target_pairs={{0,1},{1,0},{2,3},{3,2},{4,5},{5,4},{6,7},{7,6},{8,9},{9,8},{10,11... | collective-permute-start | bytes 1572872 | tf_op jit(solution)/shard_map/ppermute | solution.py:62
  81.7 4.3 %collective-permute-start.19 = (f16[8,64,1024]{2,1,0:T(8,128)(2,1)S(1)}, f16[8,64,1024]{2,1,0:T(8,128)(2,1)S(1)}, u32[]{:S(2)}, u32[]{:S(2)}) collective-permute-start(f16[8,64,1024]{2,1,0:T(8,128)(2,1)S(1)} %multiply_convert_fusion.1), channel_id=1, source_target_pairs={{0,1},{1,0},{2,3},{3,2},{4,5},{5,4},{6,7},{7,6},{8,9},{9,8},{10,11... | collective-permute-start | bytes 3145736 | tf_op jit(solution)/shard_map/ppermute | solution.py:62
  82.2 3.8 %collective-permute-start.20 = (f32[64,64]{1,0:T(8,128)S(1)}, f32[64,64]{1,0:T(8,128)S(1)}, u32[]{:S(2)}, u32[]{:S(2)}) collective-permute-start(f32[64,64]{1,0:T(8,128)S(1)} %get-tuple-element.94), channel_id=1, source_target_pairs={{0,1},{1,0},{2,3},{3,2},{4,5},{5,4},{6,7},{7,6},{8,9},{9,8},{10,11... | collective-permute-start | bytes 49160 | tf_op jit(solution)/shard_map/ppermute | solution.py:62
  87.1 9.4 %collective-permute-start.22 = (f16[2,2,32,1024]{3,2,1,0:T(8,128)(2,1)S(1)}, f16[2,2,32,1024]{3,2,1,0:T(8,128)(2,1)S(1)}, u32[]{:S(2)}, u32[]{:S(2)}) collective-permute-start(f16[2,2,32,1024]{3,2,1,0:T(8,128)(2,1)S(1)} %multiply_convert_fusion.4), channel_id=1, source_target_pairs={{0,4},{1,5},{2,6},{3,7},{4,0},{5,1},{6,2},{7,3},{8,12},{9,13},{10,... | collective-permute-start | bytes 786440 | tf_op jit(solution)/shard_map/ppermute | solution.py:62
  87.1 4.0 %collective-permute-start.23 = (f32[64,64]{1,0:T(8,128)S(1)}, f32[64,64]{1,0:T(8,128)S(1)}, u32[]{:S(2)}, u32[]{:S(2)}) collective-permute-start(f32[64,64]{1,0:T(8,128)S(1)} %add.117), channel_id=1, source_target_pairs={{0,2},{1,3},{2,0},{3,1},{4,6},{5,7},{6,4},{7,5},{8,10},{9,11},{10,... | collective-permute-start | bytes 49160 | tf_op jit(solution)/shard_map/ppermute | solution.py:62
  91.1 5.4 %collective-permute-start.24 = (f32[64,64]{1,0:T(8,128)S(1)}, f32[64,64]{1,0:T(8,128)S(1)}, u32[]{:S(2)}, u32[]{:S(2)}) collective-permute-start(f32[64,64]{1,0:T(8,128)S(1)} %add.120), channel_id=1, source_target_pairs={{0,4},{1,5},{2,6},{3,7},{4,0},{5,1},{6,2},{7,3},{8,12},{9,13},{10,... | collective-permute-start | bytes 49160 | tf_op jit(solution)/shard_map/ppermute | solution.py:62
  93.2 7.3 %collective-permute-start.21 = (f16[2,2,32,1024]{3,2,0,1:T(8,128)(2,1)S(1)}, f16[2,2,32,1024]{3,2,0,1:T(8,128)(2,1)S(1)}, u32[]{:S(2)}, u32[]{:S(2)}) collective-permute-start(f16[2,2,32,1024]{3,2,0,1:T(8,128)(2,1)S(1)} %multiply_convert_fusion.5), channel_id=1, source_target_pairs={{0,2},{1,3},{2,0},{3,1},{4,6},{5,7},{6,4},{7,5},{8,10},{9,11},{10,... | collective-permute-start | bytes 786440 | tf_op jit(solution)/shard_map/ppermute | solution.py:62
  100.7 6.8 %collective-permute-start.27 = (f32[64,64]{1,0:T(8,128)S(1)}, f32[64,64]{1,0:T(8,128)S(1)}, u32[]{:S(2)}, u32[]{:S(2)}) collective-permute-start(f32[64,64]{1,0:T(8,128)S(1)} %add.121), channel_id=1, source_target_pairs={{0,8},{1,9},{2,10},{3,11},{4,12},{5,13},{6,14},{7,15},{8,0},{9,1},... | collective-permute-start | bytes 49160 | tf_op jit(solution)/shard_map/ppermute | solution.py:62
  102.5 8.2 %collective-permute-start.26 = (f16[2,32,1024]{2,1,0:T(8,128)(2,1)}, f16[2,32,1024]{2,1,0:T(8,128)(2,1)}, u32[]{:S(2)}, u32[]{:S(2)}) collective-permute-start(f16[2,32,1024]{2,1,0:T(8,128)(2,1)} %multiply_convert_fusion.8), channel_id=1, source_target_pairs={{0,8},{1,9},{2,10},{3,11},{4,12},{5,13},{6,14},{7,15},{8,0},{9,1},... | collective-permute-start | bytes 393224 | tf_op jit(solution)/shard_map/ppermute | solution.py:62
  104.5 7.2 %collective-permute-start.25 = (f16[2,32,1024]{2,1,0:T(8,128)(2,1)S(1)}, f16[2,32,1024]{2,1,0:T(8,128)(2,1)}, u32[]{:S(2)}, u32[]{:S(2)}) collective-permute-start(f16[2,32,1024]{2,1,0:T(8,128)(2,1)S(1)} %multiply_convert_fusion.9), channel_id=1, source_target_pairs={{0,4},{1,5},{2,6},{3,7},{4,0},{5,1},{6,2},{7,3},{8,12},{9,13},{10,... | collective-permute-start | bytes 393224 | tf_op jit(solution)/shard_map/ppermute | solution.py:62
  112.9 4.3 %collective-permute-start.30 = (f16[32,1024]{1,0:T(8,128)(2,1)S(1)}, f16[32,1024]{1,0:T(8,128)(2,1)S(1)}, u32[]{:S(2)}, u32[]{:S(2)}) collective-permute-start(f16[32,1024]{1,0:T(8,128)(2,1)S(1)} %multiply_convert_fusion.12), channel_id=1, source_target_pairs={{0,2},{1,3},{2,0},{3,1},{4,6},{5,7},{6,4},{7,5},{8,10},{9,11},{10,... | collective-permute-start | bytes 196616 | tf_op jit(solution)/shard_map/ppermute | solution.py:62
  114.4 5.2 %collective-permute-start.28 = (f16[32,1024]{1,0:T(8,128)(2,1)S(1)}, f16[32,1024]{1,0:T(8,128)(2,1)S(1)}, u32[]{:S(2)}, u32[]{:S(2)}) collective-permute-start(f16[32,1024]{1,0:T(8,128)(2,1)S(1)} %multiply_convert_fusion.13), channel_id=1, source_target_pairs={{0,8},{1,9},{2,10},{3,11},{4,12},{5,13},{6,14},{7,15},{8,0},{9,1},... | collective-permute-start | bytes 196616 | tf_op jit(solution)/shard_map/ppermute | solution.py:62
  120.9 6.2 %collective-permute-start.31 = (bf16[1,32,1024]{2,1,0:T(8,128)(2,1)S(1)}, bf16[1,32,1024]{2,1,0:T(8,128)(2,1)S(1)}, u32[]{:S(2)}, u32[]{:S(2)}) collective-permute-start(bf16[1,32,1024]{2,1,0:T(8,128)(2,1)S(1)} %get-tuple-element.164), channel_id=1, source_target_pairs={{0,4},{1,5},{2,6},{3,7},{4,0},{5,1},{6,2},{7,3},{8,12},{9,13},{10,... | collective-permute-start | bytes 196616 | tf_op jit(solution)/shard_map/ppermute | solution.py:62
  120.9 6.2 %collective-permute-start.29 = (bf16[1,32,1024]{2,1,0:T(8,128)(2,1)S(1)}, bf16[1,32,1024]{2,1,0:T(8,128)(2,1)S(1)}, u32[]{:S(2)}, u32[]{:S(2)}) collective-permute-start(bf16[1,32,1024]{2,1,0:T(8,128)(2,1)S(1)} %get-tuple-element.186), channel_id=1, source_target_pairs={{0,8},{1,9},{2,10},{3,11},{4,12},{5,13},{6,14},{7,15},{8,0},{9,1},... | collective-permute-start | bytes 196616 | tf_op jit(solution)/shard_map/ppermute | solution.py:62
  127.1 6.9 %collective-permute-start.32 = (bf16[2,32,1024]{2,1,0:T(8,128)(2,1)S(1)}, bf16[2,32,1024]{2,1,0:T(8,128)(2,1)S(1)}, u32[]{:S(2)}, u32[]{:S(2)}) collective-permute-start(bf16[2,32,1024]{2,1,0:T(8,128)(2,1)S(1)} %pad_maximum_fusion.8), channel_id=1, source_target_pairs={{0,4},{1,5},{2,6},{3,7},{4,0},{5,1},{6,2},{7,3},{8,12},{9,13},{10,... | collective-permute-start | bytes 393224 | tf_op jit(solution)/shard_map/ppermute | solution.py:62
  129.1 7.3 %collective-permute-start.33 = (bf16[2,32,1024]{2,1,0:T(8,128)(2,1)S(1)}, bf16[2,32,1024]{2,1,0:T(8,128)(2,1)S(1)}, u32[]{:S(2)}, u32[]{:S(2)}) collective-permute-start(bf16[2,32,1024]{2,1,0:T(8,128)(2,1)S(1)} %pad_maximum_fusion.9), channel_id=1, source_target_pairs={{0,8},{1,9},{2,10},{3,11},{4,12},{5,13},{6,14},{7,15},{8,0},{9,1},... | collective-permute-start | bytes 393224 | tf_op jit(solution)/shard_map/ppermute | solution.py:62
  136.4 6.4 %collective-permute-start.36 = (bf16[4,32,1024]{2,1,0:T(8,128)(2,1)S(1)}, bf16[4,32,1024]{2,1,0:T(8,128)(2,1)S(1)}, u32[]{:S(2)}, u32[]{:S(2)}) collective-permute-start(bf16[4,32,1024]{2,1,0:T(8,128)(2,1)S(1)} %pad_maximum_fusion.5), channel_id=1, source_target_pairs={{0,2},{1,3},{2,0},{3,1},{4,6},{5,7},{6,4},{7,5},{8,10},{9,11},{10,... | collective-permute-start | bytes 786440 | tf_op jit(solution)/shard_map/ppermute | solution.py:62
  137.0 8.6 %collective-permute-start.34 = (bf16[4,32,1024]{2,1,0:T(8,128)(2,1)S(1)}, bf16[4,32,1024]{2,1,0:T(8,128)(2,1)S(1)}, u32[]{:S(2)}, u32[]{:S(2)}) collective-permute-start(bf16[4,32,1024]{2,1,0:T(8,128)(2,1)S(1)} %pad_maximum_fusion.4), channel_id=1, source_target_pairs={{0,2},{1,3},{2,0},{3,1},{4,6},{5,7},{6,4},{7,5},{8,10},{9,11},{10,... | collective-permute-start | bytes 786440 | tf_op jit(solution)/shard_map/ppermute | solution.py:62
  142.8 8.0 %collective-permute-start.37 = (bf16[8,32,1024]{2,1,0:T(8,128)(2,1)S(1)}, bf16[8,32,1024]{2,1,0:T(8,128)(2,1)S(1)}, u32[]{:S(2)}, u32[]{:S(2)}) collective-permute-start(bf16[8,32,1024]{2,1,0:T(8,128)(2,1)S(1)} %constant_dynamic-update-slice_fusion.2.refs_1_.refs_3_.refs_5_.refs_7_), channel_id=1, source_target_pairs={{0,1},{1,0},{2,3},{3,2},{4,5},{5,4},{6,7},{7,6},{8,9},{9,8},{10,11... | collective-permute-start | bytes 1572872 | tf_op jit(solution)/shard_map/ppermute | solution.py:62
  145.7 5.2 %collective-permute-start.35 = (bf16[8,32,1024]{2,1,0:T(8,128)(2,1)S(1)}, bf16[8,32,1024]{2,1,0:T(8,128)(2,1)S(1)}, u32[]{:S(2)}, u32[]{:S(2)}) collective-permute-start(bf16[8,32,1024]{2,1,0:T(8,128)(2,1)S(1)} %constant_dynamic-update-slice_fusion.refs_0_.refs_2_.refs_4_.refs_6_), channel_id=1, source_target_pairs={{0,1},{1,0},{2,3},{3,2},{4,5},{5,4},{6,7},{7,6},{8,9},{9,8},{10,11... | collective-permute-start | bytes 1572872 | tf_op jit(solution)/shard_map/ppermute | solution.py:62
  160.3 4.4 %collective-permute-start.38 = (f16[8,64,1024]{2,1,0:T(8,128)(2,1)S(1)}, f16[8,64,1024]{2,1,0:T(8,128)(2,1)S(1)}, u32[]{:S(2)}, u32[]{:S(2)}) collective-permute-start(f16[8,64,1024]{2,1,0:T(8,128)(2,1)S(1)} %multiply_convert_fusion), channel_id=1, source_target_pairs={{0,1},{1,0},{2,3},{3,2},{4,5},{5,4},{6,7},{7,6},{8,9},{9,8},{10,11... | collective-permute-start | bytes 3145736 | tf_op jit(solution)/shard_map/ppermute | solution.py:62
  160.8 3.8 %collective-permute-start.39 = (f32[64,64]{1,0:T(8,128)S(1)}, f32[64,64]{1,0:T(8,128)S(1)}, u32[]{:S(2)}, u32[]{:S(2)}) collective-permute-start(f32[64,64]{1,0:T(8,128)S(1)} %get-tuple-element.127), channel_id=1, source_target_pairs={{0,1},{1,0},{2,3},{3,2},{4,5},{5,4},{6,7},{7,6},{8,9},{9,8},{10,11... | collective-permute-start | bytes 49160 | tf_op jit(solution)/shard_map/ppermute | solution.py:62
  165.8 9.4 %collective-permute-start.41 = (f16[2,2,32,1024]{3,2,1,0:T(8,128)(2,1)S(1)}, f16[2,2,32,1024]{3,2,1,0:T(8,128)(2,1)S(1)}, u32[]{:S(2)}, u32[]{:S(2)}) collective-permute-start(f16[2,2,32,1024]{3,2,1,0:T(8,128)(2,1)S(1)} %multiply_convert_fusion.2), channel_id=1, source_target_pairs={{0,4},{1,5},{2,6},{3,7},{4,0},{5,1},{6,2},{7,3},{8,12},{9,13},{10,... | collective-permute-start | bytes 786440 | tf_op jit(solution)/shard_map/ppermute | solution.py:62
  165.9 4.0 %collective-permute-start.42 = (f32[64,64]{1,0:T(8,128)S(1)}, f32[64,64]{1,0:T(8,128)S(1)}, u32[]{:S(2)}, u32[]{:S(2)}) collective-permute-start(f32[64,64]{1,0:T(8,128)S(1)} %add.130), channel_id=1, source_target_pairs={{0,2},{1,3},{2,0},{3,1},{4,6},{5,7},{6,4},{7,5},{8,10},{9,11},{10,... | collective-permute-start | bytes 49160 | tf_op jit(solution)/shard_map/ppermute | solution.py:62
  169.8 5.3 %collective-permute-start.43 = (f32[64,64]{1,0:T(8,128)S(1)}, f32[64,64]{1,0:T(8,128)S(1)}, u32[]{:S(2)}, u32[]{:S(2)}) collective-permute-start(f32[64,64]{1,0:T(8,128)S(1)} %add.133), channel_id=1, source_target_pairs={{0,4},{1,5},{2,6},{3,7},{4,0},{5,1},{6,2},{7,3},{8,12},{9,13},{10,... | collective-permute-start | bytes 49160 | tf_op jit(solution)/shard_map/ppermute | solution.py:62
  171.9 7.3 %collective-permute-start.40 = (f16[2,2,32,1024]{3,2,0,1:T(8,128)(2,1)S(1)}, f16[2,2,32,1024]{3,2,0,1:T(8,128)(2,1)S(1)}, u32[]{:S(2)}, u32[]{:S(2)}) collective-permute-start(f16[2,2,32,1024]{3,2,0,1:T(8,128)(2,1)S(1)} %multiply_convert_fusion.3), channel_id=1, source_target_pairs={{0,2},{1,3},{2,0},{3,1},{4,6},{5,7},{6,4},{7,5},{8,10},{9,11},{10,... | collective-permute-start | bytes 786440 | tf_op jit(solution)/shard_map/ppermute | solution.py:62
  179.4 6.1 %collective-permute-start.46 = (f32[64,64]{1,0:T(8,128)S(1)}, f32[64,64]{1,0:T(8,128)S(1)}, u32[]{:S(2)}, u32[]{:S(2)}) collective-permute-start(f32[64,64]{1,0:T(8,128)S(1)} %add.134), channel_id=1, source_target_pairs={{0,8},{1,9},{2,10},{3,11},{4,12},{5,13},{6,14},{7,15},{8,0},{9,1},... | collective-permute-start | bytes 49160 | tf_op jit(solution)/shard_map/ppermute | solution.py:62
  180.2 8.0 %collective-permute-start.45 = (f16[2,32,1024]{2,1,0:T(8,128)(2,1)S(1)}, f16[2,32,1024]{2,1,0:T(8,128)(2,1)S(1)}, u32[]{:S(2)}, u32[]{:S(2)}) collective-permute-start(f16[2,32,1024]{2,1,0:T(8,128)(2,1)S(1)} %multiply_convert_fusion.6), channel_id=1, source_target_pairs={{0,8},{1,9},{2,10},{3,11},{4,12},{5,13},{6,14},{7,15},{8,0},{9,1},... | collective-permute-start | bytes 393224 | tf_op jit(solution)/shard_map/ppermute | solution.py:62
  182.6 5.7 %collective-permute-start.44 = (f16[2,32,1024]{2,1,0:T(8,128)(2,1)S(1)}, f16[2,32,1024]{2,1,0:T(8,128)(2,1)S(1)}, u32[]{:S(2)}, u32[]{:S(2)}) collective-permute-start(f16[2,32,1024]{2,1,0:T(8,128)(2,1)S(1)} %multiply_convert_fusion.7), channel_id=1, source_target_pairs={{0,4},{1,5},{2,6},{3,7},{4,0},{5,1},{6,2},{7,3},{8,12},{9,13},{10,... | collective-permute-start | bytes 393224 | tf_op jit(solution)/shard_map/ppermute | solution.py:62
  188.5 7.2 %collective-permute-start.48 = (f16[32,1024]{1,0:T(8,128)(2,1)S(1)}, f16[32,1024]{1,0:T(8,128)(2,1)S(1)}, u32[]{:S(2)}, u32[]{:S(2)}) collective-permute-start(f16[32,1024]{1,0:T(8,128)(2,1)S(1)} %multiply_convert_fusion.10), channel_id=1, source_target_pairs={{0,2},{1,3},{2,0},{3,1},{4,6},{5,7},{6,4},{7,5},{8,10},{9,11},{10,... | collective-permute-start | bytes 196616 | tf_op jit(solution)/shard_map/ppermute | solution.py:62
  189.3 7.2 %collective-permute-start.47 = (f16[32,1024]{1,0:T(8,128)(2,1)S(1)}, f16[32,1024]{1,0:T(8,128)(2,1)S(1)}, u32[]{:S(2)}, u32[]{:S(2)}) collective-permute-start(f16[32,1024]{1,0:T(8,128)(2,1)S(1)} %multiply_convert_fusion.11), channel_id=1, source_target_pairs={{0,8},{1,9},{2,10},{3,11},{4,12},{5,13},{6,14},{7,15},{8,0},{9,1},... | collective-permute-start | bytes 196616 | tf_op jit(solution)/shard_map/ppermute | solution.py:62
  (9 other events, 46.7 us)

commit v6 on v5

--- a/solution.py
+++ b/solution.py
@@ -95,7 +95,7 @@
 HBM = pl.BlockSpec(memory_space=pltpu.HBM)
 
 
-def call(kernel, name, n, grid, in_specs, out_shapes, out_specs, acts, scratch=()):
+def call(kernel, name, n, grid, in_specs, out_shapes, out_specs, acts, scratch=(), aliases=None):
     rows, d = acts.shape
     return pl.pallas_call(
         kernel,
@@ -113,18 +113,24 @@
         ),
         compiler_params=pltpu.CompilerParams(vmem_limit_bytes=20 << 20),
         cost_estimate=pl.CostEstimate(flops=K * rows * d, bytes_accessed=rows * d + 2 * K * d, transcendentals=0),
+        input_output_aliases=aliases or {},
         name=name,
     )
 
 
-def sums_kernel(half, me, labels, counts, acts, out, weight, kept, sems, member):
+def count_of(row_data):
+    return lax.shift_right_logical(row_data[...], 6).astype(F32)
+
+
+def sums_kernel(half, me, row_data, acts, out, weight, kept, sems, member):
     step = pl.program_id(0)
 
     @pl.when(step == 0)
     def _():
         start_copies(acts, kept, sems, me, half)
         concept = lax.broadcasted_iota(jnp.int32, member.shape, 0)
-        full = jnp.where(labels[...] == concept, counts[...].astype(F32), 0.0)
+        label = row_data[...] & (K - 1)
+        full = jnp.where(label == concept, count_of(row_data), 0.0)
         member[...] = full.astype(BF16)
         weight[...] = jnp.sum(full, axis=1, keepdims=True)
 
@@ -134,7 +140,7 @@
         out[u] = jnp.dot(member[...], kept[t], preferred_element_type=F32)
 
 
-def class_sums(me, labels, counts, acts, n, half):
+def class_sums(me, row_data, acts, n, half):
     rows, d = acts.shape
     f = d // n
     return call(
@@ -142,7 +148,7 @@
         "class_sums",
         n,
         n // 2 // UNROLL,
-        [whole(1, rows), whole(1, rows), HBM],
+        [whole(1, rows), HBM],
         (
             jax.ShapeDtypeStruct((n // 2, K, f), F32),
             jax.ShapeDtypeStruct((K, 1), F32),
@@ -150,7 +156,7 @@
         (pl.BlockSpec((UNROLL, K, f), lambda i, me: (i, 0, 0)), whole(K, 1)),
         acts,
         [pltpu.VMEM((K, rows), BF16)],
-    )(me, labels, counts, acts)
+    )(me, row_data, acts)
 
 
 def inner(left, right):
@@ -253,7 +259,7 @@
     panels, ins, starts, given, outs, grams, made, scratch = (
         [refs.pop(0) for _ in range(size)] for size in parts
     )
-    acts, counts, total_weight, start = ins
+    acts, row_data, total_weight, start = ins
     probed, along, bound, out = outs
     kept, sems, weighted, sum_of = scratch
     step = pl.program_id(0)
@@ -277,7 +283,7 @@
         probed[...] = sum_of[...].T
         norms = finish_second(probed, *grams, (*given, *made)) if second else finish_first(*grams)
         bound[...] = (1.02 * BOUND * BOUND * d**0.5) * total_weight[...] * norms
-        weighted[...] = (counts[...].astype(F32) * probed[...]).astype(BF16)
+        weighted[...] = (count_of(row_data) * probed[...]).astype(BF16)
         along[...] = outer(probed[...], weighted[...].astype(F32))
 
     @pl.when(step >= steps)
@@ -286,7 +292,7 @@
             out[u] = jnp.dot(weighted[...], kept[(step - steps) * UNROLL + u], preferred_element_type=F32)
 
 
-def probe_and_send(me, panels, acts, counts, total_weight, starts, given, n, shifts):
+def probe_and_send(me, panels, acts, row_data, total_weight, starts, given, n, shifts):
     rows, d = acts.shape
     f = d // n
     s = n // 2 // UNROLL
@@ -316,37 +322,48 @@
         + (whole(K, K),) * (count + made),
         acts,
         [pltpu.VMEM((K, rows), BF16), pltpu.VMEM((rows, K), F32)],
-    )(me, *operands, acts, counts, total_weight, *starts, *given)
-
-
-def keep_kernel(me, probed, counts, acts, out, kept, sems, weighted):
+    )(me, *operands, acts, row_data, total_weight, *starts, *given)
+
+
+def keep_kernel(base, me, probed, row_data, acts, *refs):
+    out, kept, sems, weighted = refs[-4:]
     step = pl.program_id(0)
 
+    def copy(t):
+        return block_copy(acts, kept, sems, me, 0, t)
+
     @pl.when(step == 0)
     def _():
-        start_copies(acts, kept, sems, me, 0)
-        weighted[...] = (counts[...].astype(F32) * probed[...]).astype(BF16)
+        lax.fori_loop(base, base + pl.num_programs(0) * UNROLL, lambda t, c: (copy(t).start(), c)[1], 0)
+        weighted[...] = (count_of(row_data) * probed[...]).astype(BF16)
 
     for u in range(UNROLL):
-        t = step * UNROLL + u
-        block_copy(acts, kept, sems, me, 0, t).wait()
+        t = base + step * UNROLL + u
+        copy(t).wait()
         out[u] = jnp.dot(weighted[...], kept[t], preferred_element_type=F32)
 
 
-def panel_keep(me, probed, counts, acts, n):
+def panel_keep(me, probed, row_data, acts, n, part=None, into=None):
     rows, d = acts.shape
     f = d // n
+    steps = n // 2 // UNROLL
+    first = 0
+    if part is not None:
+        steps //= 2
+        first = part * steps
+    more = () if into is None else (into,)
     return call(
-        keep_kernel,
+        functools.partial(keep_kernel, first * UNROLL),
         "panel_keep",
         n,
-        n // 2 // UNROLL,
-        [whole(K, rows), whole(1, rows), HBM],
+        steps,
+        [whole(K, rows), whole(1, rows), HBM] + [pl.BlockSpec(memory_space=pl.ANY)] * len(more),
         jax.ShapeDtypeStruct((n // 2, K, f), F32),
-        pl.BlockSpec((UNROLL, K, f), lambda i, me: (i, 0, 0)),
+        pl.BlockSpec((UNROLL, K, f), lambda i, me: (i + first, 0, 0)),
         acts,
         [pltpu.VMEM((K, rows), BF16)],
-    )(me, probed, counts, acts)
+        {4: 0} if more else {},
+    )(me, probed, row_data, acts, *more)
 
 
 def alpha_kernel(along, current, total_weight, alpha_t, inverse):
@@ -417,22 +434,21 @@
     return keep, send, [other for other in left if other != bit]
 
 
-def reduce_scatter(blocks, n, swap_a, swap_b, along, work=None, args=()):
+def reduce_scatter(blocks, n, swap_a, swap_b, along, waiting, work=None, args=()):
     bits = n.bit_length() - 2
     shape = (2,) * bits + (HALF, blocks.shape[2])
     a, b = blocks[:, :HALF].reshape(shape), blocks[:, HALF:].reshape(shape)
     left_a = left_b = [1 << i for i in range(bits, 0, -1)]
     order_a, order_b = hop_bits(n)
-    waiting, done = list(order_a), ()
+    waiting, done = list(waiting), ()
     for phase, (bit_a, bit_b) in enumerate(zip(order_a, order_b)):
         keep_a, send_a, left_a = split_blocks(a, left_a, bit_a)
         keep_b, send_b, left_b = split_blocks(b, left_b, bit_b)
         tied = args if phase == 1 else done
         send_a, send_b, along, tied = lax.optimization_barrier((send_a, send_b, along, tied))
         a, b = keep_a + swap_a(send_a, bit_a), keep_b + swap_b(send_b, bit_b)
-        for bit in waiting[:2]:
-            along = along + swap(along, bit, n)
-        waiting = waiting[2:]
+        if waiting:
+            along = along + swap(along, waiting.pop(0), n)
         if work is not None and phase >= 1:
             done = work(*tied) if phase == 1 else tied
     return a, b, along, done
@@ -452,9 +468,9 @@
     a, b = top.astype(BF16)[None], low.astype(BF16)[None]
     done = ()
     for phase, (bit_a, bit_b) in enumerate(zip(*orders)):
+        tied = args if phase == 1 else done
+        a, b, tied = lax.optimization_barrier((a, b, tied))
         if work is not None and phase >= 1:
-            tied = args if phase == 1 else done
-            a, b, tied = lax.optimization_barrier((a, b, tied))
             done = work(*tied) if phase == 1 else tied
         a = jnp.concatenate([a, swap(a, bit_a, n)], axis=0)
         b = jnp.concatenate([b, swap(b, bit_b, n)], axis=0)
@@ -465,28 +481,36 @@
     rows, d = activations.shape
     activations = pltpu.with_memory_space_constraint(activations, pltpu.HBM)
     me = lax.axis_index("dp").astype(jnp.int32).reshape(1)
-    labels = labels.reshape(1, rows)
-    counts = counts.reshape(1, rows)
+    row_data = (counts * K + labels).reshape(1, rows)
     order_y, order_z = hop_bits(n)
-    order_a, order_b = order_y[::-1], order_z
+    order_a, order_b = order_y[::-1], order_z[::-1]
     shifts = [[bit.bit_length() - 1 for bit in order] for order in (order_a, order_b)]
 
     root = Root(n, BOUND * 4 * rows * n)
-    sent, weight = class_sums(me, labels, counts, activations, n, 1)
+    sent, weight = class_sums(me, row_data, activations, n, 1)
     weight = weight.T
     got = root(sent, 1)
     weight = weight + swap(weight, 1, n)
-    kept, _ = class_sums(me, labels, counts, activations, n, 0)
-    top, low, weight, _ = reduce_scatter(kept + got, n, root, root, weight)
+    kept, _ = class_sums(me, row_data, activations, n, 0)
+    top, low, weight, _ = reduce_scatter(kept + got, n, root, root, weight, order_y)
     class_weight = weight.T
     total_weight = jnp.sum(class_weight, keepdims=True)
     over, back = class_weight, jnp.sqrt(class_weight)
     base = (top / over[:HALF]) * back[:HALF], (low / over[HALF:]) * back[HALF:]
 
-    def scatter(probed, along, bound, sent, work, args):
+    def scatter(probed, along, bound, sent, early, work, args):
         got = grow(swap(shrink(sent, bound), 1, n), bound)
         along = along + swap(along, 1, n)
-        blocks = panel_keep(me, probed, counts, activations, n) + got
+        waiting = order_y
+        if early:
+            kept = panel_keep(me, probed, row_data, activations, n, 0)
+            kept, along = lax.optimization_barrier((kept, along))
+            along = along + swap(along, waiting[0], n)
+            kept = panel_keep(me, probed, row_data, activations, n, 1, kept)
+            waiting = waiting[1:]
+        else:
+            kept = panel_keep(me, probed, row_data, activations, n)
+        blocks = kept + got
         top, low = bound[:HALF], bound[HALF:]
         return reduce_scatter(
             blocks,
@@ -494,6 +518,7 @@
             lambda x, bit: grow(swap(shrink(x, top), bit, n), top),
             lambda x, bit: grow(swap(shrink(x, low), bit, n), low),
             along,
+            waiting,
             work,
             args,
         )
@@ -503,10 +528,10 @@
     base_near, base_far, _ = gather(*base, n, orders)
     starts = probe(me, (base_near,), activations, n, shifts)
     first, along, bound, sent, current = probe_and_send(
-        me, (base_far,), activations, counts, total_weight, starts, (), n, shifts
+        me, (base_far,), activations, row_data, total_weight, starts, (), n, shifts
     )
     panel_a, panel_b, along, (offset,) = scatter(
-        first, along, bound, sent,
+        first, along, bound, sent, False,
         lambda *args: small(offset_kernel, "offset", (strip,), *args), (*base, current, total_weight),
     )
     image = panel_a / total_weight + offset[:HALF], panel_b / total_weight + offset[HALF:]
@@ -517,10 +542,10 @@
     )
     starts = probe(me, (near, base_near), activations, n, shifts)
     probed, along, bound, sent, _, _, renewed, mixed, beta_t = probe_and_send(
-        me, (far, base_far), activations, counts, total_weight, starts, (first, current, alpha_t, inverse), n, shifts
+        me, (far, base_far), activations, row_data, total_weight, starts, (first, current, alpha_t, inverse), n, shifts
     )
     panel_a, panel_b, along, (fixed, cross_t) = scatter(
-        probed, along, bound, sent,
+        probed, along, bound, sent, True,
         lambda *args: small(before_kernel, "before", (square,) * 2, *args),
         (current, renewed, mixed, beta_t, total_weight),
     )

time: 200 us -> 197 us (0.985)
  waiting for transfers between devices: 70.1 us -> 59.9 us
  starting transfers between devices: 51.2 us -> 58 us
    ppermute x49, waiting for transfers between devices: 70.1 us -> 59.9 us  [swap(): return lax.ppermute(value, 'dp', [(i, i ^ bit) for i in range(n)])]
    ppermute x49, starting transfers between devices: 51.2 us -> 58 us  [swap(): return lax.ppermute(value, 'dp', [(i, i ^ bit) for i in range(n)])]
    pallas_call x2 -> x3, Pallas kernels: 7.09 us -> 8.04 us  [panel_keep(): call(functools.partial(keep_kernel, first * UNROLL), 'panel_keep', n, ste...]
  transfers between devices with their start and end apart: 49 -> 49, of which waited for: 23 -> 30; matrix products, arithmetic and copies ran while one was open for 4% -> 4% of each run, Pallas kernels for 18% -> 19%
where the time goes in v6:
time: 197 us; the launch traced here: 196 us
  waiting for transfers between devices  59.9 us (30%)
  Pallas kernels  58.6 us (30%)
  starting transfers between devices  58 us (29%)
  other arithmetic  16.6 us (8%)
    ppermute x49, waiting for transfers between devices, swap(): return lax.ppermute(value, 'dp', [(i, i ^ bit) for i in range(n)])  59.9 us
    ppermute x49, starting transfers between devices, swap(): return lax.ppermute(value, 'dp', [(i, i ^ bit) for i in range(n)])  58 us
    pallas_call x5, Pallas kernels, small(): pl.pallas_call(kernel, out_shape=tuple((jax.ShapeDtypeStruct(shape, F32)...  17 us
    pallas_call x2, Pallas kernels, probe_and_send(): call(functools.partial(send_kernel, s, count, d), 'probe_and_send', n, 2...  16.5 us
    pallas_call x2, Pallas kernels, probe(): call(functools.partial(probe_kernel, count), 'probe', n, n // 2 // UNROLL...  10.1 us
    pallas_call x3, Pallas kernels, panel_keep(): call(functools.partial(keep_kernel, first * UNROLL), 'panel_keep', n, ste...  8.04 us
    pallas_call x2, Pallas kernels, class_sums(): call(functools.partial(sums_kernel, half), 'class_sums', n, n // 2 // UNR...  7 us
    add x14, other arithmetic, reduce_scatter(): a, b = (keep_a + swap_a(send_a, bit_a), keep_b + swap_b(send_b, bit_b))  4.51 us
  transfers between devices with their start and end apart: 49, of which 30 were waited for; matrix products, arithmetic and copies ran while one was open for 4% of the time, Pallas kernels for 19%

profile of v6, /device:TPU:0, one launch (start us, length us, event | category | flops | bytes accessed | tf_op | source)
XLA Modules:
  0.0 196.3 jit_solution(12002802549707713858)
XLA Ops:
  1.3 3.3 %class_sums.3 = (f32[8,64,1024]{2,1,0:T(8,128)S(1)}, f32[64,1]{1,0:T(8,128)S(1)}) custom-call(s32[1]{0:T(128)} %bitcast.me, s32[1,384]{1,0:T(1,128)S(1)} %reshape.72.row_data.refs_9_.refs_17_, bf16[384,16384]{1,0:T(8,128)(2,1)} %acts.9), custom_call_target="tpu_custom_call" | custom-call | flops 402653184 | bytes 8388608 | tf_op jit(solution)/shard_map/class_sums/pallas_call | solution.py:146
  6.3 3.7 %class_sums.2 = (f32[8,64,1024]{2,1,0:T(8,128)S(1)}, f32[64,1]{1,0:T(8,128)}) custom-call(s32[1]{0:T(128)} %bitcast.me, s32[1,384]{1,0:T(1,128)S(1)} %reshape.72.row_data.refs_9_.refs_17_, bf16[384,16384]{1,0:T(8,128)(2,1)} %acts.9), custom_call_target="tpu_custom_call" | custom-call | flops 402653184 | bytes 8388608 | tf_op jit(solution)/shard_map/class_sums/pallas_call | solution.py:146
  11.3 3.1 %collective-permute-start.3 = (f16[2,2,32,1024]{3,2,0,1:T(8,128)(2,1)S(1)}, f16[2,2,32,1024]{3,2,0,1:T(8,128)(2,1)S(1)}, u32[]{:S(2)}, u32[]{:S(2)}) collective-permute-start(f16[2,2,32,1024]{3,2,0,1:T(8,128)(2,1)S(1)} %fusion.6), channel_id=1, source_target_pairs={{0,4},{1,5},{2,6},{3,7},{4,0},{5,1},{6,2},{7,3},{8,12},{9,13},{10,... | collective-permute-start | bytes 786440 | tf_op jit(solution)/shard_map/ppermute | solution.py:62
  14.4 1.5 collective-permute-start.4
  18.0 3.0 %collective-permute-done.3 = f16[2,2,32,1024]{3,2,0,1:T(8,128)(2,1)S(1)} collective-permute-done((f16[2,2,32,1024]{3,2,0,1:T(8,128)(2,1)S(1)}, f16[2,2,32,1024]{3,2,0,1:T(8,128)(2,1)S(1)}, u32[]{:S(2)}, u32[]{:S(2)}) %collective-permute-start.3) | collective-permute-done | bytes 262176 | tf_op jit(solution)/shard_map/ppermute | solution.py:62
  21.1 2.9 %collective-permute-done.2 = f16[2,2,32,1024]{3,2,0,1:T(8,128)(2,1)S(1)} collective-permute-done((f16[2,2,32,1024]{3,2,0,1:T(8,128)(2,1)S(1)}, f16[2,2,32,1024]{3,2,0,1:T(8,128)(2,1)S(1)}, u32[]{:S(2)}, u32[]{:S(2)}) %collective-permute-start.2) | collective-permute-done | bytes 262176 | tf_op jit(solution)/shard_map/ppermute | solution.py:62
  24.7 2.7 %collective-permute-start.6 = (f16[2,32,1024]{2,1,0:T(8,128)(2,1)S(1)}, f16[2,32,1024]{2,1,0:T(8,128)(2,1)S(1)}, u32[]{:S(2)}, u32[]{:S(2)}) collective-permute-start(f16[2,32,1024]{2,1,0:T(8,128)(2,1)S(1)} %fusion.16), channel_id=1, source_target_pairs={{0,8},{1,9},{2,10},{3,11},{4,12},{5,13},{6,14},{7,15},{8,0},{9,1},... | collective-permute-start | bytes 393224 | tf_op jit(solution)/shard_map/ppermute | solution.py:62
  27.5 1.6 collective-permute-start.5
  29.2 3.2 %collective-permute-done.6 = f16[2,32,1024]{2,1,0:T(8,128)(2,1)S(1)} collective-permute-done((f16[2,32,1024]{2,1,0:T(8,128)(2,1)S(1)}, f16[2,32,1024]{2,1,0:T(8,128)(2,1)S(1)}, u32[]{:S(2)}, u32[]{:S(2)}) %collective-permute-start.6) | collective-permute-done | bytes 131104 | tf_op jit(solution)/shard_map/ppermute | solution.py:62
  34.7 2.1 %collective-permute-start.8 = (f16[32,1024]{1,0:T(8,128)(2,1)S(1)}, f16[32,1024]{1,0:T(8,128)(2,1)S(1)}, u32[]{:S(2)}, u32[]{:S(2)}) collective-permute-start(f16[32,1024]{1,0:T(8,128)(2,1)S(1)} %fusion.23), channel_id=1, source_target_pairs={{0,8},{1,9},{2,10},{3,11},{4,12},{5,13},{6,14},{7,15},{8,0},{9,1},... | collective-permute-start | bytes 196616 | tf_op jit(solution)/shard_map/ppermute | solution.py:62
  40.6 2.2 %collective-permute-start.11 = (bf16[1,32,1024]{2,1,0:T(8,128)(2,1)S(1)}, bf16[1,32,1024]{2,1,0:T(8,128)(2,1)S(1)}, u32[]{:S(2)}, u32[]{:S(2)}) collective-permute-start(bf16[1,32,1024]{2,1,0:T(8,128)(2,1)S(1)} %get-tuple-element.99), channel_id=1, source_target_pairs={{0,8},{1,9},{2,10},{3,11},{4,12},{5,13},{6,14},{7,15},{8,0},{9,1},... | collective-permute-start | bytes 196616 | tf_op jit(solution)/shard_map/ppermute | solution.py:62
  44.1 1.8 collective-permute-done.11
  47.1 2.4 %collective-permute-start.13 = (bf16[2,32,1024]{2,1,0:T(8,128)(2,1)S(1)}, bf16[2,32,1024]{2,1,0:T(8,128)(2,1)S(1)}, u32[]{:S(2)}, u32[]{:S(2)}) collective-permute-start(bf16[2,32,1024]{2,1,0:T(8,128)(2,1)S(1)} %pad_maximum_fusion.4), channel_id=1, source_target_pairs={{0,4},{1,5},{2,6},{3,7},{4,0},{5,1},{6,2},{7,3},{8,12},{9,13},{10,... | collective-permute-start | bytes 393224 | tf_op jit(solution)/shard_map/ppermute | solution.py:62
  49.5 3.2 %collective-permute-start.14 = (bf16[2,32,1024]{2,1,0:T(8,128)(2,1)S(1)}, bf16[2,32,1024]{2,1,0:T(8,128)(2,1)S(1)}, u32[]{:S(2)}, u32[]{:S(2)}) collective-permute-start(bf16[2,32,1024]{2,1,0:T(8,128)(2,1)S(1)} %pad_maximum_fusion.5), channel_id=1, source_target_pairs={{0,8},{1,9},{2,10},{3,11},{4,12},{5,13},{6,14},{7,15},{8,0},{9,1},... | collective-permute-start | bytes 393224 | tf_op jit(solution)/shard_map/ppermute | solution.py:62
  53.3 2.5 %collective-permute-done.14 = bf16[2,32,1024]{2,1,0:T(8,128)(2,1)S(1)} collective-permute-done((bf16[2,32,1024]{2,1,0:T(8,128)(2,1)S(1)}, bf16[2,32,1024]{2,1,0:T(8,128)(2,1)S(1)}, u32[]{:S(2)}, u32[]{:S(2)}) %collective-permute-start.14) | collective-permute-done | bytes 131104 | tf_op jit(solution)/shard_map/ppermute | solution.py:62
  55.8 3.7 %collective-permute-start.17 = (bf16[4,32,1024]{2,1,0:T(8,128)(2,1)S(1)}, bf16[4,32,1024]{2,1,0:T(8,128)(2,1)S(1)}, u32[]{:S(2)}, u32[]{:S(2)}) collective-permute-start(bf16[4,32,1024]{2,1,0:T(8,128)(2,1)S(1)} %pad_maximum_fusion.1), channel_id=1, source_target_pairs={{0,4},{1,5},{2,6},{3,7},{4,0},{5,1},{6,2},{7,3},{8,12},{9,13},{10,... | collective-permute-start | bytes 786440 | tf_op jit(solution)/shard_map/ppermute | solution.py:62
  59.5 1.5 collective-permute-start.15
  61.0 2.8 %collective-permute-done.17 = bf16[4,32,1024]{2,1,0:T(8,128)(2,1)S(1)} collective-permute-done((bf16[4,32,1024]{2,1,0:T(8,128)(2,1)S(1)}, bf16[4,32,1024]{2,1,0:T(8,128)(2,1)S(1)}, u32[]{:S(2)}, u32[]{:S(2)}) %collective-permute-start.17) | collective-permute-done | bytes 262176 | tf_op jit(solution)/shard_map/ppermute | solution.py:62
  63.9 1.9 collective-permute-done.15
  66.0 5.1 %probe.2 = (f32[384,64]{1,0:T(8,128)S(1)}, f32[64,64]{1,0:T(8,128)S(1)}) custom-call(s32[1]{0:T(128)} %bitcast.me, bf16[8,32,1024]{2,1,0:T(8,128)(2,1)S(1)} %constant_dynamic-update-slice_fusion.refs_0_.refs_2_.refs_4_.refs_6_.refs_8_.refs_10_.refs_12_.refs_14_, ...), custom_call_target="tpu_custom_call" | custom-call | flops 402653184 | bytes 8388608 | tf_op jit(solution)/shard_map/probe/pallas_call | solution.py:213
  71.0 7.5 %probe_and_send.2 = (f32[64,384]{1,0:T(8,128)S(1)}, f32[64,64]{1,0:T(8,128)S(1)}, f32[64,1]{1,0:T(8,128)S(1)}, f32[8,64,1024]{2,1,0:T(8,128)S(1)}, f32[64,64]{1,0:T(8,128)S(1)}) custom-call(s32[1]{0:T(128)} %bitcast.me, bf16[8,32,1024]{2,1,0:T(8,128)(2,1)S(1)} %collective-permute-done.16.refs_0_.refs_2_.refs_4_.refs_6_.refs_8_.refs_10_.refs_12_.refs_14_, ...), custom_call_target="tpu_custom_call" | custom-call | flops 402653184 | bytes 8388608 | tf_op jit(solution)/shard_map/probe_and_send/pallas_call | solution.py:303
  79.7 3.5 %panel_keep.3 = f32[8,64,1024]{2,1,0:T(8,128)S(1)} custom-call(s32[1]{0:T(128)} %bitcast.me, f32[64,384]{1,0:T(8,128)S(1)} %get-tuple-element.107.probed.refs_22_, s32[1,384]{1,0:T(1,128)S(1)} %reshape.72.row_data.refs_9_.refs_17_, bf16[384,16384]{1,0:T(8,128)(2,1)} %acts.9), custom_call_target="tpu_custom_call" | custom-call | flops 402653184 | bytes 8388608 | tf_op jit(solution)/shard_map/panel_keep/pallas_call | solution.py:355
  87.2 1.7 collective-permute-done.23
  88.9 4.2 %collective-permute-done.22 = f16[2,2,32,1024]{3,2,1,0:T(8,128)(2,1)S(1)} collective-permute-done((f16[2,2,32,1024]{3,2,1,0:T(8,128)(2,1)S(1)}, f16[2,2,32,1024]{3,2,1,0:T(8,128)(2,1)S(1)}, u32[]{:S(2)}, u32[]{:S(2)}) %collective-permute-start.22) | collective-permute-done | bytes 262176 | tf_op jit(solution)/shard_map/ppermute | solution.py:62
  94.7 1.7 collective-permute-start.26
  99.1 2.7 %offset.1 = f32[64,1024]{1,0:T(8,128)} custom-call(f32[32,1024]{1,0:T(8,128)} %get-tuple-element.118.base_a, f32[32,1024]{1,0:T(8,128)} %get-tuple-element.119.base_b, f32[64,64]{1,0:T(8,128)} %copy-done, f32[1,1]{1,0:T(1,128)} %bitcast.21.refs_10_.total_weight.refs_18_), custom_call_target="tpu_custom_call" | custom-call | flops 67108864 | bytes 1048576 | tf_op jit(solution)/shard_map/offset/pallas_call | solution.py:416
  101.8 3.6 %collective-permute-done.25 = f16[2,32,1024]{2,1,0:T(8,128)(2,1)} collective-permute-done((f16[2,32,1024]{2,1,0:T(8,128)(2,1)}, f16[2,32,1024]{2,1,0:T(8,128)(2,1)}, u32[]{:S(2)}, u32[]{:S(2)}) %collective-permute-start.25) | collective-permute-done | bytes 131104 | tf_op jit(solution)/shard_map/ppermute | solution.py:62
  109.0 3.0 %collective-permute-done.28 = f16[32,1024]{1,0:T(8,128)(2,1)S(1)} collective-permute-done((f16[32,1024]{1,0:T(8,128)(2,1)S(1)}, f16[32,1024]{1,0:T(8,128)(2,1)S(1)}, u32[]{:S(2)}, u32[]{:S(2)}) %collective-permute-start.28) | collective-permute-done | bytes 65568 | tf_op jit(solution)/shard_map/ppermute | solution.py:62
  111.9 2.0 %collective-permute-done.27 = f16[32,1024]{1,0:T(8,128)(2,1)S(1)} collective-permute-done((f16[32,1024]{1,0:T(8,128)(2,1)S(1)}, f16[32,1024]{1,0:T(8,128)(2,1)S(1)}, u32[]{:S(2)}, u32[]{:S(2)}) %collective-permute-start.27) | collective-permute-done | bytes 65568 | tf_op jit(solution)/shard_map/ppermute | solution.py:62
  115.5 2.7 %collective-permute-start.31 = (f32[64,64]{1,0:T(8,128)S(1)}, f32[64,64]{1,0:T(8,128)S(1)}, u32[]{:S(2)}, u32[]{:S(2)}) collective-permute-start(f32[64,64]{1,0:T(8,128)S(1)} %add.127), channel_id=1, source_target_pairs={{0,8},{1,9},{2,10},{3,11},{4,12},{5,13},{6,14},{7,15},{8,0},{9,1},... | collective-permute-start | bytes 49160 | tf_op jit(solution)/shard_map/ppermute | solution.py:62
  118.2 2.6 %collective-permute-done.31 = f32[64,64]{1,0:T(8,128)S(1)} collective-permute-done((f32[64,64]{1,0:T(8,128)S(1)}, f32[64,64]{1,0:T(8,128)S(1)}, u32[]{:S(2)}, u32[]{:S(2)}) %collective-permute-start.31) | collective-permute-done | bytes 16416 | tf_op jit(solution)/shard_map/ppermute | solution.py:62
  122.4 3.3 %collective-permute-done.30 = bf16[1,32,1024]{2,1,0:T(8,128)(2,1)S(1)} collective-permute-done((bf16[1,32,1024]{2,1,0:T(8,128)(2,1)S(1)}, bf16[1,32,1024]{2,1,0:T(8,128)(2,1)S(1)}, u32[]{:S(2)}, u32[]{:S(2)}) %collective-permute-start.30) | collective-permute-done | bytes 65568 | tf_op jit(solution)/shard_map/ppermute | solution.py:62
  125.7 1.7 collective-permute-start.32
  128.2 4.3 %alpha.1 = (f32[64,64]{1,0:T(8,128)}, f32[64,64]{1,0:T(8,128)}) custom-call(f32[64,64]{1,0:T(8,128)} %add.132.along, f32[64,64]{1,0:T(8,128)} %copy-done, f32[1,1]{1,0:T(1,128)} %bitcast.21.refs_10_.total_weight.refs_18_), custom_call_target="tpu_custom_call" | custom-call | flops 67108864 | bytes 1048576 | tf_op jit(solution)/shard_map/alpha/pallas_call | solution.py:416
  133.4 3.5 %collective-permute-start.36 = (bf16[4,32,1024]{2,1,0:T(8,128)(2,1)S(1)}, bf16[4,32,1024]{2,1,0:T(8,128)(2,1)S(1)}, u32[]{:S(2)}, u32[]{:S(2)}) collective-permute-start(bf16[4,32,1024]{2,1,0:T(8,128)(2,1)S(1)} %pad_maximum_fusion.3), channel_id=1, source_target_pairs={{0,4},{1,5},{2,6},{3,7},{4,0},{5,1},{6,2},{7,3},{8,12},{9,13},{10,... | collective-permute-start | bytes 786440 | tf_op jit(solution)/shard_map/ppermute | solution.py:62
  138.0 3.4 %collective-permute-done.36 = bf16[4,32,1024]{2,1,0:T(8,128)(2,1)S(1)} collective-permute-done((bf16[4,32,1024]{2,1,0:T(8,128)(2,1)S(1)}, bf16[4,32,1024]{2,1,0:T(8,128)(2,1)S(1)}, u32[]{:S(2)}, u32[]{:S(2)}) %collective-permute-start.36) | collective-permute-done | bytes 262176 | tf_op jit(solution)/shard_map/ppermute | solution.py:62
  141.4 1.9 collective-permute-done.34
  143.5 5.0 %probe.3 = (f32[384,64]{1,0:T(8,128)S(1)}, f32[64,64]{1,0:T(8,128)S(1)}, f32[64,64]{1,0:T(8,128)S(1)}) custom-call(s32[1]{0:T(128)} %bitcast.me, bf16[8,32,1024]{2,1,0:T(8,128)(2,1)S(1)} %constant_dynamic-update-slice_fusion.4.refs_0_.refs_2_.refs_4_.refs_6_, bf16[8,32,1024]{2,1,0:T(8,128)(2,1)S(1)} %constant_dynamic-update-slice_fusion.6.refs_1_.refs_3_.refs_5_.refs_7_, ...), custom_call_target="tpu_custom_call" | custom-call | flops 402653184 | bytes 8388608 | tf_op jit(solution)/shard_map/probe/pallas_call | solution.py:213
  148.6 9.0 %probe_and_send.3 = (f32[64,384]{1,0:T(8,128)S(1)}, f32[64,64]{1,0:T(8,128)S(1)}, f32[64,1]{1,0:T(8,128)S(1)}, f32[8,64,1024]{2,1,0:T(8,128)S(1)}, f32[64,64]{1,...) custom-call(s32[1]{0:T(128)} %bitcast.me, ...), custom_call_target="tpu_custom_call" | custom-call | flops 402653184 | bytes 8388608 | tf_op jit(solution)/shard_map/probe_and_send/pallas_call | solution.py:303
  158.8 2.3 %panel_keep.4.refs_0_ = f32[8,64,1024]{2,1,0:T(8,128)S(1)} custom-call(s32[1]{0:T(128)} %bitcast.me, f32[64,384]{1,0:T(8,128)S(1)} %get-tuple-element.142.probed, s32[1,384]{1,0:T(1,128)S(1)} %reshape.72.row_data.refs_9_.refs_17_, bf16[384,16384]{1,0:T(8,128)(2,1)} %acts.9), custom_call_target="tpu_custom_call" | custom-call | flops 402653184 | bytes 8388608 | tf_op jit(solution)/shard_map/panel_keep/pallas_call | solution.py:355
  162.1 2.3 %panel_keep.5 = f32[8,64,1024]{2,1,0:T(8,128)S(1)} custom-call(s32[1]{0:T(128)} %bitcast.me, f32[64,384]{1,0:T(8,128)S(1)} %get-tuple-element.142.probed, s32[1,384]{1,0:T(1,128)S(1)} %reshape.72.row_data.refs_9_.refs_17_, bf16[384,16384]{1,0:T(8,128)(2,1)} %acts.9, f32[8,64,1024]{2,1,0:T(8,128)S(1)} %panel_keep.4.refs_0_), custom_call_target="tpu_custom_call", output_to_operand_aliasing={{}: (4, {})} | custom-call | flops 402653184 | bytes 8388608 | tf_op jit(solution)/shard_map/panel_keep/pallas_call | solution.py:355
  166.8 1.5 collective-permute-start.43
  169.4 5.2 %collective-permute-done.43 = f32[64,64]{1,0:T(8,128)S(1)} collective-permute-done((f32[64,64]{1,0:T(8,128)S(1)}, f32[64,64]{1,0:T(8,128)S(1)}, u32[]{:S(2)}, u32[]{:S(2)}) %collective-permute-start.43) | collective-permute-done | bytes 16416 | tf_op jit(solution)/shard_map/ppermute | solution.py:62
  176.4 2.5 %collective-permute-start.45 = (f16[2,32,1024]{2,1,0:T(8,128)(2,1)S(1)}, f16[2,32,1024]{2,1,0:T(8,128)(2,1)S(1)}, u32[]{:S(2)}, u32[]{:S(2)}) collective-permute-start(f16[2,32,1024]{2,1,0:T(8,128)(2,1)S(1)} %multiply_convert_fusion.6), channel_id=1, source_target_pairs={{0,8},{1,9},{2,10},{3,11},{4,12},{5,13},{6,14},{7,15},{8,0},{9,1},... | collective-permute-start | bytes 393224 | tf_op jit(solution)/shard_map/ppermute | solution.py:62
  179.4 2.5 %before.1 = (f32[64,64]{1,0:T(8,128)}, f32[64,64]{1,0:T(8,128)}) custom-call(f32[64,64]{1,0:T(8,128)} %copy-done, f32[64,64]{1,0:T(8,128)} %copy-done.4, f32[64,64]{1,0:T(8,128)} %copy-done.6, f32[64,64]{1,0:T(8,128)} %copy-done.5, f32[1,1]{1,0:T(1,128)} %bitcast.21.refs_10_.total_weight.refs_18_), custom_call_target="tpu_custom_call" | custom-call | flops 67108864 | bytes 1048576 | tf_op jit(solution)/shard_map/before/pallas_call | solution.py:416
  182.5 1.5 collective-permute-done.45
  187.3 5.4 %last.1 = (f32[64,1024]{1,0:T(8,128)}, f32[64,1024]{1,0:T(8,128)}, f32[64,64]{1,0:T(8,128)}) custom-call(f32[64,64]{1,0:T(8,128)} %add.141.along, f32[64,64]{1,0:T(8,128)} %get-tuple-element.165.fixed, f32[64,64]{1,0:T(8,128)} %get-tuple-element.166.cross_t, f32[64,64]{1,0:T(8,128)} %copy-done.4, f32[64,64]{1,0:T(8,128)} %copy-done.5, ...), custom_call_target="tpu_custom_call" | custom-call | flops 67108864 | bytes 1048576 | tf_op jit(solution)/shard_map/last/pallas_call | solution.py:416
  194.2 2.1 %end.1 = f32[64,1024]{1,0:T(8,128)} custom-call(f32[64,1024]{1,0:T(8,128)} %get-tuple-element.168.rest, f32[64,64]{1,0:T(8,128)} %get-tuple-element.169.on_panel, f32[32,1024]{1,0:T(8,128)} %fusion.34.panel_a, f32[32,1024]{1,0:T(8,128)} %fusion.33.panel_b), custom_call_target="tpu_custom_call" | custom-call | flops 67108864 | bytes 1048576 | tf_op jit(solution)/shard_map/end/pallas_call | solution.py:416
  (183 shorter events, 48.1 us)
Async XLA Ops:
  5.6 4.5 %collective-permute-start = (f16[8,64,1024]{2,1,0:T(8,128)(2,1)S(1)}, f16[8,64,1024]{2,1,0:T(8,128)(2,1)S(1)}, u32[]{:S(2)}, u32[]{:S(2)}) collective-permute-start(f16[8,64,1024]{2,1,0:T(8,128)(2,1)S(1)} %fusion), channel_id=1, source_target_pairs={{0,1},{1,0},{2,3},{3,2},{4,5},{5,4},{6,7},{7,6},{8,9},{9,8},{10,11... | collective-permute-start | bytes 3145736 | tf_op jit(solution)/shard_map/ppermute | solution.py:62
  6.2 3.8 %collective-permute-start.1 = (f32[1,64]{1,0:T(1,128)S(1)}, f32[1,64]{1,0:T(1,128)S(1)}, u32[]{:S(2)}, u32[]{:S(2)}) collective-permute-start(f32[1,64]{1,0:T(1,128)S(1)} %bitcast.173), channel_id=1, source_target_pairs={{0,1},{1,0},{2,3},{3,2},{4,5},{5,4},{6,7},{7,6},{8,9},{9,8},{10,11... | collective-permute-start | bytes 776 | tf_op jit(solution)/shard_map/ppermute | solution.py:62
  11.3 9.6 %collective-permute-start.3 = (f16[2,2,32,1024]{3,2,0,1:T(8,128)(2,1)S(1)}, f16[2,2,32,1024]{3,2,0,1:T(8,128)(2,1)S(1)}, u32[]{:S(2)}, u32[]{:S(2)}) collective-permute-start(f16[2,2,32,1024]{3,2,0,1:T(8,128)(2,1)S(1)} %fusion.6), channel_id=1, source_target_pairs={{0,4},{1,5},{2,6},{3,7},{4,0},{5,1},{6,2},{7,3},{8,12},{9,13},{10,... | collective-permute-start | bytes 786440 | tf_op jit(solution)/shard_map/ppermute | solution.py:62
  14.4 3.5 %collective-permute-start.4 = (f32[1,64]{1,0:T(1,128)S(1)}, f32[1,64]{1,0:T(1,128)S(1)}, u32[]{:S(2)}, u32[]{:S(2)}) collective-permute-start(f32[1,64]{1,0:T(1,128)S(1)} %bitcast_add_fusion), channel_id=1, source_target_pairs={{0,2},{1,3},{2,0},{3,1},{4,6},{5,7},{6,4},{7,5},{8,10},{9,11},{10,... | collective-permute-start | bytes 776 | tf_op jit(solution)/shard_map/ppermute | solution.py:62
  16.2 7.8 %collective-permute-start.2 = (f16[2,2,32,1024]{3,2,0,1:T(8,128)(2,1)S(1)}, f16[2,2,32,1024]{3,2,0,1:T(8,128)(2,1)S(1)}, u32[]{:S(2)}, u32[]{:S(2)}) collective-permute-start(f16[2,2,32,1024]{3,2,0,1:T(8,128)(2,1)S(1)} %fusion.3), channel_id=1, source_target_pairs={{0,2},{1,3},{2,0},{3,1},{4,6},{5,7},{6,4},{7,5},{8,10},{9,11},{10,... | collective-permute-start | bytes 786440 | tf_op jit(solution)/shard_map/ppermute | solution.py:62
  24.1 5.1 %collective-permute-start.7 = (f32[1,64]{1,0:T(1,128)S(1)}, f32[1,64]{1,0:T(1,128)S(1)}, u32[]{:S(2)}, u32[]{:S(2)}) collective-permute-start(f32[1,64]{1,0:T(1,128)S(1)} %add.113), channel_id=1, source_target_pairs={{0,4},{1,5},{2,6},{3,7},{4,0},{5,1},{6,2},{7,3},{8,12},{9,13},{10,... | collective-permute-start | bytes 776 | tf_op jit(solution)/shard_map/ppermute | solution.py:62
  24.7 7.6 %collective-permute-start.6 = (f16[2,32,1024]{2,1,0:T(8,128)(2,1)S(1)}, f16[2,32,1024]{2,1,0:T(8,128)(2,1)S(1)}, u32[]{:S(2)}, u32[]{:S(2)}) collective-permute-start(f16[2,32,1024]{2,1,0:T(8,128)(2,1)S(1)} %fusion.16), channel_id=1, source_target_pairs={{0,8},{1,9},{2,10},{3,11},{4,12},{5,13},{6,14},{7,15},{8,0},{9,1},... | collective-permute-start | bytes 393224 | tf_op jit(solution)/shard_map/ppermute | solution.py:62
  27.5 5.3 %collective-permute-start.5 = (f16[2,32,1024]{2,1,0:T(8,128)(2,1)S(1)}, f16[2,32,1024]{2,1,0:T(8,128)(2,1)S(1)}, u32[]{:S(2)}, u32[]{:S(2)}) collective-permute-start(f16[2,32,1024]{2,1,0:T(8,128)(2,1)S(1)} %fusion.13), channel_id=1, source_target_pairs={{0,4},{1,5},{2,6},{3,7},{4,0},{5,1},{6,2},{7,3},{8,12},{9,13},{10,... | collective-permute-start | bytes 393224 | tf_op jit(solution)/shard_map/ppermute | solution.py:62
  33.0 4.6 %collective-permute-start.9 = (f32[1,64]{1,0:T(1,128)S(1)}, f32[1,64]{1,0:T(1,128)S(1)}, u32[]{:S(2)}, u32[]{:S(2)}) collective-permute-start(f32[1,64]{1,0:T(1,128)S(1)} %add.116), channel_id=1, source_target_pairs={{0,8},{1,9},{2,10},{3,11},{4,12},{5,13},{6,14},{7,15},{8,0},{9,1},... | collective-permute-start | bytes 776 | tf_op jit(solution)/shard_map/ppermute | solution.py:62
  34.1 4.3 %collective-permute-start.10 = (f16[32,1024]{1,0:T(8,128)(2,1)S(1)}, f16[32,1024]{1,0:T(8,128)(2,1)S(1)}, u32[]{:S(2)}, u32[]{:S(2)}) collective-permute-start(f16[32,1024]{1,0:T(8,128)(2,1)S(1)} %fusion.28), channel_id=1, source_target_pairs={{0,2},{1,3},{2,0},{3,1},{4,6},{5,7},{6,4},{7,5},{8,10},{9,11},{10,... | collective-permute-start | bytes 196616 | tf_op jit(solution)/shard_map/ppermute | solution.py:62
  34.7 5.2 %collective-permute-start.8 = (f16[32,1024]{1,0:T(8,128)(2,1)S(1)}, f16[32,1024]{1,0:T(8,128)(2,1)S(1)}, u32[]{:S(2)}, u32[]{:S(2)}) collective-permute-start(f16[32,1024]{1,0:T(8,128)(2,1)S(1)} %fusion.23), channel_id=1, source_target_pairs={{0,8},{1,9},{2,10},{3,11},{4,12},{5,13},{6,14},{7,15},{8,0},{9,1},... | collective-permute-start | bytes 196616 | tf_op jit(solution)/shard_map/ppermute | solution.py:62
  40.6 5.3 %collective-permute-start.11 = (bf16[1,32,1024]{2,1,0:T(8,128)(2,1)S(1)}, bf16[1,32,1024]{2,1,0:T(8,128)(2,1)S(1)}, u32[]{:S(2)}, u32[]{:S(2)}) collective-permute-start(bf16[1,32,1024]{2,1,0:T(8,128)(2,1)S(1)} %get-tuple-element.99), channel_id=1, source_target_pairs={{0,8},{1,9},{2,10},{3,11},{4,12},{5,13},{6,14},{7,15},{8,0},{9,1},... | collective-permute-start | bytes 196616 | tf_op jit(solution)/shard_map/ppermute | solution.py:62
  42.8 4.3 %collective-permute-start.12 = (bf16[1,32,1024]{2,1,0:T(8,128)(2,1)S(1)}, bf16[1,32,1024]{2,1,0:T(8,128)(2,1)S(1)}, u32[]{:S(2)}, u32[]{:S(2)}) collective-permute-start(bf16[1,32,1024]{2,1,0:T(8,128)(2,1)S(1)} %get-tuple-element.100), channel_id=1, source_target_pairs={{0,2},{1,3},{2,0},{3,1},{4,6},{5,7},{6,4},{7,5},{8,10},{9,11},{10,... | collective-permute-start | bytes 196616 | tf_op jit(solution)/shard_map/ppermute | solution.py:62
  47.1 6.2 %collective-permute-start.13 = (bf16[2,32,1024]{2,1,0:T(8,128)(2,1)S(1)}, bf16[2,32,1024]{2,1,0:T(8,128)(2,1)S(1)}, u32[]{:S(2)}, u32[]{:S(2)}) collective-permute-start(bf16[2,32,1024]{2,1,0:T(8,128)(2,1)S(1)} %pad_maximum_fusion.4), channel_id=1, source_target_pairs={{0,4},{1,5},{2,6},{3,7},{4,0},{5,1},{6,2},{7,3},{8,12},{9,13},{10,... | collective-permute-start | bytes 393224 | tf_op jit(solution)/shard_map/ppermute | solution.py:62
  49.5 6.3 %collective-permute-start.14 = (bf16[2,32,1024]{2,1,0:T(8,128)(2,1)S(1)}, bf16[2,32,1024]{2,1,0:T(8,128)(2,1)S(1)}, u32[]{:S(2)}, u32[]{:S(2)}) collective-permute-start(bf16[2,32,1024]{2,1,0:T(8,128)(2,1)S(1)} %pad_maximum_fusion.5), channel_id=1, source_target_pairs={{0,8},{1,9},{2,10},{3,11},{4,12},{5,13},{6,14},{7,15},{8,0},{9,1},... | collective-permute-start | bytes 393224 | tf_op jit(solution)/shard_map/ppermute | solution.py:62
  55.8 8.0 %collective-permute-start.17 = (bf16[4,32,1024]{2,1,0:T(8,128)(2,1)S(1)}, bf16[4,32,1024]{2,1,0:T(8,128)(2,1)S(1)}, u32[]{:S(2)}, u32[]{:S(2)}) collective-permute-start(bf16[4,32,1024]{2,1,0:T(8,128)(2,1)S(1)} %pad_maximum_fusion.1), channel_id=1, source_target_pairs={{0,4},{1,5},{2,6},{3,7},{4,0},{5,1},{6,2},{7,3},{8,12},{9,13},{10,... | collective-permute-start | bytes 786440 | tf_op jit(solution)/shard_map/ppermute | solution.py:62
  59.5 6.4 %collective-permute-start.15 = (bf16[4,32,1024]{2,1,0:T(8,128)(2,1)S(1)}, bf16[4,32,1024]{2,1,0:T(8,128)(2,1)S(1)}, u32[]{:S(2)}, u32[]{:S(2)}) collective-permute-start(bf16[4,32,1024]{2,1,0:T(8,128)(2,1)S(1)} %pad_maximum_fusion), channel_id=1, source_target_pairs={{0,2},{1,3},{2,0},{3,1},{4,6},{5,7},{6,4},{7,5},{8,10},{9,11},{10,... | collective-permute-start | bytes 786440 | tf_op jit(solution)/shard_map/ppermute | solution.py:62
  63.9 7.2 %collective-permute-start.18 = (bf16[8,32,1024]{2,1,0:T(8,128)(2,1)S(1)}, bf16[8,32,1024]{2,1,0:T(8,128)(2,1)S(1)}, u32[]{:S(2)}, u32[]{:S(2)}) collective-permute-start(bf16[8,32,1024]{2,1,0:T(8,128)(2,1)S(1)} %constant_dynamic-update-slice_fusion.2.refs_1_.refs_3_.refs_5_.refs_7_.refs_9_.refs_11_.refs_13_.r, ...), channel_id=1, source_target_pairs={{0,1},{1,0},{2,3},{3,2},{4,5},{5,4},{6,7},{7,6},{8,9},{9,8},{10,11... | collective-permute-start | bytes 1572872 | tf_op jit(solution)/shard_map/ppermute | solution.py:62
  65.9 5.2 %collective-permute-start.16 = (bf16[8,32,1024]{2,1,0:T(8,128)(2,1)S(1)}, bf16[8,32,1024]{2,1,0:T(8,128)(2,1)S(1)}, u32[]{:S(2)}, u32[]{:S(2)}) collective-permute-start(bf16[8,32,1024]{2,1,0:T(8,128)(2,1)S(1)} %constant_dynamic-update-slice_fusion.refs_0_.refs_2_.refs_4_.refs_6_.refs_8_.refs_10_.refs_12_.ref, ...), channel_id=1, source_target_pairs={{0,1},{1,0},{2,3},{3,2},{4,5},{5,4},{6,7},{7,6},{8,9},{9,8},{10,11... | collective-permute-start | bytes 1572872 | tf_op jit(solution)/shard_map/ppermute | solution.py:62
  79.0 4.3 %collective-permute-start.19 = (f16[8,64,1024]{2,1,0:T(8,128)(2,1)S(1)}, f16[8,64,1024]{2,1,0:T(8,128)(2,1)S(1)}, u32[]{:S(2)}, u32[]{:S(2)}) collective-permute-start(f16[8,64,1024]{2,1,0:T(8,128)(2,1)S(1)} %multiply_convert_fusion.1), channel_id=1, source_target_pairs={{0,1},{1,0},{2,3},{3,2},{4,5},{5,4},{6,7},{7,6},{8,9},{9,8},{10,11... | collective-permute-start | bytes 3145736 | tf_op jit(solution)/shard_map/ppermute | solution.py:62
  79.5 3.8 %collective-permute-start.20 = (f32[64,64]{1,0:T(8,128)S(1)}, f32[64,64]{1,0:T(8,128)S(1)}, u32[]{:S(2)}, u32[]{:S(2)}) collective-permute-start(f32[64,64]{1,0:T(8,128)S(1)} %get-tuple-element.110), channel_id=1, source_target_pairs={{0,1},{1,0},{2,3},{3,2},{4,5},{5,4},{6,7},{7,6},{8,9},{9,8},{10,11... | collective-permute-start | bytes 49160 | tf_op jit(solution)/shard_map/ppermute | solution.py:62
  84.4 8.7 %collective-permute-start.22 = (f16[2,2,32,1024]{3,2,1,0:T(8,128)(2,1)S(1)}, f16[2,2,32,1024]{3,2,1,0:T(8,128)(2,1)S(1)}, u32[]{:S(2)}, u32[]{:S(2)}) collective-permute-start(f16[2,2,32,1024]{3,2,1,0:T(8,128)(2,1)S(1)} %multiply_convert_fusion.4), channel_id=1, source_target_pairs={{0,4},{1,5},{2,6},{3,7},{4,0},{5,1},{6,2},{7,3},{8,12},{9,13},{10,... | collective-permute-start | bytes 786440 | tf_op jit(solution)/shard_map/ppermute | solution.py:62
  85.0 3.9 %collective-permute-start.23 = (f32[64,64]{1,0:T(8,128)S(1)}, f32[64,64]{1,0:T(8,128)S(1)}, u32[]{:S(2)}, u32[]{:S(2)}) collective-permute-start(f32[64,64]{1,0:T(8,128)S(1)} %add.121), channel_id=1, source_target_pairs={{0,2},{1,3},{2,0},{3,1},{4,6},{5,7},{6,4},{7,5},{8,10},{9,11},{10,... | collective-permute-start | bytes 49160 | tf_op jit(solution)/shard_map/ppermute | solution.py:62
  86.6 8.0 %collective-permute-start.21 = (f16[2,2,32,1024]{3,2,0,1:T(8,128)(2,1)S(1)}, f16[2,2,32,1024]{3,2,0,1:T(8,128)(2,1)S(1)}, u32[]{:S(2)}, u32[]{:S(2)}) collective-permute-start(f16[2,2,32,1024]{3,2,0,1:T(8,128)(2,1)S(1)} %multiply_convert_fusion.5), channel_id=1, source_target_pairs={{0,2},{1,3},{2,0},{3,1},{4,6},{5,7},{6,4},{7,5},{8,10},{9,11},{10,... | collective-permute-start | bytes 786440 | tf_op jit(solution)/shard_map/ppermute | solution.py:62
  94.7 7.1 %collective-permute-start.26 = (f32[64,64]{1,0:T(8,128)S(1)}, f32[64,64]{1,0:T(8,128)S(1)}, u32[]{:S(2)}, u32[]{:S(2)}) collective-permute-start(f32[64,64]{1,0:T(8,128)S(1)} %add.124), channel_id=1, source_target_pairs={{0,4},{1,5},{2,6},{3,7},{4,0},{5,1},{6,2},{7,3},{8,12},{9,13},{10,... | collective-permute-start | bytes 49160 | tf_op jit(solution)/shard_map/ppermute | solution.py:62
  97.2 8.1 %collective-permute-start.25 = (f16[2,32,1024]{2,1,0:T(8,128)(2,1)}, f16[2,32,1024]{2,1,0:T(8,128)(2,1)}, u32[]{:S(2)}, u32[]{:S(2)}) collective-permute-start(f16[2,32,1024]{2,1,0:T(8,128)(2,1)} %multiply_convert_fusion.8), channel_id=1, source_target_pairs={{0,8},{1,9},{2,10},{3,11},{4,12},{5,13},{6,14},{7,15},{8,0},{9,1},... | collective-permute-start | bytes 393224 | tf_op jit(solution)/shard_map/ppermute | solution.py:62
  98.7 7.7 %collective-permute-start.24 = (f16[2,32,1024]{2,1,0:T(8,128)(2,1)S(1)}, f16[2,32,1024]{2,1,0:T(8,128)(2,1)}, u32[]{:S(2)}, u32[]{:S(2)}) collective-permute-start(f16[2,32,1024]{2,1,0:T(8,128)(2,1)S(1)} %multiply_convert_fusion.9), channel_id=1, source_target_pairs={{0,4},{1,5},{2,6},{3,7},{4,0},{5,1},{6,2},{7,3},{8,12},{9,13},{10,... | collective-permute-start | bytes 393224 | tf_op jit(solution)/shard_map/ppermute | solution.py:62
  107.6 4.3 %collective-permute-start.28 = (f16[32,1024]{1,0:T(8,128)(2,1)S(1)}, f16[32,1024]{1,0:T(8,128)(2,1)S(1)}, u32[]{:S(2)}, u32[]{:S(2)}) collective-permute-start(f16[32,1024]{1,0:T(8,128)(2,1)S(1)} %multiply_convert_fusion.12), channel_id=1, source_target_pairs={{0,2},{1,3},{2,0},{3,1},{4,6},{5,7},{6,4},{7,5},{8,10},{9,11},{10,... | collective-permute-start | bytes 196616 | tf_op jit(solution)/shard_map/ppermute | solution.py:62
  108.8 5.2 %collective-permute-start.27 = (f16[32,1024]{1,0:T(8,128)(2,1)S(1)}, f16[32,1024]{1,0:T(8,128)(2,1)S(1)}, u32[]{:S(2)}, u32[]{:S(2)}) collective-permute-start(f16[32,1024]{1,0:T(8,128)(2,1)S(1)} %multiply_convert_fusion.13), channel_id=1, source_target_pairs={{0,8},{1,9},{2,10},{3,11},{4,12},{5,13},{6,14},{7,15},{8,0},{9,1},... | collective-permute-start | bytes 196616 | tf_op jit(solution)/shard_map/ppermute | solution.py:62
  115.3 7.0 %collective-permute-start.29 = (bf16[1,32,1024]{2,1,0:T(8,128)(2,1)S(1)}, bf16[1,32,1024]{2,1,0:T(8,128)(2,1)S(1)}, u32[]{:S(2)}, u32[]{:S(2)}) collective-permute-start(bf16[1,32,1024]{2,1,0:T(8,128)(2,1)S(1)} %get-tuple-element.125), channel_id=1, source_target_pairs={{0,8},{1,9},{2,10},{3,11},{4,12},{5,13},{6,14},{7,15},{8,0},{9,1},... | collective-permute-start | bytes 196616 | tf_op jit(solution)/shard_map/ppermute | solution.py:62
  115.5 5.3 %collective-permute-start.31 = (f32[64,64]{1,0:T(8,128)S(1)}, f32[64,64]{1,0:T(8,128)S(1)}, u32[]{:S(2)}, u32[]{:S(2)}) collective-permute-start(f32[64,64]{1,0:T(8,128)S(1)} %add.127), channel_id=1, source_target_pairs={{0,8},{1,9},{2,10},{3,11},{4,12},{5,13},{6,14},{7,15},{8,0},{9,1},... | collective-permute-start | bytes 49160 | tf_op jit(solution)/shard_map/ppermute | solution.py:62
  121.5 4.3 %collective-permute-start.30 = (bf16[1,32,1024]{2,1,0:T(8,128)(2,1)S(1)}, bf16[1,32,1024]{2,1,0:T(8,128)(2,1)S(1)}, u32[]{:S(2)}, u32[]{:S(2)}) collective-permute-start(bf16[1,32,1024]{2,1,0:T(8,128)(2,1)S(1)} %get-tuple-element.126), channel_id=1, source_target_pairs={{0,2},{1,3},{2,0},{3,1},{4,6},{5,7},{6,4},{7,5},{8,10},{9,11},{10,... | collective-permute-start | bytes 196616 | tf_op jit(solution)/shard_map/ppermute | solution.py:62
  125.7 6.7 %collective-permute-start.32 = (bf16[2,32,1024]{2,1,0:T(8,128)(2,1)S(1)}, bf16[2,32,1024]{2,1,0:T(8,128)(2,1)S(1)}, u32[]{:S(2)}, u32[]{:S(2)}) collective-permute-start(bf16[2,32,1024]{2,1,0:T(8,128)(2,1)S(1)} %pad_maximum_fusion.6), channel_id=1, source_target_pairs={{0,4},{1,5},{2,6},{3,7},{4,0},{5,1},{6,2},{7,3},{8,12},{9,13},{10,... | collective-permute-start | bytes 393224 | tf_op jit(solution)/shard_map/ppermute | solution.py:62
  127.4 6.0 %collective-permute-start.33 = (bf16[2,32,1024]{2,1,0:T(8,128)(2,1)S(1)}, bf16[2,32,1024]{2,1,0:T(8,128)(2,1)S(1)}, u32[]{:S(2)}, u32[]{:S(2)}) collective-permute-start(bf16[2,32,1024]{2,1,0:T(8,128)(2,1)S(1)} %pad_maximum_fusion.7), channel_id=1, source_target_pairs={{0,8},{1,9},{2,10},{3,11},{4,12},{5,13},{6,14},{7,15},{8,0},{9,1},... | collective-permute-start | bytes 393224 | tf_op jit(solution)/shard_map/ppermute | solution.py:62
  133.4 7.9 %collective-permute-start.36 = (bf16[4,32,1024]{2,1,0:T(8,128)(2,1)S(1)}, bf16[4,32,1024]{2,1,0:T(8,128)(2,1)S(1)}, u32[]{:S(2)}, u32[]{:S(2)}) collective-permute-start(bf16[4,32,1024]{2,1,0:T(8,128)(2,1)S(1)} %pad_maximum_fusion.3), channel_id=1, source_target_pairs={{0,4},{1,5},{2,6},{3,7},{4,0},{5,1},{6,2},{7,3},{8,12},{9,13},{10,... | collective-permute-start | bytes 786440 | tf_op jit(solution)/shard_map/ppermute | solution.py:62
  137.0 6.4 %collective-permute-start.34 = (bf16[4,32,1024]{2,1,0:T(8,128)(2,1)S(1)}, bf16[4,32,1024]{2,1,0:T(8,128)(2,1)S(1)}, u32[]{:S(2)}, u32[]{:S(2)}) collective-permute-start(bf16[4,32,1024]{2,1,0:T(8,128)(2,1)S(1)} %pad_maximum_fusion.2), channel_id=1, source_target_pairs={{0,2},{1,3},{2,0},{3,1},{4,6},{5,7},{6,4},{7,5},{8,10},{9,11},{10,... | collective-permute-start | bytes 786440 | tf_op jit(solution)/shard_map/ppermute | solution.py:62
  141.4 7.2 %collective-permute-start.37 = (bf16[8,32,1024]{2,1,0:T(8,128)(2,1)S(1)}, bf16[8,32,1024]{2,1,0:T(8,128)(2,1)S(1)}, u32[]{:S(2)}, u32[]{:S(2)}) collective-permute-start(bf16[8,32,1024]{2,1,0:T(8,128)(2,1)S(1)} %constant_dynamic-update-slice_fusion.6.refs_1_.refs_3_.refs_5_.refs_7_), channel_id=1, source_target_pairs={{0,1},{1,0},{2,3},{3,2},{4,5},{5,4},{6,7},{7,6},{8,9},{9,8},{10,11... | collective-permute-start | bytes 1572872 | tf_op jit(solution)/shard_map/ppermute | solution.py:62
  143.4 5.1 %collective-permute-start.35 = (bf16[8,32,1024]{2,1,0:T(8,128)(2,1)S(1)}, bf16[8,32,1024]{2,1,0:T(8,128)(2,1)S(1)}, u32[]{:S(2)}, u32[]{:S(2)}) collective-permute-start(bf16[8,32,1024]{2,1,0:T(8,128)(2,1)S(1)} %constant_dynamic-update-slice_fusion.4.refs_0_.refs_2_.refs_4_.refs_6_), channel_id=1, source_target_pairs={{0,1},{1,0},{2,3},{3,2},{4,5},{5,4},{6,7},{7,6},{8,9},{9,8},{10,11... | collective-permute-start | bytes 1572872 | tf_op jit(solution)/shard_map/ppermute | solution.py:62
  158.1 7.0 %collective-permute-start.39 = (f16[8,64,1024]{2,1,0:T(8,128)(2,1)S(1)}, f16[8,64,1024]{2,1,0:T(8,128)(2,1)S(1)}, u32[]{:S(2)}, u32[]{:S(2)}) collective-permute-start(f16[8,64,1024]{2,1,0:T(8,128)(2,1)S(1)} %multiply_convert_fusion), channel_id=1, source_target_pairs={{0,1},{1,0},{2,3},{3,2},{4,5},{5,4},{6,7},{7,6},{8,9},{9,8},{10,11... | collective-permute-start | bytes 3145736 | tf_op jit(solution)/shard_map/ppermute | solution.py:62
  161.1 4.0 %collective-permute-start.40 = (f32[64,64]{1,0:T(8,128)S(1)}, f32[64,64]{1,0:T(8,128)S(1)}, u32[]{:S(2)}, u32[]{:S(2)}) collective-permute-start(f32[64,64]{1,0:T(8,128)S(1)} %add.133), channel_id=1, source_target_pairs={{0,2},{1,3},{2,0},{3,1},{4,6},{5,7},{6,4},{7,5},{8,10},{9,11},{10,... | collective-permute-start | bytes 49160 | tf_op jit(solution)/shard_map/ppermute | solution.py:62
  166.2 8.5 %collective-permute-start.42 = (f16[2,2,32,1024]{3,2,1,0:T(8,128)(2,1)S(1)}, f16[2,2,32,1024]{3,2,1,0:T(8,128)(2,1)S(1)}, u32[]{:S(2)}, u32[]{:S(2)}) collective-permute-start(f16[2,2,32,1024]{3,2,1,0:T(8,128)(2,1)S(1)} %multiply_convert_fusion.2), channel_id=1, source_target_pairs={{0,4},{1,5},{2,6},{3,7},{4,0},{5,1},{6,2},{7,3},{8,12},{9,13},{10,... | collective-permute-start | bytes 786440 | tf_op jit(solution)/shard_map/ppermute | solution.py:62
  166.8 7.9 %collective-permute-start.43 = (f32[64,64]{1,0:T(8,128)S(1)}, f32[64,64]{1,0:T(8,128)S(1)}, u32[]{:S(2)}, u32[]{:S(2)}) collective-permute-start(f32[64,64]{1,0:T(8,128)S(1)} %add.135), channel_id=1, source_target_pairs={{0,4},{1,5},{2,6},{3,7},{4,0},{5,1},{6,2},{7,3},{8,12},{9,13},{10,... | collective-permute-start | bytes 49160 | tf_op jit(solution)/shard_map/ppermute | solution.py:62
  168.4 7.2 %collective-permute-start.41 = (f16[2,2,32,1024]{3,2,0,1:T(8,128)(2,1)S(1)}, f16[2,2,32,1024]{3,2,0,1:T(8,128)(2,1)S(1)}, u32[]{:S(2)}, u32[]{:S(2)}) collective-permute-start(f16[2,2,32,1024]{3,2,0,1:T(8,128)(2,1)S(1)} %multiply_convert_fusion.3), channel_id=1, source_target_pairs={{0,2},{1,3},{2,0},{3,1},{4,6},{5,7},{6,4},{7,5},{8,10},{9,11},{10,... | collective-permute-start | bytes 786440 | tf_op jit(solution)/shard_map/ppermute | solution.py:62
  175.8 6.2 %collective-permute-start.46 = (f32[64,64]{1,0:T(8,128)S(1)}, f32[64,64]{1,0:T(8,128)S(1)}, u32[]{:S(2)}, u32[]{:S(2)}) collective-permute-start(f32[64,64]{1,0:T(8,128)S(1)} %add.138), channel_id=1, source_target_pairs={{0,8},{1,9},{2,10},{3,11},{4,12},{5,13},{6,14},{7,15},{8,0},{9,1},... | collective-permute-start | bytes 49160 | tf_op jit(solution)/shard_map/ppermute | solution.py:62
  176.4 7.7 %collective-permute-start.45 = (f16[2,32,1024]{2,1,0:T(8,128)(2,1)S(1)}, f16[2,32,1024]{2,1,0:T(8,128)(2,1)S(1)}, u32[]{:S(2)}, u32[]{:S(2)}) collective-permute-start(f16[2,32,1024]{2,1,0:T(8,128)(2,1)S(1)} %multiply_convert_fusion.6), channel_id=1, source_target_pairs={{0,8},{1,9},{2,10},{3,11},{4,12},{5,13},{6,14},{7,15},{8,0},{9,1},... | collective-permute-start | bytes 393224 | tf_op jit(solution)/shard_map/ppermute | solution.py:62
  179.0 5.9 %collective-permute-start.44 = (f16[2,32,1024]{2,1,0:T(8,128)(2,1)S(1)}, f16[2,32,1024]{2,1,0:T(8,128)(2,1)S(1)}, u32[]{:S(2)}, u32[]{:S(2)}) collective-permute-start(f16[2,32,1024]{2,1,0:T(8,128)(2,1)S(1)} %multiply_convert_fusion.7), channel_id=1, source_target_pairs={{0,4},{1,5},{2,6},{3,7},{4,0},{5,1},{6,2},{7,3},{8,12},{9,13},{10,... | collective-permute-start | bytes 393224 | tf_op jit(solution)/shard_map/ppermute | solution.py:62
  185.1 7.6 %collective-permute-start.48 = (f16[32,1024]{1,0:T(8,128)(2,1)S(1)}, f16[32,1024]{1,0:T(8,128)(2,1)S(1)}, u32[]{:S(2)}, u32[]{:S(2)}) collective-permute-start(f16[32,1024]{1,0:T(8,128)(2,1)S(1)} %multiply_convert_fusion.10), channel_id=1, source_target_pairs={{0,2},{1,3},{2,0},{3,1},{4,6},{5,7},{6,4},{7,5},{8,10},{9,11},{10,... | collective-permute-start | bytes 196616 | tf_op jit(solution)/shard_map/ppermute | solution.py:62
  186.0 7.5 %collective-permute-start.47 = (f16[32,1024]{1,0:T(8,128)(2,1)S(1)}, f16[32,1024]{1,0:T(8,128)(2,1)S(1)}, u32[]{:S(2)}, u32[]{:S(2)}) collective-permute-start(f16[32,1024]{1,0:T(8,128)(2,1)S(1)} %multiply_convert_fusion.11), channel_id=1, source_target_pairs={{0,8},{1,9},{2,10},{3,11},{4,12},{5,13},{6,14},{7,15},{8,0},{9,1},... | collective-permute-start | bytes 196616 | tf_op jit(solution)/shard_map/ppermute | solution.py:62
  (9 other events, 41.9 us)

commit v7 on v0

v7 whole, which is shorter than its diff:
```python
import functools

import jax
import jax.numpy as jnp
from jax import lax
from jax.experimental import pallas as pl
from jax.experimental.pallas import tpu as pltpu
from jax.sharding import PartitionSpec as P

K = 64
HALF = K // 2
RIDGE = 0.1
BOUND = 18.0
TOP = 60000.0
TINY = 1e-30
F32, BF16, F16 = jnp.float32, jnp.bfloat16, jnp.float16


def precise(left, right):
    return jnp.dot(left, right, precision=lax.Precision.HIGHEST, preferred_element_type=F32)


def outer(left, right):
    return lax.dot_general(
        left, right, (((1,), (1,)), ((), ())), precision=lax.Precision.HIGHEST, preferred_element_type=F32
    )


def symmetric(matrix):
    return 0.5 * (matrix + matrix.T)


def solve_positive(*works):
    index = lax.broadcasted_iota(jnp.int32, (K, 1), 0)
    works = list(works)
    for first in range(0, K, 8):
        spread = [[jnp.broadcast_to(w[:, first + j : first + j + 1], w.shape) for j in range(8)] for w in works]
        for k in range(8):
            at = slice(first + k, first + k + 1)
            row = index == first + k
            for i, columns in enumerate(spread):
                column, inv = columns[k], 1.0 / columns[k][at]
                scaled = works[i][at] * inv
                works[i] = jnp.where(row, scaled, works[i] - column * scaled)
                for j in range(k + 1, 8):
                    scaled = columns[j][at] * inv
                    columns[j] = jnp.where(row, scaled, columns[j] - column * scaled)
    return [work[:, K:] for work in works]


def beside(matrix, target):
    return jnp.concatenate([matrix, target], axis=1)


def identity():
    eye = lax.broadcasted_iota(jnp.int32, (K, K), 0) == lax.broadcasted_iota(jnp.int32, (K, K), 1)
    return jnp.where(eye, 1.0, 0.0)


def rows_of(core, first, second):
    return jnp.where(core == 0, jnp.concatenate([first, second], axis=0), jnp.concatenate([second, first], axis=0))


class Hops:
    def __init__(self, n):
        self.n = n
        self.count = n.bit_length() - 2
        ups = list(range(self.count))
        self.orders = ups, ups[1:] + ups[:1]

    def swap(self, value, bit):
        return lax.ppermute(value, "dp", [(i, i ^ bit) for i in range(self.n)])

    def across(self, value, hop):
        return lax.ppermute(value, "dp", [(i, i ^ (2 << self.orders[i & 1][hop])) for i in range(self.n)])

    def _both(self, core, fn):
        zero, one = fn(self.orders[0]), fn(self.orders[1])
        return zero + core * (one - zero)

    def chip(self, seat, core):
        def place(order):
            return sum(((seat >> (self.count - 1 - i)) & 1) << b for i, b in enumerate(order))

        return self._both(core, place)

    def seat(self, chip, core):
        def place(order):
            return sum(((chip >> b) & 1) << (self.count - 1 - i) for i, b in enumerate(order))

        return self._both(core, place)

    def other_seat(self, seat, core):
        return self.seat(self.chip(seat, core), 1 - core)


def block_copy(hops, acts, kept, sems, me, t):
    f = kept.shape[2]
    index = me[0]
    first = pl.multiple_of(((index >> 1) ^ hops.chip(t, index & 1)) * f, f)
    return pltpu.make_async_copy(acts.at[:, pl.ds(first, f)], kept.at[t], sems.at[t])


def start_copies(hops, acts, kept, sems, me):
    def start(t, carry):
        block_copy(hops, acts, kept, sems, me, t).start()
        return carry

    lax.fori_loop(0, kept.shape[0], start, 0)


def whole(*shape):
    return pl.BlockSpec(shape, lambda i, me: (0,) * len(shape))


HBM = pl.BlockSpec(memory_space=pltpu.HBM)


def call(kernel, name, n, grid, in_specs, outs, acts, scratch):
    rows, d = acts.shape
    return pl.pallas_call(
        kernel,
        out_shape=tuple(jax.ShapeDtypeStruct(shape, F32) for shape, _ in outs),
        grid_spec=pltpu.PrefetchScalarGridSpec(
            num_scalar_prefetch=1,
            grid=(grid,),
            in_specs=in_specs,
            out_specs=tuple(spec for _, spec in outs),
            scratch_shapes=[
                pltpu.VMEM((n // 2, rows, 2 * d // n), BF16),
                pltpu.SemaphoreType.DMA((n // 2,)),
                *scratch,
            ],
        ),
        compiler_params=pltpu.CompilerParams(vmem_limit_bytes=28 << 20),
        cost_estimate=pl.CostEstimate(
            flops=2 * grid * K * rows * d // n, bytes_accessed=2 * rows * d + 4 * K * d, transcendentals=0
        ),
        name=name,
    )


def block_outs(hops, n, f, before):
    def here(i, me):
        return (jnp.maximum(i - before, 0), 0, 0)

    def there(i, me):
        return (hops.other_seat(jnp.maximum(i - before, 0), me[0] & 1), 0, 0)

    shape = (n // 2, HALF, f)
    return [(shape, pl.BlockSpec((1, HALF, f), here)), (shape, pl.BlockSpec((1, HALF, f), there))]


def count_of(row_data):
    return lax.shift_right_logical(row_data[...], 6).astype(F32)


def sums_kernel(hops, me, row_data, acts, keep, send, weight, kept, sems, member):
    step = pl.program_id(0)

    @pl.when(step == 0)
    def _():
        start_copies(hops, acts, kept, sems, me)
        concept = lax.broadcasted_iota(jnp.int32, member.shape, 0)
        full = jnp.where((row_data[...] & (K - 1)) == concept, count_of(row_data), 0.0)
        weight[...] = jnp.sum(full, axis=1, keepdims=True)
        member[...] = rows_of(me[0] & 1, full[:HALF], full[HALF:]).astype(BF16)

    block_copy(hops, acts, kept, sems, me, step).wait()
    block = jnp.dot(member[...], kept[step], preferred_element_type=F32)
    keep[0] = block[:HALF]
    send[0] = block[HALF:]


def class_sums(hops, me, row_data, acts):
    n = hops.n
    rows, d = acts.shape
    return call(
        functools.partial(sums_kernel, hops),
        "class_sums",
        n,
        n // 2,
        [whole(1, rows), HBM],
        block_outs(hops, n, 2 * d // n, 0) + [((K, 1), whole(K, 1))],
        acts,
        [pltpu.VMEM((K, rows), BF16)],
    )(me, row_data, acts)


def inner(left, right):
    return lax.dot_general(left, right, (((1,), (1,)), ((), ())), preferred_element_type=F32)


def diagonal(matrix):
    kept = matrix * identity()
    return jnp.sum(kept, axis=1, keepdims=True), jnp.sum(kept, axis=0, keepdims=True)


def finish_first(gram):
    current = symmetric(gram[...])
    gram[...] = current
    return jnp.sqrt(diagonal(current)[0])


def finish_second(probed, image_image, base_image, more):
    first, current, alpha_t, inverse, renewed, mixed, beta_t = more
    both = jnp.concatenate([base_image[...], symmetric(image_image[...])], axis=0)
    moved = outer(both, alpha_t[...])
    moved, twice = moved[:K], precise(alpha_t[...], moved[K:])
    new = symmetric(current[...] - moved - moved.T + twice)
    beta = precise(new, inverse[...])
    renewed[...] = new
    mixed[...] = current[...] - moved
    beta_t[...] = beta
    mix = jnp.concatenate([beta, -alpha_t[...]], axis=1)
    probed[...] = first[...] + precise(mix, jnp.concatenate([first[...], probed[...]], axis=0))
    base_col, base_row = diagonal(current[...])
    _, image_row = diagonal(image_image[...])
    norms = jnp.sqrt(base_col)
    norms += jnp.sum(jnp.abs(beta) * jnp.sqrt(base_row), axis=1, keepdims=True)
    return norms + jnp.sum(jnp.abs(alpha_t[...]) * jnp.sqrt(image_row), axis=1, keepdims=True)


def covariance_kernel(hops, count, d, me, *refs):
    steps = hops.n // 2
    second = count == 2
    refs = list(refs)
    panels, ins, given, outs, grams, made, scratch = (
        [refs.pop(0) for _ in range(size)] for size in (4 * count, 3, 4 * second, 6, count, 3 * second, 5)
    )
    acts, row_data, total_weight = ins
    keep, send, probed, along, back, back_row = outs
    kept, sems, weighted, sum_of, inv = scratch
    step = pl.program_id(0)
    core = me[0] & 1

    @pl.when(step == 0)
    def _():
        start_copies(hops, acts, kept, sems, me)
        for ref in (sum_of, *grams):
            ref[...] = jnp.zeros_like(ref)

    @pl.when(step < steps)
    def _():
        across = hops.other_seat(step, core)
        both = []
        for i in range(count):
            own_low, own_high, low, high = panels[4 * i : 4 * i + 4]
            own = jnp.where(step < steps // 2, own_low[0], own_high[0])
            other = jnp.where(across < steps // 2, low[0], high[0])
            both.append(rows_of(core, own, other))
        block_copy(hops, acts, kept, sems, me, step).wait()
        sum_of[...] += inner(kept[step], both[0])
        for gram, panel in zip(grams, both):
            gram[...] += inner(panel, both[0])

    @pl.when(step == steps)
    def _():
        probed[...] = sum_of[...].T
        norms = finish_second(probed, *grams, (*given, *made)) if second else finish_first(*grams)
        bound = jnp.maximum((1.02 * BOUND * BOUND * d**0.5) * total_weight[...] * norms, TINY)
        scale = bound * (1.0 / TOP)
        back[...] = jnp.where(core == 0, scale[:HALF], scale[HALF:])
        back_row[...] = jnp.sum(scale * identity(), axis=0, keepdims=True)
        inv[...] = rows_of(core, TOP / bound[:HALF], TOP / bound[HALF:])
        whole_weighted = count_of(row_data) * probed[...]
        rounded = whole_weighted.astype(BF16)
        weighted[...] = rows_of(core, rounded[:HALF], rounded[HALF:])
        along[...] = outer(probed[...], rounded.astype(F32))

    @pl.when(step >= steps)
    def _():
        block = jnp.dot(weighted[...], kept[step - steps], preferred_element_type=F32) * inv[...]
        keep[0] = block[:HALF]
        send[0] = block[HALF:]


def covariance(hops, me, panels, acts, row_data, total_weight, given):
    n = hops.n
    rows, d = acts.shape
    f = 2 * d // n
    s = n // 2
    count = len(panels)
    made = 3 if given else 0

    def spec(other, high):
        def pick(i, me):
            seat = jnp.minimum(i, s - 1)
            if other:
                seat = hops.other_seat(seat, me[0] & 1)
            return (jnp.maximum(seat - s // 2, 0) if high else jnp.minimum(seat, s // 2 - 1), 0, 0)

        return pl.BlockSpec((1, HALF, f), pick)

    specs = [spec(False, False), spec(False, True), spec(True, False), spec(True, True)] * count
    return call(
        functools.partial(covariance_kernel, hops, count, d),
        "covariance",
        n,
        2 * s,
        specs + [HBM, whole(1, rows), whole(1, 1)] + [whole(*x.shape) for x in given],
        block_outs(hops, n, f, s)
        + [(shape, whole(*shape)) for shape in ((K, rows), (K, K), (HALF, 1), (1, K))]
        + [((K, K), whole(K, K))] * (count + made),
        acts,
        [pltpu.VMEM((K, rows), BF16), pltpu.VMEM((rows, K), F32), pltpu.VMEM((K, 1), F32)],
    )(me, *[x for panel in panels for x in panel], acts, row_data, total_weight, *given)


def alpha_kernel(along, current, total_weight, alpha_t, inverse):
    now = current[...]
    curvature = (along[...] - precise(now, now)) / total_weight[...] + RIDGE * now
    alpha, inv = solve_positive(beside(symmetric(curvature), now), beside(now, identity()))
    alpha_t[...] = alpha.T
    inverse[...] = symmetric(inv)


def offset_kernel(me, own, other, current, total_weight, offset):
    core = me[0] & 1
    part = jnp.where(core == 0, current[:HALF], current[HALF:]) / total_weight[...]
    offset[...] = RIDGE * own[...] - precise(part, rows_of(core, own[...], other[...]))


def before_kernel(current, renewed, mixed, beta_t, total_weight, fixed, cross_t):
    now, beta, weight = current[...], beta_t[...], total_weight[...]
    cross = mixed[...] + outer(now, beta)
    length = renewed[...] + outer(mixed[...].T, beta) + precise(beta, cross)
    turned = cross.T
    cross_t[...] = turned
    fixed[...] = RIDGE * length - outer(turned, turned) / weight


def last_kernel(
    me, along, fixed, cross_t, renewed, beta_t, alpha_t, total_weight, back_row,
    base_own, base_other, image_own, image_other, solved, rest, on_panel,
):
    core = me[0] & 1
    weight = total_weight[...]
    curvature = symmetric(along[...] / weight + fixed[...])
    step = solve_positive(beside(curvature, renewed[...]))[0].T
    scaled = step * (back_row[...] / weight)
    on_panel[...] = jnp.where(core == 0, scaled, beside(scaled[:, HALF:], scaled[:, :HALF]))
    alpha = alpha_t[...]
    all_three = precise(step, jnp.concatenate([identity() + beta_t[...], alpha, cross_t[...]], axis=1))
    direction_base, direction_image = all_three[:, :K], all_three[:, K : 2 * K]
    crossed = all_three[:, 2 * K :] / weight
    f = solved.shape[1]
    here = pl.ds(pl.multiple_of(core * f, f), f)
    base = rows_of(core, base_own[:, here], base_other[:, here])
    image = rows_of(core, image_own[:, here], image_other[:, here])
    both = jnp.concatenate([base, image], axis=0)
    solved[...] = precise(beside(alpha + direction_base, -direction_image), both)
    rest[...] = precise(
        beside(identity() - RIDGE * direction_base + crossed, RIDGE * direction_image - alpha), both
    )


def small(kernel, name, outs, *args):
    specs = [pl.BlockSpec(memory_space=pltpu.SMEM if x.dtype == jnp.int32 else pltpu.VMEM) for x in args]
    return pl.pallas_call(
        kernel, out_shape=tuple(jax.ShapeDtypeStruct(shape, F32) for shape in outs), name=name, in_specs=specs,
        cost_estimate=pl.CostEstimate(flops=1 << 26, bytes_accessed=1 << 20, transcendentals=0),
    )(*args)


def plain(value):
    return value.astype(F16)


def widen(value):
    return value.astype(F32)


def root_code(bound):
    scale = TOP / bound**0.5

    def code(value):
        root = jnp.sqrt(jnp.abs(value)) * scale
        return jnp.where(value < 0, -root, root).astype(F16)

    def decode(value):
        value = value.astype(F32)
        return value * jnp.abs(value) * (1.0 / scale**2)

    return code, decode


def reduce_scatter(hops, keep, send, codec, along, early=0, work=None, args=()):
    code, decode = codec
    got = hops.swap(code(send), 1)
    along = along + hops.swap(along, 1)
    value, done = keep + decode(got), ()
    for hop in range(hops.count):
        half = value.shape[0] // 2
        tied = args if hop == 1 else done
        send, along, tied = lax.optimization_barrier((code(value[half:]), along, tied))
        value = value[:half] + decode(hops.across(send, hop))
        along = along + hops.swap(along, 2 << hop)
        if work is not None and hop >= 1:
            done = work(*tied) if hop == 1 else tied
    value, along = lax.optimization_barrier((value, along)) if not early else (value, along)
    return value[0], along, done


def gather(hops, own, work=None, args=()):
    value, done = own.astype(BF16)[None], ()
    for hop in reversed(range(hops.count)):
        second = hop == hops.count - 2
        tied = args if second else done
        value, tied = lax.optimization_barrier((value, tied))
        got = hops.across(value, hop)
        if hop == 0:
            low = hops.swap(value, 1)
            return (value, got, low, hops.swap(got, 1)), tied
        if work is not None and (second or done):
            done = work(*tied) if second else tied
        value = jnp.concatenate([value, got], axis=0)


def per_device(n, activations, labels, counts):
    rows, d = activations.shape
    hops = Hops(n)
    activations = pltpu.with_memory_space_constraint(activations, pltpu.HBM)
    index = lax.axis_index("dp").astype(jnp.int32)
    core, me = index & 1, index.reshape(1)
    row_data = (counts * K + labels).reshape(1, rows)
    square, strip, chip_strip = (K, K), (K, d // n), (HALF, 2 * d // n)

    keep, send, weight = class_sums(hops, me, row_data, activations)
    sums, weight, _ = reduce_scatter(hops, keep, send, root_code(BOUND * 4 * rows * n), weight.T)
    total_weight = jnp.sum(weight, keepdims=True)
    class_weight = lax.dynamic_slice_in_dim(weight, core * HALF, HALF, axis=1).T
    base = (sums / class_weight) * jnp.sqrt(class_weight)

    base_all, _ = gather(hops, base)
    keep, send, first, along, back, _, current = covariance(
        hops, me, (base_all,), activations, row_data, total_weight, ()
    )
    base_other = hops.swap(base, 1)
    panel, along, (offset,) = reduce_scatter(
        hops, keep, send, (plain, widen), along, 0,
        lambda *args: small(offset_kernel, "offset", (chip_strip,), *args),
        (me, base, base_other, current, total_weight),
    )
    image = panel * (back / total_weight) + offset

    image_all, (alpha_t, inverse) = gather(
        hops, image,
        lambda *args: small(alpha_kernel, "alpha", (square,) * 2, *args), (along, current, total_weight),
    )
    keep, send, _, along, _, back_row, _, _, renewed, mixed, beta_t = covariance(
        hops, me, (image_all, base_all), activations, row_data, total_weight, (first, current, alpha_t, inverse)
    )
    image_other = hops.swap(image, 1)
    panel, along, (fixed, cross_t) = reduce_scatter(
        hops, keep, send, (plain, widen), along, 1,
        lambda *args: small(before_kernel, "before", (square,) * 2, *args),
        (current, renewed, mixed, beta_t, total_weight),
    )
    by_core = panel.reshape(HALF, 2, d // n)
    mine = lax.dynamic_index_in_dim(by_core, core, 1, keepdims=False)
    theirs = widen(hops.swap(plain(lax.dynamic_index_in_dim(by_core, 1 - core, 1, keepdims=False)), 1))
    solved, rest, on_panel = small(
        last_kernel, "last", (strip, strip, square),
        me, along, fixed, cross_t, renewed, beta_t, alpha_t, total_weight, back_row,
        base, base_other, image, image_other,
    )
    residual = rest - precise(on_panel, jnp.concatenate([mine, theirs], axis=0))
    return (solved.T, residual.T)


def solution(mesh):
    in_specs = (P(("groups", "dp"), None), P(("groups", "dp")), P(("groups", "dp")))
    out_specs = (P(("groups", "dp"), None), P(("groups", "dp"), None))
    return jax.shard_map(
        functools.partial(per_device, mesh.shape["dp"]),
        mesh=mesh,
        in_specs=in_specs,
        out_specs=out_specs,
        check_vma=False,
    )
```

time: 588 us -> 209 us (0.36)
  blocking collectives: 211 us -> 0 us
  waiting for transfers between devices: 260 us -> 114 us
  matrix products: 62 us -> 1.11 us
  Pallas kernels: 0 us -> 47.3 us
  starting transfers between devices: 0.43 us -> 28.6 us
  other arithmetic: 39.4 us -> 12.4 us
  between operations: 14.1 us -> 1.12 us
    psum x4 -> x0, blocking collectives: 211 us -> none  [the longest x2 118 us: per_device(): lax.psum((precise(class_means.T, direction), precise(direction.T, panel),...]
    reduce_scatter x3 -> x0, waiting for transfers between devices: 180 us -> none  [the longest x2 140 us: per_device(): lax.psum_scatter(contract_rows(activations, weighted), 'dp', scatter_dime...]
    ppermute x0 -> x37, waiting for transfers between devices: none -> 114 us  [the longest x22 60.4 us: swap(): return lax.ppermute(value, 'dp', [(i, i ^ bit) for i in range(self.n)])]
    all_gather x2 -> x0, waiting for transfers between devices: 80.2 us -> none  [per_device(): lax.all_gather(direction.astype(jnp.bfloat16), 'dp', axis=0, tiled=True)]
    dot_general x19 -> x1, matrix products: 60.7 us -> 1.11 us  [precise(): jnp.dot(left, right, precision=lax.Precision.HIGHEST, preferred_element_t...]
    pallas_call x0 -> x7, Pallas kernels: none -> 47.3 us  [the longest x2 26.9 us: covariance(): call(functools.partial(covariance_kernel, hops, count, d), 'covariance',...]
    another operation x15 -> x6, other arithmetic: 36.2 us -> 0.91 us  [the longest x9 19.6 us: solve_positive(): jnp.linalg.cholesky(matrix)]
    ppermute x0 -> x37, starting transfers between devices: none -> 28.6 us  [the longest x15 19.2 us: across(): lax.ppermute(value, 'dp', [(i, i ^ 2 << self.orders[i & 1][hop]) for i in...]
  transfers between devices with their start and end apart: 5 -> 37, of which waited for: 5 -> 22; matrix products, arithmetic and copies ran while one was open for 0% -> 2% of each run, Pallas kernels for 0% -> 7%
where the time goes in v7:
time: 209 us; the launch traced here: 208 us
  waiting for transfers between devices  114 us (55%)
  Pallas kernels  47.3 us (23%)
  starting transfers between devices  28.6 us (14%)
  other arithmetic  12.4 us (6%)
  local copies, waits for them, and re-layouts  3.53 us (2%)
    ppermute x22, waiting for transfers between devices, swap(): return lax.ppermute(value, 'dp', [(i, i ^ bit) for i in range(self.n)])  60.4 us
    ppermute x15, waiting for transfers between devices, across(): lax.ppermute(value, 'dp', [(i, i ^ 2 << self.orders[i & 1][hop]) for i in...  54 us
    pallas_call x2, Pallas kernels, covariance(): call(functools.partial(covariance_kernel, hops, count, d), 'covariance',...  26.9 us
    ppermute x15, starting transfers between devices, across(): lax.ppermute(value, 'dp', [(i, i ^ 2 << self.orders[i & 1][hop]) for i in...  19.2 us
    pallas_call x4, Pallas kernels, small(): pl.pallas_call(kernel, out_shape=tuple((jax.ShapeDtypeStruct(shape, F32)...  15.2 us
    ppermute x22, starting transfers between devices, swap(): return lax.ppermute(value, 'dp', [(i, i ^ bit) for i in range(self.n)])  9.39 us
    pallas_call x1, Pallas kernels, class_sums(): call(functools.partial(sums_kernel, hops), 'class_sums', n, n // 2, [whol...  5.14 us
  transfers between devices with their start and end apart: 37, of which 22 were waited for; matrix products, arithmetic and copies ran while one was open for 2% of the time, Pallas kernels for 7%

profile of v7, /device:TPU:0, one launch (start us, length us, event | category | flops | bytes accessed | tf_op | source)
XLA Modules:
  0.0 208.4 jit_solution(17533188775047569924)
XLA Ops:
  1.3 5.1 %class_sums.1 = (f32[8,32,2048]{2,1,0:T(8,128)S(1)}, f32[8,32,2048]{2,1,0:T(8,128)S(1)}, f32[64,1]{1,0:T(8,128)S(1)}) custom-call(s32[1]{0:T(128)} %bitcast.me, s32[1,384]{1,0:T(1,128)S(1)} %reshape.36.row_data.refs_5_.refs_9_, bf16[384,16384]{1,0:T(8,128)(2,1)} %refs_8_.1), custom_call_target="tpu_custom_call" | custom-call | flops 402653184 | bytes 16777216 | tf_op jit(solution)/shard_map/class_sums/pallas_call | solution.py:178
  6.5 1.9 fusion
  9.1 2.1 collective-permute-done.1
  12.3 3.0 %collective-permute-start.2 = (f16[4,32,2048]{2,1,0:T(8,128)(2,1)S(1)}, f16[4,32,2048]{2,1,0:T(8,128)(2,1)S(1)}, u32[]{:S(2)}, u32[]{:S(2)}) collective-permute-start(f16[4,32,2048]{2,1,0:T(8,128)(2,1)S(1)} %fusion.3), channel_id=1, source_target_pairs={{0,2},{1,5},{2,0},{3,7},{4,6},{5,1},{6,4},{7,3},{8,10},{9,13},{10,... | collective-permute-start | bytes 1572872 | tf_op jit(solution)/shard_map/ppermute | solution.py:75
  15.3 7.1 %collective-permute-done.3 = f32[1,64]{1,0:T(1,128)S(1)} collective-permute-done((f32[1,64]{1,0:T(1,128)S(1)}, f32[1,64]{1,0:T(1,128)S(1)}, u32[]{:S(2)}, u32[]{:S(2)}) %collective-permute-start.3) | collective-permute-done | bytes 288 | tf_op jit(solution)/shard_map/ppermute | solution.py:72
  22.9 2.1 %collective-permute-start.4 = (f16[2,32,2048]{2,1,0:T(8,128)(2,1)S(1)}, f16[2,32,2048]{2,1,0:T(8,128)(2,1)S(1)}, u32[]{:S(2)}, u32[]{:S(2)}) collective-permute-start(f16[2,32,2048]{2,1,0:T(8,128)(2,1)S(1)} %fusion.6), channel_id=1, source_target_pairs={{0,4},{1,9},{2,6},{3,11},{4,0},{5,13},{6,2},{7,15},{8,12},{9,1},{1... | collective-permute-start | bytes 786440 | tf_op jit(solution)/shard_map/ppermute | solution.py:75
  25.2 5.9 %collective-permute-done.5 = f32[1,64]{1,0:T(1,128)S(1)} collective-permute-done((f32[1,64]{1,0:T(1,128)S(1)}, f32[1,64]{1,0:T(1,128)S(1)}, u32[]{:S(2)}, u32[]{:S(2)}) %collective-permute-start.5) | collective-permute-done | bytes 288 | tf_op jit(solution)/shard_map/ppermute | solution.py:72
  31.3 3.3 %collective-permute-start.6 = (f16[1,32,2048]{2,1,0:T(8,128)(2,1)S(1)}, f16[1,32,2048]{2,1,0:T(8,128)(2,1)S(1)}, u32[]{:S(2)}, u32[]{:S(2)}) collective-permute-start(f16[1,32,2048]{2,1,0:T(8,128)(2,1)S(1)} %fusion.9), channel_id=1, source_target_pairs={{0,8},{1,3},{2,10},{3,1},{4,12},{5,7},{6,14},{7,5},{8,0},{9,11},{1... | collective-permute-start | bytes 393224 | tf_op jit(solution)/shard_map/ppermute | solution.py:75
  34.7 4.4 %collective-permute-done.7 = f32[1,64]{1,0:T(1,128)S(1)} collective-permute-done((f32[1,64]{1,0:T(1,128)S(1)}, f32[1,64]{1,0:T(1,128)S(1)}, u32[]{:S(2)}, u32[]{:S(2)}) %collective-permute-start.7) | collective-permute-done | bytes 288 | tf_op jit(solution)/shard_map/ppermute | solution.py:72
  39.3 1.5 collective-permute-start.8
  40.9 9.4 %collective-permute-done.8 = bf16[1,32,2048]{2,1,0:T(8,128)(2,1)S(1)} collective-permute-done((bf16[1,32,2048]{2,1,0:T(8,128)(2,1)S(1)}, bf16[1,32,2048]{2,1,0:T(8,128)(2,1)S(1)}, u32[]{:S(2)}, u32[]{:S(2)}) %collective-permute-start.8) | collective-permute-done | bytes 131104 | tf_op jit(solution)/shard_map/ppermute | solution.py:75
  50.5 8.2 %collective-permute-done.9 = bf16[2,32,2048]{2,1,0:T(8,128)(2,1)S(1)} collective-permute-done((bf16[2,32,2048]{2,1,0:T(8,128)(2,1)S(1)}, bf16[2,32,2048]{2,1,0:T(8,128)(2,1)S(1)}, u32[]{:S(2)}, u32[]{:S(2)}) %collective-permute-start.9) | collective-permute-done | bytes 262176 | tf_op jit(solution)/shard_map/ppermute | solution.py:75
  58.7 3.0 %collective-permute-start.10 = (bf16[4,32,2048]{2,1,0:T(8,128)(2,1)S(1)}, bf16[4,32,2048]{2,1,0:T(8,128)(2,1)S(1)}, u32[]{:S(2)}, u32[]{:S(2)}) collective-permute-start(bf16[4,32,2048]{2,1,0:T(8,128)(2,1)S(1)} %pad_maximum_fusion.refs_0_.refs_4_), channel_id=1, source_target_pairs={{0,2},{1,5},{2,0},{3,7},{4,6},{5,1},{6,4},{7,3},{8,10},{9,13},{10,... | collective-permute-start | bytes 1572872 | tf_op jit(solution)/shard_map/ppermute | solution.py:75
  61.7 7.2 %collective-permute-done.10.refs_1_.refs_5_ = bf16[4,32,2048]{2,1,0:T(8,128)(2,1)S(1)} collective-permute-done((bf16[4,32,2048]{2,1,0:T(8,128)(2,1)S(1)}, bf16[4,32,2048]{2,1,0:T(8,128)(2,1)S(1)}, u32[]{:S(2)}, u32[]{:S(2)}) %collective-permute-start.10) | collective-permute-done | bytes 524320 | tf_op jit(solution)/shard_map/ppermute | solution.py:75
  69.5 1.3 collective-permute-done.12.refs_3_.refs_7_
  70.8 12.5 %covariance.2 = (f32[8,32,2048]{2,1,0:T(8,128)S(1)}, f32[8,32,2048]{2,1,0:T(8,128)S(1)}, f32[64,384]{1,0:T(8,128)S(1)}, f32[64,64]{1,0:T(8,128)S(1)}, f32[32,1]{...) custom-call(s32[1]{0:T(128)} %bitcast.me, bf16[4,32,2048]{2,1,0:T(8,128)(2,1)S(1)} %pad_maximum_fusion.refs_0_.refs_4_, ...), custom_call_target="tpu_custom_call" | custom-call | flops 805306368 | bytes 16777216 | tf_op jit(solution)/shard_map/covariance/pallas_call | solution.py:296
  84.0 2.2 %collective-permute-done.14 = f32[64,64]{1,0:T(8,128)S(1)} collective-permute-done((f32[64,64]{1,0:T(8,128)S(1)}, f32[64,64]{1,0:T(8,128)S(1)}, u32[]{:S(2)}, u32[]{:S(2)}) %collective-permute-start.14) | collective-permute-done | bytes 16416 | tf_op jit(solution)/shard_map/ppermute | solution.py:72
  86.6 2.1 %collective-permute-start.15 = (f16[4,32,2048]{2,1,0:T(8,128)(2,1)S(1)}, f16[4,32,2048]{2,1,0:T(8,128)(2,1)S(1)}, u32[]{:S(2)}, u32[]{:S(2)}) collective-permute-start(f16[4,32,2048]{2,1,0:T(8,128)(2,1)S(1)} %slice_convert_fusion.1), channel_id=1, source_target_pairs={{0,2},{1,5},{2,0},{3,7},{4,6},{5,1},{6,4},{7,3},{8,10},{9,13},{10,... | collective-permute-start | bytes 1572872 | tf_op jit(solution)/shard_map/ppermute | solution.py:75
  89.0 7.2 %collective-permute-done.16 = f32[64,64]{1,0:T(8,128)S(1)} collective-permute-done((f32[64,64]{1,0:T(8,128)S(1)}, f32[64,64]{1,0:T(8,128)S(1)}, u32[]{:S(2)}, u32[]{:S(2)}) %collective-permute-start.16) | collective-permute-done | bytes 16416 | tf_op jit(solution)/shard_map/ppermute | solution.py:72
  96.4 0.7 slice_convert_fusion.3
  97.9 1.9 collective-permute-start.19
  99.9 2.8 %offset.1 = f32[32,2048]{1,0:T(8,128)} custom-call(s32[1]{0:T(128)} %bitcast.me, f32[32,2048]{1,0:T(8,128)} %copy-done.8, f32[32,2048]{1,0:T(8,128)} %copy-done.11, f32[64,64]{1,0:T(8,128)} %copy-done, f32[1,1]{1,0:T(1,128)} %bitcast.2.refs_6_.total_weight.refs_10_), custom_call_target="tpu_custom_call" | custom-call | flops 67108864 | bytes 1048576 | tf_op jit(solution)/shard_map/offset/pallas_call | solution.py:360
  102.6 4.8 %collective-permute-done.19 = f32[64,64]{1,0:T(8,128)S(1)} collective-permute-done((f32[64,64]{1,0:T(8,128)S(1)}, f32[64,64]{1,0:T(8,128)S(1)}, u32[]{:S(2)}, u32[]{:S(2)}) %collective-permute-start.19) | collective-permute-done | bytes 16416 | tf_op jit(solution)/shard_map/ppermute | solution.py:72
  107.5 1.0 slice_add_fusion.3
  109.0 2.5 %collective-permute-start.21 = (f32[64,64]{1,0:T(8,128)S(1)}, f32[64,64]{1,0:T(8,128)S(1)}, u32[]{:S(2)}, u32[]{:S(2)}) collective-permute-start(f32[64,64]{1,0:T(8,128)S(1)} %add.104), channel_id=1, source_target_pairs={{0,8},{1,9},{2,10},{3,11},{4,12},{5,13},{6,14},{7,15},{8,0},{9,1},... | collective-permute-start | bytes 49160 | tf_op jit(solution)/shard_map/ppermute | solution.py:72
  111.6 0.7 divide_reduce_fusion
  112.3 3.9 %collective-permute-done.21 = f32[64,64]{1,0:T(8,128)S(1)} collective-permute-done((f32[64,64]{1,0:T(8,128)S(1)}, f32[64,64]{1,0:T(8,128)S(1)}, u32[]{:S(2)}, u32[]{:S(2)}) %collective-permute-start.21) | collective-permute-done | bytes 16416 | tf_op jit(solution)/shard_map/ppermute | solution.py:72
  117.3 10.8 %collective-permute-done.22 = bf16[1,32,2048]{2,1,0:T(8,128)(2,1)S(1)} collective-permute-done((bf16[1,32,2048]{2,1,0:T(8,128)(2,1)S(1)}, bf16[1,32,2048]{2,1,0:T(8,128)(2,1)S(1)}, u32[]{:S(2)}, u32[]{:S(2)}) %collective-permute-start.22) | collective-permute-done | bytes 131104 | tf_op jit(solution)/shard_map/ppermute | solution.py:75
  128.2 4.4 %alpha.1 = (f32[64,64]{1,0:T(8,128)}, f32[64,64]{1,0:T(8,128)}) custom-call(f32[64,64]{1,0:T(8,128)} %add.106.along, f32[64,64]{1,0:T(8,128)} %copy-done, f32[1,1]{1,0:T(1,128)} %bitcast.2.refs_6_.total_weight.refs_10_), custom_call_target="tpu_custom_call" | custom-call | flops 67108864 | bytes 1048576 | tf_op jit(solution)/shard_map/alpha/pallas_call | solution.py:360
  132.6 4.5 %collective-permute-done.23 = bf16[2,32,2048]{2,1,0:T(8,128)(2,1)S(1)} collective-permute-done((bf16[2,32,2048]{2,1,0:T(8,128)(2,1)S(1)}, bf16[2,32,2048]{2,1,0:T(8,128)(2,1)S(1)}, u32[]{:S(2)}, u32[]{:S(2)}) %collective-permute-start.23) | collective-permute-done | bytes 262176 | tf_op jit(solution)/shard_map/ppermute | solution.py:75
  137.1 1.5 collective-permute-start.24
  138.6 7.8 %collective-permute-done.24.refs_1_ = bf16[4,32,2048]{2,1,0:T(8,128)(2,1)S(1)} collective-permute-done((bf16[4,32,2048]{2,1,0:T(8,128)(2,1)S(1)}, bf16[4,32,2048]{2,1,0:T(8,128)(2,1)S(1)}, u32[]{:S(2)}, u32[]{:S(2)}) %collective-permute-start.24) | collective-permute-done | bytes 524320 | tf_op jit(solution)/shard_map/ppermute | solution.py:75
  146.4 1.9 collective-permute-done.26.refs_3_
  148.3 0.8 copy-done.2
  149.1 0.8 copy-done.3
  149.8 14.4 %covariance.3 = (f32[8,32,2048]{2,1,0:T(8,128)S(1)}, f32[8,32,2048]{2,1,0:T(8,128)S(1)}, f32[64,384]{1,0:T(8,128)}, f32[64,64]{1,0:T(8,128)S(1)}, f32[32,1]{1,0:...) custom-call(s32[1]{0:T(128)} %bitcast.me, ...), custom_call_target="tpu_custom_call" | custom-call | flops 805306368 | bytes 16777216 | tf_op jit(solution)/shard_map/covariance/pallas_call | solution.py:296
  165.0 2.2 %collective-permute-done.28 = f32[64,64]{1,0:T(8,128)S(1)} collective-permute-done((f32[64,64]{1,0:T(8,128)S(1)}, f32[64,64]{1,0:T(8,128)S(1)}, u32[]{:S(2)}, u32[]{:S(2)}) %collective-permute-start.28) | collective-permute-done | bytes 16416 | tf_op jit(solution)/shard_map/ppermute | solution.py:72
  167.6 1.5 collective-permute-start.29
  169.7 7.5 %collective-permute-done.30 = f32[64,64]{1,0:T(8,128)S(1)} collective-permute-done((f32[64,64]{1,0:T(8,128)S(1)}, f32[64,64]{1,0:T(8,128)S(1)}, u32[]{:S(2)}, u32[]{:S(2)}) %collective-permute-start.30) | collective-permute-done | bytes 16416 | tf_op jit(solution)/shard_map/ppermute | solution.py:72
  177.5 2.0 collective-permute-start.32
  179.5 2.5 %before.1 = (f32[64,64]{1,0:T(8,128)}, f32[64,64]{1,0:T(8,128)}) custom-call(f32[64,64]{1,0:T(8,128)} %copy-done, f32[64,64]{1,0:T(8,128)} %copy-done.4, f32[64,64]{1,0:T(8,128)} %copy-done.7, f32[64,64]{1,0:T(8,128)} %copy-done.5, f32[1,1]{1,0:T(1,128)} %bitcast.2.refs_6_.total_weight.refs_10_), custom_call_target="tpu_custom_call" | custom-call | flops 67108864 | bytes 1048576 | tf_op jit(solution)/shard_map/before/pallas_call | solution.py:360
  182.0 4.7 %collective-permute-done.32 = f32[64,64]{1,0:T(8,128)S(1)} collective-permute-done((f32[64,64]{1,0:T(8,128)S(1)}, f32[64,64]{1,0:T(8,128)S(1)}, u32[]{:S(2)}, u32[]{:S(2)}) %collective-permute-start.32) | collective-permute-done | bytes 16416 | tf_op jit(solution)/shard_map/ppermute | solution.py:72
  187.0 6.1 %collective-permute-done.35 = f16[1,32,2048]{2,1,0:T(8,128)(2,1)S(1)} collective-permute-done((f16[1,32,2048]{2,1,0:T(8,128)(2,1)S(1)}, f16[1,32,2048]{2,1,0:T(8,128)(2,1)S(1)}, u32[]{:S(2)}, u32[]{:S(2)}) %collective-permute-start.35) | collective-permute-done | bytes 131104 | tf_op jit(solution)/shard_map/ppermute | solution.py:75
  193.9 4.8 %collective-permute-done.33 = f32[64,64]{1,0:T(8,128)S(1)} collective-permute-done((f32[64,64]{1,0:T(8,128)S(1)}, f32[64,64]{1,0:T(8,128)S(1)}, u32[]{:S(2)}, u32[]{:S(2)}) %collective-permute-start.33) | collective-permute-done | bytes 16416 | tf_op jit(solution)/shard_map/ppermute | solution.py:72
  199.3 0.7 copy-done.12
  200.0 5.6 %last.1 = (f32[64,1024]{1,0:T(8,128)}, f32[64,1024]{1,0:T(8,128)}, f32[64,64]{1,0:T(8,128)}) custom-call(s32[1]{0:T(128)} %bitcast.me, f32[64,64]{1,0:T(8,128)} %add.114.along, f32[64,64]{1,0:T(8,128)} %get-tuple-element.125.fixed, f32[64,64]{1,0:T(8,128)} %get-tuple-element.126.cross_t, f32[64,64]{1,0:T(8,128)} %copy-done.4, f32[64,64]{1,0:T(8,128)} %copy-done.5, ...), custom_call_target="tpu_custom_call" | custom-call | flops 67108864 | bytes 1048576 | tf_op jit(solution)/shard_map/last/pallas_call | solution.py:360
  205.6 1.1 fusion.12
  206.7 1.7 subtract_bitcast_fusion
  (115 shorter events, 12.2 us)
Async XLA Ops:
  8.4 3.0 %collective-permute-start = (f16[8,32,2048]{2,1,0:T(8,128)(2,1)}, f16[8,32,2048]{2,1,0:T(8,128)(2,1)S(1)}, u32[]{:S(2)}, u32[]{:S(2)}) collective-permute-start(f16[8,32,2048]{2,1,0:T(8,128)(2,1)} %fusion), channel_id=1, source_target_pairs={{0,1},{1,0},{2,3},{3,2},{4,5},{5,4},{6,7},{7,6},{8,9},{9,8},{10,11... | collective-permute-start | bytes 3145736 | tf_op jit(solution)/shard_map/ppermute | solution.py:72
  9.0 2.2 %collective-permute-start.1 = (f32[1,64]{1,0:T(1,128)S(1)}, f32[1,64]{1,0:T(1,128)S(1)}, u32[]{:S(2)}, u32[]{:S(2)}) collective-permute-start(f32[1,64]{1,0:T(1,128)S(1)} %bitcast.28), channel_id=1, source_target_pairs={{0,1},{1,0},{2,3},{3,2},{4,5},{5,4},{6,7},{7,6},{8,9},{9,8},{10,11... | collective-permute-start | bytes 776 | tf_op jit(solution)/shard_map/ppermute | solution.py:72
  12.3 10.2 %collective-permute-start.2 = (f16[4,32,2048]{2,1,0:T(8,128)(2,1)S(1)}, f16[4,32,2048]{2,1,0:T(8,128)(2,1)S(1)}, u32[]{:S(2)}, u32[]{:S(2)}) collective-permute-start(f16[4,32,2048]{2,1,0:T(8,128)(2,1)S(1)} %fusion.3), channel_id=1, source_target_pairs={{0,2},{1,5},{2,0},{3,7},{4,6},{5,1},{6,4},{7,3},{8,10},{9,13},{10,... | collective-permute-start | bytes 1572872 | tf_op jit(solution)/shard_map/ppermute | solution.py:75
  15.2 7.2 %collective-permute-start.3 = (f32[1,64]{1,0:T(1,128)S(1)}, f32[1,64]{1,0:T(1,128)S(1)}, u32[]{:S(2)}, u32[]{:S(2)}) collective-permute-start(f32[1,64]{1,0:T(1,128)S(1)} %bitcast_add_fusion), channel_id=1, source_target_pairs={{0,2},{1,3},{2,0},{3,1},{4,6},{5,7},{6,4},{7,5},{8,10},{9,11},{10,... | collective-permute-start | bytes 776 | tf_op jit(solution)/shard_map/ppermute | solution.py:72
  22.9 8.1 %collective-permute-start.4 = (f16[2,32,2048]{2,1,0:T(8,128)(2,1)S(1)}, f16[2,32,2048]{2,1,0:T(8,128)(2,1)S(1)}, u32[]{:S(2)}, u32[]{:S(2)}) collective-permute-start(f16[2,32,2048]{2,1,0:T(8,128)(2,1)S(1)} %fusion.6), channel_id=1, source_target_pairs={{0,4},{1,9},{2,6},{3,11},{4,0},{5,13},{6,2},{7,15},{8,12},{9,1},{1... | collective-permute-start | bytes 786440 | tf_op jit(solution)/shard_map/ppermute | solution.py:75
  25.1 6.0 %collective-permute-start.5 = (f32[1,64]{1,0:T(1,128)S(1)}, f32[1,64]{1,0:T(1,128)S(1)}, u32[]{:S(2)}, u32[]{:S(2)}) collective-permute-start(f32[1,64]{1,0:T(1,128)S(1)} %add.93), channel_id=1, source_target_pairs={{0,4},{1,5},{2,6},{3,7},{4,0},{5,1},{6,2},{7,3},{8,12},{9,13},{10,... | collective-permute-start | bytes 776 | tf_op jit(solution)/shard_map/ppermute | solution.py:72
  31.3 7.8 %collective-permute-start.6 = (f16[1,32,2048]{2,1,0:T(8,128)(2,1)S(1)}, f16[1,32,2048]{2,1,0:T(8,128)(2,1)S(1)}, u32[]{:S(2)}, u32[]{:S(2)}) collective-permute-start(f16[1,32,2048]{2,1,0:T(8,128)(2,1)S(1)} %fusion.9), channel_id=1, source_target_pairs={{0,8},{1,3},{2,10},{3,1},{4,12},{5,7},{6,14},{7,5},{8,0},{9,11},{1... | collective-permute-start | bytes 393224 | tf_op jit(solution)/shard_map/ppermute | solution.py:75
  34.6 4.5 %collective-permute-start.7 = (f32[1,64]{1,0:T(1,128)S(1)}, f32[1,64]{1,0:T(1,128)S(1)}, u32[]{:S(2)}, u32[]{:S(2)}) collective-permute-start(f32[1,64]{1,0:T(1,128)S(1)} %add.95), channel_id=1, source_target_pairs={{0,8},{1,9},{2,10},{3,11},{4,12},{5,13},{6,14},{7,15},{8,0},{9,1},... | collective-permute-start | bytes 776 | tf_op jit(solution)/shard_map/ppermute | solution.py:72
  39.3 10.9 %collective-permute-start.8 = (bf16[1,32,2048]{2,1,0:T(8,128)(2,1)S(1)}, bf16[1,32,2048]{2,1,0:T(8,128)(2,1)S(1)}, u32[]{:S(2)}, u32[]{:S(2)}) collective-permute-start(bf16[1,32,2048]{2,1,0:T(8,128)(2,1)S(1)} %multiply_convert_fusion), channel_id=1, source_target_pairs={{0,8},{1,3},{2,10},{3,1},{4,12},{5,7},{6,14},{7,5},{8,0},{9,11},{1... | collective-permute-start | bytes 393224 | tf_op jit(solution)/shard_map/ppermute | solution.py:75
  50.3 8.4 %collective-permute-start.9 = (bf16[2,32,2048]{2,1,0:T(8,128)(2,1)S(1)}, bf16[2,32,2048]{2,1,0:T(8,128)(2,1)S(1)}, u32[]{:S(2)}, u32[]{:S(2)}) collective-permute-start(bf16[2,32,2048]{2,1,0:T(8,128)(2,1)S(1)} %pad_maximum_fusion.2), channel_id=1, source_target_pairs={{0,4},{1,9},{2,6},{3,11},{4,0},{5,13},{6,2},{7,15},{8,12},{9,1},{1... | collective-permute-start | bytes 786440 | tf_op jit(solution)/shard_map/ppermute | solution.py:75
  58.7 10.1 %collective-permute-start.10 = (bf16[4,32,2048]{2,1,0:T(8,128)(2,1)S(1)}, bf16[4,32,2048]{2,1,0:T(8,128)(2,1)S(1)}, u32[]{:S(2)}, u32[]{:S(2)}) collective-permute-start(bf16[4,32,2048]{2,1,0:T(8,128)(2,1)S(1)} %pad_maximum_fusion.refs_0_.refs_4_), channel_id=1, source_target_pairs={{0,2},{1,5},{2,0},{3,7},{4,6},{5,1},{6,4},{7,3},{8,10},{9,13},{10,... | collective-permute-start | bytes 1572872 | tf_op jit(solution)/shard_map/ppermute | solution.py:75
  61.7 7.8 %collective-permute-start.11 = (bf16[4,32,2048]{2,1,0:T(8,128)(2,1)S(1)}, bf16[4,32,2048]{2,1,0:T(8,128)(2,1)S(1)}, u32[]{:S(2)}, u32[]{:S(2)}) collective-permute-start(bf16[4,32,2048]{2,1,0:T(8,128)(2,1)S(1)} %pad_maximum_fusion.refs_0_.refs_4_), channel_id=1, source_target_pairs={{0,1},{1,0},{2,3},{3,2},{4,5},{5,4},{6,7},{7,6},{8,9},{9,8},{10,11... | collective-permute-start | bytes 1572872 | tf_op jit(solution)/shard_map/ppermute | solution.py:72
  68.8 1.9 collective-permute-start.12
  83.3 3.3 %copy-start = (f32[64,64]{1,0:T(8,128)}, f32[64,64]{1,0:T(8,128)S(1)}, u32[]{:S(2)}) copy-start(f32[64,64]{1,0:T(8,128)S(1)} %get-tuple-element.117.current.refs_12_) | copy-start | bytes 49156
  83.4 2.8 %collective-permute-start.13 = (f16[8,32,2048]{2,1,0:T(8,128)(2,1)S(1)}, f16[8,32,2048]{2,1,0:T(8,128)(2,1)S(1)}, u32[]{:S(2)}, u32[]{:S(2)}) collective-permute-start(f16[8,32,2048]{2,1,0:T(8,128)(2,1)S(1)} %convert_element_type.85), channel_id=1, source_target_pairs={{0,1},{1,0},{2,3},{3,2},{4,5},{5,4},{6,7},{7,6},{8,9},{9,8},{10,11... | collective-permute-start | bytes 3145736 | tf_op jit(solution)/shard_map/ppermute | solution.py:72
  83.6 2.6 %collective-permute-start.14 = (f32[64,64]{1,0:T(8,128)S(1)}, f32[64,64]{1,0:T(8,128)S(1)}, u32[]{:S(2)}, u32[]{:S(2)}) collective-permute-start(f32[64,64]{1,0:T(8,128)S(1)} %get-tuple-element.80), channel_id=1, source_target_pairs={{0,1},{1,0},{2,3},{3,2},{4,5},{5,4},{6,7},{7,6},{8,9},{9,8},{10,11... | collective-permute-start | bytes 49160 | tf_op jit(solution)/shard_map/ppermute | solution.py:72
  86.6 9.6 %collective-permute-start.15 = (f16[4,32,2048]{2,1,0:T(8,128)(2,1)S(1)}, f16[4,32,2048]{2,1,0:T(8,128)(2,1)S(1)}, u32[]{:S(2)}, u32[]{:S(2)}) collective-permute-start(f16[4,32,2048]{2,1,0:T(8,128)(2,1)S(1)} %slice_convert_fusion.1), channel_id=1, source_target_pairs={{0,2},{1,5},{2,0},{3,7},{4,6},{5,1},{6,4},{7,3},{8,10},{9,13},{10,... | collective-permute-start | bytes 1572872 | tf_op jit(solution)/shard_map/ppermute | solution.py:75
  88.7 7.5 %collective-permute-start.16 = (f32[64,64]{1,0:T(8,128)S(1)}, f32[64,64]{1,0:T(8,128)S(1)}, u32[]{:S(2)}, u32[]{:S(2)}) collective-permute-start(f32[64,64]{1,0:T(8,128)S(1)} %add.100), channel_id=1, source_target_pairs={{0,2},{1,3},{2,0},{3,1},{4,6},{5,7},{6,4},{7,5},{8,10},{9,11},{10,... | collective-permute-start | bytes 49160 | tf_op jit(solution)/shard_map/ppermute | solution.py:72
  88.9 7.5 %copy-start.8 = (f32[32,2048]{1,0:T(8,128)}, f32[32,2048]{1,0:T(8,128)S(1)}, u32[]{:S(2)}) copy-start(f32[32,2048]{1,0:T(8,128)S(1)} %fusion.17.own.base_own) | copy-start | bytes 786436
  88.9 8.2 %collective-permute-start.17 = (f32[32,2048]{1,0:T(8,128)S(1)}, f32[32,2048]{1,0:T(8,128)S(1)}, u32[]{:S(2)}, u32[]{:S(2)}) collective-permute-start(f32[32,2048]{1,0:T(8,128)S(1)} %fusion.17.own.base_own), channel_id=1, source_target_pairs={{0,1},{1,0},{2,3},{3,2},{4,5},{5,4},{6,7},{7,6},{8,9},{9,8},{10,11... | collective-permute-start | bytes 786440 | tf_op jit(solution)/shard_map/ppermute | solution.py:72
  97.8 9.6 %collective-permute-start.18 = (f16[2,32,2048]{2,1,0:T(8,128)(2,1)}, f16[2,32,2048]{2,1,0:T(8,128)(2,1)}, u32[]{:S(2)}, u32[]{:S(2)}) collective-permute-start(f16[2,32,2048]{2,1,0:T(8,128)(2,1)} %slice_convert_fusion.3), channel_id=1, source_target_pairs={{0,4},{1,9},{2,6},{3,11},{4,0},{5,13},{6,2},{7,15},{8,12},{9,1},{1... | collective-permute-start | bytes 786440 | tf_op jit(solution)/shard_map/ppermute | solution.py:75
  97.9 9.6 %collective-permute-start.19 = (f32[64,64]{1,0:T(8,128)S(1)}, f32[64,64]{1,0:T(8,128)S(1)}, u32[]{:S(2)}, u32[]{:S(2)}) collective-permute-start(f32[64,64]{1,0:T(8,128)S(1)} %add.102), channel_id=1, source_target_pairs={{0,4},{1,5},{2,6},{3,7},{4,0},{5,1},{6,2},{7,3},{8,12},{9,13},{10,... | collective-permute-start | bytes 49160 | tf_op jit(solution)/shard_map/ppermute | solution.py:72
  102.6 14.2 %copy-start.9 = (f32[32,2048]{1,0:T(8,128)S(1)}, f32[32,2048]{1,0:T(8,128)}, u32[]{:S(2)}) copy-start(f32[32,2048]{1,0:T(8,128)} %offset.1) | copy-start | bytes 786436
  108.5 39.8 %copy-start.1 = (f32[64,64]{1,0:T(8,128)S(1)}, f32[64,64]{1,0:T(8,128)}, u32[]{:S(2)}) copy-start(f32[64,64]{1,0:T(8,128)} %copy-done) | copy-start | bytes 49156
  108.6 8.3 %collective-permute-start.20 = (f16[1,32,2048]{2,1,0:T(8,128)(2,1)S(1)}, f16[1,32,2048]{2,1,0:T(8,128)(2,1)S(1)}, u32[]{:S(2)}, u32[]{:S(2)}) collective-permute-start(f16[1,32,2048]{2,1,0:T(8,128)(2,1)S(1)} %slice_convert_fusion.5), channel_id=1, source_target_pairs={{0,8},{1,3},{2,10},{3,1},{4,12},{5,7},{6,14},{7,5},{8,0},{9,11},{1... | collective-permute-start | bytes 393224 | tf_op jit(solution)/shard_map/ppermute | solution.py:75
  109.0 7.2 %collective-permute-start.21 = (f32[64,64]{1,0:T(8,128)S(1)}, f32[64,64]{1,0:T(8,128)S(1)}, u32[]{:S(2)}, u32[]{:S(2)}) collective-permute-start(f32[64,64]{1,0:T(8,128)S(1)} %add.104), channel_id=1, source_target_pairs={{0,8},{1,9},{2,10},{3,11},{4,12},{5,13},{6,14},{7,15},{8,0},{9,1},... | collective-permute-start | bytes 49160 | tf_op jit(solution)/shard_map/ppermute | solution.py:72
  117.0 70.0 %copy-start.10 = (f32[32,2048]{1,0:T(8,128)}, f32[32,2048]{1,0:T(8,128)S(1)}, u32[]{:S(2)}) copy-start(f32[32,2048]{1,0:T(8,128)S(1)} %get-tuple-element.133.image_own) | copy-start | bytes 786436
  117.0 11.1 %collective-permute-start.22 = (bf16[1,32,2048]{2,1,0:T(8,128)(2,1)S(1)}, bf16[1,32,2048]{2,1,0:T(8,128)(2,1)S(1)}, u32[]{:S(2)}, u32[]{:S(2)}) collective-permute-start(bf16[1,32,2048]{2,1,0:T(8,128)(2,1)S(1)} %get-tuple-element.132), channel_id=1, source_target_pairs={{0,8},{1,3},{2,10},{3,1},{4,12},{5,7},{6,14},{7,5},{8,0},{9,11},{1... | collective-permute-start | bytes 393224 | tf_op jit(solution)/shard_map/ppermute | solution.py:75
  128.1 9.0 %collective-permute-start.23 = (bf16[2,32,2048]{2,1,0:T(8,128)(2,1)S(1)}, bf16[2,32,2048]{2,1,0:T(8,128)(2,1)S(1)}, u32[]{:S(2)}, u32[]{:S(2)}) collective-permute-start(bf16[2,32,2048]{2,1,0:T(8,128)(2,1)S(1)} %pad_maximum_fusion.3), channel_id=1, source_target_pairs={{0,4},{1,9},{2,6},{3,11},{4,0},{5,13},{6,2},{7,15},{8,12},{9,1},{1... | collective-permute-start | bytes 786440 | tf_op jit(solution)/shard_map/ppermute | solution.py:75
  137.1 9.2 %collective-permute-start.24 = (bf16[4,32,2048]{2,1,0:T(8,128)(2,1)S(1)}, bf16[4,32,2048]{2,1,0:T(8,128)(2,1)S(1)}, u32[]{:S(2)}, u32[]{:S(2)}) collective-permute-start(bf16[4,32,2048]{2,1,0:T(8,128)(2,1)S(1)} %pad_maximum_fusion.1.refs_0_), channel_id=1, source_target_pairs={{0,2},{1,5},{2,0},{3,7},{4,6},{5,1},{6,4},{7,3},{8,10},{9,13},{10,... | collective-permute-start | bytes 1572872 | tf_op jit(solution)/shard_map/ppermute | solution.py:75
  138.6 7.8 %collective-permute-start.25 = (bf16[4,32,2048]{2,1,0:T(8,128)(2,1)S(1)}, bf16[4,32,2048]{2,1,0:T(8,128)(2,1)S(1)}, u32[]{:S(2)}, u32[]{:S(2)}) collective-permute-start(bf16[4,32,2048]{2,1,0:T(8,128)(2,1)S(1)} %pad_maximum_fusion.1.refs_0_), channel_id=1, source_target_pairs={{0,1},{1,0},{2,3},{3,2},{4,5},{5,4},{6,7},{7,6},{8,9},{9,8},{10,11... | collective-permute-start | bytes 1572872 | tf_op jit(solution)/shard_map/ppermute | solution.py:72
  146.4 1.9 collective-permute-start.26
  148.3 0.8 copy-start.2
  149.1 0.8 copy-start.3
  164.2 3.3 %copy-start.4 = (f32[64,64]{1,0:T(8,128)}, f32[64,64]{1,0:T(8,128)S(1)}, u32[]{:S(2)}) copy-start(f32[64,64]{1,0:T(8,128)S(1)} %get-tuple-element.118.renewed) | copy-start | bytes 49156
  164.2 3.3 %copy-start.5 = (f32[64,64]{1,0:T(8,128)}, f32[64,64]{1,0:T(8,128)S(1)}, u32[]{:S(2)}) copy-start(f32[64,64]{1,0:T(8,128)S(1)} %get-tuple-element.120.beta_t) | copy-start | bytes 49156
  164.2 3.3 %copy-start.6 = (f32[1,64]{1,0:T(1,128)}, f32[1,64]{1,0:T(1,128)S(1)}, u32[]{:S(2)}) copy-start(f32[1,64]{1,0:T(1,128)S(1)} %get-tuple-element.127.back_row) | copy-start | bytes 772
  164.3 3.3 %copy-start.7 = (f32[64,64]{1,0:T(8,128)}, f32[64,64]{1,0:T(8,128)S(1)}, u32[]{:S(2)}) copy-start(f32[64,64]{1,0:T(8,128)S(1)} %get-tuple-element.119.mixed) | copy-start | bytes 49156
  164.4 2.8 %collective-permute-start.27 = (f16[8,32,2048]{2,1,0:T(8,128)(2,1)S(1)}, f16[8,32,2048]{2,1,0:T(8,128)(2,1)S(1)}, u32[]{:S(2)}, u32[]{:S(2)}) collective-permute-start(f16[8,32,2048]{2,1,0:T(8,128)(2,1)S(1)} %convert_element_type.91), channel_id=1, source_target_pairs={{0,1},{1,0},{2,3},{3,2},{4,5},{5,4},{6,7},{7,6},{8,9},{9,8},{10,11... | collective-permute-start | bytes 3145736 | tf_op jit(solution)/shard_map/ppermute | solution.py:72
  164.6 2.6 %collective-permute-start.28 = (f32[64,64]{1,0:T(8,128)S(1)}, f32[64,64]{1,0:T(8,128)S(1)}, u32[]{:S(2)}, u32[]{:S(2)}) collective-permute-start(f32[64,64]{1,0:T(8,128)S(1)} %get-tuple-element.109), channel_id=1, source_target_pairs={{0,1},{1,0},{2,3},{3,2},{4,5},{5,4},{6,7},{7,6},{8,9},{9,8},{10,11... | collective-permute-start | bytes 49160 | tf_op jit(solution)/shard_map/ppermute | solution.py:72
  167.6 9.6 %collective-permute-start.29 = (f16[4,32,2048]{2,1,0:T(8,128)(2,1)S(1)}, f16[4,32,2048]{2,1,0:T(8,128)(2,1)S(1)}, u32[]{:S(2)}, u32[]{:S(2)}) collective-permute-start(f16[4,32,2048]{2,1,0:T(8,128)(2,1)S(1)} %slice_convert_fusion), channel_id=1, source_target_pairs={{0,2},{1,5},{2,0},{3,7},{4,6},{5,1},{6,4},{7,3},{8,10},{9,13},{10,... | collective-permute-start | bytes 1572872 | tf_op jit(solution)/shard_map/ppermute | solution.py:75
  169.1 8.1 %collective-permute-start.30 = (f32[64,64]{1,0:T(8,128)S(1)}, f32[64,64]{1,0:T(8,128)S(1)}, u32[]{:S(2)}, u32[]{:S(2)}) collective-permute-start(f32[64,64]{1,0:T(8,128)S(1)} %add.109), channel_id=1, source_target_pairs={{0,2},{1,3},{2,0},{3,1},{4,6},{5,7},{6,4},{7,5},{8,10},{9,11},{10,... | collective-permute-start | bytes 49160 | tf_op jit(solution)/shard_map/ppermute | solution.py:72
  177.4 9.3 %collective-permute-start.31 = (f16[2,32,2048]{2,1,0:T(8,128)(2,1)S(1)}, f16[2,32,2048]{2,1,0:T(8,128)(2,1)S(1)}, u32[]{:S(2)}, u32[]{:S(2)}) collective-permute-start(f16[2,32,2048]{2,1,0:T(8,128)(2,1)S(1)} %slice_convert_fusion.2), channel_id=1, source_target_pairs={{0,4},{1,9},{2,6},{3,11},{4,0},{5,13},{6,2},{7,15},{8,12},{9,1},{1... | collective-permute-start | bytes 786440 | tf_op jit(solution)/shard_map/ppermute | solution.py:75
  177.5 9.2 %collective-permute-start.32 = (f32[64,64]{1,0:T(8,128)S(1)}, f32[64,64]{1,0:T(8,128)S(1)}, u32[]{:S(2)}, u32[]{:S(2)}) collective-permute-start(f32[64,64]{1,0:T(8,128)S(1)} %add.111), channel_id=1, source_target_pairs={{0,4},{1,5},{2,6},{3,7},{4,0},{5,1},{6,2},{7,3},{8,12},{9,13},{10,... | collective-permute-start | bytes 49160 | tf_op jit(solution)/shard_map/ppermute | solution.py:72
  186.8 6.3 %collective-permute-start.35 = (f16[1,32,2048]{2,1,0:T(8,128)(2,1)S(1)}, f16[1,32,2048]{2,1,0:T(8,128)(2,1)S(1)}, u32[]{:S(2)}, u32[]{:S(2)}) collective-permute-start(f16[1,32,2048]{2,1,0:T(8,128)(2,1)S(1)} %slice_convert_fusion.4), channel_id=1, source_target_pairs={{0,8},{1,3},{2,10},{3,1},{4,12},{5,7},{6,14},{7,5},{8,0},{9,11},{1... | collective-permute-start | bytes 393224 | tf_op jit(solution)/shard_map/ppermute | solution.py:75
  186.9 12.3 %collective-permute-start.34 = (f32[32,2048]{1,0:T(8,128)S(1)}, f32[32,2048]{1,0:T(8,128)S(1)}, u32[]{:S(2)}, u32[]{:S(2)}) collective-permute-start(f32[32,2048]{1,0:T(8,128)S(1)} %get-tuple-element.133.image_own), channel_id=1, source_target_pairs={{0,1},{1,0},{2,3},{3,2},{4,5},{5,4},{6,7},{7,6},{8,9},{9,8},{10,11... | collective-permute-start | bytes 786440 | tf_op jit(solution)/shard_map/ppermute | solution.py:72
  193.7 11.9 %collective-permute-start.36 = (f16[32,1024]{1,0:T(8,128)(2,1)S(1)}, f16[32,1024]{1,0:T(8,128)(2,1)S(1)}, u32[]{:S(2)}, u32[]{:S(2)}) collective-permute-start(f16[32,1024]{1,0:T(8,128)(2,1)S(1)} %fusion.18), channel_id=1, source_target_pairs={{0,1},{1,0},{2,3},{3,2},{4,5},{5,4},{6,7},{7,6},{8,9},{9,8},{10,11... | collective-permute-start | bytes 196616 | tf_op jit(solution)/shard_map/ppermute | solution.py:72
  193.8 4.9 %collective-permute-start.33 = (f32[64,64]{1,0:T(8,128)S(1)}, f32[64,64]{1,0:T(8,128)S(1)}, u32[]{:S(2)}, u32[]{:S(2)}) collective-permute-start(f32[64,64]{1,0:T(8,128)S(1)} %add.113), channel_id=1, source_target_pairs={{0,8},{1,9},{2,10},{3,11},{4,12},{5,13},{6,14},{7,15},{8,0},{9,1},... | collective-permute-start | bytes 49160 | tf_op jit(solution)/shard_map/ppermute | solution.py:72
  (2 other events, 1.4 us)

commit v8 on v6

--- a/solution.py
+++ b/solution.py
@@ -254,13 +254,13 @@
 
 def send_kernel(steps, count, d, me, *refs):
     second = count == 2
-    parts = [2 * UNROLL * count, 4, count, 4 * second, 4, count, 3 * second, 4]
+    parts = [2 * UNROLL * count, 4, count, 4 * second, 6, count, 3 * second, 4]
     refs = list(refs)
     panels, ins, starts, given, outs, grams, made, scratch = (
         [refs.pop(0) for _ in range(size)] for size in parts
     )
     acts, row_data, total_weight, start = ins
-    probed, along, bound, out = outs
+    probed, along, inv, back, back_row, out = outs
     kept, sems, weighted, sum_of = scratch
     step = pl.program_id(0)
 
@@ -282,14 +282,18 @@
     def _():
         probed[...] = sum_of[...].T
         norms = finish_second(probed, *grams, (*given, *made)) if second else finish_first(*grams)
-        bound[...] = (1.02 * BOUND * BOUND * d**0.5) * total_weight[...] * norms
+        bound = jnp.maximum((1.02 * BOUND * BOUND * d**0.5) * total_weight[...] * norms, TINY)
+        inv[...] = TOP / bound
+        back[...] = bound * (1.0 / TOP)
+        back_row[...] = jnp.sum(bound * (1.0 / TOP) * identity(), axis=0, keepdims=True)
         weighted[...] = (count_of(row_data) * probed[...]).astype(BF16)
         along[...] = outer(probed[...], weighted[...].astype(F32))
 
     @pl.when(step >= steps)
     def _():
         for u in range(UNROLL):
-            out[u] = jnp.dot(weighted[...], kept[(step - steps) * UNROLL + u], preferred_element_type=F32)
+            block = jnp.dot(weighted[...], kept[(step - steps) * UNROLL + u], preferred_element_type=F32)
+            out[u] = block * inv[...]
 
 
 def probe_and_send(me, panels, acts, row_data, total_weight, starts, given, n, shifts):
@@ -310,6 +314,8 @@
             jax.ShapeDtypeStruct((K, rows), F32),
             square,
             jax.ShapeDtypeStruct((K, 1), F32),
+            jax.ShapeDtypeStruct((K, 1), F32),
+            jax.ShapeDtypeStruct((1, K), F32),
             jax.ShapeDtypeStruct((n // 2, K, f), F32),
         )
         + (square,) * (count + made),
@@ -317,6 +323,8 @@
             whole(K, rows),
             whole(K, K),
             whole(K, 1),
+            whole(K, 1),
+            whole(1, K),
             pl.BlockSpec((UNROLL, K, f), lambda i, me: (jnp.maximum(i - s, 0), 0, 0)),
         )
         + (whole(K, K),) * (count + made),
@@ -325,7 +333,7 @@
     )(me, *operands, acts, row_data, total_weight, *starts, *given)
 
 
-def keep_kernel(base, me, probed, row_data, acts, *refs):
+def keep_kernel(base, me, probed, row_data, inv, acts, *refs):
     out, kept, sems, weighted = refs[-4:]
     step = pl.program_id(0)
 
@@ -340,10 +348,10 @@
     for u in range(UNROLL):
         t = base + step * UNROLL + u
         copy(t).wait()
-        out[u] = jnp.dot(weighted[...], kept[t], preferred_element_type=F32)
-
-
-def panel_keep(me, probed, row_data, acts, n, part=None, into=None):
+        out[u] = jnp.dot(weighted[...], kept[t], preferred_element_type=F32) * inv[...]
+
+
+def panel_keep(me, probed, row_data, inv, acts, n, part=None, into=None):
     rows, d = acts.shape
     f = d // n
     steps = n // 2 // UNROLL
@@ -357,13 +365,13 @@
         "panel_keep",
         n,
         steps,
-        [whole(K, rows), whole(1, rows), HBM] + [pl.BlockSpec(memory_space=pl.ANY)] * len(more),
+        [whole(K, rows), whole(1, rows), whole(K, 1), HBM] + [pl.BlockSpec(memory_space=pl.ANY)] * len(more),
         jax.ShapeDtypeStruct((n // 2, K, f), F32),
         pl.BlockSpec((UNROLL, K, f), lambda i, me: (i + first, 0, 0)),
         acts,
         [pltpu.VMEM((K, rows), BF16)],
-        {4: 0} if more else {},
-    )(me, probed, row_data, acts, *more)
+        {5: 0} if more else {},
+    )(me, probed, row_data, inv, acts, *more)
 
 
 def alpha_kernel(along, current, total_weight, alpha_t, inverse):
@@ -389,13 +397,13 @@
 
 
 def last_kernel(
-    along, fixed, cross_t, renewed, beta_t, alpha_t, total_weight, base_a, base_b, image_a, image_b,
+    along, fixed, cross_t, renewed, beta_t, alpha_t, total_weight, back_row, base_a, base_b, image_a, image_b,
     solved, rest, on_panel,
 ):
     weight = total_weight[...]
     curvature = symmetric(along[...] / weight + fixed[...])
     step = solve_positive(beside(curvature, renewed[...]))[0].T
-    on_panel[...] = step / weight
+    on_panel[...] = step * (back_row[...] / weight)
     alpha = alpha_t[...]
     all_three = precise(step, jnp.concatenate([identity() + beta_t[...], alpha, cross_t[...]], axis=1))
     direction_base, direction_image = all_three[:, :K], all_three[:, K : 2 * K]
@@ -407,11 +415,6 @@
     )
 
 
-def end_kernel(rest, on_panel, panel_a, panel_b, residual):
-    panel = jnp.concatenate([panel_a[...], panel_b[...]], axis=0)
-    residual[...] = rest[...] - precise(on_panel[...], panel)
-
-
 def small(kernel, name, outs, *args):
     return pl.pallas_call(
         kernel, out_shape=tuple(jax.ShapeDtypeStruct(shape, F32) for shape in outs), name=name,
@@ -419,12 +422,8 @@
     )(*args)
 
 
-def shrink(value, bound):
-    return (value * (TOP / jnp.maximum(bound, TINY))).astype(F16)
-
-
-def grow(value, bound):
-    return value.astype(F32) * (jnp.maximum(bound, TINY) * (1.0 / TOP))
+def plain(n):
+    return lambda value, bit: swap(value.astype(F16), bit, n).astype(F32)
 
 
 def split_blocks(value, left, bit):
@@ -434,7 +433,7 @@
     return keep, send, [other for other in left if other != bit]
 
 
-def reduce_scatter(blocks, n, swap_a, swap_b, along, waiting, work=None, args=()):
+def reduce_scatter(blocks, n, swap_a, swap_b, along, waiting, work=None, args=(), along_ends=True):
     bits = n.bit_length() - 2
     shape = (2,) * bits + (HALF, blocks.shape[2])
     a, b = blocks[:, :HALF].reshape(shape), blocks[:, HALF:].reshape(shape)
@@ -451,6 +450,8 @@
             along = along + swap(along, waiting.pop(0), n)
         if work is not None and phase >= 1:
             done = work(*tied) if phase == 1 else tied
+    if along_ends:
+        a, b, along = lax.optimization_barrier((a, b, along))
     return a, b, along, done
 
 
@@ -498,62 +499,53 @@
     over, back = class_weight, jnp.sqrt(class_weight)
     base = (top / over[:HALF]) * back[:HALF], (low / over[HALF:]) * back[HALF:]
 
-    def scatter(probed, along, bound, sent, early, work, args):
-        got = grow(swap(shrink(sent, bound), 1, n), bound)
+    def scatter(probed, along, inv, sent, early, work, args):
+        hop = plain(n)
+        got = hop(sent, 1)
         along = along + swap(along, 1, n)
         waiting = order_y
         if early:
-            kept = panel_keep(me, probed, row_data, activations, n, 0)
+            kept = panel_keep(me, probed, row_data, inv, activations, n, 0)
             kept, along = lax.optimization_barrier((kept, along))
             along = along + swap(along, waiting[0], n)
-            kept = panel_keep(me, probed, row_data, activations, n, 1, kept)
+            kept = panel_keep(me, probed, row_data, inv, activations, n, 1, kept)
             waiting = waiting[1:]
         else:
-            kept = panel_keep(me, probed, row_data, activations, n)
-        blocks = kept + got
-        top, low = bound[:HALF], bound[HALF:]
-        return reduce_scatter(
-            blocks,
-            n,
-            lambda x, bit: grow(swap(shrink(x, top), bit, n), top),
-            lambda x, bit: grow(swap(shrink(x, low), bit, n), low),
-            along,
-            waiting,
-            work,
-            args,
-        )
+            kept = panel_keep(me, probed, row_data, inv, activations, n)
+        return reduce_scatter(kept + got, n, hop, hop, along, waiting, work, args, not early)
 
     square, strip = (K, K), (K, d // n)
     orders = order_a, order_b
     base_near, base_far, _ = gather(*base, n, orders)
     starts = probe(me, (base_near,), activations, n, shifts)
-    first, along, bound, sent, current = probe_and_send(
+    first, along, inv, back, _, sent, current = probe_and_send(
         me, (base_far,), activations, row_data, total_weight, starts, (), n, shifts
     )
     panel_a, panel_b, along, (offset,) = scatter(
-        first, along, bound, sent, False,
+        first, along, inv, sent, False,
         lambda *args: small(offset_kernel, "offset", (strip,), *args), (*base, current, total_weight),
     )
-    image = panel_a / total_weight + offset[:HALF], panel_b / total_weight + offset[HALF:]
+    back = back / total_weight
+    image = panel_a * back[:HALF] + offset[:HALF], panel_b * back[HALF:] + offset[HALF:]
 
     near, far, (alpha_t, inverse) = gather(
         *image, n, orders,
         lambda *args: small(alpha_kernel, "alpha", (square,) * 2, *args), (along, current, total_weight),
     )
     starts = probe(me, (near, base_near), activations, n, shifts)
-    probed, along, bound, sent, _, _, renewed, mixed, beta_t = probe_and_send(
+    probed, along, inv, _, back_row, sent, _, _, renewed, mixed, beta_t = probe_and_send(
         me, (far, base_far), activations, row_data, total_weight, starts, (first, current, alpha_t, inverse), n, shifts
     )
     panel_a, panel_b, along, (fixed, cross_t) = scatter(
-        probed, along, bound, sent, True,
+        probed, along, inv, sent, True,
         lambda *args: small(before_kernel, "before", (square,) * 2, *args),
         (current, renewed, mixed, beta_t, total_weight),
     )
     solved, rest, on_panel = small(
         last_kernel, "last", (strip, strip, square),
-        along, fixed, cross_t, renewed, beta_t, alpha_t, total_weight, *base, *image,
-    )
-    (residual,) = small(end_kernel, "end", (strip,), rest, on_panel, panel_a, panel_b)
+        along, fixed, cross_t, renewed, beta_t, alpha_t, total_weight, back_row, *base, *image,
+    )
+    residual = rest - precise(on_panel, jnp.concatenate([panel_a, panel_b], axis=0))
     return (solved.T, residual.T)
 
 

time: 197 us -> 191 us (0.970)
  other arithmetic: 16.6 us -> 13.6 us
  waiting for transfers between devices: 59.9 us -> 57 us
    ppermute x49, waiting for transfers between devices: 59.9 us -> 57 us  [swap(): return lax.ppermute(value, 'dp', [(i, i ^ bit) for i in range(n)])]
    add x14 -> x18, other arithmetic: 4.51 us -> 1.78 us  [reduce_scatter(): a, b = (keep_a + swap_a(send_a, bit_a), keep_b + swap_b(send_b, bit_b))]
    pallas_call x5 -> x4, Pallas kernels: 17 us -> 15.1 us  [small(): pl.pallas_call(kernel, out_shape=tuple((jax.ShapeDtypeStruct(shape, F32)...]
  transfers between devices with their start and end apart: 49 -> 49, of which waited for: 30 -> 31; matrix products, arithmetic and copies ran while one was open for 4% -> 3% of each run, Pallas kernels for 19% -> 19%
where the time goes in v8:
time: 191 us; the launch traced here: 190 us
  starting transfers between devices  57.9 us (30%)
  Pallas kernels  57.4 us (30%)
  waiting for transfers between devices  57 us (30%)
  other arithmetic  13.6 us (7%)
    ppermute x49, starting transfers between devices, swap(): return lax.ppermute(value, 'dp', [(i, i ^ bit) for i in range(n)])  57.9 us
    ppermute x49, waiting for transfers between devices, swap(): return lax.ppermute(value, 'dp', [(i, i ^ bit) for i in range(n)])  57 us
    pallas_call x2, Pallas kernels, probe_and_send(): call(functools.partial(send_kernel, s, count, d), 'probe_and_send', n, 2...  17.1 us
    pallas_call x4, Pallas kernels, small(): pl.pallas_call(kernel, out_shape=tuple((jax.ShapeDtypeStruct(shape, F32)...  15.1 us
    pallas_call x2, Pallas kernels, probe(): call(functools.partial(probe_kernel, count), 'probe', n, n // 2 // UNROLL...  10.1 us
    pallas_call x3, Pallas kernels, panel_keep(): call(functools.partial(keep_kernel, first * UNROLL), 'panel_keep', n, ste...  8.03 us
    pallas_call x2, Pallas kernels, class_sums(): call(functools.partial(sums_kernel, half), 'class_sums', n, n // 2 // UNR...  7 us
  transfers between devices with their start and end apart: 49, of which 31 were waited for; matrix products, arithmetic and copies ran while one was open for 3% of the time, Pallas kernels for 19%

profile of v8, /device:TPU:0, one launch (start us, length us, event | category | flops | bytes accessed | tf_op | source)
XLA Modules:
  0.0 190.5 jit_solution(984388961587429363)
XLA Ops:
  1.3 3.3 %class_sums.3 = (f32[8,64,1024]{2,1,0:T(8,128)S(1)}, f32[64,1]{1,0:T(8,128)S(1)}) custom-call(s32[1]{0:T(128)} %bitcast.me, s32[1,384]{1,0:T(1,128)S(1)} %reshape.54.row_data.refs_9_.refs_17_, bf16[384,16384]{1,0:T(8,128)(2,1)} %acts.9), custom_call_target="tpu_custom_call" | custom-call | flops 402653184 | bytes 8388608 | tf_op jit(solution)/shard_map/class_sums/pallas_call | solution.py:146
  6.3 3.7 %class_sums.2 = (f32[8,64,1024]{2,1,0:T(8,128)S(1)}, f32[64,1]{1,0:T(8,128)}) custom-call(s32[1]{0:T(128)} %bitcast.me, s32[1,384]{1,0:T(1,128)S(1)} %reshape.54.row_data.refs_9_.refs_17_, bf16[384,16384]{1,0:T(8,128)(2,1)} %acts.9), custom_call_target="tpu_custom_call" | custom-call | flops 402653184 | bytes 8388608 | tf_op jit(solution)/shard_map/class_sums/pallas_call | solution.py:146
  11.3 3.1 %collective-permute-start.3 = (f16[2,2,32,1024]{3,2,0,1:T(8,128)(2,1)S(1)}, f16[2,2,32,1024]{3,2,0,1:T(8,128)(2,1)S(1)}, u32[]{:S(2)}, u32[]{:S(2)}) collective-permute-start(f16[2,2,32,1024]{3,2,0,1:T(8,128)(2,1)S(1)} %fusion.6), channel_id=1, source_target_pairs={{0,4},{1,5},{2,6},{3,7},{4,0},{5,1},{6,2},{7,3},{8,12},{9,13},{10,... | collective-permute-start | bytes 786440 | tf_op jit(solution)/shard_map/ppermute | solution.py:62
  14.4 1.5 collective-permute-start.4
  18.0 3.0 %collective-permute-done.3 = f16[2,2,32,1024]{3,2,0,1:T(8,128)(2,1)S(1)} collective-permute-done((f16[2,2,32,1024]{3,2,0,1:T(8,128)(2,1)S(1)}, f16[2,2,32,1024]{3,2,0,1:T(8,128)(2,1)S(1)}, u32[]{:S(2)}, u32[]{:S(2)}) %collective-permute-start.3) | collective-permute-done | bytes 262176 | tf_op jit(solution)/shard_map/ppermute | solution.py:62
  21.1 2.9 %collective-permute-done.2 = f16[2,2,32,1024]{3,2,0,1:T(8,128)(2,1)S(1)} collective-permute-done((f16[2,2,32,1024]{3,2,0,1:T(8,128)(2,1)S(1)}, f16[2,2,32,1024]{3,2,0,1:T(8,128)(2,1)S(1)}, u32[]{:S(2)}, u32[]{:S(2)}) %collective-permute-start.2) | collective-permute-done | bytes 262176 | tf_op jit(solution)/shard_map/ppermute | solution.py:62
  24.7 2.7 %collective-permute-start.6 = (f16[2,32,1024]{2,1,0:T(8,128)(2,1)S(1)}, f16[2,32,1024]{2,1,0:T(8,128)(2,1)S(1)}, u32[]{:S(2)}, u32[]{:S(2)}) collective-permute-start(f16[2,32,1024]{2,1,0:T(8,128)(2,1)S(1)} %fusion.16), channel_id=1, source_target_pairs={{0,8},{1,9},{2,10},{3,11},{4,12},{5,13},{6,14},{7,15},{8,0},{9,1},... | collective-permute-start | bytes 393224 | tf_op jit(solution)/shard_map/ppermute | solution.py:62
  27.5 1.6 collective-permute-start.5
  29.2 3.2 %collective-permute-done.6 = f16[2,32,1024]{2,1,0:T(8,128)(2,1)S(1)} collective-permute-done((f16[2,32,1024]{2,1,0:T(8,128)(2,1)S(1)}, f16[2,32,1024]{2,1,0:T(8,128)(2,1)S(1)}, u32[]{:S(2)}, u32[]{:S(2)}) %collective-permute-start.6) | collective-permute-done | bytes 131104 | tf_op jit(solution)/shard_map/ppermute | solution.py:62
  34.7 2.2 %collective-permute-start.8 = (f16[32,1024]{1,0:T(8,128)(2,1)S(1)}, f16[32,1024]{1,0:T(8,128)(2,1)S(1)}, u32[]{:S(2)}, u32[]{:S(2)}) collective-permute-start(f16[32,1024]{1,0:T(8,128)(2,1)S(1)} %fusion.27), channel_id=1, source_target_pairs={{0,8},{1,9},{2,10},{3,11},{4,12},{5,13},{6,14},{7,15},{8,0},{9,1},... | collective-permute-start | bytes 196616 | tf_op jit(solution)/shard_map/ppermute | solution.py:62
  38.4 1.5 collective-permute-done.8
  41.6 2.2 %collective-permute-start.11 = (bf16[1,32,1024]{2,1,0:T(8,128)(2,1)S(1)}, bf16[1,32,1024]{2,1,0:T(8,128)(2,1)S(1)}, u32[]{:S(2)}, u32[]{:S(2)}) collective-permute-start(bf16[1,32,1024]{2,1,0:T(8,128)(2,1)S(1)} %get-tuple-element.110), channel_id=1, source_target_pairs={{0,8},{1,9},{2,10},{3,11},{4,12},{5,13},{6,14},{7,15},{8,0},{9,1},... | collective-permute-start | bytes 196616 | tf_op jit(solution)/shard_map/ppermute | solution.py:62
  45.1 1.8 collective-permute-done.11
  48.1 2.2 %collective-permute-start.13 = (bf16[2,32,1024]{2,1,0:T(8,128)(2,1)S(1)}, bf16[2,32,1024]{2,1,0:T(8,128)(2,1)S(1)}, u32[]{:S(2)}, u32[]{:S(2)}) collective-permute-start(bf16[2,32,1024]{2,1,0:T(8,128)(2,1)S(1)} %pad_maximum_fusion.4), channel_id=1, source_target_pairs={{0,4},{1,5},{2,6},{3,7},{4,0},{5,1},{6,2},{7,3},{8,12},{9,13},{10,... | collective-permute-start | bytes 393224 | tf_op jit(solution)/shard_map/ppermute | solution.py:62
  50.3 3.1 %collective-permute-start.14 = (bf16[2,32,1024]{2,1,0:T(8,128)(2,1)S(1)}, bf16[2,32,1024]{2,1,0:T(8,128)(2,1)S(1)}, u32[]{:S(2)}, u32[]{:S(2)}) collective-permute-start(bf16[2,32,1024]{2,1,0:T(8,128)(2,1)S(1)} %pad_maximum_fusion.5), channel_id=1, source_target_pairs={{0,8},{1,9},{2,10},{3,11},{4,12},{5,13},{6,14},{7,15},{8,0},{9,1},... | collective-permute-start | bytes 393224 | tf_op jit(solution)/shard_map/ppermute | solution.py:62
  54.2 2.5 %collective-permute-done.14 = bf16[2,32,1024]{2,1,0:T(8,128)(2,1)S(1)} collective-permute-done((bf16[2,32,1024]{2,1,0:T(8,128)(2,1)S(1)}, bf16[2,32,1024]{2,1,0:T(8,128)(2,1)S(1)}, u32[]{:S(2)}, u32[]{:S(2)}) %collective-permute-start.14) | collective-permute-done | bytes 131104 | tf_op jit(solution)/shard_map/ppermute | solution.py:62
  56.7 3.5 %collective-permute-start.17 = (bf16[4,32,1024]{2,1,0:T(8,128)(2,1)S(1)}, bf16[4,32,1024]{2,1,0:T(8,128)(2,1)S(1)}, u32[]{:S(2)}, u32[]{:S(2)}) collective-permute-start(bf16[4,32,1024]{2,1,0:T(8,128)(2,1)S(1)} %pad_maximum_fusion.1), channel_id=1, source_target_pairs={{0,4},{1,5},{2,6},{3,7},{4,0},{5,1},{6,2},{7,3},{8,12},{9,13},{10,... | collective-permute-start | bytes 786440 | tf_op jit(solution)/shard_map/ppermute | solution.py:62
  61.7 3.0 %collective-permute-done.17 = bf16[4,32,1024]{2,1,0:T(8,128)(2,1)S(1)} collective-permute-done((bf16[4,32,1024]{2,1,0:T(8,128)(2,1)S(1)}, bf16[4,32,1024]{2,1,0:T(8,128)(2,1)S(1)}, u32[]{:S(2)}, u32[]{:S(2)}) %collective-permute-start.17) | collective-permute-done | bytes 262176 | tf_op jit(solution)/shard_map/ppermute | solution.py:62
  64.7 1.9 %collective-permute-done.15 = bf16[4,32,1024]{2,1,0:T(8,128)(2,1)S(1)} collective-permute-done((bf16[4,32,1024]{2,1,0:T(8,128)(2,1)S(1)}, bf16[4,32,1024]{2,1,0:T(8,128)(2,1)S(1)}, u32[]{:S(2)}, u32[]{:S(2)}) %collective-permute-start.15) | collective-permute-done | bytes 262176 | tf_op jit(solution)/shard_map/ppermute | solution.py:62
  66.7 5.1 %probe.2 = (f32[384,64]{1,0:T(8,128)S(1)}, f32[64,64]{1,0:T(8,128)S(1)}) custom-call(s32[1]{0:T(128)} %bitcast.me, bf16[8,32,1024]{2,1,0:T(8,128)(2,1)S(1)} %constant_dynamic-update-slice_fusion.refs_0_.refs_2_.refs_4_.refs_6_.refs_8_.refs_10_.refs_12_.refs_14_, ...), custom_call_target="tpu_custom_call" | custom-call | flops 402653184 | bytes 8388608 | tf_op jit(solution)/shard_map/probe/pallas_call | solution.py:213
  71.8 8.0 %probe_and_send.2 = (f32[64,384]{1,0:T(8,128)S(1)}, f32[64,64]{1,0:T(8,128)S(1)}, f32[64,1]{1,0:T(8,128)S(1)}, f32[64,1]{1,0:T(8,128)S(1)}, f32[1,64]{1,0:T(1,12...) custom-call(s32[1]{0:T(128)} %bitcast.me, ...), custom_call_target="tpu_custom_call" | custom-call | flops 402653184 | bytes 8388608 | tf_op jit(solution)/shard_map/probe_and_send/pallas_call | solution.py:307
  80.6 3.5 %panel_keep.3 = f32[8,64,1024]{2,1,0:T(8,128)S(1)} custom-call(s32[1]{0:T(128)} %bitcast.me, f32[64,384]{1,0:T(8,128)S(1)} %get-tuple-element.118.probed.refs_22_, s32[1,384]{1,0:T(1,128)S(1)} %reshape.54.row_data.refs_9_.refs_17_, f32[64,1]{1,0:T(8,128)S(1)} %get-tuple-element.119.inv, bf16[384,16384]{1,0:T(8,128)(2,1)} %acts.9), custom_call_target="tpu_custom_call" | custom-call | flops 402653184 | bytes 8388608 | tf_op jit(solution)/shard_map/panel_keep/pallas_call | solution.py:363
  87.7 1.9 %collective-permute-done.23 = f32[64,64]{1,0:T(8,128)S(1)} collective-permute-done((f32[64,64]{1,0:T(8,128)S(1)}, f32[64,64]{1,0:T(8,128)S(1)}, u32[]{:S(2)}, u32[]{:S(2)}) %collective-permute-start.23) | collective-permute-done | bytes 16416 | tf_op jit(solution)/shard_map/ppermute | solution.py:62
  89.7 4.1 %collective-permute-done.22 = f16[2,2,32,1024]{3,2,1,0:T(8,128)(2,1)S(1)} collective-permute-done((f16[2,2,32,1024]{3,2,1,0:T(8,128)(2,1)S(1)}, f16[2,2,32,1024]{3,2,1,0:T(8,128)(2,1)S(1)}, u32[]{:S(2)}, u32[]{:S(2)}) %collective-permute-start.22) | collective-permute-done | bytes 262176 | tf_op jit(solution)/shard_map/ppermute | solution.py:62
  95.2 1.6 collective-permute-start.26
  100.7 2.7 %offset.1 = f32[64,1024]{1,0:T(8,128)} custom-call(f32[32,1024]{1,0:T(8,128)} %get-tuple-element.129.base_a, f32[32,1024]{1,0:T(8,128)} %get-tuple-element.130.base_b, f32[64,64]{1,0:T(8,128)} %copy-done, f32[1,1]{1,0:T(1,128)} %bitcast.21.refs_10_.total_weight.refs_18_), custom_call_target="tpu_custom_call" | custom-call | flops 67108864 | bytes 1048576 | tf_op jit(solution)/shard_map/offset/pallas_call | solution.py:419
  103.5 2.1 %collective-permute-done.25 = f16[2,32,1024]{2,1,0:T(8,128)(2,1)S(1)} collective-permute-done((f16[2,32,1024]{2,1,0:T(8,128)(2,1)}, f16[2,32,1024]{2,1,0:T(8,128)(2,1)S(1)}, u32[]{:S(2)}, u32[]{:S(2)}) %collective-permute-start.25) | collective-permute-done | bytes 131104 | tf_op jit(solution)/shard_map/ppermute | solution.py:62
  109.4 3.0 %collective-permute-start.27 = (f16[32,1024]{1,0:T(8,128)(2,1)S(1)}, f16[32,1024]{1,0:T(8,128)(2,1)S(1)}, u32[]{:S(2)}, u32[]{:S(2)}) collective-permute-start(f16[32,1024]{1,0:T(8,128)(2,1)S(1)} %convert_element_type.164), channel_id=1, source_target_pairs={{0,8},{1,9},{2,10},{3,11},{4,12},{5,13},{6,14},{7,15},{8,0},{9,1},... | collective-permute-start | bytes 196616 | tf_op jit(solution)/shard_map/ppermute | solution.py:62
  115.5 2.9 %collective-permute-start.30 = (bf16[1,32,1024]{2,1,0:T(8,128)(2,1)S(1)}, bf16[1,32,1024]{2,1,0:T(8,128)(2,1)S(1)}, u32[]{:S(2)}, u32[]{:S(2)}) collective-permute-start(bf16[1,32,1024]{2,1,0:T(8,128)(2,1)S(1)} %get-tuple-element.140), channel_id=1, source_target_pairs={{0,8},{1,9},{2,10},{3,11},{4,12},{5,13},{6,14},{7,15},{8,0},{9,1},... | collective-permute-start | bytes 196616 | tf_op jit(solution)/shard_map/ppermute | solution.py:62
  118.9 1.9 collective-permute-done.30
  120.8 1.8 collective-permute-done.31
  122.7 1.6 collective-permute-start.33
  124.4 4.4 %alpha.1 = (f32[64,64]{1,0:T(8,128)}, f32[64,64]{1,0:T(8,128)}) custom-call(f32[64,64]{1,0:T(8,128)} %add.130.along, f32[64,64]{1,0:T(8,128)} %copy-done, f32[1,1]{1,0:T(1,128)} %bitcast.21.refs_10_.total_weight.refs_18_), custom_call_target="tpu_custom_call" | custom-call | flops 67108864 | bytes 1048576 | tf_op jit(solution)/shard_map/alpha/pallas_call | solution.py:419
  129.5 3.1 %collective-permute-start.36 = (bf16[4,32,1024]{2,1,0:T(8,128)(2,1)S(1)}, bf16[4,32,1024]{2,1,0:T(8,128)(2,1)S(1)}, u32[]{:S(2)}, u32[]{:S(2)}) collective-permute-start(bf16[4,32,1024]{2,1,0:T(8,128)(2,1)S(1)} %pad_maximum_fusion.3), channel_id=1, source_target_pairs={{0,4},{1,5},{2,6},{3,7},{4,0},{5,1},{6,2},{7,3},{8,12},{9,13},{10,... | collective-permute-start | bytes 786440 | tf_op jit(solution)/shard_map/ppermute | solution.py:62
  133.1 3.8 %collective-permute-done.36 = bf16[4,32,1024]{2,1,0:T(8,128)(2,1)S(1)} collective-permute-done((bf16[4,32,1024]{2,1,0:T(8,128)(2,1)S(1)}, bf16[4,32,1024]{2,1,0:T(8,128)(2,1)S(1)}, u32[]{:S(2)}, u32[]{:S(2)}) %collective-permute-start.36) | collective-permute-done | bytes 262176 | tf_op jit(solution)/shard_map/ppermute | solution.py:62
  137.0 1.9 %collective-permute-done.34 = bf16[4,32,1024]{2,1,0:T(8,128)(2,1)S(1)} collective-permute-done((bf16[4,32,1024]{2,1,0:T(8,128)(2,1)S(1)}, bf16[4,32,1024]{2,1,0:T(8,128)(2,1)S(1)}, u32[]{:S(2)}, u32[]{:S(2)}) %collective-permute-start.34) | collective-permute-done | bytes 262176 | tf_op jit(solution)/shard_map/ppermute | solution.py:62
  139.1 5.0 %probe.3 = (f32[384,64]{1,0:T(8,128)S(1)}, f32[64,64]{1,0:T(8,128)S(1)}, f32[64,64]{1,0:T(8,128)S(1)}) custom-call(s32[1]{0:T(128)} %bitcast.me, bf16[8,32,1024]{2,1,0:T(8,128)(2,1)S(1)} %constant_dynamic-update-slice_fusion.4.refs_0_.refs_2_.refs_4_.refs_6_, bf16[8,32,1024]{2,1,0:T(8,128)(2,1)S(1)} %constant_dynamic-update-slice_fusion.6.refs_1_.refs_3_.refs_5_.refs_7_, ...), custom_call_target="tpu_custom_call" | custom-call | flops 402653184 | bytes 8388608 | tf_op jit(solution)/shard_map/probe/pallas_call | solution.py:213
  144.2 9.1 %probe_and_send.3 = (f32[64,384]{1,0:T(8,128)S(1)}, f32[64,64]{1,0:T(8,128)S(1)}, f32[64,1]{1,0:T(8,128)S(1)}, f32[64,1]{1,0:T(8,128)}, f32[1,64]{1,0:T(1,128)S(...) custom-call(s32[1]{0:T(128)} %bitcast.me, ...), custom_call_target="tpu_custom_call" | custom-call | flops 402653184 | bytes 8388608 | tf_op jit(solution)/shard_map/probe_and_send/pallas_call | solution.py:307
  154.1 2.3 %panel_keep.4.refs_0_ = f32[8,64,1024]{2,1,0:T(8,128)S(1)} custom-call(s32[1]{0:T(128)} %bitcast.me, f32[64,384]{1,0:T(8,128)S(1)} %get-tuple-element.157.probed, s32[1,384]{1,0:T(1,128)S(1)} %reshape.54.row_data.refs_9_.refs_17_, f32[64,1]{1,0:T(8,128)S(1)} %get-tuple-element.158.inv, bf16[384,16384]{1,0:T(8,128)(2,1)} %acts.9), custom_call_target="tpu_custom_call" | custom-call | flops 402653184 | bytes 8388608 | tf_op jit(solution)/shard_map/panel_keep/pallas_call | solution.py:363
  157.0 2.3 %panel_keep.5 = f32[8,64,1024]{2,1,0:T(8,128)S(1)} custom-call(s32[1]{0:T(128)} %bitcast.me, f32[64,384]{1,0:T(8,128)S(1)} %get-tuple-element.157.probed, s32[1,384]{1,0:T(1,128)S(1)} %reshape.54.row_data.refs_9_.refs_17_, f32[64,1]{1,0:T(8,128)S(1)} %get-tuple-element.158.inv, bf16[384,16384]{1,0:T(8,128)(2,1)} %acts.9, ...), custom_call_target="tpu_custom_call", output_to_operand_aliasing={{}: (5, {})} | custom-call | flops 402653184 | bytes 8388608 | tf_op jit(solution)/shard_map/panel_keep/pallas_call | solution.py:363
  161.9 1.5 collective-permute-start.43
  164.1 5.5 %collective-permute-done.43 = f32[64,64]{1,0:T(8,128)S(1)} collective-permute-done((f32[64,64]{1,0:T(8,128)S(1)}, f32[64,64]{1,0:T(8,128)S(1)}, u32[]{:S(2)}, u32[]{:S(2)}) %collective-permute-start.43) | collective-permute-done | bytes 16416 | tf_op jit(solution)/shard_map/ppermute | solution.py:62
  171.6 2.0 %collective-permute-start.46 = (f32[64,64]{1,0:T(8,128)S(1)}, f32[64,64]{1,0:T(8,128)S(1)}, u32[]{:S(2)}, u32[]{:S(2)}) collective-permute-start(f32[64,64]{1,0:T(8,128)S(1)} %add.138), channel_id=1, source_target_pairs={{0,8},{1,9},{2,10},{3,11},{4,12},{5,13},{6,14},{7,15},{8,0},{9,1},... | collective-permute-start | bytes 49160 | tf_op jit(solution)/shard_map/ppermute | solution.py:62
  174.1 2.5 %before.1 = (f32[64,64]{1,0:T(8,128)}, f32[64,64]{1,0:T(8,128)}) custom-call(f32[64,64]{1,0:T(8,128)} %copy-done, f32[64,64]{1,0:T(8,128)} %copy-done.4, f32[64,64]{1,0:T(8,128)} %copy-done.7, f32[64,64]{1,0:T(8,128)} %copy-done.5, f32[1,1]{1,0:T(1,128)} %bitcast.21.refs_10_.total_weight.refs_18_), custom_call_target="tpu_custom_call" | custom-call | flops 67108864 | bytes 1048576 | tf_op jit(solution)/shard_map/before/pallas_call | solution.py:419
  176.6 2.1 %collective-permute-done.46 = f32[64,64]{1,0:T(8,128)S(1)} collective-permute-done((f32[64,64]{1,0:T(8,128)S(1)}, f32[64,64]{1,0:T(8,128)S(1)}, u32[]{:S(2)}, u32[]{:S(2)}) %collective-permute-start.46) | collective-permute-done | bytes 16416 | tf_op jit(solution)/shard_map/ppermute | solution.py:62
  180.1 1.9 collective-permute-start.48
  182.1 5.5 %last.1 = (f32[64,1024]{1,0:T(8,128)}, f32[64,1024]{1,0:T(8,128)}, f32[64,64]{1,0:T(8,128)}) custom-call(f32[64,64]{1,0:T(8,128)} %add.141.along, f32[64,64]{1,0:T(8,128)} %get-tuple-element.180.fixed, f32[64,64]{1,0:T(8,128)} %get-tuple-element.181.cross_t, f32[64,64]{1,0:T(8,128)} %copy-done.4, f32[64,64]{1,0:T(8,128)} %copy-done.5, ...), custom_call_target="tpu_custom_call" | custom-call | flops 67108864 | bytes 1048576 | tf_op jit(solution)/shard_map/last/pallas_call | solution.py:419
  188.8 1.7 subtract_bitcast_fusion
  (188 shorter events, 45.3 us)
Async XLA Ops:
  5.6 4.5 %collective-permute-start = (f16[8,64,1024]{2,1,0:T(8,128)(2,1)S(1)}, f16[8,64,1024]{2,1,0:T(8,128)(2,1)S(1)}, u32[]{:S(2)}, u32[]{:S(2)}) collective-permute-start(f16[8,64,1024]{2,1,0:T(8,128)(2,1)S(1)} %fusion), channel_id=1, source_target_pairs={{0,1},{1,0},{2,3},{3,2},{4,5},{5,4},{6,7},{7,6},{8,9},{9,8},{10,11... | collective-permute-start | bytes 3145736 | tf_op jit(solution)/shard_map/ppermute | solution.py:62
  6.2 3.8 %collective-permute-start.1 = (f32[1,64]{1,0:T(1,128)S(1)}, f32[1,64]{1,0:T(1,128)S(1)}, u32[]{:S(2)}, u32[]{:S(2)}) collective-permute-start(f32[1,64]{1,0:T(1,128)S(1)} %bitcast.160), channel_id=1, source_target_pairs={{0,1},{1,0},{2,3},{3,2},{4,5},{5,4},{6,7},{7,6},{8,9},{9,8},{10,11... | collective-permute-start | bytes 776 | tf_op jit(solution)/shard_map/ppermute | solution.py:62
  11.3 9.6 %collective-permute-start.3 = (f16[2,2,32,1024]{3,2,0,1:T(8,128)(2,1)S(1)}, f16[2,2,32,1024]{3,2,0,1:T(8,128)(2,1)S(1)}, u32[]{:S(2)}, u32[]{:S(2)}) collective-permute-start(f16[2,2,32,1024]{3,2,0,1:T(8,128)(2,1)S(1)} %fusion.6), channel_id=1, source_target_pairs={{0,4},{1,5},{2,6},{3,7},{4,0},{5,1},{6,2},{7,3},{8,12},{9,13},{10,... | collective-permute-start | bytes 786440 | tf_op jit(solution)/shard_map/ppermute | solution.py:62
  14.4 3.5 %collective-permute-start.4 = (f32[1,64]{1,0:T(1,128)S(1)}, f32[1,64]{1,0:T(1,128)S(1)}, u32[]{:S(2)}, u32[]{:S(2)}) collective-permute-start(f32[1,64]{1,0:T(1,128)S(1)} %bitcast_add_fusion), channel_id=1, source_target_pairs={{0,2},{1,3},{2,0},{3,1},{4,6},{5,7},{6,4},{7,5},{8,10},{9,11},{10,... | collective-permute-start | bytes 776 | tf_op jit(solution)/shard_map/ppermute | solution.py:62
  16.2 7.8 %collective-permute-start.2 = (f16[2,2,32,1024]{3,2,0,1:T(8,128)(2,1)S(1)}, f16[2,2,32,1024]{3,2,0,1:T(8,128)(2,1)S(1)}, u32[]{:S(2)}, u32[]{:S(2)}) collective-permute-start(f16[2,2,32,1024]{3,2,0,1:T(8,128)(2,1)S(1)} %fusion.3), channel_id=1, source_target_pairs={{0,2},{1,3},{2,0},{3,1},{4,6},{5,7},{6,4},{7,5},{8,10},{9,11},{10,... | collective-permute-start | bytes 786440 | tf_op jit(solution)/shard_map/ppermute | solution.py:62
  24.1 5.1 %collective-permute-start.7 = (f32[1,64]{1,0:T(1,128)S(1)}, f32[1,64]{1,0:T(1,128)S(1)}, u32[]{:S(2)}, u32[]{:S(2)}) collective-permute-start(f32[1,64]{1,0:T(1,128)S(1)} %add.113), channel_id=1, source_target_pairs={{0,4},{1,5},{2,6},{3,7},{4,0},{5,1},{6,2},{7,3},{8,12},{9,13},{10,... | collective-permute-start | bytes 776 | tf_op jit(solution)/shard_map/ppermute | solution.py:62
  24.7 7.6 %collective-permute-start.6 = (f16[2,32,1024]{2,1,0:T(8,128)(2,1)S(1)}, f16[2,32,1024]{2,1,0:T(8,128)(2,1)S(1)}, u32[]{:S(2)}, u32[]{:S(2)}) collective-permute-start(f16[2,32,1024]{2,1,0:T(8,128)(2,1)S(1)} %fusion.16), channel_id=1, source_target_pairs={{0,8},{1,9},{2,10},{3,11},{4,12},{5,13},{6,14},{7,15},{8,0},{9,1},... | collective-permute-start | bytes 393224 | tf_op jit(solution)/shard_map/ppermute | solution.py:62
  27.5 5.3 %collective-permute-start.5 = (f16[2,32,1024]{2,1,0:T(8,128)(2,1)S(1)}, f16[2,32,1024]{2,1,0:T(8,128)(2,1)S(1)}, u32[]{:S(2)}, u32[]{:S(2)}) collective-permute-start(f16[2,32,1024]{2,1,0:T(8,128)(2,1)S(1)} %fusion.13), channel_id=1, source_target_pairs={{0,4},{1,5},{2,6},{3,7},{4,0},{5,1},{6,2},{7,3},{8,12},{9,13},{10,... | collective-permute-start | bytes 393224 | tf_op jit(solution)/shard_map/ppermute | solution.py:62
  32.9 4.6 %collective-permute-start.10 = (f32[1,64]{1,0:T(1,128)S(1)}, f32[1,64]{1,0:T(1,128)S(1)}, u32[]{:S(2)}, u32[]{:S(2)}) collective-permute-start(f32[1,64]{1,0:T(1,128)S(1)} %add.116), channel_id=1, source_target_pairs={{0,8},{1,9},{2,10},{3,11},{4,12},{5,13},{6,14},{7,15},{8,0},{9,1},... | collective-permute-start | bytes 776 | tf_op jit(solution)/shard_map/ppermute | solution.py:62
  34.1 4.3 %collective-permute-start.9 = (f16[32,1024]{1,0:T(8,128)(2,1)S(1)}, f16[32,1024]{1,0:T(8,128)(2,1)S(1)}, u32[]{:S(2)}, u32[]{:S(2)}) collective-permute-start(f16[32,1024]{1,0:T(8,128)(2,1)S(1)} %fusion.30), channel_id=1, source_target_pairs={{0,2},{1,3},{2,0},{3,1},{4,6},{5,7},{6,4},{7,5},{8,10},{9,11},{10,... | collective-permute-start | bytes 196616 | tf_op jit(solution)/shard_map/ppermute | solution.py:62
  34.7 5.2 %collective-permute-start.8 = (f16[32,1024]{1,0:T(8,128)(2,1)S(1)}, f16[32,1024]{1,0:T(8,128)(2,1)S(1)}, u32[]{:S(2)}, u32[]{:S(2)}) collective-permute-start(f16[32,1024]{1,0:T(8,128)(2,1)S(1)} %fusion.27), channel_id=1, source_target_pairs={{0,8},{1,9},{2,10},{3,11},{4,12},{5,13},{6,14},{7,15},{8,0},{9,1},... | collective-permute-start | bytes 196616 | tf_op jit(solution)/shard_map/ppermute | solution.py:62
  41.6 5.3 %collective-permute-start.11 = (bf16[1,32,1024]{2,1,0:T(8,128)(2,1)S(1)}, bf16[1,32,1024]{2,1,0:T(8,128)(2,1)S(1)}, u32[]{:S(2)}, u32[]{:S(2)}) collective-permute-start(bf16[1,32,1024]{2,1,0:T(8,128)(2,1)S(1)} %get-tuple-element.110), channel_id=1, source_target_pairs={{0,8},{1,9},{2,10},{3,11},{4,12},{5,13},{6,14},{7,15},{8,0},{9,1},... | collective-permute-start | bytes 196616 | tf_op jit(solution)/shard_map/ppermute | solution.py:62
  43.8 4.3 %collective-permute-start.12 = (bf16[1,32,1024]{2,1,0:T(8,128)(2,1)S(1)}, bf16[1,32,1024]{2,1,0:T(8,128)(2,1)S(1)}, u32[]{:S(2)}, u32[]{:S(2)}) collective-permute-start(bf16[1,32,1024]{2,1,0:T(8,128)(2,1)S(1)} %get-tuple-element.111), channel_id=1, source_target_pairs={{0,2},{1,3},{2,0},{3,1},{4,6},{5,7},{6,4},{7,5},{8,10},{9,11},{10,... | collective-permute-start | bytes 196616 | tf_op jit(solution)/shard_map/ppermute | solution.py:62
  48.1 6.1 %collective-permute-start.13 = (bf16[2,32,1024]{2,1,0:T(8,128)(2,1)S(1)}, bf16[2,32,1024]{2,1,0:T(8,128)(2,1)S(1)}, u32[]{:S(2)}, u32[]{:S(2)}) collective-permute-start(bf16[2,32,1024]{2,1,0:T(8,128)(2,1)S(1)} %pad_maximum_fusion.4), channel_id=1, source_target_pairs={{0,4},{1,5},{2,6},{3,7},{4,0},{5,1},{6,2},{7,3},{8,12},{9,13},{10,... | collective-permute-start | bytes 393224 | tf_op jit(solution)/shard_map/ppermute | solution.py:62
  50.3 6.4 %collective-permute-start.14 = (bf16[2,32,1024]{2,1,0:T(8,128)(2,1)S(1)}, bf16[2,32,1024]{2,1,0:T(8,128)(2,1)S(1)}, u32[]{:S(2)}, u32[]{:S(2)}) collective-permute-start(bf16[2,32,1024]{2,1,0:T(8,128)(2,1)S(1)} %pad_maximum_fusion.5), channel_id=1, source_target_pairs={{0,8},{1,9},{2,10},{3,11},{4,12},{5,13},{6,14},{7,15},{8,0},{9,1},... | collective-permute-start | bytes 393224 | tf_op jit(solution)/shard_map/ppermute | solution.py:62
  56.7 7.9 %collective-permute-start.17 = (bf16[4,32,1024]{2,1,0:T(8,128)(2,1)S(1)}, bf16[4,32,1024]{2,1,0:T(8,128)(2,1)S(1)}, u32[]{:S(2)}, u32[]{:S(2)}) collective-permute-start(bf16[4,32,1024]{2,1,0:T(8,128)(2,1)S(1)} %pad_maximum_fusion.1), channel_id=1, source_target_pairs={{0,4},{1,5},{2,6},{3,7},{4,0},{5,1},{6,2},{7,3},{8,12},{9,13},{10,... | collective-permute-start | bytes 786440 | tf_op jit(solution)/shard_map/ppermute | solution.py:62
  60.3 6.4 %collective-permute-start.15 = (bf16[4,32,1024]{2,1,0:T(8,128)(2,1)S(1)}, bf16[4,32,1024]{2,1,0:T(8,128)(2,1)S(1)}, u32[]{:S(2)}, u32[]{:S(2)}) collective-permute-start(bf16[4,32,1024]{2,1,0:T(8,128)(2,1)S(1)} %pad_maximum_fusion), channel_id=1, source_target_pairs={{0,2},{1,3},{2,0},{3,1},{4,6},{5,7},{6,4},{7,5},{8,10},{9,11},{10,... | collective-permute-start | bytes 786440 | tf_op jit(solution)/shard_map/ppermute | solution.py:62
  64.6 7.2 %collective-permute-start.18 = (bf16[8,32,1024]{2,1,0:T(8,128)(2,1)S(1)}, bf16[8,32,1024]{2,1,0:T(8,128)(2,1)S(1)}, u32[]{:S(2)}, u32[]{:S(2)}) collective-permute-start(bf16[8,32,1024]{2,1,0:T(8,128)(2,1)S(1)} %constant_dynamic-update-slice_fusion.2.refs_1_.refs_3_.refs_5_.refs_7_.refs_9_.refs_11_.refs_13_.r, ...), channel_id=1, source_target_pairs={{0,1},{1,0},{2,3},{3,2},{4,5},{5,4},{6,7},{7,6},{8,9},{9,8},{10,11... | collective-permute-start | bytes 1572872 | tf_op jit(solution)/shard_map/ppermute | solution.py:62
  66.6 5.2 %collective-permute-start.16 = (bf16[8,32,1024]{2,1,0:T(8,128)(2,1)S(1)}, bf16[8,32,1024]{2,1,0:T(8,128)(2,1)S(1)}, u32[]{:S(2)}, u32[]{:S(2)}) collective-permute-start(bf16[8,32,1024]{2,1,0:T(8,128)(2,1)S(1)} %constant_dynamic-update-slice_fusion.refs_0_.refs_2_.refs_4_.refs_6_.refs_8_.refs_10_.refs_12_.ref, ...), channel_id=1, source_target_pairs={{0,1},{1,0},{2,3},{3,2},{4,5},{5,4},{6,7},{7,6},{8,9},{9,8},{10,11... | collective-permute-start | bytes 1572872 | tf_op jit(solution)/shard_map/ppermute | solution.py:62
  80.0 4.1 %collective-permute-start.19 = (f16[8,64,1024]{2,1,0:T(8,128)(2,1)S(1)}, f16[8,64,1024]{2,1,0:T(8,128)(2,1)S(1)}, u32[]{:S(2)}, u32[]{:S(2)}) collective-permute-start(f16[8,64,1024]{2,1,0:T(8,128)(2,1)S(1)} %convert_element_type.154), channel_id=1, source_target_pairs={{0,1},{1,0},{2,3},{3,2},{4,5},{5,4},{6,7},{7,6},{8,9},{9,8},{10,11... | collective-permute-start | bytes 3145736 | tf_op jit(solution)/shard_map/ppermute | solution.py:62
  80.5 3.6 %collective-permute-start.20 = (f32[64,64]{1,0:T(8,128)S(1)}, f32[64,64]{1,0:T(8,128)S(1)}, u32[]{:S(2)}, u32[]{:S(2)}) collective-permute-start(f32[64,64]{1,0:T(8,128)S(1)} %get-tuple-element.121), channel_id=1, source_target_pairs={{0,1},{1,0},{2,3},{3,2},{4,5},{5,4},{6,7},{7,6},{8,9},{9,8},{10,11... | collective-permute-start | bytes 49160 | tf_op jit(solution)/shard_map/ppermute | solution.py:62
  85.0 8.7 %collective-permute-start.22 = (f16[2,2,32,1024]{3,2,1,0:T(8,128)(2,1)S(1)}, f16[2,2,32,1024]{3,2,1,0:T(8,128)(2,1)S(1)}, u32[]{:S(2)}, u32[]{:S(2)}) collective-permute-start(f16[2,2,32,1024]{3,2,1,0:T(8,128)(2,1)S(1)} %convert_element_type.158), channel_id=1, source_target_pairs={{0,4},{1,5},{2,6},{3,7},{4,0},{5,1},{6,2},{7,3},{8,12},{9,13},{10,... | collective-permute-start | bytes 786440 | tf_op jit(solution)/shard_map/ppermute | solution.py:62
  85.6 4.1 %collective-permute-start.23 = (f32[64,64]{1,0:T(8,128)S(1)}, f32[64,64]{1,0:T(8,128)S(1)}, u32[]{:S(2)}, u32[]{:S(2)}) collective-permute-start(f32[64,64]{1,0:T(8,128)S(1)} %add.121), channel_id=1, source_target_pairs={{0,2},{1,3},{2,0},{3,1},{4,6},{5,7},{6,4},{7,5},{8,10},{9,11},{10,... | collective-permute-start | bytes 49160 | tf_op jit(solution)/shard_map/ppermute | solution.py:62
  87.0 8.1 %collective-permute-start.21 = (f16[2,2,32,1024]{3,2,0,1:T(8,128)(2,1)S(1)}, f16[2,2,32,1024]{3,2,0,1:T(8,128)(2,1)S(1)}, u32[]{:S(2)}, u32[]{:S(2)}) collective-permute-start(f16[2,2,32,1024]{3,2,0,1:T(8,128)(2,1)S(1)} %convert_element_type.156), channel_id=1, source_target_pairs={{0,2},{1,3},{2,0},{3,1},{4,6},{5,7},{6,4},{7,5},{8,10},{9,11},{10,... | collective-permute-start | bytes 786440 | tf_op jit(solution)/shard_map/ppermute | solution.py:62
  95.2 8.2 %collective-permute-start.26 = (f32[64,64]{1,0:T(8,128)S(1)}, f32[64,64]{1,0:T(8,128)S(1)}, u32[]{:S(2)}, u32[]{:S(2)}) collective-permute-start(f32[64,64]{1,0:T(8,128)S(1)} %add.124), channel_id=1, source_target_pairs={{0,4},{1,5},{2,6},{3,7},{4,0},{5,1},{6,2},{7,3},{8,12},{9,13},{10,... | collective-permute-start | bytes 49160 | tf_op jit(solution)/shard_map/ppermute | solution.py:62
  97.5 8.1 %collective-permute-start.25 = (f16[2,32,1024]{2,1,0:T(8,128)(2,1)}, f16[2,32,1024]{2,1,0:T(8,128)(2,1)S(1)}, u32[]{:S(2)}, u32[]{:S(2)}) collective-permute-start(f16[2,32,1024]{2,1,0:T(8,128)(2,1)} %convert_element_type.162), channel_id=1, source_target_pairs={{0,8},{1,9},{2,10},{3,11},{4,12},{5,13},{6,14},{7,15},{8,0},{9,1},... | collective-permute-start | bytes 393224 | tf_op jit(solution)/shard_map/ppermute | solution.py:62
  99.9 6.7 %collective-permute-start.24 = (f16[2,32,1024]{2,1,0:T(8,128)(2,1)}, f16[2,32,1024]{2,1,0:T(8,128)(2,1)}, u32[]{:S(2)}, u32[]{:S(2)}) collective-permute-start(f16[2,32,1024]{2,1,0:T(8,128)(2,1)} %convert_element_type.160), channel_id=1, source_target_pairs={{0,4},{1,5},{2,6},{3,7},{4,0},{5,1},{6,2},{7,3},{8,12},{9,13},{10,... | collective-permute-start | bytes 393224 | tf_op jit(solution)/shard_map/ppermute | solution.py:62
  107.6 5.2 %collective-permute-start.29 = (f32[64,64]{1,0:T(8,128)S(1)}, f32[64,64]{1,0:T(8,128)S(1)}, u32[]{:S(2)}, u32[]{:S(2)}) collective-permute-start(f32[64,64]{1,0:T(8,128)S(1)} %add.127), channel_id=1, source_target_pairs={{0,8},{1,9},{2,10},{3,11},{4,12},{5,13},{6,14},{7,15},{8,0},{9,1},... | collective-permute-start | bytes 49160 | tf_op jit(solution)/shard_map/ppermute | solution.py:62
  108.0 5.4 %collective-permute-start.28 = (f16[32,1024]{1,0:T(8,128)(2,1)S(1)}, f16[32,1024]{1,0:T(8,128)(2,1)S(1)}, u32[]{:S(2)}, u32[]{:S(2)}) collective-permute-start(f16[32,1024]{1,0:T(8,128)(2,1)S(1)} %convert_element_type.166), channel_id=1, source_target_pairs={{0,2},{1,3},{2,0},{3,1},{4,6},{5,7},{6,4},{7,5},{8,10},{9,11},{10,... | collective-permute-start | bytes 196616 | tf_op jit(solution)/shard_map/ppermute | solution.py:62
  109.4 5.2 %collective-permute-start.27 = (f16[32,1024]{1,0:T(8,128)(2,1)S(1)}, f16[32,1024]{1,0:T(8,128)(2,1)S(1)}, u32[]{:S(2)}, u32[]{:S(2)}) collective-permute-start(f16[32,1024]{1,0:T(8,128)(2,1)S(1)} %convert_element_type.164), channel_id=1, source_target_pairs={{0,8},{1,9},{2,10},{3,11},{4,12},{5,13},{6,14},{7,15},{8,0},{9,1},... | collective-permute-start | bytes 196616 | tf_op jit(solution)/shard_map/ppermute | solution.py:62
  115.5 5.3 %collective-permute-start.30 = (bf16[1,32,1024]{2,1,0:T(8,128)(2,1)S(1)}, bf16[1,32,1024]{2,1,0:T(8,128)(2,1)S(1)}, u32[]{:S(2)}, u32[]{:S(2)}) collective-permute-start(bf16[1,32,1024]{2,1,0:T(8,128)(2,1)S(1)} %get-tuple-element.140), channel_id=1, source_target_pairs={{0,8},{1,9},{2,10},{3,11},{4,12},{5,13},{6,14},{7,15},{8,0},{9,1},... | collective-permute-start | bytes 196616 | tf_op jit(solution)/shard_map/ppermute | solution.py:62
  118.4 4.3 %collective-permute-start.31 = (bf16[1,32,1024]{2,1,0:T(8,128)(2,1)S(1)}, bf16[1,32,1024]{2,1,0:T(8,128)(2,1)S(1)}, u32[]{:S(2)}, u32[]{:S(2)}) collective-permute-start(bf16[1,32,1024]{2,1,0:T(8,128)(2,1)S(1)} %get-tuple-element.141), channel_id=1, source_target_pairs={{0,2},{1,3},{2,0},{3,1},{4,6},{5,7},{6,4},{7,5},{8,10},{9,11},{10,... | collective-permute-start | bytes 196616 | tf_op jit(solution)/shard_map/ppermute | solution.py:62
  122.7 6.8 %collective-permute-start.32 = (bf16[2,32,1024]{2,1,0:T(8,128)(2,1)S(1)}, bf16[2,32,1024]{2,1,0:T(8,128)(2,1)S(1)}, u32[]{:S(2)}, u32[]{:S(2)}) collective-permute-start(bf16[2,32,1024]{2,1,0:T(8,128)(2,1)S(1)} %pad_maximum_fusion.6), channel_id=1, source_target_pairs={{0,4},{1,5},{2,6},{3,7},{4,0},{5,1},{6,2},{7,3},{8,12},{9,13},{10,... | collective-permute-start | bytes 393224 | tf_op jit(solution)/shard_map/ppermute | solution.py:62
  122.7 6.7 %collective-permute-start.33 = (bf16[2,32,1024]{2,1,0:T(8,128)(2,1)S(1)}, bf16[2,32,1024]{2,1,0:T(8,128)(2,1)S(1)}, u32[]{:S(2)}, u32[]{:S(2)}) collective-permute-start(bf16[2,32,1024]{2,1,0:T(8,128)(2,1)S(1)} %pad_maximum_fusion.7), channel_id=1, source_target_pairs={{0,8},{1,9},{2,10},{3,11},{4,12},{5,13},{6,14},{7,15},{8,0},{9,1},... | collective-permute-start | bytes 393224 | tf_op jit(solution)/shard_map/ppermute | solution.py:62
  129.5 7.4 %collective-permute-start.36 = (bf16[4,32,1024]{2,1,0:T(8,128)(2,1)S(1)}, bf16[4,32,1024]{2,1,0:T(8,128)(2,1)S(1)}, u32[]{:S(2)}, u32[]{:S(2)}) collective-permute-start(bf16[4,32,1024]{2,1,0:T(8,128)(2,1)S(1)} %pad_maximum_fusion.3), channel_id=1, source_target_pairs={{0,4},{1,5},{2,6},{3,7},{4,0},{5,1},{6,2},{7,3},{8,12},{9,13},{10,... | collective-permute-start | bytes 786440 | tf_op jit(solution)/shard_map/ppermute | solution.py:62
  132.6 6.4 %collective-permute-start.34 = (bf16[4,32,1024]{2,1,0:T(8,128)(2,1)S(1)}, bf16[4,32,1024]{2,1,0:T(8,128)(2,1)S(1)}, u32[]{:S(2)}, u32[]{:S(2)}) collective-permute-start(bf16[4,32,1024]{2,1,0:T(8,128)(2,1)S(1)} %pad_maximum_fusion.2), channel_id=1, source_target_pairs={{0,2},{1,3},{2,0},{3,1},{4,6},{5,7},{6,4},{7,5},{8,10},{9,11},{10,... | collective-permute-start | bytes 786440 | tf_op jit(solution)/shard_map/ppermute | solution.py:62
  136.9 7.2 %collective-permute-start.37 = (bf16[8,32,1024]{2,1,0:T(8,128)(2,1)S(1)}, bf16[8,32,1024]{2,1,0:T(8,128)(2,1)S(1)}, u32[]{:S(2)}, u32[]{:S(2)}) collective-permute-start(bf16[8,32,1024]{2,1,0:T(8,128)(2,1)S(1)} %constant_dynamic-update-slice_fusion.6.refs_1_.refs_3_.refs_5_.refs_7_), channel_id=1, source_target_pairs={{0,1},{1,0},{2,3},{3,2},{4,5},{5,4},{6,7},{7,6},{8,9},{9,8},{10,11... | collective-permute-start | bytes 1572872 | tf_op jit(solution)/shard_map/ppermute | solution.py:62
  139.0 5.1 %collective-permute-start.35 = (bf16[8,32,1024]{2,1,0:T(8,128)(2,1)S(1)}, bf16[8,32,1024]{2,1,0:T(8,128)(2,1)S(1)}, u32[]{:S(2)}, u32[]{:S(2)}) collective-permute-start(bf16[8,32,1024]{2,1,0:T(8,128)(2,1)S(1)} %constant_dynamic-update-slice_fusion.4.refs_0_.refs_2_.refs_4_.refs_6_), channel_id=1, source_target_pairs={{0,1},{1,0},{2,3},{3,2},{4,5},{5,4},{6,7},{7,6},{8,9},{9,8},{10,11... | collective-permute-start | bytes 1572872 | tf_op jit(solution)/shard_map/ppermute | solution.py:62
  153.5 6.9 %collective-permute-start.39 = (f16[8,64,1024]{2,1,0:T(8,128)(2,1)S(1)}, f16[8,64,1024]{2,1,0:T(8,128)(2,1)S(1)}, u32[]{:S(2)}, u32[]{:S(2)}) collective-permute-start(f16[8,64,1024]{2,1,0:T(8,128)(2,1)S(1)} %convert_element_type.170), channel_id=1, source_target_pairs={{0,1},{1,0},{2,3},{3,2},{4,5},{5,4},{6,7},{7,6},{8,9},{9,8},{10,11... | collective-permute-start | bytes 3145736 | tf_op jit(solution)/shard_map/ppermute | solution.py:62
  156.4 4.0 %collective-permute-start.40 = (f32[64,64]{1,0:T(8,128)S(1)}, f32[64,64]{1,0:T(8,128)S(1)}, u32[]{:S(2)}, u32[]{:S(2)}) collective-permute-start(f32[64,64]{1,0:T(8,128)S(1)} %add.133), channel_id=1, source_target_pairs={{0,2},{1,3},{2,0},{3,1},{4,6},{5,7},{6,4},{7,5},{8,10},{9,11},{10,... | collective-permute-start | bytes 49160 | tf_op jit(solution)/shard_map/ppermute | solution.py:62
  161.4 8.3 %collective-permute-start.42 = (f16[2,2,32,1024]{3,2,1,0:T(8,128)(2,1)S(1)}, f16[2,2,32,1024]{3,2,1,0:T(8,128)(2,1)S(1)}, u32[]{:S(2)}, u32[]{:S(2)}) collective-permute-start(f16[2,2,32,1024]{3,2,1,0:T(8,128)(2,1)S(1)} %convert_element_type.174), channel_id=1, source_target_pairs={{0,4},{1,5},{2,6},{3,7},{4,0},{5,1},{6,2},{7,3},{8,12},{9,13},{10,... | collective-permute-start | bytes 786440 | tf_op jit(solution)/shard_map/ppermute | solution.py:62
  161.9 7.7 %collective-permute-start.43 = (f32[64,64]{1,0:T(8,128)S(1)}, f32[64,64]{1,0:T(8,128)S(1)}, u32[]{:S(2)}, u32[]{:S(2)}) collective-permute-start(f32[64,64]{1,0:T(8,128)S(1)} %add.135), channel_id=1, source_target_pairs={{0,4},{1,5},{2,6},{3,7},{4,0},{5,1},{6,2},{7,3},{8,12},{9,13},{10,... | collective-permute-start | bytes 49160 | tf_op jit(solution)/shard_map/ppermute | solution.py:62
  163.5 7.0 %collective-permute-start.41 = (f16[2,2,32,1024]{3,2,0,1:T(8,128)(2,1)S(1)}, f16[2,2,32,1024]{3,2,0,1:T(8,128)(2,1)S(1)}, u32[]{:S(2)}, u32[]{:S(2)}) collective-permute-start(f16[2,2,32,1024]{3,2,0,1:T(8,128)(2,1)S(1)} %convert_element_type.172), channel_id=1, source_target_pairs={{0,2},{1,3},{2,0},{3,1},{4,6},{5,7},{6,4},{7,5},{8,10},{9,11},{10,... | collective-permute-start | bytes 786440 | tf_op jit(solution)/shard_map/ppermute | solution.py:62
  170.6 8.7 %collective-permute-start.45 = (f16[2,32,1024]{2,1,0:T(8,128)(2,1)S(1)}, f16[2,32,1024]{2,1,0:T(8,128)(2,1)S(1)}, u32[]{:S(2)}, u32[]{:S(2)}) collective-permute-start(f16[2,32,1024]{2,1,0:T(8,128)(2,1)S(1)} %convert_element_type.178), channel_id=1, source_target_pairs={{0,8},{1,9},{2,10},{3,11},{4,12},{5,13},{6,14},{7,15},{8,0},{9,1},... | collective-permute-start | bytes 393224 | tf_op jit(solution)/shard_map/ppermute | solution.py:62
  171.6 7.2 %collective-permute-start.46 = (f32[64,64]{1,0:T(8,128)S(1)}, f32[64,64]{1,0:T(8,128)S(1)}, u32[]{:S(2)}, u32[]{:S(2)}) collective-permute-start(f32[64,64]{1,0:T(8,128)S(1)} %add.138), channel_id=1, source_target_pairs={{0,8},{1,9},{2,10},{3,11},{4,12},{5,13},{6,14},{7,15},{8,0},{9,1},... | collective-permute-start | bytes 49160 | tf_op jit(solution)/shard_map/ppermute | solution.py:62
  173.6 6.4 %collective-permute-start.44 = (f16[2,32,1024]{2,1,0:T(8,128)(2,1)S(1)}, f16[2,32,1024]{2,1,0:T(8,128)(2,1)S(1)}, u32[]{:S(2)}, u32[]{:S(2)}) collective-permute-start(f16[2,32,1024]{2,1,0:T(8,128)(2,1)S(1)} %convert_element_type.176), channel_id=1, source_target_pairs={{0,4},{1,5},{2,6},{3,7},{4,0},{5,1},{6,2},{7,3},{8,12},{9,13},{10,... | collective-permute-start | bytes 393224 | tf_op jit(solution)/shard_map/ppermute | solution.py:62
  180.1 7.5 %collective-permute-start.48 = (f16[32,1024]{1,0:T(8,128)(2,1)S(1)}, f16[32,1024]{1,0:T(8,128)(2,1)S(1)}, u32[]{:S(2)}, u32[]{:S(2)}) collective-permute-start(f16[32,1024]{1,0:T(8,128)(2,1)S(1)} %convert_element_type.182), channel_id=1, source_target_pairs={{0,2},{1,3},{2,0},{3,1},{4,6},{5,7},{6,4},{7,5},{8,10},{9,11},{10,... | collective-permute-start | bytes 196616 | tf_op jit(solution)/shard_map/ppermute | solution.py:62
  182.0 5.6 %collective-permute-start.47 = (f16[32,1024]{1,0:T(8,128)(2,1)S(1)}, f16[32,1024]{1,0:T(8,128)(2,1)S(1)}, u32[]{:S(2)}, u32[]{:S(2)}) collective-permute-start(f16[32,1024]{1,0:T(8,128)(2,1)S(1)} %convert_element_type.180), channel_id=1, source_target_pairs={{0,8},{1,9},{2,10},{3,11},{4,12},{5,13},{6,14},{7,15},{8,0},{9,1},... | collective-permute-start | bytes 196616 | tf_op jit(solution)/shard_map/ppermute | solution.py:62
  (10 other events, 42.2 us)

commit v9 on v8

--- a/solution.py
+++ b/solution.py
@@ -13,7 +13,7 @@
 BOUND = 18.0
 TOP = 60000.0
 TINY = 1e-30
-UNROLL = 4
+UNROLL = 2
 F32, BF16, F16 = jnp.float32, jnp.bfloat16, jnp.float16
 
 
@@ -188,38 +188,79 @@
         gram[...] = x
 
 
+def load_kernel(acts, out, sems):
+    count = sems.shape[0]
+    f = acts.shape[1] // count
+
+    def copy(t):
+        columns = pl.ds(pl.multiple_of(t * f, f), f)
+        return pltpu.make_async_copy(acts.at[:, columns], out.at[:, columns], sems.at[t])
+
+    lax.fori_loop(0, count, lambda t, c: (copy(t).start(), c)[1], 0)
+    lax.fori_loop(0, count, lambda t, c: (copy(t).wait(), c)[1], 0)
+
+
+def load(acts):
+    return pl.pallas_call(
+        load_kernel,
+        out_shape=jax.ShapeDtypeStruct(acts.shape, acts.dtype),
+        in_specs=[HBM],
+        out_specs=pl.BlockSpec(memory_space=pltpu.VMEM),
+        scratch_shapes=[pltpu.SemaphoreType.DMA((8,))],
+        compiler_params=pltpu.CompilerParams(vmem_limit_bytes=16 << 20),
+        cost_estimate=pl.CostEstimate(flops=0, bytes_accessed=4 * acts.size, transcendentals=0),
+        name="load",
+    )(acts)
+
+
+def near_call(kernel, name, n, grid, in_specs, out_shapes, out_specs, acts, scratch=(), aliases=None):
+    rows, d = acts.shape
+    return pl.pallas_call(
+        kernel,
+        out_shape=out_shapes,
+        grid_spec=pltpu.PrefetchScalarGridSpec(
+            num_scalar_prefetch=1, grid=(grid,), in_specs=in_specs, out_specs=out_specs, scratch_shapes=scratch
+        ),
+        compiler_params=pltpu.CompilerParams(vmem_limit_bytes=12 << 20),
+        cost_estimate=pl.CostEstimate(flops=K * rows * d, bytes_accessed=rows * d + 2 * K * d, transcendentals=0),
+        input_output_aliases=aliases or {},
+        name=name,
+    )
+
+
+def act_specs(rows, f, half, block):
+    return [
+        pl.BlockSpec((rows, f), lambda i, me, u=u: (0, me[0] ^ (2 * (block(i) + u) + half))) for u in range(UNROLL)
+    ]
+
+
 def probe_kernel(count, me, *refs):
-    panels, refs = refs[: 2 * UNROLL * count], refs[2 * UNROLL * count :]
-    acts, probed, *grams, kept, sems = refs
-    step = pl.program_id(0)
-
-    @pl.when(step == 0)
-    def _():
-        start_copies(acts, kept, sems, me, 0)
-        for ref in (probed, *grams):
+    panels, acts, outs = refs[: 2 * UNROLL * count], refs[2 * UNROLL * count : -1 - count], refs[-1 - count :]
+    probed, *grams = outs
+
+    @pl.when(pl.program_id(0) == 0)
+    def _():
+        for ref in outs:
             ref[...] = jnp.zeros_like(ref)
 
-    def block(u):
-        block_copy(acts, kept, sems, me, 0, step * UNROLL + u).wait()
-        return kept[step * UNROLL + u]
-
-    add_blocks(panels, count, block, probed, grams)
+    add_blocks(panels, count, lambda u: acts[u][...], probed, grams)
 
 
 def probe(me, panels, acts, n, shifts):
     rows, d = acts.shape
+    f = d // n
     count = len(panels)
-    specs, operands = panel_operands(panels, n, d // n, shifts)
-    return call(
+    specs, operands = panel_operands(panels, n, f, shifts)
+    return near_call(
         functools.partial(probe_kernel, count),
         "probe",
         n,
         n // 2 // UNROLL,
-        specs + [HBM],
+        specs + act_specs(rows, f, 0, lambda i: i * UNROLL),
         (jax.ShapeDtypeStruct((rows, K), F32),) + (jax.ShapeDtypeStruct((K, K), F32),) * count,
         (whole(rows, K),) + (whole(K, K),) * count,
         acts,
-    )(me, *operands, acts)
+    )(me, *operands, *[acts] * UNROLL)
 
 
 def diagonal(matrix):
@@ -254,29 +295,24 @@
 
 def send_kernel(steps, count, d, me, *refs):
     second = count == 2
-    parts = [2 * UNROLL * count, 4, count, 4 * second, 6, count, 3 * second, 4]
+    parts = [2 * UNROLL * count, UNROLL, 3, count, 4 * second, 6, count, 3 * second, 2]
     refs = list(refs)
-    panels, ins, starts, given, outs, grams, made, scratch = (
+    panels, acts, ins, starts, given, outs, grams, made, scratch = (
         [refs.pop(0) for _ in range(size)] for size in parts
     )
-    acts, row_data, total_weight, start = ins
+    row_data, total_weight, start = ins
     probed, along, inv, back, back_row, out = outs
-    kept, sems, weighted, sum_of = scratch
+    weighted, sum_of = scratch
     step = pl.program_id(0)
 
     @pl.when(step == 0)
     def _():
-        start_copies(acts, kept, sems, me, 1)
         for ref, begin in zip((sum_of, *grams), (start, *starts)):
             ref[...] = begin[...]
 
     @pl.when(step < steps)
     def _():
-        def block(u):
-            block_copy(acts, kept, sems, me, 1, step * UNROLL + u).wait()
-            return kept[step * UNROLL + u]
-
-        add_blocks(panels, count, block, sum_of, grams)
+        add_blocks(panels, count, lambda u: acts[u][...], sum_of, grams)
 
     @pl.when(step == steps)
     def _():
@@ -292,7 +328,7 @@
     @pl.when(step >= steps)
     def _():
         for u in range(UNROLL):
-            block = jnp.dot(weighted[...], kept[(step - steps) * UNROLL + u], preferred_element_type=F32)
+            block = jnp.dot(weighted[...], acts[u][...], preferred_element_type=F32)
             out[u] = block * inv[...]
 
 
@@ -304,12 +340,15 @@
     square = jax.ShapeDtypeStruct((K, K), F32)
     made = 3 if given else 0
     specs, operands = panel_operands(panels, n, f, shifts)
-    return call(
+    return near_call(
         functools.partial(send_kernel, s, count, d),
         "probe_and_send",
         n,
         2 * s,
-        specs + [HBM, whole(1, rows), whole(1, 1)] + [whole(*x.shape) for x in (*starts, *given)],
+        specs
+        + act_specs(rows, f, 1, lambda i: jnp.where(i < s, i, i - s) * UNROLL)
+        + [whole(1, rows), whole(1, 1)]
+        + [whole(*x.shape) for x in (*starts, *given)],
         (
             jax.ShapeDtypeStruct((K, rows), F32),
             square,
@@ -330,25 +369,18 @@
         + (whole(K, K),) * (count + made),
         acts,
         [pltpu.VMEM((K, rows), BF16), pltpu.VMEM((rows, K), F32)],
-    )(me, *operands, acts, row_data, total_weight, *starts, *given)
-
-
-def keep_kernel(base, me, probed, row_data, inv, acts, *refs):
-    out, kept, sems, weighted = refs[-4:]
-    step = pl.program_id(0)
-
-    def copy(t):
-        return block_copy(acts, kept, sems, me, 0, t)
-
-    @pl.when(step == 0)
-    def _():
-        lax.fori_loop(base, base + pl.num_programs(0) * UNROLL, lambda t, c: (copy(t).start(), c)[1], 0)
+    )(me, *operands, *[acts] * UNROLL, row_data, total_weight, *starts, *given)
+
+
+def keep_kernel(me, probed, row_data, inv, *refs):
+    acts, out, weighted = refs[:UNROLL], refs[-2], refs[-1]
+
+    @pl.when(pl.program_id(0) == 0)
+    def _():
         weighted[...] = (count_of(row_data) * probed[...]).astype(BF16)
 
     for u in range(UNROLL):
-        t = base + step * UNROLL + u
-        copy(t).wait()
-        out[u] = jnp.dot(weighted[...], kept[t], preferred_element_type=F32) * inv[...]
+        out[u] = jnp.dot(weighted[...], acts[u][...], preferred_element_type=F32) * inv[...]
 
 
 def panel_keep(me, probed, row_data, inv, acts, n, part=None, into=None):
@@ -360,18 +392,20 @@
         steps //= 2
         first = part * steps
     more = () if into is None else (into,)
-    return call(
-        functools.partial(keep_kernel, first * UNROLL),
+    return near_call(
+        keep_kernel,
         "panel_keep",
         n,
         steps,
-        [whole(K, rows), whole(1, rows), whole(K, 1), HBM] + [pl.BlockSpec(memory_space=pl.ANY)] * len(more),
+        [whole(K, rows), whole(1, rows), whole(K, 1)]
+        + act_specs(rows, f, 0, lambda i: (i + first) * UNROLL)
+        + [pl.BlockSpec(memory_space=pl.ANY)] * len(more),
         jax.ShapeDtypeStruct((n // 2, K, f), F32),
         pl.BlockSpec((UNROLL, K, f), lambda i, me: (i + first, 0, 0)),
         acts,
         [pltpu.VMEM((K, rows), BF16)],
-        {5: 0} if more else {},
-    )(me, probed, row_data, inv, acts, *more)
+        {4 + UNROLL: 0} if more else {},
+    )(me, probed, row_data, inv, *[acts] * UNROLL, *more)
 
 
 def alpha_kernel(along, current, total_weight, alpha_t, inverse):
@@ -465,17 +499,18 @@
         return got * jnp.abs(got) * (1.0 / self.scale**2)
 
 
-def gather(top, low, n, orders, work=None, args=()):
+def gather(top, low, n, orders, acts, work=None, args=()):
     a, b = top.astype(BF16)[None], low.astype(BF16)[None]
     done = ()
     for phase, (bit_a, bit_b) in enumerate(zip(*orders)):
         tied = args if phase == 1 else done
-        a, b, tied = lax.optimization_barrier((a, b, tied))
+        a, b, tied, acts = lax.optimization_barrier((a, b, tied, acts))
         if work is not None and phase >= 1:
             done = work(*tied) if phase == 1 else tied
         a = jnp.concatenate([a, swap(a, bit_a, n)], axis=0)
         b = jnp.concatenate([b, swap(b, bit_b, n)], axis=0)
-    return (a, b), (swap(a, 1, n), swap(b, 1, n)), done
+    near, a, b = lax.optimization_barrier((load(acts), a, b))
+    return (a, b), (swap(a, 1, n), swap(b, 1, n)), near, done
 
 
 def per_device(n, activations, labels, counts):
@@ -496,48 +531,48 @@
     top, low, weight, _ = reduce_scatter(kept + got, n, root, root, weight, order_y)
     class_weight = weight.T
     total_weight = jnp.sum(class_weight, keepdims=True)
-    over, back = class_weight, jnp.sqrt(class_weight)
-    base = (top / over[:HALF]) * back[:HALF], (low / over[HALF:]) * back[HALF:]
-
-    def scatter(probed, along, inv, sent, early, work, args):
+    factor = 1.0 / jnp.sqrt(class_weight)
+    base = top * factor[:HALF], low * factor[HALF:]
+
+    def scatter(close, probed, along, inv, sent, early, work, args):
         hop = plain(n)
         got = hop(sent, 1)
         along = along + swap(along, 1, n)
         waiting = order_y
         if early:
-            kept = panel_keep(me, probed, row_data, inv, activations, n, 0)
+            kept = panel_keep(me, probed, row_data, inv, close, n, 0)
             kept, along = lax.optimization_barrier((kept, along))
             along = along + swap(along, waiting[0], n)
-            kept = panel_keep(me, probed, row_data, inv, activations, n, 1, kept)
+            kept = panel_keep(me, probed, row_data, inv, close, n, 1, kept)
             waiting = waiting[1:]
         else:
-            kept = panel_keep(me, probed, row_data, inv, activations, n)
+            kept = panel_keep(me, probed, row_data, inv, close, n)
         return reduce_scatter(kept + got, n, hop, hop, along, waiting, work, args, not early)
 
     square, strip = (K, K), (K, d // n)
     orders = order_a, order_b
-    base_near, base_far, _ = gather(*base, n, orders)
-    starts = probe(me, (base_near,), activations, n, shifts)
+    base_near, base_far, close, _ = gather(*base, n, orders, activations)
+    starts = probe(me, (base_near,), close, n, shifts)
     first, along, inv, back, _, sent, current = probe_and_send(
-        me, (base_far,), activations, row_data, total_weight, starts, (), n, shifts
+        me, (base_far,), close, row_data, total_weight, starts, (), n, shifts
     )
     panel_a, panel_b, along, (offset,) = scatter(
-        first, along, inv, sent, False,
+        close, first, along, inv, sent, False,
         lambda *args: small(offset_kernel, "offset", (strip,), *args), (*base, current, total_weight),
     )
     back = back / total_weight
     image = panel_a * back[:HALF] + offset[:HALF], panel_b * back[HALF:] + offset[HALF:]
 
-    near, far, (alpha_t, inverse) = gather(
-        *image, n, orders,
+    near, far, close, (alpha_t, inverse) = gather(
+        *image, n, orders, activations,
         lambda *args: small(alpha_kernel, "alpha", (square,) * 2, *args), (along, current, total_weight),
     )
-    starts = probe(me, (near, base_near), activations, n, shifts)
+    starts = probe(me, (near, base_near), close, n, shifts)
     probed, along, inv, _, back_row, sent, _, _, renewed, mixed, beta_t = probe_and_send(
-        me, (far, base_far), activations, row_data, total_weight, starts, (first, current, alpha_t, inverse), n, shifts
+        me, (far, base_far), close, row_data, total_weight, starts, (first, current, alpha_t, inverse), n, shifts
     )
     panel_a, panel_b, along, (fixed, cross_t) = scatter(
-        probed, along, inv, sent, True,
+        close, probed, along, inv, sent, True,
         lambda *args: small(before_kernel, "before", (square,) * 2, *args),
         (current, renewed, mixed, beta_t, total_weight),
     )

time: 191 us -> 183 us (0.958)
  waiting for transfers between devices: 57 us -> 48.8 us
    ppermute x49, waiting for transfers between devices: 57 us -> 48.8 us  [swap(): return lax.ppermute(value, 'dp', [(i, i ^ bit) for i in range(n)])]
    pallas_call x7 -> x9, Pallas kernels: 35.3 us -> 36 us  [the longest x2 15.3 us: probe_and_send(): near_call(functools.partial(send_kernel, s, count, d), 'probe_and_send',...]
  transfers between devices with their start and end apart: 49 -> 49, of which waited for: 31 -> 30; matrix products, arithmetic and copies ran while one was open for 3% -> 3% of each run, Pallas kernels for 19% -> 22%
where the time goes in v9:
time: 183 us
  Pallas kernels  58.4 us (32%)
  starting transfers between devices  56.8 us (31%)
  waiting for transfers between devices  48.8 us (27%)
  other arithmetic  13.9 us (8%)
  local copies, waits for them, and re-layouts  2.05 us (1%)
    ppermute x49, starting transfers between devices, swap(): return lax.ppermute(value, 'dp', [(i, i ^ bit) for i in range(n)])  56.8 us
    ppermute x49, waiting for transfers between devices, swap(): return lax.ppermute(value, 'dp', [(i, i ^ bit) for i in range(n)])  48.8 us
    pallas_call x4, Pallas kernels, small(): pl.pallas_call(kernel, out_shape=tuple((jax.ShapeDtypeStruct(shape, F32)...  15.4 us
    pallas_call x2, Pallas kernels, probe_and_send(): near_call(functools.partial(send_kernel, s, count, d), 'probe_and_send',...  15.3 us
    pallas_call x2, Pallas kernels, load(): pl.pallas_call(load_kernel, out_shape=jax.ShapeDtypeStruct(acts.shape, ac...  9.44 us
    pallas_call x2, Pallas kernels, class_sums(): call(functools.partial(sums_kernel, half), 'class_sums', n, n // 2 // UNR...  7.03 us
    pallas_call x2, Pallas kernels, probe(): near_call(functools.partial(probe_kernel, count), 'probe', n, n // 2 // U...  6.44 us
    pallas_call x3, Pallas kernels, panel_keep(): near_call(keep_kernel, 'panel_keep', n, steps, [whole(K, rows), whole(1,...  4.78 us
  transfers between devices with their start and end apart: 49, of which 30 were waited for; matrix products, arithmetic and copies ran while one was open for 3% of the time, Pallas kernels for 22%

profile of v9, /device:TPU:0, one launch (start us, length us, event | category | flops | bytes accessed | tf_op | source)
XLA Modules:
  0.0 182.5 jit_solution(12835308019516406077)
XLA Ops:
  1.3 3.3 %class_sums.3 = (f32[8,64,1024]{2,1,0:T(8,128)S(1)}, f32[64,1]{1,0:T(8,128)S(1)}) custom-call(s32[1]{0:T(128)} %bitcast.me, s32[1,384]{1,0:T(1,128)S(1)} %reshape.50.row_data.refs_6_.refs_10_, bf16[384,16384]{1,0:T(8,128)(2,1)} %acts.5), custom_call_target="tpu_custom_call" | custom-call | flops 402653184 | bytes 8388608 | tf_op jit(solution)/shard_map/class_sums/pallas_call | solution.py:146
  6.3 3.7 %class_sums.2 = (f32[8,64,1024]{2,1,0:T(8,128)S(1)}, f32[64,1]{1,0:T(8,128)}) custom-call(s32[1]{0:T(128)} %bitcast.me, s32[1,384]{1,0:T(1,128)S(1)} %reshape.50.row_data.refs_6_.refs_10_, bf16[384,16384]{1,0:T(8,128)(2,1)} %acts.5), custom_call_target="tpu_custom_call" | custom-call | flops 402653184 | bytes 8388608 | tf_op jit(solution)/shard_map/class_sums/pallas_call | solution.py:146
  11.4 3.1 %collective-permute-start.3 = (f16[2,2,32,1024]{3,2,0,1:T(8,128)(2,1)S(1)}, f16[2,2,32,1024]{3,2,0,1:T(8,128)(2,1)S(1)}, u32[]{:S(2)}, u32[]{:S(2)}) collective-permute-start(f16[2,2,32,1024]{3,2,0,1:T(8,128)(2,1)S(1)} %fusion.6), channel_id=1, source_target_pairs={{0,4},{1,5},{2,6},{3,7},{4,0},{5,1},{6,2},{7,3},{8,12},{9,13},{10,... | collective-permute-start | bytes 786440 | tf_op jit(solution)/shard_map/ppermute | solution.py:62
  14.5 1.5 collective-permute-start.4
  18.0 3.0 %collective-permute-done.3 = f16[2,2,32,1024]{3,2,0,1:T(8,128)(2,1)S(1)} collective-permute-done((f16[2,2,32,1024]{3,2,0,1:T(8,128)(2,1)S(1)}, f16[2,2,32,1024]{3,2,0,1:T(8,128)(2,1)S(1)}, u32[]{:S(2)}, u32[]{:S(2)}) %collective-permute-start.3) | collective-permute-done | bytes 262176 | tf_op jit(solution)/shard_map/ppermute | solution.py:62
  21.1 2.9 %collective-permute-done.2 = f16[2,2,32,1024]{3,2,0,1:T(8,128)(2,1)S(1)} collective-permute-done((f16[2,2,32,1024]{3,2,0,1:T(8,128)(2,1)S(1)}, f16[2,2,32,1024]{3,2,0,1:T(8,128)(2,1)S(1)}, u32[]{:S(2)}, u32[]{:S(2)}) %collective-permute-start.2) | collective-permute-done | bytes 262176 | tf_op jit(solution)/shard_map/ppermute | solution.py:62
  24.8 2.7 %collective-permute-start.6 = (f16[2,32,1024]{2,1,0:T(8,128)(2,1)S(1)}, f16[2,32,1024]{2,1,0:T(8,128)(2,1)S(1)}, u32[]{:S(2)}, u32[]{:S(2)}) collective-permute-start(f16[2,32,1024]{2,1,0:T(8,128)(2,1)S(1)} %fusion.16), channel_id=1, source_target_pairs={{0,8},{1,9},{2,10},{3,11},{4,12},{5,13},{6,14},{7,15},{8,0},{9,1},... | collective-permute-start | bytes 393224 | tf_op jit(solution)/shard_map/ppermute | solution.py:62
  27.5 1.6 collective-permute-start.5
  29.2 3.2 %collective-permute-done.6 = f16[2,32,1024]{2,1,0:T(8,128)(2,1)S(1)} collective-permute-done((f16[2,32,1024]{2,1,0:T(8,128)(2,1)S(1)}, f16[2,32,1024]{2,1,0:T(8,128)(2,1)S(1)}, u32[]{:S(2)}, u32[]{:S(2)}) %collective-permute-start.6) | collective-permute-done | bytes 131104 | tf_op jit(solution)/shard_map/ppermute | solution.py:62
  34.7 2.2 %collective-permute-start.8 = (f16[32,1024]{1,0:T(8,128)(2,1)S(1)}, f16[32,1024]{1,0:T(8,128)(2,1)S(1)}, u32[]{:S(2)}, u32[]{:S(2)}) collective-permute-start(f16[32,1024]{1,0:T(8,128)(2,1)S(1)} %fusion.27), channel_id=1, source_target_pairs={{0,8},{1,9},{2,10},{3,11},{4,12},{5,13},{6,14},{7,15},{8,0},{9,1},... | collective-permute-start | bytes 196616 | tf_op jit(solution)/shard_map/ppermute | solution.py:62
  38.5 1.5 collective-permute-done.8
  41.5 2.2 %collective-permute-start.11 = (bf16[1,32,1024]{2,1,0:T(8,128)(2,1)S(1)}, bf16[1,32,1024]{2,1,0:T(8,128)(2,1)S(1)}, u32[]{:S(2)}, u32[]{:S(2)}) collective-permute-start(bf16[1,32,1024]{2,1,0:T(8,128)(2,1)S(1)} %get-tuple-element.122), channel_id=1, source_target_pairs={{0,8},{1,9},{2,10},{3,11},{4,12},{5,13},{6,14},{7,15},{8,0},{9,1},... | collective-permute-start | bytes 196616 | tf_op jit(solution)/shard_map/ppermute | solution.py:62
  45.1 1.8 collective-permute-done.11
  48.1 2.1 %collective-permute-start.13 = (bf16[2,32,1024]{2,1,0:T(8,128)(2,1)S(1)}, bf16[2,32,1024]{2,1,0:T(8,128)(2,1)S(1)}, u32[]{:S(2)}, u32[]{:S(2)}) collective-permute-start(bf16[2,32,1024]{2,1,0:T(8,128)(2,1)S(1)} %pad_maximum_fusion.8), channel_id=1, source_target_pairs={{0,4},{1,5},{2,6},{3,7},{4,0},{5,1},{6,2},{7,3},{8,12},{9,13},{10,... | collective-permute-start | bytes 393224 | tf_op jit(solution)/shard_map/ppermute | solution.py:62
  50.2 3.2 %collective-permute-start.14 = (bf16[2,32,1024]{2,1,0:T(8,128)(2,1)S(1)}, bf16[2,32,1024]{2,1,0:T(8,128)(2,1)S(1)}, u32[]{:S(2)}, u32[]{:S(2)}) collective-permute-start(bf16[2,32,1024]{2,1,0:T(8,128)(2,1)S(1)} %pad_maximum_fusion.9), channel_id=1, source_target_pairs={{0,8},{1,9},{2,10},{3,11},{4,12},{5,13},{6,14},{7,15},{8,0},{9,1},... | collective-permute-start | bytes 393224 | tf_op jit(solution)/shard_map/ppermute | solution.py:62
  53.6 3.3 %collective-permute-done.14 = bf16[2,32,1024]{2,1,0:T(8,128)(2,1)S(1)} collective-permute-done((bf16[2,32,1024]{2,1,0:T(8,128)(2,1)S(1)}, bf16[2,32,1024]{2,1,0:T(8,128)(2,1)S(1)}, u32[]{:S(2)}, u32[]{:S(2)}) %collective-permute-start.14) | collective-permute-done | bytes 131104 | tf_op jit(solution)/shard_map/ppermute | solution.py:62
  56.9 1.5 collective-permute-start.15
  58.4 3.5 %collective-permute-start.16 = (bf16[4,32,1024]{2,1,0:T(8,128)(2,1)S(1)}, bf16[4,32,1024]{2,1,0:T(8,128)(2,1)S(1)}, u32[]{:S(2)}, u32[]{:S(2)}) collective-permute-start(bf16[4,32,1024]{2,1,0:T(8,128)(2,1)S(1)} %pad_maximum_fusion.5), channel_id=1, source_target_pairs={{0,4},{1,5},{2,6},{3,7},{4,0},{5,1},{6,2},{7,3},{8,12},{9,13},{10,... | collective-permute-start | bytes 786440 | tf_op jit(solution)/shard_map/ppermute | solution.py:62
  62.0 4.7 %load.2.refs_4_.refs_5_.refs_0_.refs_1_ = bf16[384,16384]{1,0:T(8,128)(2,1)S(1)} custom-call(bf16[384,16384]{1,0:T(8,128)(2,1)} %acts.5), custom_call_target="tpu_custom_call" | custom-call | bytes 25165824 | tf_op jit(solution)/shard_map/load/pallas_call | solution.py:204
  67.4 3.1 %probe.2 = (f32[384,64]{1,0:T(8,128)S(1)}, f32[64,64]{1,0:T(8,128)S(1)}) custom-call(s32[1]{0:T(128)} %bitcast.me, bf16[8,32,1024]{2,1,0:T(8,128)(2,1)S(1)} %pad_maximum_fusion.refs_0_.refs_2_.refs_4_.refs_6_, bf16[8,32,1024]{2,1,0:T(8,128)(2,1)S(1)} %pad_maximum_fusion.1.refs_1_.refs_3_.refs_5_.refs_7_, ...), custom_call_target="tpu_custom_call" | custom-call | flops 402653184 | bytes 8388608 | tf_op jit(solution)/shard_map/probe/pallas_call | solution.py:254
  70.5 7.0 %probe_and_send.2 = (f32[64,384]{1,0:T(8,128)S(1)}, f32[64,64]{1,0:T(8,128)S(1)}, f32[64,1]{1,0:T(8,128)S(1)}, f32[64,1]{1,0:T(8,128)S(1)}, f32[1,64]{1,0:T(1,12...) custom-call(s32[1]{0:T(128)} %bitcast.me, ...), custom_call_target="tpu_custom_call" | custom-call | flops 402653184 | bytes 8388608 | tf_op jit(solution)/shard_map/probe_and_send/pallas_call | solution.py:343
  78.3 2.3 %panel_keep.3 = f32[8,64,1024]{2,1,0:T(8,128)S(1)} custom-call(s32[1]{0:T(128)} %bitcast.me, f32[64,384]{1,0:T(8,128)S(1)} %get-tuple-element.136.probed.refs_15_, s32[1,384]{1,0:T(1,128)S(1)} %reshape.50.row_data.refs_6_.refs_10_, f32[64,1]{1,0:T(8,128)S(1)} %get-tuple-element.137.inv, bf16[384,16384]{1,0:T(8,128)(2,1)S(1)} %load.2.refs_4_.refs_5_.refs_0_.refs_1_, ...), custom_call_target="tpu_custom_call" | custom-call | flops 402653184 | bytes 8388608 | tf_op jit(solution)/shard_map/panel_keep/pallas_call | solution.py:395
  81.4 1.6 collective-permute-start.22
  83.2 1.9 %collective-permute-start.21 = (f16[2,2,32,1024]{3,2,0,1:T(8,128)(2,1)S(1)}, f16[2,2,32,1024]{3,2,0,1:T(8,128)(2,1)S(1)}, u32[]{:S(2)}, u32[]{:S(2)}) collective-permute-start(f16[2,2,32,1024]{3,2,0,1:T(8,128)(2,1)S(1)} %convert_element_type.156), channel_id=1, source_target_pairs={{0,2},{1,3},{2,0},{3,1},{4,6},{5,7},{6,4},{7,5},{8,10},{9,11},{10,... | collective-permute-start | bytes 786440 | tf_op jit(solution)/shard_map/ppermute | solution.py:62
  85.2 2.2 %collective-permute-done.23 = f32[64,64]{1,0:T(8,128)S(1)} collective-permute-done((f32[64,64]{1,0:T(8,128)S(1)}, f32[64,64]{1,0:T(8,128)S(1)}, u32[]{:S(2)}, u32[]{:S(2)}) %collective-permute-start.23) | collective-permute-done | bytes 16416 | tf_op jit(solution)/shard_map/ppermute | solution.py:62
  87.3 2.5 %collective-permute-done.22 = f16[2,2,32,1024]{3,2,1,0:T(8,128)(2,1)S(1)} collective-permute-done((f16[2,2,32,1024]{3,2,1,0:T(8,128)(2,1)S(1)}, f16[2,2,32,1024]{3,2,1,0:T(8,128)(2,1)S(1)}, u32[]{:S(2)}, u32[]{:S(2)}) %collective-permute-start.22) | collective-permute-done | bytes 262176 | tf_op jit(solution)/shard_map/ppermute | solution.py:62
  89.9 1.9 %collective-permute-done.21 = f16[2,2,32,1024]{3,2,0,1:T(8,128)(2,1)S(1)} collective-permute-done((f16[2,2,32,1024]{3,2,0,1:T(8,128)(2,1)S(1)}, f16[2,2,32,1024]{3,2,0,1:T(8,128)(2,1)S(1)}, u32[]{:S(2)}, u32[]{:S(2)}) %collective-permute-start.21) | collective-permute-done | bytes 262176 | tf_op jit(solution)/shard_map/ppermute | solution.py:62
  93.1 1.4 collective-permute-start.25
  96.7 2.8 %offset.1 = f32[64,1024]{1,0:T(8,128)} custom-call(f32[32,1024]{1,0:T(8,128)} %get-tuple-element.147.base_a, f32[32,1024]{1,0:T(8,128)} %get-tuple-element.148.base_b, f32[64,64]{1,0:T(8,128)} %copy-done, f32[1,1]{1,0:T(1,128)} %bitcast.19.refs_7_.total_weight.refs_11_), custom_call_target="tpu_custom_call" | custom-call | flops 67108864 | bytes 1048576 | tf_op jit(solution)/shard_map/offset/pallas_call | solution.py:453
  99.5 1.7 collective-permute-done.25
  105.0 2.2 %collective-permute-start.27 = (f16[32,1024]{1,0:T(8,128)(2,1)S(1)}, f16[32,1024]{1,0:T(8,128)(2,1)S(1)}, u32[]{:S(2)}, u32[]{:S(2)}) collective-permute-start(f16[32,1024]{1,0:T(8,128)(2,1)S(1)} %convert_element_type.164), channel_id=1, source_target_pairs={{0,8},{1,9},{2,10},{3,11},{4,12},{5,13},{6,14},{7,15},{8,0},{9,1},... | collective-permute-start | bytes 196616 | tf_op jit(solution)/shard_map/ppermute | solution.py:62
  111.1 2.2 %collective-permute-start.30 = (bf16[1,32,1024]{2,1,0:T(8,128)(2,1)S(1)}, bf16[1,32,1024]{2,1,0:T(8,128)(2,1)S(1)}, u32[]{:S(2)}, u32[]{:S(2)}) collective-permute-start(bf16[1,32,1024]{2,1,0:T(8,128)(2,1)S(1)} %get-tuple-element.158), channel_id=1, source_target_pairs={{0,8},{1,9},{2,10},{3,11},{4,12},{5,13},{6,14},{7,15},{8,0},{9,1},... | collective-permute-start | bytes 196616 | tf_op jit(solution)/shard_map/ppermute | solution.py:62
  114.0 2.3 %collective-permute-done.30 = bf16[1,32,1024]{2,1,0:T(8,128)(2,1)S(1)} collective-permute-done((bf16[1,32,1024]{2,1,0:T(8,128)(2,1)S(1)}, bf16[1,32,1024]{2,1,0:T(8,128)(2,1)S(1)}, u32[]{:S(2)}, u32[]{:S(2)}) %collective-permute-start.30) | collective-permute-done | bytes 65568 | tf_op jit(solution)/shard_map/ppermute | solution.py:62
  120.0 4.4 %alpha.1 = (f32[64,64]{1,0:T(8,128)}, f32[64,64]{1,0:T(8,128)}) custom-call(f32[64,64]{1,0:T(8,128)} %add.130.along, f32[64,64]{1,0:T(8,128)} %copy-done, f32[1,1]{1,0:T(1,128)} %bitcast.19.refs_7_.total_weight.refs_11_), custom_call_target="tpu_custom_call" | custom-call | flops 67108864 | bytes 1048576 | tf_op jit(solution)/shard_map/alpha/pallas_call | solution.py:453
  124.4 1.4 collective-permute-done.33
  125.9 1.4 collective-permute-start.34
  127.2 4.7 %load.3.refs_8_.refs_9_.refs_0_.refs_1_ = bf16[384,16384]{1,0:T(8,128)(2,1)S(1)} custom-call(bf16[384,16384]{1,0:T(8,128)(2,1)} %acts.5), custom_call_target="tpu_custom_call" | custom-call | bytes 25165824 | tf_op jit(solution)/shard_map/load/pallas_call | solution.py:204
  134.3 3.4 %probe.3 = (f32[384,64]{1,0:T(8,128)S(1)}, f32[64,64]{1,0:T(8,128)S(1)}, f32[64,64]{1,0:T(8,128)S(1)}) custom-call(s32[1]{0:T(128)} %bitcast.me, bf16[8,32,1024]{2,1,0:T(8,128)(2,1)S(1)} %pad_maximum_fusion.2.refs_0_.refs_2_, bf16[8,32,1024]{2,1,0:T(8,128)(2,1)S(1)} %pad_maximum_fusion.3.refs_1_.refs_3_, ...), custom_call_target="tpu_custom_call" | custom-call | flops 402653184 | bytes 8388608 | tf_op jit(solution)/shard_map/probe/pallas_call | solution.py:254
  137.7 8.3 %probe_and_send.3 = (f32[64,384]{1,0:T(8,128)S(1)}, f32[64,64]{1,0:T(8,128)S(1)}, f32[64,1]{1,0:T(8,128)S(1)}, f32[64,1]{1,0:T(8,128)}, f32[1,64]{1,0:T(1,128)S(...) custom-call(s32[1]{0:T(128)} %bitcast.me, ...), custom_call_target="tpu_custom_call" | custom-call | flops 402653184 | bytes 8388608 | tf_op jit(solution)/shard_map/probe_and_send/pallas_call | solution.py:343
  150.3 1.3 panel_keep.5
  151.7 1.8 %collective-permute-done.40 = f32[64,64]{1,0:T(8,128)S(1)} collective-permute-done((f32[64,64]{1,0:T(8,128)S(1)}, f32[64,64]{1,0:T(8,128)S(1)}, u32[]{:S(2)}, u32[]{:S(2)}) %collective-permute-start.40) | collective-permute-done | bytes 16416 | tf_op jit(solution)/shard_map/ppermute | solution.py:62
  154.9 1.6 collective-permute-start.43
  157.3 5.0 %collective-permute-done.43 = f32[64,64]{1,0:T(8,128)S(1)} collective-permute-done((f32[64,64]{1,0:T(8,128)S(1)}, f32[64,64]{1,0:T(8,128)S(1)}, u32[]{:S(2)}, u32[]{:S(2)}) %collective-permute-start.43) | collective-permute-done | bytes 16416 | tf_op jit(solution)/shard_map/ppermute | solution.py:62
  163.3 1.7 collective-permute-start.45
  166.8 2.6 %before.1 = (f32[64,64]{1,0:T(8,128)}, f32[64,64]{1,0:T(8,128)}) custom-call(f32[64,64]{1,0:T(8,128)} %copy-done, f32[64,64]{1,0:T(8,128)} %copy-done.3, f32[64,64]{1,0:T(8,128)} %copy-done.7, f32[64,64]{1,0:T(8,128)} %copy-done.4, f32[1,1]{1,0:T(1,128)} %bitcast.19.refs_7_.total_weight.refs_11_), custom_call_target="tpu_custom_call" | custom-call | flops 67108864 | bytes 1048576 | tf_op jit(solution)/shard_map/before/pallas_call | solution.py:453
  169.4 2.0 %collective-permute-done.46 = f32[64,64]{1,0:T(8,128)S(1)} collective-permute-done((f32[64,64]{1,0:T(8,128)S(1)}, f32[64,64]{1,0:T(8,128)S(1)}, u32[]{:S(2)}, u32[]{:S(2)}) %collective-permute-start.46) | collective-permute-done | bytes 16416 | tf_op jit(solution)/shard_map/ppermute | solution.py:62
  174.1 5.5 %last.1 = (f32[64,1024]{1,0:T(8,128)}, f32[64,1024]{1,0:T(8,128)}, f32[64,64]{1,0:T(8,128)}) custom-call(f32[64,64]{1,0:T(8,128)} %add.141.along, f32[64,64]{1,0:T(8,128)} %get-tuple-element.204.fixed, f32[64,64]{1,0:T(8,128)} %get-tuple-element.205.cross_t, f32[64,64]{1,0:T(8,128)} %copy-done.3, f32[64,64]{1,0:T(8,128)} %copy-done.4, ...), custom_call_target="tpu_custom_call" | custom-call | flops 67108864 | bytes 1048576 | tf_op jit(solution)/shard_map/last/pallas_call | solution.py:453
  180.8 1.7 subtract_bitcast_fusion
  (185 shorter events, 48.0 us)
Async XLA Ops:
  5.6 4.5 %collective-permute-start = (f16[8,64,1024]{2,1,0:T(8,128)(2,1)S(1)}, f16[8,64,1024]{2,1,0:T(8,128)(2,1)S(1)}, u32[]{:S(2)}, u32[]{:S(2)}) collective-permute-start(f16[8,64,1024]{2,1,0:T(8,128)(2,1)S(1)} %fusion), channel_id=1, source_target_pairs={{0,1},{1,0},{2,3},{3,2},{4,5},{5,4},{6,7},{7,6},{8,9},{9,8},{10,11... | collective-permute-start | bytes 3145736 | tf_op jit(solution)/shard_map/ppermute | solution.py:62
  6.2 3.8 %collective-permute-start.1 = (f32[1,64]{1,0:T(1,128)S(1)}, f32[1,64]{1,0:T(1,128)S(1)}, u32[]{:S(2)}, u32[]{:S(2)}) collective-permute-start(f32[1,64]{1,0:T(1,128)S(1)} %bitcast.156), channel_id=1, source_target_pairs={{0,1},{1,0},{2,3},{3,2},{4,5},{5,4},{6,7},{7,6},{8,9},{9,8},{10,11... | collective-permute-start | bytes 776 | tf_op jit(solution)/shard_map/ppermute | solution.py:62
  11.4 9.6 %collective-permute-start.3 = (f16[2,2,32,1024]{3,2,0,1:T(8,128)(2,1)S(1)}, f16[2,2,32,1024]{3,2,0,1:T(8,128)(2,1)S(1)}, u32[]{:S(2)}, u32[]{:S(2)}) collective-permute-start(f16[2,2,32,1024]{3,2,0,1:T(8,128)(2,1)S(1)} %fusion.6), channel_id=1, source_target_pairs={{0,4},{1,5},{2,6},{3,7},{4,0},{5,1},{6,2},{7,3},{8,12},{9,13},{10,... | collective-permute-start | bytes 786440 | tf_op jit(solution)/shard_map/ppermute | solution.py:62
  14.5 3.5 %collective-permute-start.4 = (f32[1,64]{1,0:T(1,128)S(1)}, f32[1,64]{1,0:T(1,128)S(1)}, u32[]{:S(2)}, u32[]{:S(2)}) collective-permute-start(f32[1,64]{1,0:T(1,128)S(1)} %bitcast_add_fusion), channel_id=1, source_target_pairs={{0,2},{1,3},{2,0},{3,1},{4,6},{5,7},{6,4},{7,5},{8,10},{9,11},{10,... | collective-permute-start | bytes 776 | tf_op jit(solution)/shard_map/ppermute | solution.py:62
  16.2 7.8 %collective-permute-start.2 = (f16[2,2,32,1024]{3,2,0,1:T(8,128)(2,1)S(1)}, f16[2,2,32,1024]{3,2,0,1:T(8,128)(2,1)S(1)}, u32[]{:S(2)}, u32[]{:S(2)}) collective-permute-start(f16[2,2,32,1024]{3,2,0,1:T(8,128)(2,1)S(1)} %fusion.3), channel_id=1, source_target_pairs={{0,2},{1,3},{2,0},{3,1},{4,6},{5,7},{6,4},{7,5},{8,10},{9,11},{10,... | collective-permute-start | bytes 786440 | tf_op jit(solution)/shard_map/ppermute | solution.py:62
  24.1 5.1 %collective-permute-start.7 = (f32[1,64]{1,0:T(1,128)S(1)}, f32[1,64]{1,0:T(1,128)S(1)}, u32[]{:S(2)}, u32[]{:S(2)}) collective-permute-start(f32[1,64]{1,0:T(1,128)S(1)} %add.113), channel_id=1, source_target_pairs={{0,4},{1,5},{2,6},{3,7},{4,0},{5,1},{6,2},{7,3},{8,12},{9,13},{10,... | collective-permute-start | bytes 776 | tf_op jit(solution)/shard_map/ppermute | solution.py:62
  24.8 7.6 %collective-permute-start.6 = (f16[2,32,1024]{2,1,0:T(8,128)(2,1)S(1)}, f16[2,32,1024]{2,1,0:T(8,128)(2,1)S(1)}, u32[]{:S(2)}, u32[]{:S(2)}) collective-permute-start(f16[2,32,1024]{2,1,0:T(8,128)(2,1)S(1)} %fusion.16), channel_id=1, source_target_pairs={{0,8},{1,9},{2,10},{3,11},{4,12},{5,13},{6,14},{7,15},{8,0},{9,1},... | collective-permute-start | bytes 393224 | tf_op jit(solution)/shard_map/ppermute | solution.py:62
  27.5 5.3 %collective-permute-start.5 = (f16[2,32,1024]{2,1,0:T(8,128)(2,1)S(1)}, f16[2,32,1024]{2,1,0:T(8,128)(2,1)S(1)}, u32[]{:S(2)}, u32[]{:S(2)}) collective-permute-start(f16[2,32,1024]{2,1,0:T(8,128)(2,1)S(1)} %fusion.13), channel_id=1, source_target_pairs={{0,4},{1,5},{2,6},{3,7},{4,0},{5,1},{6,2},{7,3},{8,12},{9,13},{10,... | collective-permute-start | bytes 393224 | tf_op jit(solution)/shard_map/ppermute | solution.py:62
  32.9 4.6 %collective-permute-start.10 = (f32[1,64]{1,0:T(1,128)S(1)}, f32[1,64]{1,0:T(1,128)S(1)}, u32[]{:S(2)}, u32[]{:S(2)}) collective-permute-start(f32[1,64]{1,0:T(1,128)S(1)} %add.116), channel_id=1, source_target_pairs={{0,8},{1,9},{2,10},{3,11},{4,12},{5,13},{6,14},{7,15},{8,0},{9,1},... | collective-permute-start | bytes 776 | tf_op jit(solution)/shard_map/ppermute | solution.py:62
  34.1 4.3 %collective-permute-start.9 = (f16[32,1024]{1,0:T(8,128)(2,1)S(1)}, f16[32,1024]{1,0:T(8,128)(2,1)S(1)}, u32[]{:S(2)}, u32[]{:S(2)}) collective-permute-start(f16[32,1024]{1,0:T(8,128)(2,1)S(1)} %fusion.30), channel_id=1, source_target_pairs={{0,2},{1,3},{2,0},{3,1},{4,6},{5,7},{6,4},{7,5},{8,10},{9,11},{10,... | collective-permute-start | bytes 196616 | tf_op jit(solution)/shard_map/ppermute | solution.py:62
  34.7 5.2 %collective-permute-start.8 = (f16[32,1024]{1,0:T(8,128)(2,1)S(1)}, f16[32,1024]{1,0:T(8,128)(2,1)S(1)}, u32[]{:S(2)}, u32[]{:S(2)}) collective-permute-start(f16[32,1024]{1,0:T(8,128)(2,1)S(1)} %fusion.27), channel_id=1, source_target_pairs={{0,8},{1,9},{2,10},{3,11},{4,12},{5,13},{6,14},{7,15},{8,0},{9,1},... | collective-permute-start | bytes 196616 | tf_op jit(solution)/shard_map/ppermute | solution.py:62
  41.5 5.3 %collective-permute-start.11 = (bf16[1,32,1024]{2,1,0:T(8,128)(2,1)S(1)}, bf16[1,32,1024]{2,1,0:T(8,128)(2,1)S(1)}, u32[]{:S(2)}, u32[]{:S(2)}) collective-permute-start(bf16[1,32,1024]{2,1,0:T(8,128)(2,1)S(1)} %get-tuple-element.122), channel_id=1, source_target_pairs={{0,8},{1,9},{2,10},{3,11},{4,12},{5,13},{6,14},{7,15},{8,0},{9,1},... | collective-permute-start | bytes 196616 | tf_op jit(solution)/shard_map/ppermute | solution.py:62
  43.8 4.3 %collective-permute-start.12 = (bf16[1,32,1024]{2,1,0:T(8,128)(2,1)S(1)}, bf16[1,32,1024]{2,1,0:T(8,128)(2,1)S(1)}, u32[]{:S(2)}, u32[]{:S(2)}) collective-permute-start(bf16[1,32,1024]{2,1,0:T(8,128)(2,1)S(1)} %get-tuple-element.123), channel_id=1, source_target_pairs={{0,2},{1,3},{2,0},{3,1},{4,6},{5,7},{6,4},{7,5},{8,10},{9,11},{10,... | collective-permute-start | bytes 196616 | tf_op jit(solution)/shard_map/ppermute | solution.py:62
  48.1 5.6 %collective-permute-start.13 = (bf16[2,32,1024]{2,1,0:T(8,128)(2,1)S(1)}, bf16[2,32,1024]{2,1,0:T(8,128)(2,1)S(1)}, u32[]{:S(2)}, u32[]{:S(2)}) collective-permute-start(bf16[2,32,1024]{2,1,0:T(8,128)(2,1)S(1)} %pad_maximum_fusion.8), channel_id=1, source_target_pairs={{0,4},{1,5},{2,6},{3,7},{4,0},{5,1},{6,2},{7,3},{8,12},{9,13},{10,... | collective-permute-start | bytes 393224 | tf_op jit(solution)/shard_map/ppermute | solution.py:62
  50.2 6.7 %collective-permute-start.14 = (bf16[2,32,1024]{2,1,0:T(8,128)(2,1)S(1)}, bf16[2,32,1024]{2,1,0:T(8,128)(2,1)S(1)}, u32[]{:S(2)}, u32[]{:S(2)}) collective-permute-start(bf16[2,32,1024]{2,1,0:T(8,128)(2,1)S(1)} %pad_maximum_fusion.9), channel_id=1, source_target_pairs={{0,8},{1,9},{2,10},{3,11},{4,12},{5,13},{6,14},{7,15},{8,0},{9,1},... | collective-permute-start | bytes 393224 | tf_op jit(solution)/shard_map/ppermute | solution.py:62
  56.9 9.8 %collective-permute-start.15 = (bf16[4,32,1024]{2,1,0:T(8,128)(2,1)S(1)}, bf16[4,32,1024]{2,1,0:T(8,128)(2,1)S(1)}, u32[]{:S(2)}, u32[]{:S(2)}) collective-permute-start(bf16[4,32,1024]{2,1,0:T(8,128)(2,1)S(1)} %pad_maximum_fusion.4), channel_id=1, source_target_pairs={{0,2},{1,3},{2,0},{3,1},{4,6},{5,7},{6,4},{7,5},{8,10},{9,11},{10,... | collective-permute-start | bytes 786440 | tf_op jit(solution)/shard_map/ppermute | solution.py:62
  58.4 8.3 %collective-permute-start.16 = (bf16[4,32,1024]{2,1,0:T(8,128)(2,1)S(1)}, bf16[4,32,1024]{2,1,0:T(8,128)(2,1)S(1)}, u32[]{:S(2)}, u32[]{:S(2)}) collective-permute-start(bf16[4,32,1024]{2,1,0:T(8,128)(2,1)S(1)} %pad_maximum_fusion.5), channel_id=1, source_target_pairs={{0,4},{1,5},{2,6},{3,7},{4,0},{5,1},{6,2},{7,3},{8,12},{9,13},{10,... | collective-permute-start | bytes 786440 | tf_op jit(solution)/shard_map/ppermute | solution.py:62
  66.8 3.7 %collective-permute-start.17 = (bf16[8,32,1024]{2,1,0:T(8,128)(2,1)S(1)}, bf16[8,32,1024]{2,1,0:T(8,128)(2,1)S(1)}, u32[]{:S(2)}, u32[]{:S(2)}) collective-permute-start(bf16[8,32,1024]{2,1,0:T(8,128)(2,1)S(1)} %pad_maximum_fusion.refs_0_.refs_2_.refs_4_.refs_6_), channel_id=1, source_target_pairs={{0,1},{1,0},{2,3},{3,2},{4,5},{5,4},{6,7},{7,6},{8,9},{9,8},{10,11... | collective-permute-start | bytes 1572872 | tf_op jit(solution)/shard_map/ppermute | solution.py:62
  66.9 3.6 %collective-permute-start.18 = (bf16[8,32,1024]{2,1,0:T(8,128)(2,1)S(1)}, bf16[8,32,1024]{2,1,0:T(8,128)(2,1)S(1)}, u32[]{:S(2)}, u32[]{:S(2)}) collective-permute-start(bf16[8,32,1024]{2,1,0:T(8,128)(2,1)S(1)} %pad_maximum_fusion.1.refs_1_.refs_3_.refs_5_.refs_7_), channel_id=1, source_target_pairs={{0,1},{1,0},{2,3},{3,2},{4,5},{5,4},{6,7},{7,6},{8,9},{9,8},{10,11... | collective-permute-start | bytes 1572872 | tf_op jit(solution)/shard_map/ppermute | solution.py:62
  77.7 3.0 %collective-permute-start.19 = (f16[8,64,1024]{2,1,0:T(8,128)(2,1)S(1)}, f16[8,64,1024]{2,1,0:T(8,128)(2,1)S(1)}, u32[]{:S(2)}, u32[]{:S(2)}) collective-permute-start(f16[8,64,1024]{2,1,0:T(8,128)(2,1)S(1)} %convert_element_type.154), channel_id=1, source_target_pairs={{0,1},{1,0},{2,3},{3,2},{4,5},{5,4},{6,7},{7,6},{8,9},{9,8},{10,11... | collective-permute-start | bytes 3145736 | tf_op jit(solution)/shard_map/ppermute | solution.py:62
  77.9 2.8 %collective-permute-start.20 = (f32[64,64]{1,0:T(8,128)S(1)}, f32[64,64]{1,0:T(8,128)S(1)}, u32[]{:S(2)}, u32[]{:S(2)}) collective-permute-start(f32[64,64]{1,0:T(8,128)S(1)} %get-tuple-element.139), channel_id=1, source_target_pairs={{0,1},{1,0},{2,3},{3,2},{4,5},{5,4},{6,7},{7,6},{8,9},{9,8},{10,11... | collective-permute-start | bytes 49160 | tf_op jit(solution)/shard_map/ppermute | solution.py:62
  81.4 8.4 %collective-permute-start.22 = (f16[2,2,32,1024]{3,2,1,0:T(8,128)(2,1)S(1)}, f16[2,2,32,1024]{3,2,1,0:T(8,128)(2,1)S(1)}, u32[]{:S(2)}, u32[]{:S(2)}) collective-permute-start(f16[2,2,32,1024]{3,2,1,0:T(8,128)(2,1)S(1)} %convert_element_type.158), channel_id=1, source_target_pairs={{0,4},{1,5},{2,6},{3,7},{4,0},{5,1},{6,2},{7,3},{8,12},{9,13},{10,... | collective-permute-start | bytes 786440 | tf_op jit(solution)/shard_map/ppermute | solution.py:62
  83.0 4.3 %collective-permute-start.23 = (f32[64,64]{1,0:T(8,128)S(1)}, f32[64,64]{1,0:T(8,128)S(1)}, u32[]{:S(2)}, u32[]{:S(2)}) collective-permute-start(f32[64,64]{1,0:T(8,128)S(1)} %add.121), channel_id=1, source_target_pairs={{0,2},{1,3},{2,0},{3,1},{4,6},{5,7},{6,4},{7,5},{8,10},{9,11},{10,... | collective-permute-start | bytes 49160 | tf_op jit(solution)/shard_map/ppermute | solution.py:62
  83.2 8.5 %collective-permute-start.21 = (f16[2,2,32,1024]{3,2,0,1:T(8,128)(2,1)S(1)}, f16[2,2,32,1024]{3,2,0,1:T(8,128)(2,1)S(1)}, u32[]{:S(2)}, u32[]{:S(2)}) collective-permute-start(f16[2,2,32,1024]{3,2,0,1:T(8,128)(2,1)S(1)} %convert_element_type.156), channel_id=1, source_target_pairs={{0,2},{1,3},{2,0},{3,1},{4,6},{5,7},{6,4},{7,5},{8,10},{9,11},{10,... | collective-permute-start | bytes 786440 | tf_op jit(solution)/shard_map/ppermute | solution.py:62
  91.9 7.6 %collective-permute-start.26 = (f32[64,64]{1,0:T(8,128)S(1)}, f32[64,64]{1,0:T(8,128)S(1)}, u32[]{:S(2)}, u32[]{:S(2)}) collective-permute-start(f32[64,64]{1,0:T(8,128)S(1)} %add.124), channel_id=1, source_target_pairs={{0,4},{1,5},{2,6},{3,7},{4,0},{5,1},{6,2},{7,3},{8,12},{9,13},{10,... | collective-permute-start | bytes 49160 | tf_op jit(solution)/shard_map/ppermute | solution.py:62
  93.1 8.1 %collective-permute-start.25 = (f16[2,32,1024]{2,1,0:T(8,128)(2,1)}, f16[2,32,1024]{2,1,0:T(8,128)(2,1)S(1)}, u32[]{:S(2)}, u32[]{:S(2)}) collective-permute-start(f16[2,32,1024]{2,1,0:T(8,128)(2,1)} %convert_element_type.162), channel_id=1, source_target_pairs={{0,8},{1,9},{2,10},{3,11},{4,12},{5,13},{6,14},{7,15},{8,0},{9,1},... | collective-permute-start | bytes 393224 | tf_op jit(solution)/shard_map/ppermute | solution.py:62
  95.9 5.8 %collective-permute-start.24 = (f16[2,32,1024]{2,1,0:T(8,128)(2,1)}, f16[2,32,1024]{2,1,0:T(8,128)(2,1)}, u32[]{:S(2)}, u32[]{:S(2)}) collective-permute-start(f16[2,32,1024]{2,1,0:T(8,128)(2,1)} %convert_element_type.160), channel_id=1, source_target_pairs={{0,4},{1,5},{2,6},{3,7},{4,0},{5,1},{6,2},{7,3},{8,12},{9,13},{10,... | collective-permute-start | bytes 393224 | tf_op jit(solution)/shard_map/ppermute | solution.py:62
  102.7 5.8 %collective-permute-start.29 = (f32[64,64]{1,0:T(8,128)S(1)}, f32[64,64]{1,0:T(8,128)S(1)}, u32[]{:S(2)}, u32[]{:S(2)}) collective-permute-start(f32[64,64]{1,0:T(8,128)S(1)} %add.127), channel_id=1, source_target_pairs={{0,8},{1,9},{2,10},{3,11},{4,12},{5,13},{6,14},{7,15},{8,0},{9,1},... | collective-permute-start | bytes 49160 | tf_op jit(solution)/shard_map/ppermute | solution.py:62
  103.9 5.2 %collective-permute-start.28 = (f16[32,1024]{1,0:T(8,128)(2,1)S(1)}, f16[32,1024]{1,0:T(8,128)(2,1)S(1)}, u32[]{:S(2)}, u32[]{:S(2)}) collective-permute-start(f16[32,1024]{1,0:T(8,128)(2,1)S(1)} %convert_element_type.166), channel_id=1, source_target_pairs={{0,2},{1,3},{2,0},{3,1},{4,6},{5,7},{6,4},{7,5},{8,10},{9,11},{10,... | collective-permute-start | bytes 196616 | tf_op jit(solution)/shard_map/ppermute | solution.py:62
  105.0 5.2 %collective-permute-start.27 = (f16[32,1024]{1,0:T(8,128)(2,1)S(1)}, f16[32,1024]{1,0:T(8,128)(2,1)S(1)}, u32[]{:S(2)}, u32[]{:S(2)}) collective-permute-start(f16[32,1024]{1,0:T(8,128)(2,1)S(1)} %convert_element_type.164), channel_id=1, source_target_pairs={{0,8},{1,9},{2,10},{3,11},{4,12},{5,13},{6,14},{7,15},{8,0},{9,1},... | collective-permute-start | bytes 196616 | tf_op jit(solution)/shard_map/ppermute | solution.py:62
  111.1 5.2 %collective-permute-start.30 = (bf16[1,32,1024]{2,1,0:T(8,128)(2,1)S(1)}, bf16[1,32,1024]{2,1,0:T(8,128)(2,1)S(1)}, u32[]{:S(2)}, u32[]{:S(2)}) collective-permute-start(bf16[1,32,1024]{2,1,0:T(8,128)(2,1)S(1)} %get-tuple-element.158), channel_id=1, source_target_pairs={{0,8},{1,9},{2,10},{3,11},{4,12},{5,13},{6,14},{7,15},{8,0},{9,1},... | collective-permute-start | bytes 196616 | tf_op jit(solution)/shard_map/ppermute | solution.py:62
  113.3 4.3 %collective-permute-start.31 = (bf16[1,32,1024]{2,1,0:T(8,128)(2,1)S(1)}, bf16[1,32,1024]{2,1,0:T(8,128)(2,1)S(1)}, u32[]{:S(2)}, u32[]{:S(2)}) collective-permute-start(bf16[1,32,1024]{2,1,0:T(8,128)(2,1)S(1)} %get-tuple-element.159), channel_id=1, source_target_pairs={{0,2},{1,3},{2,0},{3,1},{4,6},{5,7},{6,4},{7,5},{8,10},{9,11},{10,... | collective-permute-start | bytes 196616 | tf_op jit(solution)/shard_map/ppermute | solution.py:62
  117.6 6.8 %collective-permute-start.32 = (bf16[2,32,1024]{2,1,0:T(8,128)(2,1)S(1)}, bf16[2,32,1024]{2,1,0:T(8,128)(2,1)S(1)}, u32[]{:S(2)}, u32[]{:S(2)}) collective-permute-start(bf16[2,32,1024]{2,1,0:T(8,128)(2,1)S(1)} %pad_maximum_fusion.10), channel_id=1, source_target_pairs={{0,4},{1,5},{2,6},{3,7},{4,0},{5,1},{6,2},{7,3},{8,12},{9,13},{10,... | collective-permute-start | bytes 393224 | tf_op jit(solution)/shard_map/ppermute | solution.py:62
  118.7 7.2 %collective-permute-start.33 = (bf16[2,32,1024]{2,1,0:T(8,128)(2,1)S(1)}, bf16[2,32,1024]{2,1,0:T(8,128)(2,1)S(1)}, u32[]{:S(2)}, u32[]{:S(2)}) collective-permute-start(bf16[2,32,1024]{2,1,0:T(8,128)(2,1)S(1)} %pad_maximum_fusion.11), channel_id=1, source_target_pairs={{0,8},{1,9},{2,10},{3,11},{4,12},{5,13},{6,14},{7,15},{8,0},{9,1},... | collective-permute-start | bytes 393224 | tf_op jit(solution)/shard_map/ppermute | solution.py:62
  125.9 6.4 %collective-permute-start.34 = (bf16[4,32,1024]{2,1,0:T(8,128)(2,1)S(1)}, bf16[4,32,1024]{2,1,0:T(8,128)(2,1)S(1)}, u32[]{:S(2)}, u32[]{:S(2)}) collective-permute-start(bf16[4,32,1024]{2,1,0:T(8,128)(2,1)S(1)} %pad_maximum_fusion.6), channel_id=1, source_target_pairs={{0,2},{1,3},{2,0},{3,1},{4,6},{5,7},{6,4},{7,5},{8,10},{9,11},{10,... | collective-permute-start | bytes 786440 | tf_op jit(solution)/shard_map/ppermute | solution.py:62
  127.2 6.4 %collective-permute-start.35 = (bf16[4,32,1024]{2,1,0:T(8,128)(2,1)S(1)}, bf16[4,32,1024]{2,1,0:T(8,128)(2,1)S(1)}, u32[]{:S(2)}, u32[]{:S(2)}) collective-permute-start(bf16[4,32,1024]{2,1,0:T(8,128)(2,1)S(1)} %pad_maximum_fusion.7), channel_id=1, source_target_pairs={{0,4},{1,5},{2,6},{3,7},{4,0},{5,1},{6,2},{7,3},{8,12},{9,13},{10,... | collective-permute-start | bytes 786440 | tf_op jit(solution)/shard_map/ppermute | solution.py:62
  133.7 4.0 %collective-permute-start.36 = (bf16[8,32,1024]{2,1,0:T(8,128)(2,1)S(1)}, bf16[8,32,1024]{2,1,0:T(8,128)(2,1)S(1)}, u32[]{:S(2)}, u32[]{:S(2)}) collective-permute-start(bf16[8,32,1024]{2,1,0:T(8,128)(2,1)S(1)} %pad_maximum_fusion.2.refs_0_.refs_2_), channel_id=1, source_target_pairs={{0,1},{1,0},{2,3},{3,2},{4,5},{5,4},{6,7},{7,6},{8,9},{9,8},{10,11... | collective-permute-start | bytes 1572872 | tf_op jit(solution)/shard_map/ppermute | solution.py:62
  133.8 3.9 %collective-permute-start.37 = (bf16[8,32,1024]{2,1,0:T(8,128)(2,1)S(1)}, bf16[8,32,1024]{2,1,0:T(8,128)(2,1)S(1)}, u32[]{:S(2)}, u32[]{:S(2)}) collective-permute-start(bf16[8,32,1024]{2,1,0:T(8,128)(2,1)S(1)} %pad_maximum_fusion.3.refs_1_.refs_3_), channel_id=1, source_target_pairs={{0,1},{1,0},{2,3},{3,2},{4,5},{5,4},{6,7},{7,6},{8,9},{9,8},{10,11... | collective-permute-start | bytes 1572872 | tf_op jit(solution)/shard_map/ppermute | solution.py:62
  146.8 6.7 %collective-permute-start.39 = (f16[8,64,1024]{2,1,0:T(8,128)(2,1)S(1)}, f16[8,64,1024]{2,1,0:T(8,128)(2,1)S(1)}, u32[]{:S(2)}, u32[]{:S(2)}) collective-permute-start(f16[8,64,1024]{2,1,0:T(8,128)(2,1)S(1)} %convert_element_type.170), channel_id=1, source_target_pairs={{0,1},{1,0},{2,3},{3,2},{4,5},{5,4},{6,7},{7,6},{8,9},{9,8},{10,11... | collective-permute-start | bytes 3145736 | tf_op jit(solution)/shard_map/ppermute | solution.py:62
  149.6 3.9 %collective-permute-start.40 = (f32[64,64]{1,0:T(8,128)S(1)}, f32[64,64]{1,0:T(8,128)S(1)}, u32[]{:S(2)}, u32[]{:S(2)}) collective-permute-start(f32[64,64]{1,0:T(8,128)S(1)} %add.133), channel_id=1, source_target_pairs={{0,2},{1,3},{2,0},{3,1},{4,6},{5,7},{6,4},{7,5},{8,10},{9,11},{10,... | collective-permute-start | bytes 49160 | tf_op jit(solution)/shard_map/ppermute | solution.py:62
  154.4 8.0 %collective-permute-start.42 = (f16[2,2,32,1024]{3,2,1,0:T(8,128)(2,1)S(1)}, f16[2,2,32,1024]{3,2,1,0:T(8,128)(2,1)S(1)}, u32[]{:S(2)}, u32[]{:S(2)}) collective-permute-start(f16[2,2,32,1024]{3,2,1,0:T(8,128)(2,1)S(1)} %convert_element_type.174), channel_id=1, source_target_pairs={{0,4},{1,5},{2,6},{3,7},{4,0},{5,1},{6,2},{7,3},{8,12},{9,13},{10,... | collective-permute-start | bytes 786440 | tf_op jit(solution)/shard_map/ppermute | solution.py:62
  154.9 7.5 %collective-permute-start.43 = (f32[64,64]{1,0:T(8,128)S(1)}, f32[64,64]{1,0:T(8,128)S(1)}, u32[]{:S(2)}, u32[]{:S(2)}) collective-permute-start(f32[64,64]{1,0:T(8,128)S(1)} %add.135), channel_id=1, source_target_pairs={{0,4},{1,5},{2,6},{3,7},{4,0},{5,1},{6,2},{7,3},{8,12},{9,13},{10,... | collective-permute-start | bytes 49160 | tf_op jit(solution)/shard_map/ppermute | solution.py:62
  156.5 6.7 %collective-permute-start.41 = (f16[2,2,32,1024]{3,2,0,1:T(8,128)(2,1)S(1)}, f16[2,2,32,1024]{3,2,0,1:T(8,128)(2,1)S(1)}, u32[]{:S(2)}, u32[]{:S(2)}) collective-permute-start(f16[2,2,32,1024]{3,2,0,1:T(8,128)(2,1)S(1)} %convert_element_type.172), channel_id=1, source_target_pairs={{0,2},{1,3},{2,0},{3,1},{4,6},{5,7},{6,4},{7,5},{8,10},{9,11},{10,... | collective-permute-start | bytes 786440 | tf_op jit(solution)/shard_map/ppermute | solution.py:62
  163.3 8.7 %collective-permute-start.45 = (f16[2,32,1024]{2,1,0:T(8,128)(2,1)S(1)}, f16[2,32,1024]{2,1,0:T(8,128)(2,1)S(1)}, u32[]{:S(2)}, u32[]{:S(2)}) collective-permute-start(f16[2,32,1024]{2,1,0:T(8,128)(2,1)S(1)} %convert_element_type.178), channel_id=1, source_target_pairs={{0,8},{1,9},{2,10},{3,11},{4,12},{5,13},{6,14},{7,15},{8,0},{9,1},... | collective-permute-start | bytes 393224 | tf_op jit(solution)/shard_map/ppermute | solution.py:62
  165.1 6.4 %collective-permute-start.46 = (f32[64,64]{1,0:T(8,128)S(1)}, f32[64,64]{1,0:T(8,128)S(1)}, u32[]{:S(2)}, u32[]{:S(2)}) collective-permute-start(f32[64,64]{1,0:T(8,128)S(1)} %add.138), channel_id=1, source_target_pairs={{0,8},{1,9},{2,10},{3,11},{4,12},{5,13},{6,14},{7,15},{8,0},{9,1},... | collective-permute-start | bytes 49160 | tf_op jit(solution)/shard_map/ppermute | solution.py:62
  166.3 6.2 %collective-permute-start.44 = (f16[2,32,1024]{2,1,0:T(8,128)(2,1)S(1)}, f16[2,32,1024]{2,1,0:T(8,128)(2,1)S(1)}, u32[]{:S(2)}, u32[]{:S(2)}) collective-permute-start(f16[2,32,1024]{2,1,0:T(8,128)(2,1)S(1)} %convert_element_type.176), channel_id=1, source_target_pairs={{0,4},{1,5},{2,6},{3,7},{4,0},{5,1},{6,2},{7,3},{8,12},{9,13},{10,... | collective-permute-start | bytes 393224 | tf_op jit(solution)/shard_map/ppermute | solution.py:62
  172.6 7.1 %collective-permute-start.48 = (f16[32,1024]{1,0:T(8,128)(2,1)S(1)}, f16[32,1024]{1,0:T(8,128)(2,1)S(1)}, u32[]{:S(2)}, u32[]{:S(2)}) collective-permute-start(f16[32,1024]{1,0:T(8,128)(2,1)S(1)} %convert_element_type.182), channel_id=1, source_target_pairs={{0,2},{1,3},{2,0},{3,1},{4,6},{5,7},{6,4},{7,5},{8,10},{9,11},{10,... | collective-permute-start | bytes 196616 | tf_op jit(solution)/shard_map/ppermute | solution.py:62
  173.3 6.3 %collective-permute-start.47 = (f16[32,1024]{1,0:T(8,128)(2,1)S(1)}, f16[32,1024]{1,0:T(8,128)(2,1)S(1)}, u32[]{:S(2)}, u32[]{:S(2)}) collective-permute-start(f16[32,1024]{1,0:T(8,128)(2,1)S(1)} %convert_element_type.180), channel_id=1, source_target_pairs={{0,8},{1,9},{2,10},{3,11},{4,12},{5,13},{6,14},{7,15},{8,0},{9,1},... | collective-permute-start | bytes 196616 | tf_op jit(solution)/shard_map/ppermute | solution.py:62
  (10 other events, 34.9 us)

commit v10 on v9

--- a/solution.py
+++ b/solution.py
@@ -62,6 +62,10 @@
     return lax.ppermute(value, "dp", [(i, i ^ bit) for i in range(n)])
 
 
+def quad(value, n):
+    return (value + swap(value, 1, n)) + (swap(value, 2, n) + swap(value, 3, n))
+
+
 def hop_bits(n):
     bits = [1 << i for i in range(1, n.bit_length() - 1)]
     return bits, bits[1:] + bits[:1]
@@ -95,7 +99,7 @@
 HBM = pl.BlockSpec(memory_space=pltpu.HBM)
 
 
-def call(kernel, name, n, grid, in_specs, out_shapes, out_specs, acts, scratch=(), aliases=None):
+def call(kernel, name, n, grid, in_specs, out_shapes, out_specs, acts, scratch=()):
     rows, d = acts.shape
     return pl.pallas_call(
         kernel,
@@ -113,7 +117,6 @@
         ),
         compiler_params=pltpu.CompilerParams(vmem_limit_bytes=20 << 20),
         cost_estimate=pl.CostEstimate(flops=K * rows * d, bytes_accessed=rows * d + 2 * K * d, transcendentals=0),
-        input_output_aliases=aliases or {},
         name=name,
     )
 
@@ -213,7 +216,7 @@
     )(acts)
 
 
-def near_call(kernel, name, n, grid, in_specs, out_shapes, out_specs, acts, scratch=(), aliases=None):
+def near_call(kernel, name, n, grid, in_specs, out_shapes, out_specs, acts, scratch=()):
     rows, d = acts.shape
     return pl.pallas_call(
         kernel,
@@ -223,7 +226,6 @@
         ),
         compiler_params=pltpu.CompilerParams(vmem_limit_bytes=12 << 20),
         cost_estimate=pl.CostEstimate(flops=K * rows * d, bytes_accessed=rows * d + 2 * K * d, transcendentals=0),
-        input_output_aliases=aliases or {},
         name=name,
     )
 
@@ -383,29 +385,20 @@
         out[u] = jnp.dot(weighted[...], acts[u][...], preferred_element_type=F32) * inv[...]
 
 
-def panel_keep(me, probed, row_data, inv, acts, n, part=None, into=None):
+def panel_keep(me, probed, row_data, inv, acts, n):
     rows, d = acts.shape
     f = d // n
-    steps = n // 2 // UNROLL
-    first = 0
-    if part is not None:
-        steps //= 2
-        first = part * steps
-    more = () if into is None else (into,)
     return near_call(
         keep_kernel,
         "panel_keep",
         n,
-        steps,
-        [whole(K, rows), whole(1, rows), whole(K, 1)]
-        + act_specs(rows, f, 0, lambda i: (i + first) * UNROLL)
-        + [pl.BlockSpec(memory_space=pl.ANY)] * len(more),
+        n // 2 // UNROLL,
+        [whole(K, rows), whole(1, rows), whole(K, 1)] + act_specs(rows, f, 0, lambda i: i * UNROLL),
         jax.ShapeDtypeStruct((n // 2, K, f), F32),
-        pl.BlockSpec((UNROLL, K, f), lambda i, me: (i + first, 0, 0)),
+        pl.BlockSpec((UNROLL, K, f), lambda i, me: (i, 0, 0)),
         acts,
         [pltpu.VMEM((K, rows), BF16)],
-        {4 + UNROLL: 0} if more else {},
-    )(me, probed, row_data, inv, *[acts] * UNROLL, *more)
+    )(me, probed, row_data, inv, *[acts] * UNROLL)
 
 
 def alpha_kernel(along, current, total_weight, alpha_t, inverse):
@@ -467,7 +460,7 @@
     return keep, send, [other for other in left if other != bit]
 
 
-def reduce_scatter(blocks, n, swap_a, swap_b, along, waiting, work=None, args=(), along_ends=True):
+def reduce_scatter(blocks, n, swap_a, swap_b, along, waiting, work=None, args=()):
     bits = n.bit_length() - 2
     shape = (2,) * bits + (HALF, blocks.shape[2])
     a, b = blocks[:, :HALF].reshape(shape), blocks[:, HALF:].reshape(shape)
@@ -484,8 +477,6 @@
             along = along + swap(along, waiting.pop(0), n)
         if work is not None and phase >= 1:
             done = work(*tied) if phase == 1 else tied
-    if along_ends:
-        a, b, along = lax.optimization_barrier((a, b, along))
     return a, b, along, done
 
 
@@ -526,28 +517,20 @@
     sent, weight = class_sums(me, row_data, activations, n, 1)
     weight = weight.T
     got = root(sent, 1)
-    weight = weight + swap(weight, 1, n)
+    weight = quad(weight, n)
     kept, _ = class_sums(me, row_data, activations, n, 0)
-    top, low, weight, _ = reduce_scatter(kept + got, n, root, root, weight, order_y)
+    top, low, weight, _ = reduce_scatter(kept + got, n, root, root, weight, order_y[1:])
     class_weight = weight.T
     total_weight = jnp.sum(class_weight, keepdims=True)
     factor = 1.0 / jnp.sqrt(class_weight)
     base = top * factor[:HALF], low * factor[HALF:]
 
-    def scatter(close, probed, along, inv, sent, early, work, args):
+    def scatter(close, probed, along, inv, sent, work, args):
         hop = plain(n)
         got = hop(sent, 1)
-        along = along + swap(along, 1, n)
-        waiting = order_y
-        if early:
-            kept = panel_keep(me, probed, row_data, inv, close, n, 0)
-            kept, along = lax.optimization_barrier((kept, along))
-            along = along + swap(along, waiting[0], n)
-            kept = panel_keep(me, probed, row_data, inv, close, n, 1, kept)
-            waiting = waiting[1:]
-        else:
-            kept = panel_keep(me, probed, row_data, inv, close, n)
-        return reduce_scatter(kept + got, n, hop, hop, along, waiting, work, args, not early)
+        along = quad(along, n)
+        kept = panel_keep(me, probed, row_data, inv, close, n)
+        return reduce_scatter(kept + got, n, hop, hop, along, order_y[1:], work, args)
 
     square, strip = (K, K), (K, d // n)
     orders = order_a, order_b
@@ -557,7 +540,7 @@
         me, (base_far,), close, row_data, total_weight, starts, (), n, shifts
     )
     panel_a, panel_b, along, (offset,) = scatter(
-        close, first, along, inv, sent, False,
+        close, first, along, inv, sent,
         lambda *args: small(offset_kernel, "offset", (strip,), *args), (*base, current, total_weight),
     )
     back = back / total_weight
@@ -572,7 +555,7 @@
         me, (far, base_far), close, row_data, total_weight, starts, (first, current, alpha_t, inverse), n, shifts
     )
     panel_a, panel_b, along, (fixed, cross_t) = scatter(
-        close, probed, along, inv, sent, True,
+        close, probed, along, inv, sent,
         lambda *args: small(before_kernel, "before", (square,) * 2, *args),
         (current, renewed, mixed, beta_t, total_weight),
     )
@@ -580,7 +563,7 @@
         last_kernel, "last", (strip, strip, square),
         along, fixed, cross_t, renewed, beta_t, alpha_t, total_weight, back_row, *base, *image,
     )
-    residual = rest - precise(on_panel, jnp.concatenate([panel_a, panel_b], axis=0))
+    residual = (rest - precise(on_panel[:, HALF:], panel_b)) - precise(on_panel[:, :HALF], panel_a)
     return (solved.T, residual.T)
 
 

time: 183 us -> 189 us (1.033)
  waiting for transfers between devices: 48.8 us -> 56 us
  matrix products: 1.12 us -> 3.21 us
    ppermute x49 -> x52, waiting for transfers between devices: 48.8 us -> 56 us  [swap(): return lax.ppermute(value, 'dp', [(i, i ^ bit) for i in range(n)])]
    dot_general x1 -> x2, matrix products: 1.12 us -> 3.21 us  [precise(): jnp.dot(left, right, precision=lax.Precision.HIGHEST, preferred_element_t...]
    ppermute x49 -> x52, starting transfers between devices: 56.8 us -> 55.6 us  [swap(): return lax.ppermute(value, 'dp', [(i, i ^ bit) for i in range(n)])]
    pallas_call x3 -> x2, Pallas kernels: 4.78 us -> 4.75 us  [panel_keep(): near_call(keep_kernel, 'panel_keep', n, n // 2 // UNROLL, [whole(K, rows)...]
  transfers between devices with their start and end apart: 49 -> 52, of which waited for: 30 -> 21; matrix products, arithmetic and copies ran while one was open for 3% -> 4% of each run, Pallas kernels for 22% -> 21%
where the time goes in v10:
time: 189 us; the launch traced here: 188 us
  Pallas kernels  57.5 us (30%)
  waiting for transfers between devices  56 us (30%)
  starting transfers between devices  55.6 us (29%)
  other arithmetic  12.5 us (7%)
  matrix products  3.21 us (2%)
  local copies, waits for them, and re-layouts  1.94 us (1%)
    ppermute x52, waiting for transfers between devices, swap(): return lax.ppermute(value, 'dp', [(i, i ^ bit) for i in range(n)])  56 us
    ppermute x52, starting transfers between devices, swap(): return lax.ppermute(value, 'dp', [(i, i ^ bit) for i in range(n)])  55.6 us
    pallas_call x2, Pallas kernels, probe_and_send(): near_call(functools.partial(send_kernel, s, count, d), 'probe_and_send',...  15.1 us
    pallas_call x4, Pallas kernels, small(): pl.pallas_call(kernel, out_shape=tuple((jax.ShapeDtypeStruct(shape, F32)...  14.8 us
    pallas_call x2, Pallas kernels, load(): pl.pallas_call(load_kernel, out_shape=jax.ShapeDtypeStruct(acts.shape, ac...  9.44 us
    pallas_call x2, Pallas kernels, class_sums(): call(functools.partial(sums_kernel, half), 'class_sums', n, n // 2 // UNR...  7.03 us
    pallas_call x2, Pallas kernels, probe(): near_call(functools.partial(probe_kernel, count), 'probe', n, n // 2 // U...  6.45 us
    pallas_call x2, Pallas kernels, panel_keep(): near_call(keep_kernel, 'panel_keep', n, n // 2 // UNROLL, [whole(K, rows)...  4.75 us
  transfers between devices with their start and end apart: 52, of which 21 were waited for; matrix products, arithmetic and copies ran while one was open for 4% of the time, Pallas kernels for 21%

profile of v10, /device:TPU:0, one launch (start us, length us, event | category | flops | bytes accessed | tf_op | source)
XLA Modules:
  0.0 188.3 jit_solution(6545131659252067435)
XLA Ops:
  1.3 3.3 %class_sums.3 = (f32[8,64,1024]{2,1,0:T(8,128)S(1)}, f32[64,1]{1,0:T(8,128)S(1)}) custom-call(s32[1]{0:T(128)} %bitcast.me, s32[1,384]{1,0:T(1,128)S(1)} %reshape.50.row_data.refs_6_.refs_10_, bf16[384,16384]{1,0:T(8,128)(2,1)} %acts.5), custom_call_target="tpu_custom_call" | custom-call | flops 402653184 | bytes 8388608 | tf_op jit(solution)/shard_map/class_sums/pallas_call | solution.py:149
  6.3 3.0 %collective-permute-start.2 = (f32[1,64]{1,0:T(1,128)S(1)}, f32[1,64]{1,0:T(1,128)S(1)}, u32[]{:S(2)}, u32[]{:S(2)}) collective-permute-start(f32[1,64]{1,0:T(1,128)S(1)} %bitcast.175), channel_id=1, source_target_pairs={{0,2},{1,3},{2,0},{3,1},{4,6},{5,7},{6,4},{7,5},{8,10},{9,11},{10,... | collective-permute-start | bytes 776 | tf_op jit(solution)/shard_map/ppermute | solution.py:62
  9.3 3.7 %class_sums.2 = (f32[8,64,1024]{2,1,0:T(8,128)S(1)}, f32[64,1]{1,0:T(8,128)}) custom-call(s32[1]{0:T(128)} %bitcast.me, s32[1,384]{1,0:T(1,128)S(1)} %reshape.50.row_data.refs_6_.refs_10_, bf16[384,16384]{1,0:T(8,128)(2,1)} %acts.5), custom_call_target="tpu_custom_call" | custom-call | flops 402653184 | bytes 8388608 | tf_op jit(solution)/shard_map/class_sums/pallas_call | solution.py:149
  14.4 1.6 collective-permute-start.5
  16.7 1.5 collective-permute-start.4
  18.2 5.0 %collective-permute-done.6 = f32[1,64]{1,0:T(1,128)S(1)} collective-permute-done((f32[1,64]{1,0:T(1,128)S(1)}, f32[1,64]{1,0:T(1,128)S(1)}, u32[]{:S(2)}, u32[]{:S(2)}) %collective-permute-start.6) | collective-permute-done | bytes 288 | tf_op jit(solution)/shard_map/ppermute | solution.py:62
  23.3 1.6 collective-permute-done.4
  25.1 2.7 %collective-permute-start.9 = (f32[1,64]{1,0:T(1,128)S(1)}, f32[1,64]{1,0:T(1,128)S(1)}, u32[]{:S(2)}, u32[]{:S(2)}) collective-permute-start(f32[1,64]{1,0:T(1,128)S(1)} %add.124), channel_id=1, source_target_pairs={{0,8},{1,9},{2,10},{3,11},{4,12},{5,13},{6,14},{7,15},{8,0},{9,1},... | collective-permute-start | bytes 776 | tf_op jit(solution)/shard_map/ppermute | solution.py:62
  28.4 1.7 collective-permute-start.7
  30.1 6.0 %collective-permute-done.8 = f16[2,32,1024]{2,1,0:T(8,128)(2,1)S(1)} collective-permute-done((f16[2,32,1024]{2,1,0:T(8,128)(2,1)S(1)}, f16[2,32,1024]{2,1,0:T(8,128)(2,1)S(1)}, u32[]{:S(2)}, u32[]{:S(2)}) %collective-permute-start.8) | collective-permute-done | bytes 131104 | tf_op jit(solution)/shard_map/ppermute | solution.py:62
  36.3 1.7 collective-permute-start.11
  38.8 1.5 collective-permute-start.10
  41.4 2.9 %collective-permute-done.10 = f16[32,1024]{1,0:T(8,128)(2,1)S(1)} collective-permute-done((f16[32,1024]{1,0:T(8,128)(2,1)S(1)}, f16[32,1024]{1,0:T(8,128)(2,1)S(1)}, u32[]{:S(2)}, u32[]{:S(2)}) %collective-permute-start.10) | collective-permute-done | bytes 65568 | tf_op jit(solution)/shard_map/ppermute | solution.py:62
  46.6 2.7 %collective-permute-done.13 = bf16[1,32,1024]{2,1,0:T(8,128)(2,1)S(1)} collective-permute-done((bf16[1,32,1024]{2,1,0:T(8,128)(2,1)S(1)}, bf16[1,32,1024]{2,1,0:T(8,128)(2,1)S(1)}, u32[]{:S(2)}, u32[]{:S(2)}) %collective-permute-start.13) | collective-permute-done | bytes 65568 | tf_op jit(solution)/shard_map/ppermute | solution.py:62
  49.4 3.4 %collective-permute-done.12 = bf16[1,32,1024]{2,1,0:T(8,128)(2,1)S(1)} collective-permute-done((bf16[1,32,1024]{2,1,0:T(8,128)(2,1)S(1)}, bf16[1,32,1024]{2,1,0:T(8,128)(2,1)S(1)}, u32[]{:S(2)}, u32[]{:S(2)}) %collective-permute-start.12) | collective-permute-done | bytes 65568 | tf_op jit(solution)/shard_map/ppermute | solution.py:62
  52.9 2.4 %collective-permute-start.14 = (bf16[2,32,1024]{2,1,0:T(8,128)(2,1)S(1)}, bf16[2,32,1024]{2,1,0:T(8,128)(2,1)S(1)}, u32[]{:S(2)}, u32[]{:S(2)}) collective-permute-start(bf16[2,32,1024]{2,1,0:T(8,128)(2,1)S(1)} %pad_maximum_fusion.8), channel_id=1, source_target_pairs={{0,4},{1,5},{2,6},{3,7},{4,0},{5,1},{6,2},{7,3},{8,12},{9,13},{10,... | collective-permute-start | bytes 393224 | tf_op jit(solution)/shard_map/ppermute | solution.py:62
  55.3 4.4 %collective-permute-done.15 = bf16[2,32,1024]{2,1,0:T(8,128)(2,1)S(1)} collective-permute-done((bf16[2,32,1024]{2,1,0:T(8,128)(2,1)S(1)}, bf16[2,32,1024]{2,1,0:T(8,128)(2,1)S(1)}, u32[]{:S(2)}, u32[]{:S(2)}) %collective-permute-start.15) | collective-permute-done | bytes 131104 | tf_op jit(solution)/shard_map/ppermute | solution.py:62
  61.4 1.7 collective-permute-start.16
  63.1 4.7 %load.2.refs_4_.refs_5_.refs_0_.refs_1_ = bf16[384,16384]{1,0:T(8,128)(2,1)S(1)} custom-call(bf16[384,16384]{1,0:T(8,128)(2,1)} %acts.5), custom_call_target="tpu_custom_call" | custom-call | bytes 25165824 | tf_op jit(solution)/shard_map/load/pallas_call | solution.py:207
  68.6 3.1 %probe.2 = (f32[384,64]{1,0:T(8,128)S(1)}, f32[64,64]{1,0:T(8,128)S(1)}) custom-call(s32[1]{0:T(128)} %bitcast.me, bf16[8,32,1024]{2,1,0:T(8,128)(2,1)S(1)} %pad_maximum_fusion.refs_0_.refs_2_.refs_4_.refs_6_, bf16[8,32,1024]{2,1,0:T(8,128)(2,1)S(1)} %pad_maximum_fusion.1.refs_1_.refs_3_.refs_5_.refs_7_, ...), custom_call_target="tpu_custom_call" | custom-call | flops 402653184 | bytes 8388608 | tf_op jit(solution)/shard_map/probe/pallas_call | solution.py:256
  71.7 6.8 %probe_and_send.2 = (f32[64,384]{1,0:T(8,128)S(1)}, f32[64,64]{1,0:T(8,128)S(1)}, f32[64,1]{1,0:T(8,128)S(1)}, f32[64,1]{1,0:T(8,128)S(1)}, f32[1,64]{1,0:T(1,12...) custom-call(s32[1]{0:T(128)} %bitcast.me, ...), custom_call_target="tpu_custom_call" | custom-call | flops 402653184 | bytes 8388608 | tf_op jit(solution)/shard_map/probe_and_send/pallas_call | solution.py:345
  79.3 1.6 collective-permute-start.22
  80.9 2.3 %panel_keep.2 = f32[8,64,1024]{2,1,0:T(8,128)S(1)} custom-call(s32[1]{0:T(128)} %bitcast.me, f32[64,384]{1,0:T(8,128)S(1)} %get-tuple-element.125.probed.refs_15_, s32[1,384]{1,0:T(1,128)S(1)} %reshape.50.row_data.refs_6_.refs_10_, f32[64,1]{1,0:T(8,128)S(1)} %get-tuple-element.126.inv, bf16[384,16384]{1,0:T(8,128)(2,1)S(1)} %load.2.refs_4_.refs_5_.refs_0_.refs_1_, ...), custom_call_target="tpu_custom_call" | custom-call | flops 402653184 | bytes 8388608 | tf_op jit(solution)/shard_map/panel_keep/pallas_call | solution.py:391
  85.3 1.5 collective-permute-start.25
  88.0 6.4 %collective-permute-done.26 = f32[64,64]{1,0:T(8,128)S(1)} collective-permute-done((f32[64,64]{1,0:T(8,128)S(1)}, f32[64,64]{1,0:T(8,128)S(1)}, u32[]{:S(2)}, u32[]{:S(2)}) %collective-permute-start.26) | collective-permute-done | bytes 16416 | tf_op jit(solution)/shard_map/ppermute | solution.py:62
  95.3 2.3 %collective-permute-start.29 = (f32[64,64]{1,0:T(8,128)S(1)}, f32[64,64]{1,0:T(8,128)S(1)}, u32[]{:S(2)}, u32[]{:S(2)}) collective-permute-start(f32[64,64]{1,0:T(8,128)S(1)} %add.136), channel_id=1, source_target_pairs={{0,8},{1,9},{2,10},{3,11},{4,12},{5,13},{6,14},{7,15},{8,0},{9,1},... | collective-permute-start | bytes 49160 | tf_op jit(solution)/shard_map/ppermute | solution.py:62
  100.2 1.5 collective-permute-start.27
  101.7 2.6 %offset.1 = f32[64,1024]{1,0:T(8,128)} custom-call(f32[32,1024]{1,0:T(8,128)} %get-tuple-element.136.base_a, f32[32,1024]{1,0:T(8,128)} %get-tuple-element.137.base_b, f32[64,64]{1,0:T(8,128)} %copy-done, f32[1,1]{1,0:T(1,128)} %bitcast.19.refs_7_.total_weight.refs_11_), custom_call_target="tpu_custom_call" | custom-call | flops 67108864 | bytes 1048576 | tf_op jit(solution)/shard_map/offset/pallas_call | solution.py:446
  110.0 3.6 %collective-permute-done.30 = f16[32,1024]{1,0:T(8,128)(2,1)S(1)} collective-permute-done((f16[32,1024]{1,0:T(8,128)(2,1)S(1)}, f16[32,1024]{1,0:T(8,128)(2,1)S(1)}, u32[]{:S(2)}, u32[]{:S(2)}) %collective-permute-start.30) | collective-permute-done | bytes 65568 | tf_op jit(solution)/shard_map/ppermute | solution.py:62
  115.4 1.7 collective-permute-start.32
  117.0 1.6 collective-permute-done.33
  118.6 2.2 %collective-permute-done.32 = bf16[1,32,1024]{2,1,0:T(8,128)(2,1)S(1)} collective-permute-done((bf16[1,32,1024]{2,1,0:T(8,128)(2,1)S(1)}, bf16[1,32,1024]{2,1,0:T(8,128)(2,1)S(1)}, u32[]{:S(2)}, u32[]{:S(2)}) %collective-permute-start.32) | collective-permute-done | bytes 65568 | tf_op jit(solution)/shard_map/ppermute | solution.py:62
  120.8 1.8 collective-permute-start.35
  122.6 3.2 %collective-permute-start.34 = (bf16[2,32,1024]{2,1,0:T(8,128)(2,1)S(1)}, bf16[2,32,1024]{2,1,0:T(8,128)(2,1)S(1)}, u32[]{:S(2)}, u32[]{:S(2)}) collective-permute-start(bf16[2,32,1024]{2,1,0:T(8,128)(2,1)S(1)} %pad_maximum_fusion.10), channel_id=1, source_target_pairs={{0,4},{1,5},{2,6},{3,7},{4,0},{5,1},{6,2},{7,3},{8,12},{9,13},{10,... | collective-permute-start | bytes 393224 | tf_op jit(solution)/shard_map/ppermute | solution.py:62
  125.8 4.3 %alpha.1 = (f32[64,64]{1,0:T(8,128)}, f32[64,64]{1,0:T(8,128)}) custom-call(f32[64,64]{1,0:T(8,128)} %add.139.along, f32[64,64]{1,0:T(8,128)} %copy-done, f32[1,1]{1,0:T(1,128)} %bitcast.19.refs_7_.total_weight.refs_11_), custom_call_target="tpu_custom_call" | custom-call | flops 67108864 | bytes 1048576 | tf_op jit(solution)/shard_map/alpha/pallas_call | solution.py:446
  130.2 1.7 collective-permute-start.37
  131.8 1.8 collective-permute-start.36
  133.6 4.7 %load.3.refs_8_.refs_9_.refs_0_.refs_1_ = bf16[384,16384]{1,0:T(8,128)(2,1)S(1)} custom-call(bf16[384,16384]{1,0:T(8,128)(2,1)} %acts.5), custom_call_target="tpu_custom_call" | custom-call | bytes 25165824 | tf_op jit(solution)/shard_map/load/pallas_call | solution.py:207
  139.1 3.4 %probe.3 = (f32[384,64]{1,0:T(8,128)S(1)}, f32[64,64]{1,0:T(8,128)S(1)}, f32[64,64]{1,0:T(8,128)S(1)}) custom-call(s32[1]{0:T(128)} %bitcast.me, bf16[8,32,1024]{2,1,0:T(8,128)(2,1)S(1)} %pad_maximum_fusion.2.refs_0_.refs_2_, bf16[8,32,1024]{2,1,0:T(8,128)(2,1)S(1)} %pad_maximum_fusion.3.refs_1_.refs_3_, ...), custom_call_target="tpu_custom_call" | custom-call | flops 402653184 | bytes 8388608 | tf_op jit(solution)/shard_map/probe/pallas_call | solution.py:256
  142.5 8.2 %probe_and_send.3 = (f32[64,384]{1,0:T(8,128)S(1)}, f32[64,64]{1,0:T(8,128)S(1)}, f32[64,1]{1,0:T(8,128)S(1)}, f32[64,1]{1,0:T(8,128)}, f32[1,64]{1,0:T(1,128)S(...) custom-call(s32[1]{0:T(128)} %bitcast.me, ...), custom_call_target="tpu_custom_call" | custom-call | flops 402653184 | bytes 8388608 | tf_op jit(solution)/shard_map/probe_and_send/pallas_call | solution.py:345
  152.0 1.6 collective-permute-start.42
  153.6 2.4 %panel_keep.3 = f32[8,64,1024]{2,1,0:T(8,128)S(1)} custom-call(s32[1]{0:T(128)} %bitcast.me, f32[64,384]{1,0:T(8,128)S(1)} %get-tuple-element.167.probed, s32[1,384]{1,0:T(1,128)S(1)} %reshape.50.row_data.refs_6_.refs_10_, f32[64,1]{1,0:T(8,128)S(1)} %get-tuple-element.168.inv, bf16[384,16384]{1,0:T(8,128)(2,1)S(1)} %load.3.refs_8_.refs_9_.refs_0_.refs_1_, ...), custom_call_target="tpu_custom_call" | custom-call | flops 402653184 | bytes 8388608 | tf_op jit(solution)/shard_map/panel_keep/pallas_call | solution.py:391
  160.7 6.4 %collective-permute-done.46 = f32[64,64]{1,0:T(8,128)S(1)} collective-permute-done((f32[64,64]{1,0:T(8,128)S(1)}, f32[64,64]{1,0:T(8,128)S(1)}, u32[]{:S(2)}, u32[]{:S(2)}) %collective-permute-start.46) | collective-permute-done | bytes 16416 | tf_op jit(solution)/shard_map/ppermute | solution.py:62
  168.1 1.6 collective-permute-start.48
  172.4 2.5 %before.1 = (f32[64,64]{1,0:T(8,128)}, f32[64,64]{1,0:T(8,128)}) custom-call(f32[64,64]{1,0:T(8,128)} %copy-done, f32[64,64]{1,0:T(8,128)} %copy-done.3, f32[64,64]{1,0:T(8,128)} %copy-done.7, f32[64,64]{1,0:T(8,128)} %copy-done.4, f32[1,1]{1,0:T(1,128)} %bitcast.19.refs_7_.total_weight.refs_11_), custom_call_target="tpu_custom_call" | custom-call | flops 67108864 | bytes 1048576 | tf_op jit(solution)/shard_map/before/pallas_call | solution.py:446
  174.8 2.6 %collective-permute-done.49 = f32[64,64]{1,0:T(8,128)S(1)} collective-permute-done((f32[64,64]{1,0:T(8,128)S(1)}, f32[64,64]{1,0:T(8,128)S(1)}, u32[]{:S(2)}, u32[]{:S(2)}) %collective-permute-start.49) | collective-permute-done | bytes 16416 | tf_op jit(solution)/shard_map/ppermute | solution.py:62
  179.7 5.4 %last.1 = (f32[64,1024]{1,0:T(8,128)}, f32[64,1024]{1,0:T(8,128)}, f32[64,64]{1,0:T(8,128)}) custom-call(f32[64,64]{1,0:T(8,128)} %add.153.along, f32[64,64]{1,0:T(8,128)} %get-tuple-element.188.fixed, f32[64,64]{1,0:T(8,128)} %get-tuple-element.189.cross_t, f32[64,64]{1,0:T(8,128)} %copy-done.3, f32[64,64]{1,0:T(8,128)} %copy-done.4, ...), custom_call_target="tpu_custom_call" | custom-call | flops 67108864 | bytes 1048576 | tf_op jit(solution)/shard_map/last/pallas_call | solution.py:446
  186.3 2.0 %subtract_bitcast_fusion = f32[1024,64]{0,1:T(8,128)} fusion(f32[64,1024]{1,0:T(8,128)} %get-tuple-element.192, f32[64,1024]{1,0:T(8,128)S(1)} %fusion.37, f32[2,32,1024]{2,1,0:T(8,128)S(1)} %fusion.20, f16[32,1024]{1,0:T(8,128)(2,1)S(1)} %collective-permute-done.51, f32[64,64]{1,0:T(8,128)} %get-tuple-element.193), kind=kOutput, calls=%fused_computation.67 | convolution fusion | flops 25362432 | bytes 999424 | tf_op jit(solution)/shard_map/dot_general | solution.py:21
  (181 shorter events, 40.4 us)
Async XLA Ops:
  5.6 7.5 %collective-permute-start = (f16[8,64,1024]{2,1,0:T(8,128)(2,1)S(1)}, f16[8,64,1024]{2,1,0:T(8,128)(2,1)S(1)}, u32[]{:S(2)}, u32[]{:S(2)}) collective-permute-start(f16[8,64,1024]{2,1,0:T(8,128)(2,1)S(1)} %fusion), channel_id=1, source_target_pairs={{0,1},{1,0},{2,3},{3,2},{4,5},{5,4},{6,7},{7,6},{8,9},{9,8},{10,11... | collective-permute-start | bytes 3145736 | tf_op jit(solution)/shard_map/ppermute | solution.py:62
  6.2 6.8 %collective-permute-start.1 = (f32[1,64]{1,0:T(1,128)S(1)}, f32[1,64]{1,0:T(1,128)S(1)}, u32[]{:S(2)}, u32[]{:S(2)}) collective-permute-start(f32[1,64]{1,0:T(1,128)S(1)} %bitcast.174), channel_id=1, source_target_pairs={{0,1},{1,0},{2,3},{3,2},{4,5},{5,4},{6,7},{7,6},{8,9},{9,8},{10,11... | collective-permute-start | bytes 776 | tf_op jit(solution)/shard_map/ppermute | solution.py:62
  6.3 6.7 %collective-permute-start.2 = (f32[1,64]{1,0:T(1,128)S(1)}, f32[1,64]{1,0:T(1,128)S(1)}, u32[]{:S(2)}, u32[]{:S(2)}) collective-permute-start(f32[1,64]{1,0:T(1,128)S(1)} %bitcast.175), channel_id=1, source_target_pairs={{0,2},{1,3},{2,0},{3,1},{4,6},{5,7},{6,4},{7,5},{8,10},{9,11},{10,... | collective-permute-start | bytes 776 | tf_op jit(solution)/shard_map/ppermute | solution.py:62
  9.3 3.7 %collective-permute-start.3 = (f32[1,64]{1,0:T(1,128)S(1)}, f32[1,64]{1,0:T(1,128)S(1)}, u32[]{:S(2)}, u32[]{:S(2)}) collective-permute-start(f32[1,64]{1,0:T(1,128)S(1)} %bitcast.176), channel_id=1, source_target_pairs={{0,3},{1,2},{2,1},{3,0},{4,7},{5,6},{6,5},{7,4},{8,11},{9,10},{10,... | collective-permute-start | bytes 776 | tf_op jit(solution)/shard_map/ppermute | solution.py:62
  14.4 8.8 %collective-permute-start.5 = (f16[2,2,32,1024]{3,2,0,1:T(8,128)(2,1)S(1)}, f16[2,2,32,1024]{3,2,0,1:T(8,128)(2,1)S(1)}, u32[]{:S(2)}, u32[]{:S(2)}) collective-permute-start(f16[2,2,32,1024]{3,2,0,1:T(8,128)(2,1)S(1)} %fusion.6), channel_id=1, source_target_pairs={{0,4},{1,5},{2,6},{3,7},{4,0},{5,1},{6,2},{7,3},{8,12},{9,13},{10,... | collective-permute-start | bytes 786440 | tf_op jit(solution)/shard_map/ppermute | solution.py:62
  16.0 7.2 %collective-permute-start.6 = (f32[1,64]{1,0:T(1,128)S(1)}, f32[1,64]{1,0:T(1,128)S(1)}, u32[]{:S(2)}, u32[]{:S(2)}) collective-permute-start(f32[1,64]{1,0:T(1,128)S(1)} %add_add_fusion.2), channel_id=1, source_target_pairs={{0,4},{1,5},{2,6},{3,7},{4,0},{5,1},{6,2},{7,3},{8,12},{9,13},{10,... | collective-permute-start | bytes 776 | tf_op jit(solution)/shard_map/ppermute | solution.py:62
  16.7 8.2 %collective-permute-start.4 = (f16[2,2,32,1024]{3,2,0,1:T(8,128)(2,1)S(1)}, f16[2,2,32,1024]{3,2,0,1:T(8,128)(2,1)S(1)}, u32[]{:S(2)}, u32[]{:S(2)}) collective-permute-start(f16[2,2,32,1024]{3,2,0,1:T(8,128)(2,1)S(1)} %fusion.3), channel_id=1, source_target_pairs={{0,2},{1,3},{2,0},{3,1},{4,6},{5,7},{6,4},{7,5},{8,10},{9,11},{10,... | collective-permute-start | bytes 786440 | tf_op jit(solution)/shard_map/ppermute | solution.py:62
  25.1 5.0 %collective-permute-start.9 = (f32[1,64]{1,0:T(1,128)S(1)}, f32[1,64]{1,0:T(1,128)S(1)}, u32[]{:S(2)}, u32[]{:S(2)}) collective-permute-start(f32[1,64]{1,0:T(1,128)S(1)} %add.124), channel_id=1, source_target_pairs={{0,8},{1,9},{2,10},{3,11},{4,12},{5,13},{6,14},{7,15},{8,0},{9,1},... | collective-permute-start | bytes 776 | tf_op jit(solution)/shard_map/ppermute | solution.py:62
  28.0 8.2 %collective-permute-start.8 = (f16[2,32,1024]{2,1,0:T(8,128)(2,1)S(1)}, f16[2,32,1024]{2,1,0:T(8,128)(2,1)S(1)}, u32[]{:S(2)}, u32[]{:S(2)}) collective-permute-start(f16[2,32,1024]{2,1,0:T(8,128)(2,1)S(1)} %fusion.16), channel_id=1, source_target_pairs={{0,8},{1,9},{2,10},{3,11},{4,12},{5,13},{6,14},{7,15},{8,0},{9,1},... | collective-permute-start | bytes 393224 | tf_op jit(solution)/shard_map/ppermute | solution.py:62
  28.4 7.8 %collective-permute-start.7 = (f16[2,32,1024]{2,1,0:T(8,128)(2,1)S(1)}, f16[2,32,1024]{2,1,0:T(8,128)(2,1)S(1)}, u32[]{:S(2)}, u32[]{:S(2)}) collective-permute-start(f16[2,32,1024]{2,1,0:T(8,128)(2,1)S(1)} %fusion.13), channel_id=1, source_target_pairs={{0,4},{1,5},{2,6},{3,7},{4,0},{5,1},{6,2},{7,3},{8,12},{9,13},{10,... | collective-permute-start | bytes 393224 | tf_op jit(solution)/shard_map/ppermute | solution.py:62
  36.3 4.3 %collective-permute-start.11 = (f16[32,1024]{1,0:T(8,128)(2,1)S(1)}, f16[32,1024]{1,0:T(8,128)(2,1)S(1)}, u32[]{:S(2)}, u32[]{:S(2)}) collective-permute-start(f16[32,1024]{1,0:T(8,128)(2,1)S(1)} %fusion.27), channel_id=1, source_target_pairs={{0,2},{1,3},{2,0},{3,1},{4,6},{5,7},{6,4},{7,5},{8,10},{9,11},{10,... | collective-permute-start | bytes 196616 | tf_op jit(solution)/shard_map/ppermute | solution.py:62
  38.8 5.6 %collective-permute-start.10 = (f16[32,1024]{1,0:T(8,128)(2,1)S(1)}, f16[32,1024]{1,0:T(8,128)(2,1)S(1)}, u32[]{:S(2)}, u32[]{:S(2)}) collective-permute-start(f16[32,1024]{1,0:T(8,128)(2,1)S(1)} %fusion.23), channel_id=1, source_target_pairs={{0,8},{1,9},{2,10},{3,11},{4,12},{5,13},{6,14},{7,15},{8,0},{9,1},... | collective-permute-start | bytes 196616 | tf_op jit(solution)/shard_map/ppermute | solution.py:62
  45.1 4.3 %collective-permute-start.13 = (bf16[1,32,1024]{2,1,0:T(8,128)(2,1)S(1)}, bf16[1,32,1024]{2,1,0:T(8,128)(2,1)S(1)}, u32[]{:S(2)}, u32[]{:S(2)}) collective-permute-start(bf16[1,32,1024]{2,1,0:T(8,128)(2,1)S(1)} %get-tuple-element.112), channel_id=1, source_target_pairs={{0,2},{1,3},{2,0},{3,1},{4,6},{5,7},{6,4},{7,5},{8,10},{9,11},{10,... | collective-permute-start | bytes 196616 | tf_op jit(solution)/shard_map/ppermute | solution.py:62
  45.5 7.3 %collective-permute-start.12 = (bf16[1,32,1024]{2,1,0:T(8,128)(2,1)S(1)}, bf16[1,32,1024]{2,1,0:T(8,128)(2,1)S(1)}, u32[]{:S(2)}, u32[]{:S(2)}) collective-permute-start(bf16[1,32,1024]{2,1,0:T(8,128)(2,1)S(1)} %get-tuple-element.111), channel_id=1, source_target_pairs={{0,8},{1,9},{2,10},{3,11},{4,12},{5,13},{6,14},{7,15},{8,0},{9,1},... | collective-permute-start | bytes 196616 | tf_op jit(solution)/shard_map/ppermute | solution.py:62
  52.8 6.9 %collective-permute-start.15 = (bf16[2,32,1024]{2,1,0:T(8,128)(2,1)S(1)}, bf16[2,32,1024]{2,1,0:T(8,128)(2,1)S(1)}, u32[]{:S(2)}, u32[]{:S(2)}) collective-permute-start(bf16[2,32,1024]{2,1,0:T(8,128)(2,1)S(1)} %pad_maximum_fusion.9), channel_id=1, source_target_pairs={{0,8},{1,9},{2,10},{3,11},{4,12},{5,13},{6,14},{7,15},{8,0},{9,1},... | collective-permute-start | bytes 393224 | tf_op jit(solution)/shard_map/ppermute | solution.py:62
  52.9 7.8 %collective-permute-start.14 = (bf16[2,32,1024]{2,1,0:T(8,128)(2,1)S(1)}, bf16[2,32,1024]{2,1,0:T(8,128)(2,1)S(1)}, u32[]{:S(2)}, u32[]{:S(2)}) collective-permute-start(bf16[2,32,1024]{2,1,0:T(8,128)(2,1)S(1)} %pad_maximum_fusion.8), channel_id=1, source_target_pairs={{0,4},{1,5},{2,6},{3,7},{4,0},{5,1},{6,2},{7,3},{8,12},{9,13},{10,... | collective-permute-start | bytes 393224 | tf_op jit(solution)/shard_map/ppermute | solution.py:62
  60.7 7.2 %collective-permute-start.17 = (bf16[4,32,1024]{2,1,0:T(8,128)(2,1)S(1)}, bf16[4,32,1024]{2,1,0:T(8,128)(2,1)S(1)}, u32[]{:S(2)}, u32[]{:S(2)}) collective-permute-start(bf16[4,32,1024]{2,1,0:T(8,128)(2,1)S(1)} %pad_maximum_fusion.5), channel_id=1, source_target_pairs={{0,4},{1,5},{2,6},{3,7},{4,0},{5,1},{6,2},{7,3},{8,12},{9,13},{10,... | collective-permute-start | bytes 786440 | tf_op jit(solution)/shard_map/ppermute | solution.py:62
  61.4 6.5 %collective-permute-start.16 = (bf16[4,32,1024]{2,1,0:T(8,128)(2,1)S(1)}, bf16[4,32,1024]{2,1,0:T(8,128)(2,1)S(1)}, u32[]{:S(2)}, u32[]{:S(2)}) collective-permute-start(bf16[4,32,1024]{2,1,0:T(8,128)(2,1)S(1)} %pad_maximum_fusion.4), channel_id=1, source_target_pairs={{0,2},{1,3},{2,0},{3,1},{4,6},{5,7},{6,4},{7,5},{8,10},{9,11},{10,... | collective-permute-start | bytes 786440 | tf_op jit(solution)/shard_map/ppermute | solution.py:62
  78.7 5.8 %collective-permute-start.20 = (f16[8,64,1024]{2,1,0:T(8,128)(2,1)S(1)}, f16[8,64,1024]{2,1,0:T(8,128)(2,1)S(1)}, u32[]{:S(2)}, u32[]{:S(2)}) collective-permute-start(f16[8,64,1024]{2,1,0:T(8,128)(2,1)S(1)} %convert_element_type.154), channel_id=1, source_target_pairs={{0,1},{1,0},{2,3},{3,2},{4,5},{5,4},{6,7},{7,6},{8,9},{9,8},{10,11... | collective-permute-start | bytes 3145736 | tf_op jit(solution)/shard_map/ppermute | solution.py:62
  78.9 4.4 %collective-permute-start.21 = (f32[64,64]{1,0:T(8,128)S(1)}, f32[64,64]{1,0:T(8,128)S(1)}, u32[]{:S(2)}, u32[]{:S(2)}) collective-permute-start(f32[64,64]{1,0:T(8,128)S(1)} %get-tuple-element.128), channel_id=1, source_target_pairs={{0,1},{1,0},{2,3},{3,2},{4,5},{5,4},{6,7},{7,6},{8,9},{9,8},{10,11... | collective-permute-start | bytes 49160 | tf_op jit(solution)/shard_map/ppermute | solution.py:62
  79.3 4.0 %collective-permute-start.22 = (f32[64,64]{1,0:T(8,128)S(1)}, f32[64,64]{1,0:T(8,128)S(1)}, u32[]{:S(2)}, u32[]{:S(2)}) collective-permute-start(f32[64,64]{1,0:T(8,128)S(1)} %get-tuple-element.128), channel_id=1, source_target_pairs={{0,2},{1,3},{2,0},{3,1},{4,6},{5,7},{6,4},{7,5},{8,10},{9,11},{10,... | collective-permute-start | bytes 49160 | tf_op jit(solution)/shard_map/ppermute | solution.py:62
  85.3 9.1 %collective-permute-start.25 = (f16[2,2,32,1024]{3,2,1,0:T(8,128)(2,1)S(1)}, f16[2,2,32,1024]{3,2,1,0:T(8,128)(2,1)S(1)}, u32[]{:S(2)}, u32[]{:S(2)}) collective-permute-start(f16[2,2,32,1024]{3,2,1,0:T(8,128)(2,1)S(1)} %convert_element_type.158), channel_id=1, source_target_pairs={{0,4},{1,5},{2,6},{3,7},{4,0},{5,1},{6,2},{7,3},{8,12},{9,13},{10,... | collective-permute-start | bytes 786440 | tf_op jit(solution)/shard_map/ppermute | solution.py:62
  86.8 7.5 %collective-permute-start.26 = (f32[64,64]{1,0:T(8,128)S(1)}, f32[64,64]{1,0:T(8,128)S(1)}, u32[]{:S(2)}, u32[]{:S(2)}) collective-permute-start(f32[64,64]{1,0:T(8,128)S(1)} %add_add_fusion.1), channel_id=1, source_target_pairs={{0,4},{1,5},{2,6},{3,7},{4,0},{5,1},{6,2},{7,3},{8,12},{9,13},{10,... | collective-permute-start | bytes 49160 | tf_op jit(solution)/shard_map/ppermute | solution.py:62
  87.4 7.8 %collective-permute-start.24 = (f16[2,2,32,1024]{3,2,0,1:T(8,128)(2,1)S(1)}, f16[2,2,32,1024]{3,2,0,1:T(8,128)(2,1)S(1)}, u32[]{:S(2)}, u32[]{:S(2)}) collective-permute-start(f16[2,2,32,1024]{3,2,0,1:T(8,128)(2,1)S(1)} %convert_element_type.156), channel_id=1, source_target_pairs={{0,2},{1,3},{2,0},{3,1},{4,6},{5,7},{6,4},{7,5},{8,10},{9,11},{10,... | collective-permute-start | bytes 786440 | tf_op jit(solution)/shard_map/ppermute | solution.py:62
  95.3 9.0 %collective-permute-start.29 = (f32[64,64]{1,0:T(8,128)S(1)}, f32[64,64]{1,0:T(8,128)S(1)}, u32[]{:S(2)}, u32[]{:S(2)}) collective-permute-start(f32[64,64]{1,0:T(8,128)S(1)} %add.136), channel_id=1, source_target_pairs={{0,8},{1,9},{2,10},{3,11},{4,12},{5,13},{6,14},{7,15},{8,0},{9,1},... | collective-permute-start | bytes 49160 | tf_op jit(solution)/shard_map/ppermute | solution.py:62
  98.3 8.1 %collective-permute-start.28 = (f16[2,32,1024]{2,1,0:T(8,128)(2,1)}, f16[2,32,1024]{2,1,0:T(8,128)(2,1)S(1)}, u32[]{:S(2)}, u32[]{:S(2)}) collective-permute-start(f16[2,32,1024]{2,1,0:T(8,128)(2,1)} %convert_element_type.162), channel_id=1, source_target_pairs={{0,8},{1,9},{2,10},{3,11},{4,12},{5,13},{6,14},{7,15},{8,0},{9,1},... | collective-permute-start | bytes 393224 | tf_op jit(solution)/shard_map/ppermute | solution.py:62
  100.2 6.6 %collective-permute-start.27 = (f16[2,32,1024]{2,1,0:T(8,128)(2,1)}, f16[2,32,1024]{2,1,0:T(8,128)(2,1)}, u32[]{:S(2)}, u32[]{:S(2)}) collective-permute-start(f16[2,32,1024]{2,1,0:T(8,128)(2,1)} %convert_element_type.160), channel_id=1, source_target_pairs={{0,4},{1,5},{2,6},{3,7},{4,0},{5,1},{6,2},{7,3},{8,12},{9,13},{10,... | collective-permute-start | bytes 393224 | tf_op jit(solution)/shard_map/ppermute | solution.py:62
  107.8 5.7 %collective-permute-start.30 = (f16[32,1024]{1,0:T(8,128)(2,1)S(1)}, f16[32,1024]{1,0:T(8,128)(2,1)S(1)}, u32[]{:S(2)}, u32[]{:S(2)}) collective-permute-start(f16[32,1024]{1,0:T(8,128)(2,1)S(1)} %convert_element_type.164), channel_id=1, source_target_pairs={{0,8},{1,9},{2,10},{3,11},{4,12},{5,13},{6,14},{7,15},{8,0},{9,1},... | collective-permute-start | bytes 196616 | tf_op jit(solution)/shard_map/ppermute | solution.py:62
  108.8 4.7 %collective-permute-start.31 = (f16[32,1024]{1,0:T(8,128)(2,1)S(1)}, f16[32,1024]{1,0:T(8,128)(2,1)S(1)}, u32[]{:S(2)}, u32[]{:S(2)}) collective-permute-start(f16[32,1024]{1,0:T(8,128)(2,1)S(1)} %convert_element_type.167), channel_id=1, source_target_pairs={{0,2},{1,3},{2,0},{3,1},{4,6},{5,7},{6,4},{7,5},{8,10},{9,11},{10,... | collective-permute-start | bytes 196616 | tf_op jit(solution)/shard_map/ppermute | solution.py:62
  114.3 4.3 %collective-permute-start.33 = (bf16[1,32,1024]{2,1,0:T(8,128)(2,1)S(1)}, bf16[1,32,1024]{2,1,0:T(8,128)(2,1)S(1)}, u32[]{:S(2)}, u32[]{:S(2)}) collective-permute-start(bf16[1,32,1024]{2,1,0:T(8,128)(2,1)S(1)} %get-tuple-element.145), channel_id=1, source_target_pairs={{0,2},{1,3},{2,0},{3,1},{4,6},{5,7},{6,4},{7,5},{8,10},{9,11},{10,... | collective-permute-start | bytes 196616 | tf_op jit(solution)/shard_map/ppermute | solution.py:62
  115.4 5.4 %collective-permute-start.32 = (bf16[1,32,1024]{2,1,0:T(8,128)(2,1)S(1)}, bf16[1,32,1024]{2,1,0:T(8,128)(2,1)S(1)}, u32[]{:S(2)}, u32[]{:S(2)}) collective-permute-start(bf16[1,32,1024]{2,1,0:T(8,128)(2,1)S(1)} %get-tuple-element.144), channel_id=1, source_target_pairs={{0,8},{1,9},{2,10},{3,11},{4,12},{5,13},{6,14},{7,15},{8,0},{9,1},... | collective-permute-start | bytes 196616 | tf_op jit(solution)/shard_map/ppermute | solution.py:62
  120.8 9.3 %collective-permute-start.35 = (bf16[2,32,1024]{2,1,0:T(8,128)(2,1)S(1)}, bf16[2,32,1024]{2,1,0:T(8,128)(2,1)S(1)}, u32[]{:S(2)}, u32[]{:S(2)}) collective-permute-start(bf16[2,32,1024]{2,1,0:T(8,128)(2,1)S(1)} %pad_maximum_fusion.11), channel_id=1, source_target_pairs={{0,8},{1,9},{2,10},{3,11},{4,12},{5,13},{6,14},{7,15},{8,0},{9,1},... | collective-permute-start | bytes 393224 | tf_op jit(solution)/shard_map/ppermute | solution.py:62
  122.6 7.6 %collective-permute-start.34 = (bf16[2,32,1024]{2,1,0:T(8,128)(2,1)S(1)}, bf16[2,32,1024]{2,1,0:T(8,128)(2,1)S(1)}, u32[]{:S(2)}, u32[]{:S(2)}) collective-permute-start(bf16[2,32,1024]{2,1,0:T(8,128)(2,1)S(1)} %pad_maximum_fusion.10), channel_id=1, source_target_pairs={{0,4},{1,5},{2,6},{3,7},{4,0},{5,1},{6,2},{7,3},{8,12},{9,13},{10,... | collective-permute-start | bytes 393224 | tf_op jit(solution)/shard_map/ppermute | solution.py:62
  130.2 8.2 %collective-permute-start.37 = (bf16[4,32,1024]{2,1,0:T(8,128)(2,1)S(1)}, bf16[4,32,1024]{2,1,0:T(8,128)(2,1)S(1)}, u32[]{:S(2)}, u32[]{:S(2)}) collective-permute-start(bf16[4,32,1024]{2,1,0:T(8,128)(2,1)S(1)} %pad_maximum_fusion.7), channel_id=1, source_target_pairs={{0,4},{1,5},{2,6},{3,7},{4,0},{5,1},{6,2},{7,3},{8,12},{9,13},{10,... | collective-permute-start | bytes 786440 | tf_op jit(solution)/shard_map/ppermute | solution.py:62
  131.8 6.6 %collective-permute-start.36 = (bf16[4,32,1024]{2,1,0:T(8,128)(2,1)S(1)}, bf16[4,32,1024]{2,1,0:T(8,128)(2,1)S(1)}, u32[]{:S(2)}, u32[]{:S(2)}) collective-permute-start(bf16[4,32,1024]{2,1,0:T(8,128)(2,1)S(1)} %pad_maximum_fusion.6), channel_id=1, source_target_pairs={{0,2},{1,3},{2,0},{3,1},{4,6},{5,7},{6,4},{7,5},{8,10},{9,11},{10,... | collective-permute-start | bytes 786440 | tf_op jit(solution)/shard_map/ppermute | solution.py:62
  138.5 4.0 %collective-permute-start.38 = (bf16[8,32,1024]{2,1,0:T(8,128)(2,1)S(1)}, bf16[8,32,1024]{2,1,0:T(8,128)(2,1)S(1)}, u32[]{:S(2)}, u32[]{:S(2)}) collective-permute-start(bf16[8,32,1024]{2,1,0:T(8,128)(2,1)S(1)} %pad_maximum_fusion.2.refs_0_.refs_2_), channel_id=1, source_target_pairs={{0,1},{1,0},{2,3},{3,2},{4,5},{5,4},{6,7},{7,6},{8,9},{9,8},{10,11... | collective-permute-start | bytes 1572872 | tf_op jit(solution)/shard_map/ppermute | solution.py:62
  138.6 3.9 %collective-permute-start.39 = (bf16[8,32,1024]{2,1,0:T(8,128)(2,1)S(1)}, bf16[8,32,1024]{2,1,0:T(8,128)(2,1)S(1)}, u32[]{:S(2)}, u32[]{:S(2)}) collective-permute-start(bf16[8,32,1024]{2,1,0:T(8,128)(2,1)S(1)} %pad_maximum_fusion.3.refs_1_.refs_3_), channel_id=1, source_target_pairs={{0,1},{1,0},{2,3},{3,2},{4,5},{5,4},{6,7},{7,6},{8,9},{9,8},{10,11... | collective-permute-start | bytes 1572872 | tf_op jit(solution)/shard_map/ppermute | solution.py:62
  151.4 5.8 %collective-permute-start.40 = (f16[8,64,1024]{2,1,0:T(8,128)(2,1)S(1)}, f16[8,64,1024]{2,1,0:T(8,128)(2,1)S(1)}, u32[]{:S(2)}, u32[]{:S(2)}) collective-permute-start(f16[8,64,1024]{2,1,0:T(8,128)(2,1)S(1)} %convert_element_type.170), channel_id=1, source_target_pairs={{0,1},{1,0},{2,3},{3,2},{4,5},{5,4},{6,7},{7,6},{8,9},{9,8},{10,11... | collective-permute-start | bytes 3145736 | tf_op jit(solution)/shard_map/ppermute | solution.py:62
  151.6 4.5 %collective-permute-start.41 = (f32[64,64]{1,0:T(8,128)S(1)}, f32[64,64]{1,0:T(8,128)S(1)}, u32[]{:S(2)}, u32[]{:S(2)}) collective-permute-start(f32[64,64]{1,0:T(8,128)S(1)} %get-tuple-element.170), channel_id=1, source_target_pairs={{0,1},{1,0},{2,3},{3,2},{4,5},{5,4},{6,7},{7,6},{8,9},{9,8},{10,11... | collective-permute-start | bytes 49160 | tf_op jit(solution)/shard_map/ppermute | solution.py:62
  152.0 4.0 %collective-permute-start.42 = (f32[64,64]{1,0:T(8,128)S(1)}, f32[64,64]{1,0:T(8,128)S(1)}, u32[]{:S(2)}, u32[]{:S(2)}) collective-permute-start(f32[64,64]{1,0:T(8,128)S(1)} %get-tuple-element.170), channel_id=1, source_target_pairs={{0,2},{1,3},{2,0},{3,1},{4,6},{5,7},{6,4},{7,5},{8,10},{9,11},{10,... | collective-permute-start | bytes 49160 | tf_op jit(solution)/shard_map/ppermute | solution.py:62
  158.0 9.1 %collective-permute-start.45 = (f16[2,2,32,1024]{3,2,1,0:T(8,128)(2,1)S(1)}, f16[2,2,32,1024]{3,2,1,0:T(8,128)(2,1)S(1)}, u32[]{:S(2)}, u32[]{:S(2)}) collective-permute-start(f16[2,2,32,1024]{3,2,1,0:T(8,128)(2,1)S(1)} %convert_element_type.174), channel_id=1, source_target_pairs={{0,4},{1,5},{2,6},{3,7},{4,0},{5,1},{6,2},{7,3},{8,12},{9,13},{10,... | collective-permute-start | bytes 786440 | tf_op jit(solution)/shard_map/ppermute | solution.py:62
  159.3 7.8 %collective-permute-start.46 = (f32[64,64]{1,0:T(8,128)S(1)}, f32[64,64]{1,0:T(8,128)S(1)}, u32[]{:S(2)}, u32[]{:S(2)}) collective-permute-start(f32[64,64]{1,0:T(8,128)S(1)} %add_add_fusion), channel_id=1, source_target_pairs={{0,4},{1,5},{2,6},{3,7},{4,0},{5,1},{6,2},{7,3},{8,12},{9,13},{10,... | collective-permute-start | bytes 49160 | tf_op jit(solution)/shard_map/ppermute | solution.py:62
  160.2 7.8 %collective-permute-start.44 = (f16[2,2,32,1024]{3,2,1,0:T(8,128)(2,1)S(1)}, f16[2,2,32,1024]{3,2,1,0:T(8,128)(2,1)S(1)}, u32[]{:S(2)}, u32[]{:S(2)}) collective-permute-start(f16[2,2,32,1024]{3,2,1,0:T(8,128)(2,1)S(1)} %convert_element_type.172), channel_id=1, source_target_pairs={{0,2},{1,3},{2,0},{3,1},{4,6},{5,7},{6,4},{7,5},{8,10},{9,11},{10,... | collective-permute-start | bytes 786440 | tf_op jit(solution)/shard_map/ppermute | solution.py:62
  168.1 9.9 %collective-permute-start.48 = (f16[2,32,1024]{2,1,0:T(8,128)(2,1)S(1)}, f16[2,32,1024]{2,1,0:T(8,128)(2,1)S(1)}, u32[]{:S(2)}, u32[]{:S(2)}) collective-permute-start(f16[2,32,1024]{2,1,0:T(8,128)(2,1)S(1)} %convert_element_type.178), channel_id=1, source_target_pairs={{0,8},{1,9},{2,10},{3,11},{4,12},{5,13},{6,14},{7,15},{8,0},{9,1},... | collective-permute-start | bytes 393224 | tf_op jit(solution)/shard_map/ppermute | solution.py:62
  169.7 7.7 %collective-permute-start.49 = (f32[64,64]{1,0:T(8,128)S(1)}, f32[64,64]{1,0:T(8,128)S(1)}, u32[]{:S(2)}, u32[]{:S(2)}) collective-permute-start(f32[64,64]{1,0:T(8,128)S(1)} %add.150), channel_id=1, source_target_pairs={{0,8},{1,9},{2,10},{3,11},{4,12},{5,13},{6,14},{7,15},{8,0},{9,1},... | collective-permute-start | bytes 49160 | tf_op jit(solution)/shard_map/ppermute | solution.py:62
  171.1 7.0 %collective-permute-start.47 = (f16[2,32,1024]{2,1,0:T(8,128)(2,1)S(1)}, f16[2,32,1024]{2,1,0:T(8,128)(2,1)S(1)}, u32[]{:S(2)}, u32[]{:S(2)}) collective-permute-start(f16[2,32,1024]{2,1,0:T(8,128)(2,1)S(1)} %convert_element_type.176), channel_id=1, source_target_pairs={{0,4},{1,5},{2,6},{3,7},{4,0},{5,1},{6,2},{7,3},{8,12},{9,13},{10,... | collective-permute-start | bytes 393224 | tf_op jit(solution)/shard_map/ppermute | solution.py:62
  178.2 6.9 %collective-permute-start.50 = (f16[32,1024]{1,0:T(8,128)(2,1)S(1)}, f16[32,1024]{1,0:T(8,128)(2,1)S(1)}, u32[]{:S(2)}, u32[]{:S(2)}) collective-permute-start(f16[32,1024]{1,0:T(8,128)(2,1)S(1)} %convert_element_type.180), channel_id=1, source_target_pairs={{0,2},{1,3},{2,0},{3,1},{4,6},{5,7},{6,4},{7,5},{8,10},{9,11},{10,... | collective-permute-start | bytes 196616 | tf_op jit(solution)/shard_map/ppermute | solution.py:62
  179.5 6.8 %collective-permute-start.51 = (f16[32,1024]{1,0:T(8,128)(2,1)S(1)}, f16[32,1024]{1,0:T(8,128)(2,1)S(1)}, u32[]{:S(2)}, u32[]{:S(2)}) collective-permute-start(f16[32,1024]{1,0:T(8,128)(2,1)S(1)} %convert_element_type.182), channel_id=1, source_target_pairs={{0,8},{1,9},{2,10},{3,11},{4,12},{5,13},{6,14},{7,15},{8,0},{9,1},... | collective-permute-start | bytes 196616 | tf_op jit(solution)/shard_map/ppermute | solution.py:62
  (13 other events, 55.4 us)

commit v11 on v9

--- a/solution.py
+++ b/solution.py
@@ -580,7 +580,7 @@
         last_kernel, "last", (strip, strip, square),
         along, fixed, cross_t, renewed, beta_t, alpha_t, total_weight, back_row, *base, *image,
     )
-    residual = rest - precise(on_panel, jnp.concatenate([panel_a, panel_b], axis=0))
+    residual = (rest - precise(on_panel[:, HALF:], panel_b)) - precise(on_panel[:, :HALF], panel_a)
     return (solved.T, residual.T)
 
 

time: 183 us -> 183 us (level)
  matrix products: 1.12 us -> 3.21 us
    dot_general x1 -> x2, matrix products: 1.12 us -> 3.21 us  [precise(): jnp.dot(left, right, precision=lax.Precision.HIGHEST, preferred_element_t...]
where the time goes in v11:
time: 183 us
  Pallas kernels  58.4 us (32%)
  starting transfers between devices  56.9 us (31%)
  waiting for transfers between devices  48.6 us (27%)
  other arithmetic  12.2 us (7%)
  matrix products  3.21 us (2%)
  local copies, waits for them, and re-layouts  2.01 us (1%)
    ppermute x49, starting transfers between devices, swap(): return lax.ppermute(value, 'dp', [(i, i ^ bit) for i in range(n)])  56.9 us
    ppermute x49, waiting for transfers between devices, swap(): return lax.ppermute(value, 'dp', [(i, i ^ bit) for i in range(n)])  48.6 us
    pallas_call x4, Pallas kernels, small(): pl.pallas_call(kernel, out_shape=tuple((jax.ShapeDtypeStruct(shape, F32)...  15.4 us
    pallas_call x2, Pallas kernels, probe_and_send(): near_call(functools.partial(send_kernel, s, count, d), 'probe_and_send',...  15.4 us
    pallas_call x2, Pallas kernels, load(): pl.pallas_call(load_kernel, out_shape=jax.ShapeDtypeStruct(acts.shape, ac...  9.44 us
    pallas_call x2, Pallas kernels, class_sums(): call(functools.partial(sums_kernel, half), 'class_sums', n, n // 2 // UNR...  7.03 us
    pallas_call x2, Pallas kernels, probe(): near_call(functools.partial(probe_kernel, count), 'probe', n, n // 2 // U...  6.46 us
    pallas_call x3, Pallas kernels, panel_keep(): near_call(keep_kernel, 'panel_keep', n, steps, [whole(K, rows), whole(1,...  4.78 us
  transfers between devices with their start and end apart: 49, of which 30 were waited for; matrix products, arithmetic and copies ran while one was open for 3% of the time, Pallas kernels for 22%

profile of v11, /device:TPU:0, one launch (start us, length us, event | category | flops | bytes accessed | tf_op | source)
XLA Modules:
  0.0 182.8 jit_solution(12881954508942981752)
XLA Ops:
  1.3 3.3 %class_sums.3 = (f32[8,64,1024]{2,1,0:T(8,128)S(1)}, f32[64,1]{1,0:T(8,128)S(1)}) custom-call(s32[1]{0:T(128)} %bitcast.me, s32[1,384]{1,0:T(1,128)S(1)} %reshape.50.row_data.refs_6_.refs_10_, bf16[384,16384]{1,0:T(8,128)(2,1)} %acts.5), custom_call_target="tpu_custom_call" | custom-call | flops 402653184 | bytes 8388608 | tf_op jit(solution)/shard_map/class_sums/pallas_call | solution.py:146
  6.3 3.7 %class_sums.2 = (f32[8,64,1024]{2,1,0:T(8,128)S(1)}, f32[64,1]{1,0:T(8,128)}) custom-call(s32[1]{0:T(128)} %bitcast.me, s32[1,384]{1,0:T(1,128)S(1)} %reshape.50.row_data.refs_6_.refs_10_, bf16[384,16384]{1,0:T(8,128)(2,1)} %acts.5), custom_call_target="tpu_custom_call" | custom-call | flops 402653184 | bytes 8388608 | tf_op jit(solution)/shard_map/class_sums/pallas_call | solution.py:146
  11.4 3.1 %collective-permute-start.3 = (f16[2,2,32,1024]{3,2,0,1:T(8,128)(2,1)S(1)}, f16[2,2,32,1024]{3,2,0,1:T(8,128)(2,1)S(1)}, u32[]{:S(2)}, u32[]{:S(2)}) collective-permute-start(f16[2,2,32,1024]{3,2,0,1:T(8,128)(2,1)S(1)} %fusion.6), channel_id=1, source_target_pairs={{0,4},{1,5},{2,6},{3,7},{4,0},{5,1},{6,2},{7,3},{8,12},{9,13},{10,... | collective-permute-start | bytes 786440 | tf_op jit(solution)/shard_map/ppermute | solution.py:62
  14.5 1.5 collective-permute-start.4
  18.0 3.0 %collective-permute-done.3 = f16[2,2,32,1024]{3,2,0,1:T(8,128)(2,1)S(1)} collective-permute-done((f16[2,2,32,1024]{3,2,0,1:T(8,128)(2,1)S(1)}, f16[2,2,32,1024]{3,2,0,1:T(8,128)(2,1)S(1)}, u32[]{:S(2)}, u32[]{:S(2)}) %collective-permute-start.3) | collective-permute-done | bytes 262176 | tf_op jit(solution)/shard_map/ppermute | solution.py:62
  21.1 2.9 %collective-permute-done.2 = f16[2,2,32,1024]{3,2,0,1:T(8,128)(2,1)S(1)} collective-permute-done((f16[2,2,32,1024]{3,2,0,1:T(8,128)(2,1)S(1)}, f16[2,2,32,1024]{3,2,0,1:T(8,128)(2,1)S(1)}, u32[]{:S(2)}, u32[]{:S(2)}) %collective-permute-start.2) | collective-permute-done | bytes 262176 | tf_op jit(solution)/shard_map/ppermute | solution.py:62
  24.8 2.7 %collective-permute-start.6 = (f16[2,32,1024]{2,1,0:T(8,128)(2,1)S(1)}, f16[2,32,1024]{2,1,0:T(8,128)(2,1)S(1)}, u32[]{:S(2)}, u32[]{:S(2)}) collective-permute-start(f16[2,32,1024]{2,1,0:T(8,128)(2,1)S(1)} %fusion.16), channel_id=1, source_target_pairs={{0,8},{1,9},{2,10},{3,11},{4,12},{5,13},{6,14},{7,15},{8,0},{9,1},... | collective-permute-start | bytes 393224 | tf_op jit(solution)/shard_map/ppermute | solution.py:62
  27.5 1.6 collective-permute-start.5
  29.2 3.2 %collective-permute-done.6 = f16[2,32,1024]{2,1,0:T(8,128)(2,1)S(1)} collective-permute-done((f16[2,32,1024]{2,1,0:T(8,128)(2,1)S(1)}, f16[2,32,1024]{2,1,0:T(8,128)(2,1)S(1)}, u32[]{:S(2)}, u32[]{:S(2)}) %collective-permute-start.6) | collective-permute-done | bytes 131104 | tf_op jit(solution)/shard_map/ppermute | solution.py:62
  34.7 2.2 %collective-permute-start.8 = (f16[32,1024]{1,0:T(8,128)(2,1)S(1)}, f16[32,1024]{1,0:T(8,128)(2,1)S(1)}, u32[]{:S(2)}, u32[]{:S(2)}) collective-permute-start(f16[32,1024]{1,0:T(8,128)(2,1)S(1)} %fusion.23), channel_id=1, source_target_pairs={{0,8},{1,9},{2,10},{3,11},{4,12},{5,13},{6,14},{7,15},{8,0},{9,1},... | collective-permute-start | bytes 196616 | tf_op jit(solution)/shard_map/ppermute | solution.py:62
  38.5 1.5 collective-permute-done.8
  41.6 2.2 %collective-permute-start.11 = (bf16[1,32,1024]{2,1,0:T(8,128)(2,1)S(1)}, bf16[1,32,1024]{2,1,0:T(8,128)(2,1)S(1)}, u32[]{:S(2)}, u32[]{:S(2)}) collective-permute-start(bf16[1,32,1024]{2,1,0:T(8,128)(2,1)S(1)} %get-tuple-element.122), channel_id=1, source_target_pairs={{0,8},{1,9},{2,10},{3,11},{4,12},{5,13},{6,14},{7,15},{8,0},{9,1},... | collective-permute-start | bytes 196616 | tf_op jit(solution)/shard_map/ppermute | solution.py:62
  45.1 1.8 collective-permute-done.11
  48.1 2.1 %collective-permute-start.13 = (bf16[2,32,1024]{2,1,0:T(8,128)(2,1)S(1)}, bf16[2,32,1024]{2,1,0:T(8,128)(2,1)S(1)}, u32[]{:S(2)}, u32[]{:S(2)}) collective-permute-start(bf16[2,32,1024]{2,1,0:T(8,128)(2,1)S(1)} %pad_maximum_fusion.8), channel_id=1, source_target_pairs={{0,4},{1,5},{2,6},{3,7},{4,0},{5,1},{6,2},{7,3},{8,12},{9,13},{10,... | collective-permute-start | bytes 393224 | tf_op jit(solution)/shard_map/ppermute | solution.py:62
  50.2 3.2 %collective-permute-start.14 = (bf16[2,32,1024]{2,1,0:T(8,128)(2,1)S(1)}, bf16[2,32,1024]{2,1,0:T(8,128)(2,1)S(1)}, u32[]{:S(2)}, u32[]{:S(2)}) collective-permute-start(bf16[2,32,1024]{2,1,0:T(8,128)(2,1)S(1)} %pad_maximum_fusion.9), channel_id=1, source_target_pairs={{0,8},{1,9},{2,10},{3,11},{4,12},{5,13},{6,14},{7,15},{8,0},{9,1},... | collective-permute-start | bytes 393224 | tf_op jit(solution)/shard_map/ppermute | solution.py:62
  53.6 3.3 %collective-permute-done.14 = bf16[2,32,1024]{2,1,0:T(8,128)(2,1)S(1)} collective-permute-done((bf16[2,32,1024]{2,1,0:T(8,128)(2,1)S(1)}, bf16[2,32,1024]{2,1,0:T(8,128)(2,1)S(1)}, u32[]{:S(2)}, u32[]{:S(2)}) %collective-permute-start.14) | collective-permute-done | bytes 131104 | tf_op jit(solution)/shard_map/ppermute | solution.py:62
  56.9 1.5 collective-permute-start.15
  58.4 3.5 %collective-permute-start.16 = (bf16[4,32,1024]{2,1,0:T(8,128)(2,1)S(1)}, bf16[4,32,1024]{2,1,0:T(8,128)(2,1)S(1)}, u32[]{:S(2)}, u32[]{:S(2)}) collective-permute-start(bf16[4,32,1024]{2,1,0:T(8,128)(2,1)S(1)} %pad_maximum_fusion.5), channel_id=1, source_target_pairs={{0,4},{1,5},{2,6},{3,7},{4,0},{5,1},{6,2},{7,3},{8,12},{9,13},{10,... | collective-permute-start | bytes 786440 | tf_op jit(solution)/shard_map/ppermute | solution.py:62
  62.0 4.7 %load.2.refs_4_.refs_5_.refs_0_.refs_1_ = bf16[384,16384]{1,0:T(8,128)(2,1)S(1)} custom-call(bf16[384,16384]{1,0:T(8,128)(2,1)} %acts.5), custom_call_target="tpu_custom_call" | custom-call | bytes 25165824 | tf_op jit(solution)/shard_map/load/pallas_call | solution.py:204
  67.4 3.1 %probe.2 = (f32[384,64]{1,0:T(8,128)S(1)}, f32[64,64]{1,0:T(8,128)S(1)}) custom-call(s32[1]{0:T(128)} %bitcast.me, bf16[8,32,1024]{2,1,0:T(8,128)(2,1)S(1)} %pad_maximum_fusion.refs_0_.refs_2_.refs_4_.refs_6_, bf16[8,32,1024]{2,1,0:T(8,128)(2,1)S(1)} %pad_maximum_fusion.1.refs_1_.refs_3_.refs_5_.refs_7_, ...), custom_call_target="tpu_custom_call" | custom-call | flops 402653184 | bytes 8388608 | tf_op jit(solution)/shard_map/probe/pallas_call | solution.py:254
  70.5 7.0 %probe_and_send.2 = (f32[64,384]{1,0:T(8,128)S(1)}, f32[64,64]{1,0:T(8,128)S(1)}, f32[64,1]{1,0:T(8,128)S(1)}, f32[64,1]{1,0:T(8,128)S(1)}, f32[1,64]{1,0:T(1,12...) custom-call(s32[1]{0:T(128)} %bitcast.me, ...), custom_call_target="tpu_custom_call" | custom-call | flops 402653184 | bytes 8388608 | tf_op jit(solution)/shard_map/probe_and_send/pallas_call | solution.py:343
  78.3 2.3 %panel_keep.3 = f32[8,64,1024]{2,1,0:T(8,128)S(1)} custom-call(s32[1]{0:T(128)} %bitcast.me, f32[64,384]{1,0:T(8,128)S(1)} %get-tuple-element.136.probed.refs_15_, s32[1,384]{1,0:T(1,128)S(1)} %reshape.50.row_data.refs_6_.refs_10_, f32[64,1]{1,0:T(8,128)S(1)} %get-tuple-element.137.inv, bf16[384,16384]{1,0:T(8,128)(2,1)S(1)} %load.2.refs_4_.refs_5_.refs_0_.refs_1_, ...), custom_call_target="tpu_custom_call" | custom-call | flops 402653184 | bytes 8388608 | tf_op jit(solution)/shard_map/panel_keep/pallas_call | solution.py:395
  81.4 1.6 collective-permute-start.22
  83.2 1.9 %collective-permute-start.21 = (f16[2,2,32,1024]{3,2,0,1:T(8,128)(2,1)S(1)}, f16[2,2,32,1024]{3,2,0,1:T(8,128)(2,1)S(1)}, u32[]{:S(2)}, u32[]{:S(2)}) collective-permute-start(f16[2,2,32,1024]{3,2,0,1:T(8,128)(2,1)S(1)} %convert_element_type.156), channel_id=1, source_target_pairs={{0,2},{1,3},{2,0},{3,1},{4,6},{5,7},{6,4},{7,5},{8,10},{9,11},{10,... | collective-permute-start | bytes 786440 | tf_op jit(solution)/shard_map/ppermute | solution.py:62
  85.2 2.2 %collective-permute-done.23 = f32[64,64]{1,0:T(8,128)S(1)} collective-permute-done((f32[64,64]{1,0:T(8,128)S(1)}, f32[64,64]{1,0:T(8,128)S(1)}, u32[]{:S(2)}, u32[]{:S(2)}) %collective-permute-start.23) | collective-permute-done | bytes 16416 | tf_op jit(solution)/shard_map/ppermute | solution.py:62
  87.3 2.4 %collective-permute-done.22 = f16[2,2,32,1024]{3,2,1,0:T(8,128)(2,1)S(1)} collective-permute-done((f16[2,2,32,1024]{3,2,1,0:T(8,128)(2,1)S(1)}, f16[2,2,32,1024]{3,2,1,0:T(8,128)(2,1)S(1)}, u32[]{:S(2)}, u32[]{:S(2)}) %collective-permute-start.22) | collective-permute-done | bytes 262176 | tf_op jit(solution)/shard_map/ppermute | solution.py:62
  89.9 1.9 %collective-permute-done.21 = f16[2,2,32,1024]{3,2,0,1:T(8,128)(2,1)S(1)} collective-permute-done((f16[2,2,32,1024]{3,2,0,1:T(8,128)(2,1)S(1)}, f16[2,2,32,1024]{3,2,0,1:T(8,128)(2,1)S(1)}, u32[]{:S(2)}, u32[]{:S(2)}) %collective-permute-start.21) | collective-permute-done | bytes 262176 | tf_op jit(solution)/shard_map/ppermute | solution.py:62
  93.1 1.5 collective-permute-start.25
  96.7 2.8 %offset.1 = f32[64,1024]{1,0:T(8,128)} custom-call(f32[32,1024]{1,0:T(8,128)} %get-tuple-element.147.base_a, f32[32,1024]{1,0:T(8,128)} %get-tuple-element.148.base_b, f32[64,64]{1,0:T(8,128)} %copy-done, f32[1,1]{1,0:T(1,128)} %bitcast.19.refs_7_.total_weight.refs_11_), custom_call_target="tpu_custom_call" | custom-call | flops 67108864 | bytes 1048576 | tf_op jit(solution)/shard_map/offset/pallas_call | solution.py:453
  99.5 1.7 collective-permute-done.25
  105.0 2.2 %collective-permute-start.27 = (f16[32,1024]{1,0:T(8,128)(2,1)S(1)}, f16[32,1024]{1,0:T(8,128)(2,1)S(1)}, u32[]{:S(2)}, u32[]{:S(2)}) collective-permute-start(f16[32,1024]{1,0:T(8,128)(2,1)S(1)} %convert_element_type.164), channel_id=1, source_target_pairs={{0,8},{1,9},{2,10},{3,11},{4,12},{5,13},{6,14},{7,15},{8,0},{9,1},... | collective-permute-start | bytes 196616 | tf_op jit(solution)/shard_map/ppermute | solution.py:62
  111.1 2.2 %collective-permute-start.30 = (bf16[1,32,1024]{2,1,0:T(8,128)(2,1)S(1)}, bf16[1,32,1024]{2,1,0:T(8,128)(2,1)S(1)}, u32[]{:S(2)}, u32[]{:S(2)}) collective-permute-start(bf16[1,32,1024]{2,1,0:T(8,128)(2,1)S(1)} %get-tuple-element.158), channel_id=1, source_target_pairs={{0,8},{1,9},{2,10},{3,11},{4,12},{5,13},{6,14},{7,15},{8,0},{9,1},... | collective-permute-start | bytes 196616 | tf_op jit(solution)/shard_map/ppermute | solution.py:62
  114.0 2.3 %collective-permute-done.30 = bf16[1,32,1024]{2,1,0:T(8,128)(2,1)S(1)} collective-permute-done((bf16[1,32,1024]{2,1,0:T(8,128)(2,1)S(1)}, bf16[1,32,1024]{2,1,0:T(8,128)(2,1)S(1)}, u32[]{:S(2)}, u32[]{:S(2)}) %collective-permute-start.30) | collective-permute-done | bytes 65568 | tf_op jit(solution)/shard_map/ppermute | solution.py:62
  120.0 4.4 %alpha.1 = (f32[64,64]{1,0:T(8,128)}, f32[64,64]{1,0:T(8,128)}) custom-call(f32[64,64]{1,0:T(8,128)} %add.130.along, f32[64,64]{1,0:T(8,128)} %copy-done, f32[1,1]{1,0:T(1,128)} %bitcast.19.refs_7_.total_weight.refs_11_), custom_call_target="tpu_custom_call" | custom-call | flops 67108864 | bytes 1048576 | tf_op jit(solution)/shard_map/alpha/pallas_call | solution.py:453
  124.5 1.6 collective-permute-done.33
  127.3 4.7 %load.3.refs_8_.refs_9_.refs_0_.refs_1_ = bf16[384,16384]{1,0:T(8,128)(2,1)S(1)} custom-call(bf16[384,16384]{1,0:T(8,128)(2,1)} %acts.5), custom_call_target="tpu_custom_call" | custom-call | bytes 25165824 | tf_op jit(solution)/shard_map/load/pallas_call | solution.py:204
  134.3 3.4 %probe.3 = (f32[384,64]{1,0:T(8,128)S(1)}, f32[64,64]{1,0:T(8,128)S(1)}, f32[64,64]{1,0:T(8,128)S(1)}) custom-call(s32[1]{0:T(128)} %bitcast.me, bf16[8,32,1024]{2,1,0:T(8,128)(2,1)S(1)} %pad_maximum_fusion.2.refs_0_.refs_2_, bf16[8,32,1024]{2,1,0:T(8,128)(2,1)S(1)} %pad_maximum_fusion.3.refs_1_.refs_3_, ...), custom_call_target="tpu_custom_call" | custom-call | flops 402653184 | bytes 8388608 | tf_op jit(solution)/shard_map/probe/pallas_call | solution.py:254
  137.7 8.4 %probe_and_send.3 = (f32[64,384]{1,0:T(8,128)S(1)}, f32[64,64]{1,0:T(8,128)S(1)}, f32[64,1]{1,0:T(8,128)S(1)}, f32[64,1]{1,0:T(8,128)}, f32[1,64]{1,0:T(1,128)S(...) custom-call(s32[1]{0:T(128)} %bitcast.me, ...), custom_call_target="tpu_custom_call" | custom-call | flops 402653184 | bytes 8388608 | tf_op jit(solution)/shard_map/probe_and_send/pallas_call | solution.py:343
  150.6 1.3 panel_keep.5
  151.9 1.6 collective-permute-done.40
  154.8 1.6 collective-permute-start.43
  157.5 4.8 %collective-permute-done.43 = f32[64,64]{1,0:T(8,128)S(1)} collective-permute-done((f32[64,64]{1,0:T(8,128)S(1)}, f32[64,64]{1,0:T(8,128)S(1)}, u32[]{:S(2)}, u32[]{:S(2)}) %collective-permute-start.43) | collective-permute-done | bytes 16416 | tf_op jit(solution)/shard_map/ppermute | solution.py:62
  163.3 1.7 collective-permute-start.45
  165.0 1.3 collective-permute-start.46
  166.8 2.6 %before.1 = (f32[64,64]{1,0:T(8,128)}, f32[64,64]{1,0:T(8,128)}) custom-call(f32[64,64]{1,0:T(8,128)} %copy-done, f32[64,64]{1,0:T(8,128)} %copy-done.3, f32[64,64]{1,0:T(8,128)} %copy-done.7, f32[64,64]{1,0:T(8,128)} %copy-done.4, f32[1,1]{1,0:T(1,128)} %bitcast.19.refs_7_.total_weight.refs_11_), custom_call_target="tpu_custom_call" | custom-call | flops 67108864 | bytes 1048576 | tf_op jit(solution)/shard_map/before/pallas_call | solution.py:453
  169.4 2.0 %collective-permute-done.46 = f32[64,64]{1,0:T(8,128)S(1)} collective-permute-done((f32[64,64]{1,0:T(8,128)S(1)}, f32[64,64]{1,0:T(8,128)S(1)}, u32[]{:S(2)}, u32[]{:S(2)}) %collective-permute-start.46) | collective-permute-done | bytes 16416 | tf_op jit(solution)/shard_map/ppermute | solution.py:62
  174.0 5.5 %last.1 = (f32[64,1024]{1,0:T(8,128)}, f32[64,1024]{1,0:T(8,128)}, f32[64,64]{1,0:T(8,128)}) custom-call(f32[64,64]{1,0:T(8,128)} %add.141.along, f32[64,64]{1,0:T(8,128)} %get-tuple-element.204.fixed, f32[64,64]{1,0:T(8,128)} %get-tuple-element.205.cross_t, f32[64,64]{1,0:T(8,128)} %copy-done.3, f32[64,64]{1,0:T(8,128)} %copy-done.4, ...), custom_call_target="tpu_custom_call" | custom-call | flops 67108864 | bytes 1048576 | tf_op jit(solution)/shard_map/last/pallas_call | solution.py:453
  180.7 2.0 %subtract_bitcast_fusion = f32[1024,64]{0,1:T(8,128)} fusion(f32[64,1024]{1,0:T(8,128)} %get-tuple-element.208, f32[64,1024]{1,0:T(8,128)S(1)} %fusion.35, f32[2,32,1024]{2,1,0:T(8,128)S(1)} %fusion.20, f16[32,1024]{1,0:T(8,128)(2,1)S(1)} %collective-permute-done.48, f32[64,64]{1,0:T(8,128)} %get-tuple-element.209), kind=kOutput, calls=%fused_computation.67 | convolution fusion | flops 25362432 | bytes 999424 | tf_op jit(solution)/shard_map/dot_general | solution.py:21
  (182 shorter events, 48.2 us)
Async XLA Ops:
  5.6 4.5 %collective-permute-start = (f16[8,64,1024]{2,1,0:T(8,128)(2,1)S(1)}, f16[8,64,1024]{2,1,0:T(8,128)(2,1)S(1)}, u32[]{:S(2)}, u32[]{:S(2)}) collective-permute-start(f16[8,64,1024]{2,1,0:T(8,128)(2,1)S(1)} %fusion), channel_id=1, source_target_pairs={{0,1},{1,0},{2,3},{3,2},{4,5},{5,4},{6,7},{7,6},{8,9},{9,8},{10,11... | collective-permute-start | bytes 3145736 | tf_op jit(solution)/shard_map/ppermute | solution.py:62
  6.2 3.8 %collective-permute-start.1 = (f32[1,64]{1,0:T(1,128)S(1)}, f32[1,64]{1,0:T(1,128)S(1)}, u32[]{:S(2)}, u32[]{:S(2)}) collective-permute-start(f32[1,64]{1,0:T(1,128)S(1)} %bitcast.162), channel_id=1, source_target_pairs={{0,1},{1,0},{2,3},{3,2},{4,5},{5,4},{6,7},{7,6},{8,9},{9,8},{10,11... | collective-permute-start | bytes 776 | tf_op jit(solution)/shard_map/ppermute | solution.py:62
  11.4 9.6 %collective-permute-start.3 = (f16[2,2,32,1024]{3,2,0,1:T(8,128)(2,1)S(1)}, f16[2,2,32,1024]{3,2,0,1:T(8,128)(2,1)S(1)}, u32[]{:S(2)}, u32[]{:S(2)}) collective-permute-start(f16[2,2,32,1024]{3,2,0,1:T(8,128)(2,1)S(1)} %fusion.6), channel_id=1, source_target_pairs={{0,4},{1,5},{2,6},{3,7},{4,0},{5,1},{6,2},{7,3},{8,12},{9,13},{10,... | collective-permute-start | bytes 786440 | tf_op jit(solution)/shard_map/ppermute | solution.py:62
  14.5 3.5 %collective-permute-start.4 = (f32[1,64]{1,0:T(1,128)S(1)}, f32[1,64]{1,0:T(1,128)S(1)}, u32[]{:S(2)}, u32[]{:S(2)}) collective-permute-start(f32[1,64]{1,0:T(1,128)S(1)} %bitcast_add_fusion), channel_id=1, source_target_pairs={{0,2},{1,3},{2,0},{3,1},{4,6},{5,7},{6,4},{7,5},{8,10},{9,11},{10,... | collective-permute-start | bytes 776 | tf_op jit(solution)/shard_map/ppermute | solution.py:62
  16.2 7.8 %collective-permute-start.2 = (f16[2,2,32,1024]{3,2,0,1:T(8,128)(2,1)S(1)}, f16[2,2,32,1024]{3,2,0,1:T(8,128)(2,1)S(1)}, u32[]{:S(2)}, u32[]{:S(2)}) collective-permute-start(f16[2,2,32,1024]{3,2,0,1:T(8,128)(2,1)S(1)} %fusion.3), channel_id=1, source_target_pairs={{0,2},{1,3},{2,0},{3,1},{4,6},{5,7},{6,4},{7,5},{8,10},{9,11},{10,... | collective-permute-start | bytes 786440 | tf_op jit(solution)/shard_map/ppermute | solution.py:62
  24.1 5.1 %collective-permute-start.7 = (f32[1,64]{1,0:T(1,128)S(1)}, f32[1,64]{1,0:T(1,128)S(1)}, u32[]{:S(2)}, u32[]{:S(2)}) collective-permute-start(f32[1,64]{1,0:T(1,128)S(1)} %add.113), channel_id=1, source_target_pairs={{0,4},{1,5},{2,6},{3,7},{4,0},{5,1},{6,2},{7,3},{8,12},{9,13},{10,... | collective-permute-start | bytes 776 | tf_op jit(solution)/shard_map/ppermute | solution.py:62
  24.8 7.6 %collective-permute-start.6 = (f16[2,32,1024]{2,1,0:T(8,128)(2,1)S(1)}, f16[2,32,1024]{2,1,0:T(8,128)(2,1)S(1)}, u32[]{:S(2)}, u32[]{:S(2)}) collective-permute-start(f16[2,32,1024]{2,1,0:T(8,128)(2,1)S(1)} %fusion.16), channel_id=1, source_target_pairs={{0,8},{1,9},{2,10},{3,11},{4,12},{5,13},{6,14},{7,15},{8,0},{9,1},... | collective-permute-start | bytes 393224 | tf_op jit(solution)/shard_map/ppermute | solution.py:62
  27.5 5.3 %collective-permute-start.5 = (f16[2,32,1024]{2,1,0:T(8,128)(2,1)S(1)}, f16[2,32,1024]{2,1,0:T(8,128)(2,1)S(1)}, u32[]{:S(2)}, u32[]{:S(2)}) collective-permute-start(f16[2,32,1024]{2,1,0:T(8,128)(2,1)S(1)} %fusion.13), channel_id=1, source_target_pairs={{0,4},{1,5},{2,6},{3,7},{4,0},{5,1},{6,2},{7,3},{8,12},{9,13},{10,... | collective-permute-start | bytes 393224 | tf_op jit(solution)/shard_map/ppermute | solution.py:62
  32.9 4.6 %collective-permute-start.10 = (f32[1,64]{1,0:T(1,128)S(1)}, f32[1,64]{1,0:T(1,128)S(1)}, u32[]{:S(2)}, u32[]{:S(2)}) collective-permute-start(f32[1,64]{1,0:T(1,128)S(1)} %add.116), channel_id=1, source_target_pairs={{0,8},{1,9},{2,10},{3,11},{4,12},{5,13},{6,14},{7,15},{8,0},{9,1},... | collective-permute-start | bytes 776 | tf_op jit(solution)/shard_map/ppermute | solution.py:62
  34.1 4.3 %collective-permute-start.9 = (f16[32,1024]{1,0:T(8,128)(2,1)S(1)}, f16[32,1024]{1,0:T(8,128)(2,1)S(1)}, u32[]{:S(2)}, u32[]{:S(2)}) collective-permute-start(f16[32,1024]{1,0:T(8,128)(2,1)S(1)} %fusion.26), channel_id=1, source_target_pairs={{0,2},{1,3},{2,0},{3,1},{4,6},{5,7},{6,4},{7,5},{8,10},{9,11},{10,... | collective-permute-start | bytes 196616 | tf_op jit(solution)/shard_map/ppermute | solution.py:62
  34.7 5.2 %collective-permute-start.8 = (f16[32,1024]{1,0:T(8,128)(2,1)S(1)}, f16[32,1024]{1,0:T(8,128)(2,1)S(1)}, u32[]{:S(2)}, u32[]{:S(2)}) collective-permute-start(f16[32,1024]{1,0:T(8,128)(2,1)S(1)} %fusion.23), channel_id=1, source_target_pairs={{0,8},{1,9},{2,10},{3,11},{4,12},{5,13},{6,14},{7,15},{8,0},{9,1},... | collective-permute-start | bytes 196616 | tf_op jit(solution)/shard_map/ppermute | solution.py:62
  41.6 5.3 %collective-permute-start.11 = (bf16[1,32,1024]{2,1,0:T(8,128)(2,1)S(1)}, bf16[1,32,1024]{2,1,0:T(8,128)(2,1)S(1)}, u32[]{:S(2)}, u32[]{:S(2)}) collective-permute-start(bf16[1,32,1024]{2,1,0:T(8,128)(2,1)S(1)} %get-tuple-element.122), channel_id=1, source_target_pairs={{0,8},{1,9},{2,10},{3,11},{4,12},{5,13},{6,14},{7,15},{8,0},{9,1},... | collective-permute-start | bytes 196616 | tf_op jit(solution)/shard_map/ppermute | solution.py:62
  43.8 4.3 %collective-permute-start.12 = (bf16[1,32,1024]{2,1,0:T(8,128)(2,1)S(1)}, bf16[1,32,1024]{2,1,0:T(8,128)(2,1)S(1)}, u32[]{:S(2)}, u32[]{:S(2)}) collective-permute-start(bf16[1,32,1024]{2,1,0:T(8,128)(2,1)S(1)} %get-tuple-element.123), channel_id=1, source_target_pairs={{0,2},{1,3},{2,0},{3,1},{4,6},{5,7},{6,4},{7,5},{8,10},{9,11},{10,... | collective-permute-start | bytes 196616 | tf_op jit(solution)/shard_map/ppermute | solution.py:62
  48.1 5.6 %collective-permute-start.13 = (bf16[2,32,1024]{2,1,0:T(8,128)(2,1)S(1)}, bf16[2,32,1024]{2,1,0:T(8,128)(2,1)S(1)}, u32[]{:S(2)}, u32[]{:S(2)}) collective-permute-start(bf16[2,32,1024]{2,1,0:T(8,128)(2,1)S(1)} %pad_maximum_fusion.8), channel_id=1, source_target_pairs={{0,4},{1,5},{2,6},{3,7},{4,0},{5,1},{6,2},{7,3},{8,12},{9,13},{10,... | collective-permute-start | bytes 393224 | tf_op jit(solution)/shard_map/ppermute | solution.py:62
  50.2 6.7 %collective-permute-start.14 = (bf16[2,32,1024]{2,1,0:T(8,128)(2,1)S(1)}, bf16[2,32,1024]{2,1,0:T(8,128)(2,1)S(1)}, u32[]{:S(2)}, u32[]{:S(2)}) collective-permute-start(bf16[2,32,1024]{2,1,0:T(8,128)(2,1)S(1)} %pad_maximum_fusion.9), channel_id=1, source_target_pairs={{0,8},{1,9},{2,10},{3,11},{4,12},{5,13},{6,14},{7,15},{8,0},{9,1},... | collective-permute-start | bytes 393224 | tf_op jit(solution)/shard_map/ppermute | solution.py:62
  56.9 9.8 %collective-permute-start.15 = (bf16[4,32,1024]{2,1,0:T(8,128)(2,1)S(1)}, bf16[4,32,1024]{2,1,0:T(8,128)(2,1)S(1)}, u32[]{:S(2)}, u32[]{:S(2)}) collective-permute-start(bf16[4,32,1024]{2,1,0:T(8,128)(2,1)S(1)} %pad_maximum_fusion.4), channel_id=1, source_target_pairs={{0,2},{1,3},{2,0},{3,1},{4,6},{5,7},{6,4},{7,5},{8,10},{9,11},{10,... | collective-permute-start | bytes 786440 | tf_op jit(solution)/shard_map/ppermute | solution.py:62
  58.4 8.3 %collective-permute-start.16 = (bf16[4,32,1024]{2,1,0:T(8,128)(2,1)S(1)}, bf16[4,32,1024]{2,1,0:T(8,128)(2,1)S(1)}, u32[]{:S(2)}, u32[]{:S(2)}) collective-permute-start(bf16[4,32,1024]{2,1,0:T(8,128)(2,1)S(1)} %pad_maximum_fusion.5), channel_id=1, source_target_pairs={{0,4},{1,5},{2,6},{3,7},{4,0},{5,1},{6,2},{7,3},{8,12},{9,13},{10,... | collective-permute-start | bytes 786440 | tf_op jit(solution)/shard_map/ppermute | solution.py:62
  66.8 3.7 %collective-permute-start.17 = (bf16[8,32,1024]{2,1,0:T(8,128)(2,1)S(1)}, bf16[8,32,1024]{2,1,0:T(8,128)(2,1)S(1)}, u32[]{:S(2)}, u32[]{:S(2)}) collective-permute-start(bf16[8,32,1024]{2,1,0:T(8,128)(2,1)S(1)} %pad_maximum_fusion.refs_0_.refs_2_.refs_4_.refs_6_), channel_id=1, source_target_pairs={{0,1},{1,0},{2,3},{3,2},{4,5},{5,4},{6,7},{7,6},{8,9},{9,8},{10,11... | collective-permute-start | bytes 1572872 | tf_op jit(solution)/shard_map/ppermute | solution.py:62
  66.9 3.6 %collective-permute-start.18 = (bf16[8,32,1024]{2,1,0:T(8,128)(2,1)S(1)}, bf16[8,32,1024]{2,1,0:T(8,128)(2,1)S(1)}, u32[]{:S(2)}, u32[]{:S(2)}) collective-permute-start(bf16[8,32,1024]{2,1,0:T(8,128)(2,1)S(1)} %pad_maximum_fusion.1.refs_1_.refs_3_.refs_5_.refs_7_), channel_id=1, source_target_pairs={{0,1},{1,0},{2,3},{3,2},{4,5},{5,4},{6,7},{7,6},{8,9},{9,8},{10,11... | collective-permute-start | bytes 1572872 | tf_op jit(solution)/shard_map/ppermute | solution.py:62
  77.7 3.0 %collective-permute-start.19 = (f16[8,64,1024]{2,1,0:T(8,128)(2,1)S(1)}, f16[8,64,1024]{2,1,0:T(8,128)(2,1)S(1)}, u32[]{:S(2)}, u32[]{:S(2)}) collective-permute-start(f16[8,64,1024]{2,1,0:T(8,128)(2,1)S(1)} %convert_element_type.154), channel_id=1, source_target_pairs={{0,1},{1,0},{2,3},{3,2},{4,5},{5,4},{6,7},{7,6},{8,9},{9,8},{10,11... | collective-permute-start | bytes 3145736 | tf_op jit(solution)/shard_map/ppermute | solution.py:62
  77.8 2.8 %collective-permute-start.20 = (f32[64,64]{1,0:T(8,128)S(1)}, f32[64,64]{1,0:T(8,128)S(1)}, u32[]{:S(2)}, u32[]{:S(2)}) collective-permute-start(f32[64,64]{1,0:T(8,128)S(1)} %get-tuple-element.139), channel_id=1, source_target_pairs={{0,1},{1,0},{2,3},{3,2},{4,5},{5,4},{6,7},{7,6},{8,9},{9,8},{10,11... | collective-permute-start | bytes 49160 | tf_op jit(solution)/shard_map/ppermute | solution.py:62
  81.4 8.4 %collective-permute-start.22 = (f16[2,2,32,1024]{3,2,1,0:T(8,128)(2,1)S(1)}, f16[2,2,32,1024]{3,2,1,0:T(8,128)(2,1)S(1)}, u32[]{:S(2)}, u32[]{:S(2)}) collective-permute-start(f16[2,2,32,1024]{3,2,1,0:T(8,128)(2,1)S(1)} %convert_element_type.158), channel_id=1, source_target_pairs={{0,4},{1,5},{2,6},{3,7},{4,0},{5,1},{6,2},{7,3},{8,12},{9,13},{10,... | collective-permute-start | bytes 786440 | tf_op jit(solution)/shard_map/ppermute | solution.py:62
  83.0 4.3 %collective-permute-start.23 = (f32[64,64]{1,0:T(8,128)S(1)}, f32[64,64]{1,0:T(8,128)S(1)}, u32[]{:S(2)}, u32[]{:S(2)}) collective-permute-start(f32[64,64]{1,0:T(8,128)S(1)} %add.121), channel_id=1, source_target_pairs={{0,2},{1,3},{2,0},{3,1},{4,6},{5,7},{6,4},{7,5},{8,10},{9,11},{10,... | collective-permute-start | bytes 49160 | tf_op jit(solution)/shard_map/ppermute | solution.py:62
  83.2 8.5 %collective-permute-start.21 = (f16[2,2,32,1024]{3,2,0,1:T(8,128)(2,1)S(1)}, f16[2,2,32,1024]{3,2,0,1:T(8,128)(2,1)S(1)}, u32[]{:S(2)}, u32[]{:S(2)}) collective-permute-start(f16[2,2,32,1024]{3,2,0,1:T(8,128)(2,1)S(1)} %convert_element_type.156), channel_id=1, source_target_pairs={{0,2},{1,3},{2,0},{3,1},{4,6},{5,7},{6,4},{7,5},{8,10},{9,11},{10,... | collective-permute-start | bytes 786440 | tf_op jit(solution)/shard_map/ppermute | solution.py:62
  91.9 7.6 %collective-permute-start.26 = (f32[64,64]{1,0:T(8,128)S(1)}, f32[64,64]{1,0:T(8,128)S(1)}, u32[]{:S(2)}, u32[]{:S(2)}) collective-permute-start(f32[64,64]{1,0:T(8,128)S(1)} %add.124), channel_id=1, source_target_pairs={{0,4},{1,5},{2,6},{3,7},{4,0},{5,1},{6,2},{7,3},{8,12},{9,13},{10,... | collective-permute-start | bytes 49160 | tf_op jit(solution)/shard_map/ppermute | solution.py:62
  93.1 8.1 %collective-permute-start.25 = (f16[2,32,1024]{2,1,0:T(8,128)(2,1)}, f16[2,32,1024]{2,1,0:T(8,128)(2,1)S(1)}, u32[]{:S(2)}, u32[]{:S(2)}) collective-permute-start(f16[2,32,1024]{2,1,0:T(8,128)(2,1)} %convert_element_type.162), channel_id=1, source_target_pairs={{0,8},{1,9},{2,10},{3,11},{4,12},{5,13},{6,14},{7,15},{8,0},{9,1},... | collective-permute-start | bytes 393224 | tf_op jit(solution)/shard_map/ppermute | solution.py:62
  95.9 5.8 %collective-permute-start.24 = (f16[2,32,1024]{2,1,0:T(8,128)(2,1)}, f16[2,32,1024]{2,1,0:T(8,128)(2,1)}, u32[]{:S(2)}, u32[]{:S(2)}) collective-permute-start(f16[2,32,1024]{2,1,0:T(8,128)(2,1)} %convert_element_type.160), channel_id=1, source_target_pairs={{0,4},{1,5},{2,6},{3,7},{4,0},{5,1},{6,2},{7,3},{8,12},{9,13},{10,... | collective-permute-start | bytes 393224 | tf_op jit(solution)/shard_map/ppermute | solution.py:62
  102.7 5.8 %collective-permute-start.29 = (f32[64,64]{1,0:T(8,128)S(1)}, f32[64,64]{1,0:T(8,128)S(1)}, u32[]{:S(2)}, u32[]{:S(2)}) collective-permute-start(f32[64,64]{1,0:T(8,128)S(1)} %add.127), channel_id=1, source_target_pairs={{0,8},{1,9},{2,10},{3,11},{4,12},{5,13},{6,14},{7,15},{8,0},{9,1},... | collective-permute-start | bytes 49160 | tf_op jit(solution)/shard_map/ppermute | solution.py:62
  103.9 5.2 %collective-permute-start.28 = (f16[32,1024]{1,0:T(8,128)(2,1)S(1)}, f16[32,1024]{1,0:T(8,128)(2,1)S(1)}, u32[]{:S(2)}, u32[]{:S(2)}) collective-permute-start(f16[32,1024]{1,0:T(8,128)(2,1)S(1)} %convert_element_type.166), channel_id=1, source_target_pairs={{0,2},{1,3},{2,0},{3,1},{4,6},{5,7},{6,4},{7,5},{8,10},{9,11},{10,... | collective-permute-start | bytes 196616 | tf_op jit(solution)/shard_map/ppermute | solution.py:62
  105.0 5.2 %collective-permute-start.27 = (f16[32,1024]{1,0:T(8,128)(2,1)S(1)}, f16[32,1024]{1,0:T(8,128)(2,1)S(1)}, u32[]{:S(2)}, u32[]{:S(2)}) collective-permute-start(f16[32,1024]{1,0:T(8,128)(2,1)S(1)} %convert_element_type.164), channel_id=1, source_target_pairs={{0,8},{1,9},{2,10},{3,11},{4,12},{5,13},{6,14},{7,15},{8,0},{9,1},... | collective-permute-start | bytes 196616 | tf_op jit(solution)/shard_map/ppermute | solution.py:62
  111.1 5.2 %collective-permute-start.30 = (bf16[1,32,1024]{2,1,0:T(8,128)(2,1)S(1)}, bf16[1,32,1024]{2,1,0:T(8,128)(2,1)S(1)}, u32[]{:S(2)}, u32[]{:S(2)}) collective-permute-start(bf16[1,32,1024]{2,1,0:T(8,128)(2,1)S(1)} %get-tuple-element.158), channel_id=1, source_target_pairs={{0,8},{1,9},{2,10},{3,11},{4,12},{5,13},{6,14},{7,15},{8,0},{9,1},... | collective-permute-start | bytes 196616 | tf_op jit(solution)/shard_map/ppermute | solution.py:62
  113.3 4.3 %collective-permute-start.31 = (bf16[1,32,1024]{2,1,0:T(8,128)(2,1)S(1)}, bf16[1,32,1024]{2,1,0:T(8,128)(2,1)S(1)}, u32[]{:S(2)}, u32[]{:S(2)}) collective-permute-start(bf16[1,32,1024]{2,1,0:T(8,128)(2,1)S(1)} %get-tuple-element.159), channel_id=1, source_target_pairs={{0,2},{1,3},{2,0},{3,1},{4,6},{5,7},{6,4},{7,5},{8,10},{9,11},{10,... | collective-permute-start | bytes 196616 | tf_op jit(solution)/shard_map/ppermute | solution.py:62
  117.6 6.8 %collective-permute-start.32 = (bf16[2,32,1024]{2,1,0:T(8,128)(2,1)S(1)}, bf16[2,32,1024]{2,1,0:T(8,128)(2,1)S(1)}, u32[]{:S(2)}, u32[]{:S(2)}) collective-permute-start(bf16[2,32,1024]{2,1,0:T(8,128)(2,1)S(1)} %pad_maximum_fusion.10), channel_id=1, source_target_pairs={{0,4},{1,5},{2,6},{3,7},{4,0},{5,1},{6,2},{7,3},{8,12},{9,13},{10,... | collective-permute-start | bytes 393224 | tf_op jit(solution)/shard_map/ppermute | solution.py:62
  118.7 7.4 %collective-permute-start.33 = (bf16[2,32,1024]{2,1,0:T(8,128)(2,1)S(1)}, bf16[2,32,1024]{2,1,0:T(8,128)(2,1)S(1)}, u32[]{:S(2)}, u32[]{:S(2)}) collective-permute-start(bf16[2,32,1024]{2,1,0:T(8,128)(2,1)S(1)} %pad_maximum_fusion.11), channel_id=1, source_target_pairs={{0,8},{1,9},{2,10},{3,11},{4,12},{5,13},{6,14},{7,15},{8,0},{9,1},... | collective-permute-start | bytes 393224 | tf_op jit(solution)/shard_map/ppermute | solution.py:62
  126.1 6.4 %collective-permute-start.34 = (bf16[4,32,1024]{2,1,0:T(8,128)(2,1)S(1)}, bf16[4,32,1024]{2,1,0:T(8,128)(2,1)S(1)}, u32[]{:S(2)}, u32[]{:S(2)}) collective-permute-start(bf16[4,32,1024]{2,1,0:T(8,128)(2,1)S(1)} %pad_maximum_fusion.6), channel_id=1, source_target_pairs={{0,2},{1,3},{2,0},{3,1},{4,6},{5,7},{6,4},{7,5},{8,10},{9,11},{10,... | collective-permute-start | bytes 786440 | tf_op jit(solution)/shard_map/ppermute | solution.py:62
  127.2 6.4 %collective-permute-start.35 = (bf16[4,32,1024]{2,1,0:T(8,128)(2,1)S(1)}, bf16[4,32,1024]{2,1,0:T(8,128)(2,1)S(1)}, u32[]{:S(2)}, u32[]{:S(2)}) collective-permute-start(bf16[4,32,1024]{2,1,0:T(8,128)(2,1)S(1)} %pad_maximum_fusion.7), channel_id=1, source_target_pairs={{0,4},{1,5},{2,6},{3,7},{4,0},{5,1},{6,2},{7,3},{8,12},{9,13},{10,... | collective-permute-start | bytes 786440 | tf_op jit(solution)/shard_map/ppermute | solution.py:62
  133.7 4.0 %collective-permute-start.36 = (bf16[8,32,1024]{2,1,0:T(8,128)(2,1)S(1)}, bf16[8,32,1024]{2,1,0:T(8,128)(2,1)S(1)}, u32[]{:S(2)}, u32[]{:S(2)}) collective-permute-start(bf16[8,32,1024]{2,1,0:T(8,128)(2,1)S(1)} %pad_maximum_fusion.2.refs_0_.refs_2_), channel_id=1, source_target_pairs={{0,1},{1,0},{2,3},{3,2},{4,5},{5,4},{6,7},{7,6},{8,9},{9,8},{10,11... | collective-permute-start | bytes 1572872 | tf_op jit(solution)/shard_map/ppermute | solution.py:62
  133.8 3.9 %collective-permute-start.37 = (bf16[8,32,1024]{2,1,0:T(8,128)(2,1)S(1)}, bf16[8,32,1024]{2,1,0:T(8,128)(2,1)S(1)}, u32[]{:S(2)}, u32[]{:S(2)}) collective-permute-start(bf16[8,32,1024]{2,1,0:T(8,128)(2,1)S(1)} %pad_maximum_fusion.3.refs_1_.refs_3_), channel_id=1, source_target_pairs={{0,1},{1,0},{2,3},{3,2},{4,5},{5,4},{6,7},{7,6},{8,9},{9,8},{10,11... | collective-permute-start | bytes 1572872 | tf_op jit(solution)/shard_map/ppermute | solution.py:62
  146.9 6.7 %collective-permute-start.39 = (f16[8,64,1024]{2,1,0:T(8,128)(2,1)S(1)}, f16[8,64,1024]{2,1,0:T(8,128)(2,1)S(1)}, u32[]{:S(2)}, u32[]{:S(2)}) collective-permute-start(f16[8,64,1024]{2,1,0:T(8,128)(2,1)S(1)} %convert_element_type.170), channel_id=1, source_target_pairs={{0,1},{1,0},{2,3},{3,2},{4,5},{5,4},{6,7},{7,6},{8,9},{9,8},{10,11... | collective-permute-start | bytes 3145736 | tf_op jit(solution)/shard_map/ppermute | solution.py:62
  149.7 3.9 %collective-permute-start.40 = (f32[64,64]{1,0:T(8,128)S(1)}, f32[64,64]{1,0:T(8,128)S(1)}, u32[]{:S(2)}, u32[]{:S(2)}) collective-permute-start(f32[64,64]{1,0:T(8,128)S(1)} %add.133), channel_id=1, source_target_pairs={{0,2},{1,3},{2,0},{3,1},{4,6},{5,7},{6,4},{7,5},{8,10},{9,11},{10,... | collective-permute-start | bytes 49160 | tf_op jit(solution)/shard_map/ppermute | solution.py:62
  154.3 8.0 %collective-permute-start.42 = (f16[2,2,32,1024]{3,2,1,0:T(8,128)(2,1)S(1)}, f16[2,2,32,1024]{3,2,1,0:T(8,128)(2,1)S(1)}, u32[]{:S(2)}, u32[]{:S(2)}) collective-permute-start(f16[2,2,32,1024]{3,2,1,0:T(8,128)(2,1)S(1)} %convert_element_type.174), channel_id=1, source_target_pairs={{0,4},{1,5},{2,6},{3,7},{4,0},{5,1},{6,2},{7,3},{8,12},{9,13},{10,... | collective-permute-start | bytes 786440 | tf_op jit(solution)/shard_map/ppermute | solution.py:62
  154.8 7.5 %collective-permute-start.43 = (f32[64,64]{1,0:T(8,128)S(1)}, f32[64,64]{1,0:T(8,128)S(1)}, u32[]{:S(2)}, u32[]{:S(2)}) collective-permute-start(f32[64,64]{1,0:T(8,128)S(1)} %add.135), channel_id=1, source_target_pairs={{0,4},{1,5},{2,6},{3,7},{4,0},{5,1},{6,2},{7,3},{8,12},{9,13},{10,... | collective-permute-start | bytes 49160 | tf_op jit(solution)/shard_map/ppermute | solution.py:62
  156.5 6.7 %collective-permute-start.41 = (f16[2,2,32,1024]{3,2,1,0:T(8,128)(2,1)S(1)}, f16[2,2,32,1024]{3,2,1,0:T(8,128)(2,1)S(1)}, u32[]{:S(2)}, u32[]{:S(2)}) collective-permute-start(f16[2,2,32,1024]{3,2,1,0:T(8,128)(2,1)S(1)} %convert_element_type.172), channel_id=1, source_target_pairs={{0,2},{1,3},{2,0},{3,1},{4,6},{5,7},{6,4},{7,5},{8,10},{9,11},{10,... | collective-permute-start | bytes 786440 | tf_op jit(solution)/shard_map/ppermute | solution.py:62
  163.3 8.7 %collective-permute-start.45 = (f16[2,32,1024]{2,1,0:T(8,128)(2,1)S(1)}, f16[2,32,1024]{2,1,0:T(8,128)(2,1)S(1)}, u32[]{:S(2)}, u32[]{:S(2)}) collective-permute-start(f16[2,32,1024]{2,1,0:T(8,128)(2,1)S(1)} %convert_element_type.178), channel_id=1, source_target_pairs={{0,8},{1,9},{2,10},{3,11},{4,12},{5,13},{6,14},{7,15},{8,0},{9,1},... | collective-permute-start | bytes 393224 | tf_op jit(solution)/shard_map/ppermute | solution.py:62
  165.0 6.4 %collective-permute-start.46 = (f32[64,64]{1,0:T(8,128)S(1)}, f32[64,64]{1,0:T(8,128)S(1)}, u32[]{:S(2)}, u32[]{:S(2)}) collective-permute-start(f32[64,64]{1,0:T(8,128)S(1)} %add.138), channel_id=1, source_target_pairs={{0,8},{1,9},{2,10},{3,11},{4,12},{5,13},{6,14},{7,15},{8,0},{9,1},... | collective-permute-start | bytes 49160 | tf_op jit(solution)/shard_map/ppermute | solution.py:62
  166.3 6.2 %collective-permute-start.44 = (f16[2,32,1024]{2,1,0:T(8,128)(2,1)S(1)}, f16[2,32,1024]{2,1,0:T(8,128)(2,1)S(1)}, u32[]{:S(2)}, u32[]{:S(2)}) collective-permute-start(f16[2,32,1024]{2,1,0:T(8,128)(2,1)S(1)} %convert_element_type.176), channel_id=1, source_target_pairs={{0,4},{1,5},{2,6},{3,7},{4,0},{5,1},{6,2},{7,3},{8,12},{9,13},{10,... | collective-permute-start | bytes 393224 | tf_op jit(solution)/shard_map/ppermute | solution.py:62
  172.6 7.0 %collective-permute-start.47 = (f16[32,1024]{1,0:T(8,128)(2,1)S(1)}, f16[32,1024]{1,0:T(8,128)(2,1)S(1)}, u32[]{:S(2)}, u32[]{:S(2)}) collective-permute-start(f16[32,1024]{1,0:T(8,128)(2,1)S(1)} %convert_element_type.180), channel_id=1, source_target_pairs={{0,2},{1,3},{2,0},{3,1},{4,6},{5,7},{6,4},{7,5},{8,10},{9,11},{10,... | collective-permute-start | bytes 196616 | tf_op jit(solution)/shard_map/ppermute | solution.py:62
  173.5 7.3 %collective-permute-start.48 = (f16[32,1024]{1,0:T(8,128)(2,1)S(1)}, f16[32,1024]{1,0:T(8,128)(2,1)S(1)}, u32[]{:S(2)}, u32[]{:S(2)}) collective-permute-start(f16[32,1024]{1,0:T(8,128)(2,1)S(1)} %convert_element_type.182), channel_id=1, source_target_pairs={{0,8},{1,9},{2,10},{3,11},{4,12},{5,13},{6,14},{7,15},{8,0},{9,1},... | collective-permute-start | bytes 196616 | tf_op jit(solution)/shard_map/ppermute | solution.py:62
  (10 other events, 34.9 us)
